TPU v7x, 32 devices: a whole 2x2x4 slice. The times are simulated.
32 devices in a mesh: rep: 2 (over x), key: 16 (over z, y, core).
Axes of the slice: x: 2, y: 2, z: 4, core: 2. Of those that a mesh axis runs over, the one named last changes fastest.
Arguments:
- query_tokens: bfloat16 [48, 256, 768], P('rep', 'key'), parts along dimension 0, may hold values from -110 to 110
- key_tokens: bfloat16 [48, 1024, 768], P('rep', 'key'), parts along dimension 0, may hold values from -6 to 6
- pair: bfloat16 [512, 1024, 128], P('rep', 'key'), parts along dimension 0, may hold values from -6 to 6
- key_mask: int32 [2048], P(('rep', 'key')), parts along dimension 0, may hold values 0 or 1
- span_owner: int32 [32], P('rep'), parts along dimension 0, may hold values from 0 to 15, each once
- pair_gain: float32 [128], replicated, may hold values from 0.1 to 1.9
- pair_proj: bfloat16 [128, 16], replicated, may hold values from -1 to 1
- w_query: bfloat16 [768, 768], replicated, may hold values from -0.21875 to 0.21875
- w_key: bfloat16 [768, 768], replicated, may hold values from -0.21875 to 0.21875
- w_value: bfloat16 [768, 768], replicated, may hold values from -0.21875 to 0.21875
- w_gate: bfloat16 [768, 768], replicated, may hold values from -0.21875 to 0.21875
- w_out: bfloat16 [768, 768], replicated, may hold values from -0.21875 to 0.21875
Outputs:
- attended: bfloat16 [48, 256, 768], P('rep', 'key'), parts along dimension 0
There are 2 independent parts, one for each index of `rep`. A program takes and returns all parts, laid end to end along the dimension named above; an argument that names none is the same for every part. Nothing has to cross between parts.
All inputs are finite; a program needn't handle non-finite values. No bound on the sum of `key_mask` on one device may be relied on, other than what follows from the above.
Results may differ from a plain program's by a relative error of at most 0.012.
The roundings to bfloat16 on the way count: a program that leaves them out, or rounds other values in their place, can miss the bound.
Values may be sent and summed in bfloat16 or wider, within the bound.
No kernel may reach another device: no remote copies, remote signals or barrier semaphores. Data moves between devices by JAX's collectives and lax.ppermute only.
A program may use at most 192 MiB of HBM per device.

v0:
```python
import functools
import math

import jax
import jax.numpy as jnp
from jax import lax
from jax.experimental import pallas as pl
from jax.experimental.pallas import tpu as pltpu
from jax.sharding import PartitionSpec as P


H = 16
LOG2E = 1.4426950408889634
NEG = -1e9
VMEM_LIMIT = 60 * 1024 * 1024
F32 = jnp.float32
BF16 = jnp.bfloat16


def nt_dot(a, b):
    return lax.dot_general(a, b, (((1,), (1,)), ((), ())), preferred_element_type=F32)


def nn_dot(a, b):
    return jnp.dot(a, b, preferred_element_type=F32)


def bias_kernel(hpg, mask_ref, pair_ref, gain_ref, proj_ref, *out_refs):
    fold, rows, keys, c = pair_ref.shape
    heads = proj_ref.shape[0]
    step = pl.program_id(0)
    total_rows = (out_refs[0].shape[0] - 16) // hpg
    x = jnp.swapaxes(pair_ref[...], 0, 1).reshape(rows * fold * keys, c).astype(F32)
    center = x - jnp.mean(x, axis=-1, keepdims=True)
    spread = jnp.mean(center * center, axis=-1, keepdims=True)
    normed = (center * lax.rsqrt(spread + 1e-5) * gain_ref[...]).astype(BF16)
    bias = nt_dot(proj_ref[...], normed)
    bias = bias.reshape(heads, rows, fold * keys).astype(BF16)
    for h in range(heads):
        start = pl.multiple_of((h % hpg) * total_rows + step * rows, 16)
        out_refs[h // hpg][pl.ds(start, rows), :] = bias[h]

    @pl.when(step == 0)
    def _():
        row = jnp.broadcast_to(mask_ref[...], (16, fold * keys)).astype(BF16)
        for out_ref in out_refs:
            out_ref[hpg * total_rows :, :] = row


def local_bias(pair, key_mask, pair_gain, proj_t, hpg):
    window, keys, c = pair.shape
    heads = proj_t.shape[0]
    fold = 128 // keys
    rows = window // fold
    tile = 16
    mask = jnp.tile(key_mask.astype(F32), fold)[None]
    shape = (hpg * rows + 16, 128)
    return pl.pallas_call(
        functools.partial(bias_kernel, hpg),
        grid=(rows // tile,),
        in_specs=[
            pl.BlockSpec((1, 128), lambda i: (0, 0)),
            pl.BlockSpec((fold, tile, keys, c), lambda i: (0, i, 0, 0)),
            pl.BlockSpec((1, c), lambda i: (0, 0)),
            pl.BlockSpec((heads, c), lambda i: (0, 0)),
        ],
        out_specs=[pl.BlockSpec(shape, lambda i: (0, 0))] * (heads // hpg),
        out_shape=[jax.ShapeDtypeStruct(shape, BF16)] * (heads // hpg),
        cost_estimate=pl.CostEstimate(
            flops=2 * window * keys * c * 256, bytes_accessed=window * keys * c * 2, transcendentals=0
        ),
        compiler_params=pltpu.CompilerParams(vmem_limit_bytes=VMEM_LIMIT),
        name="bias_local",
    )(mask, pair.reshape(fold, rows, keys, c), pair_gain[None], proj_t)


def pack_kernel(sizes, sg, group_ref, *refs):
    step = pl.program_id(0)
    start = 0
    for i, size in enumerate(sizes):

        @pl.when((step >= start) & (step < start + size))
        def _(i=i):
            for k in range(sg):
                out_ref = refs[(2 + i) * sg + k]
                keys = refs[k].shape[2]
                out_ref[0, :keys] = refs[k][0, 0]
                out_ref[0, keys:] = refs[sg + k][0, 0]

        start += size


def pack(group, key_groups, query_groups, first, sizes):
    sg, _, keys, width = key_groups.shape
    rows = query_groups.shape[2]
    total = sum(sizes)

    def spec(length, k):
        return pl.BlockSpec((1, 1, length, width), lambda s, g: (g[0] ^ k, first + s, 0, 0))

    def out_spec(i):
        start = sum(sizes[:i])
        return pl.BlockSpec(
            (1, keys + rows, width), lambda s, g: (jnp.clip(s - start, 0, sizes[i] - 1), 0, 0)
        )

    outs = pl.pallas_call(
        functools.partial(pack_kernel, sizes, sg),
        grid_spec=pltpu.PrefetchScalarGridSpec(
            num_scalar_prefetch=1,
            grid=(total,),
            in_specs=[spec(keys, k) for k in range(sg)] + [spec(rows, k) for k in range(sg)],
            out_specs=[out_spec(i) for i in range(len(sizes)) for _ in range(sg)],
        ),
        out_shape=[jax.ShapeDtypeStruct((size, keys + rows, width), BF16) for size in sizes for _ in range(sg)],
        cost_estimate=pl.CostEstimate(
            flops=0, bytes_accessed=4 * sg * total * (keys + rows) * width, transcendentals=0
        ),
        name="pack",
    )(group.reshape(1), *([key_groups] * sg), *([query_groups] * sg))
    return [outs[i * sg : (i + 1) * sg] for i in range(len(sizes))]


def stack_kernel(*refs):
    for i, ref in enumerate(refs[:-1]):
        refs[-1][i] = ref[...]


def stacked(parts):
    count, shape = len(parts), parts[0].shape
    rest = (0,) * (len(shape) - 1)
    block = (1,) + shape[1:] if len(shape) == 3 else shape
    steps = shape[0] if len(shape) == 3 else 1
    return pl.pallas_call(
        stack_kernel,
        grid=(steps,),
        in_specs=[pl.BlockSpec(block, lambda s: (s,) + rest)] * count,
        out_specs=pl.BlockSpec((count,) + block, lambda s: (0, s) + rest),
        out_shape=jax.ShapeDtypeStruct((count,) + shape, BF16),
        cost_estimate=pl.CostEstimate(
            flops=0, bytes_accessed=4 * count * math.prod(shape), transcendentals=0
        ),
        name="stack",
    )(*parts)


def order_kernel(hpg, keys, codes, me_ref, owner_ref, qsel_ref, *refs):
    parts, (bias_ref, mask_ref, inv_ref, x_ref) = refs[:-4], refs[-4:]
    n = len(codes)
    each = n // len(parts)
    for k, part_ref in enumerate(parts):
        x_ref[k * each : (k + 1) * each] = part_ref[...]
    fold = 128 // keys
    me = me_ref[0]
    rows = (x_ref.shape[1] - 16) // hpg
    slots = bias_ref.shape[1] // 16
    for d in range(n):
        inv_ref[owner_ref[d]] = d
    lane = lax.broadcasted_iota(jnp.int32, (16, 128), 1) // keys

    def of_tile(t):
        stored = [inv_ref[me ^ codes[t * fold + f]] ^ me for f in range(fold)]
        masks = x_ref[codes[t * fold], hpg * rows : hpg * rows + 16, :].astype(F32)
        for f in range(1, fold):
            part = x_ref[codes[t * fold + f], hpg * rows : hpg * rows + 16, :].astype(F32)
            masks = jnp.where(lane == f, part, masks)
        mask_ref[:, t * 128 : (t + 1) * 128] = masks[:8]
        return stored, masks > 0

    tiles = [of_tile(t) for t in range(n // fold)]

    def query_slot(p, carry):
        a = qsel_ref[p]
        part = a // (rows // 16)
        row = a % (rows // 16) * 16
        out = pl.multiple_of(p * 16, 16)
        for h in range(hpg):
            start = pl.multiple_of(h * rows + row, 16)
            for t, (stored, present) in enumerate(tiles):
                value = None
                for f in range(fold):
                    block = x_ref[stored[f], pl.ds(start, 16), :].astype(F32)
                    if fold == 2:
                        block = jnp.where(part == f, block, pltpu.roll(block, keys, 1))
                    value = block if value is None else jnp.where(lane == f, block, value)
                value = jnp.where(present, value * LOG2E, NEG * LOG2E)
                bias_ref[h, pl.ds(out, 16), t * 128 : (t + 1) * 128] = value
        return carry

    lax.fori_loop(0, slots, query_slot, 0)


def ordered_bias(parts, me, span_owner, qsel, hpg, keys, codes, window):
    n = len(codes)
    smem = pl.BlockSpec(memory_space=pltpu.SMEM)
    vmem = pl.BlockSpec(memory_space=pltpu.VMEM)
    return pl.pallas_call(
        functools.partial(order_kernel, hpg, keys, codes),
        in_specs=[smem, smem, smem] + [vmem] * len(parts),
        out_specs=[vmem, vmem],
        out_shape=[
            jax.ShapeDtypeStruct((hpg, window, n * keys), F32),
            jax.ShapeDtypeStruct((8, n * keys), F32),
        ],
        scratch_shapes=[
            pltpu.SMEM((n,), jnp.int32),
            pltpu.VMEM((n,) + parts[0].shape[1:], BF16),
        ],
        cost_estimate=pl.CostEstimate(
            flops=hpg * window * n * keys * 8, bytes_accessed=hpg * window * n * keys * 6, transcendentals=0
        ),
        compiler_params=pltpu.CompilerParams(vmem_limit_bytes=VMEM_LIMIT),
        name="bias_order",
    )(me.reshape(1), span_owner, qsel, *parts)


def attention_kernel(pieces, hpg, direct, keys, *refs):
    token_refs, refs = refs[:pieces], refs[pieces:]
    if not direct:
        query_ref, refs = refs[0], refs[1:]
    count = pieces if direct else 1
    bias_ref, mask_ref, wq_ref, wk_ref, wv_ref, wg_ref = refs[:6]
    out_refs, gate_ref = refs[6 : 6 + count], refs[6 + count]
    q_ref, k_ref, v_ref = refs[7 + count :]
    sg, _, _, width = token_refs[0].shape
    feats = wq_ref.shape[1]
    head_size = feats // hpg
    scale = LOG2E / math.sqrt(head_size)

    def rows_of(ref, start, stop):
        block = ref[:, 0, start:stop]
        return block.reshape(block.shape[0] * block.shape[1], width)

    for m in range(pieces):
        block = rows_of(token_refs[m], 0, keys)
        span = slice(m * sg * keys, (m + 1) * sg * keys)
        k_t = nt_dot(wk_ref[...], block)
        k_ref[:, span] = jnp.where(mask_ref[:1, span] > 0, k_t, 0.0).astype(BF16)
        v_ref[span, :] = nn_dot(block, wv_ref[...]).astype(BF16)
    if direct:
        for m in range(pieces):
            block = rows_of(token_refs[m], keys, token_refs[m].shape[2])
            span = slice(m * block.shape[0], (m + 1) * block.shape[0])
            q_ref[span, :] = nn_dot(block, wq_ref[...]).astype(BF16)
            if m == 0:
                gate_ref[0] = jax.nn.sigmoid(nn_dot(block, wg_ref[...]))
    else:
        q_ref[...] = nn_dot(query_ref[0], wq_ref[...]).astype(BF16)
        gate_ref[...] = jnp.zeros_like(gate_ref)
    q = q_ref[...]
    owner = lax.broadcasted_iota(jnp.int32, q.shape, 1) // head_size
    total = None
    for h in range(hpg):
        mine = owner == h
        scores = nn_dot(jnp.where(mine, q, jnp.zeros_like(q)), k_ref[...])
        scores = scores * scale + bias_ref[h]
        weights = jnp.exp2(scores - jnp.max(scores, axis=-1, keepdims=True))
        norm = 1.0 / jnp.sum(weights, axis=-1, keepdims=True)
        result = nn_dot((weights * norm).astype(BF16), v_ref[...])
        total = result if total is None else jnp.where(mine, result, total)
    rows = total.shape[0] // count
    for m in range(count):
        out_refs[m][0] = total[m * rows : (m + 1) * rows].astype(BF16)


def attention(arrays, queries, bias, mask, wq, wk_t, wv, w_gate, hpg, keys, query_rows):
    pieces = len(arrays)
    sg, size, rows, width = arrays[0].shape
    window = bias.shape[1]
    tokens = bias.shape[2]
    feats = wq.shape[1]
    direct = queries is None
    whole = pl.BlockSpec(memory_space=pltpu.VMEM)
    specs = [pl.BlockSpec((sg, 1, rows, width), lambda s: (0, s, 0, 0))] * pieces
    args = list(arrays)
    out_rows = [sg * query_rows] * pieces
    if not direct:
        specs.append(pl.BlockSpec((1, window, width), lambda s: (s, 0, 0)))
        args.append(queries)
        out_rows = [window]
    consts = [bias, mask, wq, wk_t, wv, w_gate]
    gate_rows = sg * query_rows
    limit = VMEM_LIMIT if tokens > 2048 else 36 * 1024 * 1024
    flops = 2 * size * (tokens * width * feats * 2 + hpg * window * tokens * 512)
    return pl.pallas_call(
        functools.partial(attention_kernel, pieces, hpg, direct, keys),
        grid=(size,),
        in_specs=specs + [whole] * len(consts),
        out_specs=[pl.BlockSpec((1, r, feats), lambda s: (s, 0, 0)) for r in out_rows]
        + [pl.BlockSpec((1, gate_rows, width), lambda s: (s, 0, 0))],
        out_shape=[jax.ShapeDtypeStruct((size, r, feats), BF16) for r in out_rows]
        + [jax.ShapeDtypeStruct((size, gate_rows, width), F32)],
        scratch_shapes=[
            pltpu.VMEM((window, feats), BF16),
            pltpu.VMEM((feats, tokens), BF16),
            pltpu.VMEM((tokens, feats), BF16),
        ],
        cost_estimate=pl.CostEstimate(
            flops=flops,
            bytes_accessed=size * tokens * width * 2 + hpg * window * tokens * 4,
            transcendentals=size * hpg * window * tokens,
        ),
        compiler_params=pltpu.CompilerParams(vmem_limit_bytes=limit),
        name="attend",
    )(*args, *consts)


def project_kernel(labels, sizes, lane_ref, *refs):
    count = len(labels)
    chunks = len(sizes)
    head_refs, refs = refs[: count * chunks], refs[count * chunks :]
    gate_refs, w_ref, refs = refs[:chunks], refs[chunks], refs[chunks + 1 :]
    out_refs, joined_ref = refs[:-1], refs[-1]
    lane = lane_ref[0]
    width = w_ref.shape[1]
    first = 0
    for c, size in enumerate(sizes):
        parts = head_refs[c * count : (c + 1) * count]
        _, rows, feats = parts[0].shape
        values = [ref[...].astype(F32).reshape(size * rows, feats) for ref in parts]
        for g in range(count):
            value = values[0]
            for label, other in zip(labels[1:], values[1:]):
                value = jnp.where(lane == g ^ label, other, value)
            joined_ref[: size * rows, g * feats : (g + 1) * feats] = value
        gate = gate_refs[c][...].reshape(size * rows, width)
        gated = (gate * joined_ref[: size * rows]).astype(BF16)
        result = nn_dot(gated, w_ref[...]).astype(BF16)
        result = result.reshape(size, len(out_refs), rows // len(out_refs), width)
        for k, out_ref in enumerate(out_refs):
            out_ref[first : first + size] = result[:, k]
        first += size


def projected(lane, heads, gates, w_out, labels, sg, query_rows):
    sizes = [x[0].shape[0] for x in heads]
    _, rows, _ = heads[0][0].shape
    width = w_out.shape[1]
    vmem = pl.BlockSpec(memory_space=pltpu.VMEM)
    flat = [x for chunk in heads for x in chunk]
    return pl.pallas_call(
        functools.partial(project_kernel, labels, sizes),
        in_specs=[pl.BlockSpec(memory_space=pltpu.SMEM)] + [vmem] * (len(flat) + len(gates) + 1),
        out_specs=[vmem] * sg,
        out_shape=[jax.ShapeDtypeStruct((sum(sizes), query_rows, width), BF16)] * sg,
        scratch_shapes=[pltpu.VMEM((max(sizes) * rows, width), F32)],
        cost_estimate=pl.CostEstimate(
            flops=2 * sum(sizes) * rows * width * width, bytes_accessed=2 * width * width, transcendentals=0
        ),
        name="project",
    )(lane.reshape(1), *flat, *gates, w_out)


def assemble_kernel(sg, firsts, group_ref, *refs):
    out_ref = refs[-1]
    group = group_ref[0]
    for i, ref in enumerate(refs[:-1]):
        first, k = firsts[i // sg], i % sg
        out_ref[group ^ k, first : first + ref.shape[0]] = ref[...]


def assembled(group, parts, firsts, shape):
    vmem = pl.BlockSpec(memory_space=pltpu.VMEM)
    return pl.pallas_call(
        functools.partial(assemble_kernel, shape[0], firsts),
        in_specs=[pl.BlockSpec(memory_space=pltpu.SMEM)] + [vmem] * len(parts),
        out_specs=vmem,
        out_shape=jax.ShapeDtypeStruct(shape, BF16),
        name="assemble",
    )(group.reshape(1), *parts)


def head_groups(n, samples):
    hg = 1
    while hg * hg < n or H % hg or samples % (n // hg):
        hg *= 2
    return hg


def local(
    query_tokens,
    key_tokens,
    pair,
    key_mask,
    span_owner,
    pair_gain,
    pair_proj,
    w_query,
    w_key,
    w_value,
    w_gate,
    w_out,
):
    n = lax.axis_size("key")
    samples, query_rows, width = query_tokens.shape
    keys = key_tokens.shape[1]
    window = pair.shape[0]
    hg = head_groups(n, samples)
    sg = n // hg
    hpg = H // hg
    feats = width // hg
    group_samples = samples // sg
    last = max(group_samples // 6, 1)
    middle = max(group_samples // 3, 1)
    sizes = [group_samples - middle - last, middle, last]
    firsts = [sum(sizes[:c]) for c in range(len(sizes))]
    direct = query_rows % 16 == 0
    me = lax.axis_index("key")
    group, lane = me // hg, me % hg

    def across(x, code):
        if code == 0:
            return x
        return lax.ppermute(x, "key", [(i, i ^ code) for i in range(n)])

    labels = [0]
    bit = hg // 2
    while bit:
        labels = labels + [m ^ bit for m in labels]
        bit //= 2
    codes = [k * hg + m for m in labels for k in range(sg)]
    code_list = jnp.array(codes, jnp.int32)
    slot_of = [0] * n
    for p, code in enumerate(codes):
        slot_of[code] = p

    key_groups = key_tokens.reshape(sg, group_samples, keys, width)
    query_groups = query_tokens.reshape(sg, group_samples, query_rows, width)

    packed = pack(group, key_groups, query_groups, 0, sizes[:1])
    packed = packed + pack(group, key_groups, query_groups, firsts[1], sizes[1:])
    got = [[across(x, k * hg) for k, x in enumerate(sent)] for sent in packed]

    relative = jnp.arange(hg) ^ lane
    proj_t = jnp.take(pair_proj.T.reshape(hg, hpg, -1), relative, axis=0).reshape(H, -1)
    pieces = local_bias(pair, key_mask, pair_gain, proj_t, hpg)
    pieces = [across(x, m) for m, x in enumerate(pieces)]
    parts = {0: stacked(pieces)}
    bit = sg // 2
    while bit:
        parts.update({k ^ bit: across(x, bit * hg) for k, x in parts.items()})
        bit //= 2
    if direct:
        each = query_rows // 16
        qsel = ((code_list ^ me)[:, None] * each + jnp.arange(each)).reshape(window // 16)
    else:
        qsel = jnp.arange(window // 16, dtype=jnp.int32)
    bias, mask = ordered_bias(
        [parts[k] for k in range(sg)], me, span_owner, qsel, hpg, keys, codes, window
    )

    def own(w):
        return lax.dynamic_slice_in_dim(w, lane * feats, feats, 1)

    wq, wk_t, wv = own(w_query), own(w_key).T, own(w_value)

    heads, gates = [], []
    previous = None
    for c, size in enumerate(sizes):
        arrays = [stacked(got[c])]
        bit = hg // 2
        while bit:
            arrays = arrays + [across(x, bit) for x in arrays]
            bit //= 2
        queries = None
        if not direct:
            order = jnp.array(slot_of, jnp.int32)[me ^ jnp.arange(n)]
            queries = jnp.concatenate([x[:, :, keys:] for x in arrays], axis=0)
            queries = jnp.swapaxes(jnp.take(queries, order, axis=0), 0, 1).reshape(size, window, width)
        if previous is not None:
            arrays, previous = lax.optimization_barrier((arrays, previous))
        results = attention(arrays, queries, bias, mask, wq, wk_t, wv, w_gate, hpg, keys, query_rows)
        results, gate = results[:-1], results[-1]
        previous = gate
        if not direct:
            blocks = jnp.take(results[0].reshape(size, n, query_rows, feats), code_list ^ me, axis=1)
            results = [
                blocks[:, i * sg : (i + 1) * sg].reshape(size, sg * query_rows, feats) for i in range(hg)
            ]
            tokens = jnp.swapaxes(arrays[0][:, :, keys:], 0, 1).reshape(size, sg * query_rows, width)
            gate = jax.nn.sigmoid(nn_dot(tokens, w_gate))
        heads.append([across(r, m) for r, m in zip(results, labels)])
        gates.append(gate)
    outs = []
    cut = len(sizes) - 1
    for span in (slice(0, cut), slice(cut, cut + 1)):
        back = projected(lane, heads[span], gates[span], w_out, labels, sg, query_rows)
        outs.extend(across(x, k * hg) for k, x in enumerate(back))
    out = assembled(group, outs, [0, firsts[cut]], (sg, group_samples, query_rows, width))
    return out.reshape(samples, query_rows, width)


def solution(mesh):
    return jax.shard_map(
        local,
        mesh=mesh,
        in_specs=(
            P("rep", "key", None),
            P("rep", "key", None),
            P("rep", "key", None),
            P(("rep", "key")),
            P("rep"),
            P(),
            P(),
            P(),
            P(),
            P(),
            P(),
            P(),
        ),
        out_specs=P("rep", "key", None),
        check_vma=False,
    )
```

profile of v0, /device:TPU:0, one launch (start us, length us, event | category | flops | bytes accessed | tf_op | source)
XLA Modules:
  0.0 241.9 jit_solution(11402856378488923909)
XLA Ops:
  0.0 3.5 %pack.2 = (bf16[3,80,768]{2,1,0:T(8,128)(2,1)}, bf16[3,80,768]{2,1,0:T(8,128)(2,1)}, bf16[3,80,768]{2,1,0:T(8,128)(2,1)}, bf16[3,80,768]{2,1,0:T(8,128)(2,1)}) custom-call(s32[1]{0:T(128)} %bitcast.group_ref, bf16[4,6,64,768]{3,2,1,0:T(8,128)(2,1)} %bitcast.18, bf16[4,6,64,768]{3,2,1,0:T(8,128)(2,1)} %bitcast.19, bf16[4,6,64,768]{3,2,1,0:T(8,128)(2,1)} %bitcast.20, ...), custom_call_target="tpu_custom_call" | custom-call | bytes 2949120 | tf_op jit(solution)/shard_map/pack/pallas_call | solution.py:107
  3.5 3.1 %collective-permute-start = (bf16[3,80,768]{2,1,0:T(8,128)(2,1)}, bf16[3,80,768]{2,1,0:T(8,128)(2,1)S(1)}, u32[]{:S(2)}, u32[]{:S(2)}) collective-permute-start(bf16[3,80,768]{2,1,0:T(8,128)(2,1)} %get-tuple-element.55), channel_id=1, source_target_pairs={{0,4},{1,5},{2,6},{3,7},{4,0},{5,1},{6,2},{7,3},{8,12},{9,13},{10,... | collective-permute-start | bytes 1105928 | tf_op jit(solution)/shard_map/ppermute | solution.py:414
  6.6 2.6 %collective-permute-start.1 = (bf16[3,80,768]{2,1,0:T(8,128)(2,1)}, bf16[3,80,768]{2,1,0:T(8,128)(2,1)S(1)}, u32[]{:S(2)}, u32[]{:S(2)}) collective-permute-start(bf16[3,80,768]{2,1,0:T(8,128)(2,1)} %get-tuple-element.56), channel_id=1, source_target_pairs={{0,8},{1,9},{2,10},{3,11},{4,12},{5,13},{6,14},{7,15},{8,0},{9,1},... | collective-permute-start | bytes 1105928 | tf_op jit(solution)/shard_map/ppermute | solution.py:414
  9.2 13.4 %collective-permute-done.refs_1_ = bf16[3,80,768]{2,1,0:T(8,128)(2,1)S(1)} collective-permute-done((bf16[3,80,768]{2,1,0:T(8,128)(2,1)}, bf16[3,80,768]{2,1,0:T(8,128)(2,1)S(1)}, u32[]{:S(2)}, u32[]{:S(2)}) %collective-permute-start) | collective-permute-done | bytes 368672 | tf_op jit(solution)/shard_map/ppermute | solution.py:414
  22.6 12.4 %collective-permute-done.1.refs_2_ = bf16[3,80,768]{2,1,0:T(8,128)(2,1)S(1)} collective-permute-done((bf16[3,80,768]{2,1,0:T(8,128)(2,1)}, bf16[3,80,768]{2,1,0:T(8,128)(2,1)S(1)}, u32[]{:S(2)}, u32[]{:S(2)}) %collective-permute-start.1) | collective-permute-done | bytes 368672 | tf_op jit(solution)/shard_map/ppermute | solution.py:414
  35.9 3.4 %stack.4.refs_0_ = bf16[4,3,80,768]{3,2,1,0:T(8,128)(2,1)} custom-call(bf16[3,80,768]{2,1,0:T(8,128)(2,1)} %get-tuple-element.54.refs_0_, bf16[3,80,768]{2,1,0:T(8,128)(2,1)} %copy-done.25, bf16[3,80,768]{2,1,0:T(8,128)(2,1)} %copy-done.26, bf16[3,80,768]{2,1,0:T(8,128)(2,1)} %copy-done.27), custom_call_target="tpu_custom_call" | custom-call | bytes 2949120 | tf_op jit(solution)/shard_map/stack/pallas_call | solution.py:134
  42.8 9.0 %bias_local.1 = (bf16[528,128]{1,0:T(8,128)(2,1)}, bf16[528,128]{1,0:T(8,128)(2,1)}, bf16[528,128]{1,0:T(8,128)(2,1)}, bf16[528,128]{1,0:T(8,128)(2,1)}) custom-call(f32[1,128]{1,0:T(1,128)} %broadcast_in_dim_tile.3.mask_ref, bf16[2,128,64,128]{3,2,1,0:T(8,128)(2,1)} %bitcast.34, f32[1,128]{1,0:T(1,128)} %bitcast.37, ...), custom_call_target="tpu_custom_call" | custom-call | flops 1073741824 | bytes 4194304 | tf_op jit(solution)/shard_map/bias_local/pallas_call | solution.py:58
  52.4 3.4 %pack.3 = (bf16[2,80,768]{2,1,0:T(8,128)(2,1)}, bf16[2,80,768]{2,1,0:T(8,128)(2,1)}, bf16[2,80,768]{2,1,0:T(8,128)(2,1)}, bf16[2,80,768]{2,1,0:T(8,128)(2,1)}, b...) custom-call(s32[1]{0:T(128)} %bitcast.group_ref, ...), custom_call_target="tpu_custom_call" | custom-call | bytes 2949120 | tf_op jit(solution)/shard_map/pack/pallas_call | solution.py:107
  55.9 7.0 %collective-permute-start.15 = (bf16[2,80,768]{2,1,0:T(8,128)(2,1)}, bf16[2,80,768]{2,1,0:T(8,128)(2,1)S(1)}, u32[]{:S(2)}, u32[]{:S(2)}) collective-permute-start(bf16[2,80,768]{2,1,0:T(8,128)(2,1)} %get-tuple-element.69), channel_id=1, source_target_pairs={{0,4},{1,5},{2,6},{3,7},{4,0},{5,1},{6,2},{7,3},{8,12},{9,13},{10,... | collective-permute-start | bytes 737288 | tf_op jit(solution)/shard_map/ppermute | solution.py:414
  65.4 8.4 %collective-permute-done.7.refs_2_ = bf16[528,128]{1,0:T(8,128)(2,1)S(1)} collective-permute-done((bf16[528,128]{1,0:T(8,128)(2,1)}, bf16[528,128]{1,0:T(8,128)(2,1)S(1)}, u32[]{:S(2)}, u32[]{:S(2)}) %collective-permute-start.7) | collective-permute-done | bytes 135200 | tf_op jit(solution)/shard_map/ppermute | solution.py:414
  73.9 5.8 %collective-permute-done.8.refs_3_ = bf16[528,128]{1,0:T(8,128)(2,1)S(1)} collective-permute-done((bf16[528,128]{1,0:T(8,128)(2,1)S(1)}, bf16[528,128]{1,0:T(8,128)(2,1)S(1)}, u32[]{:S(2)}, u32[]{:S(2)}) %collective-permute-start.8) | collective-permute-done | bytes 135200 | tf_op jit(solution)/shard_map/ppermute | solution.py:414
  82.3 9.5 %collective-permute-start.10 = (bf16[4,528,128]{2,1,0:T(8,128)(2,1)}, bf16[4,528,128]{2,1,0:T(8,128)(2,1)S(1)}, u32[]{:S(2)}, u32[]{:S(2)}) collective-permute-start(bf16[4,528,128]{2,1,0:T(8,128)(2,1)} %stack.5.refs_0_), channel_id=1, source_target_pairs={{0,8},{1,9},{2,10},{3,11},{4,12},{5,13},{6,14},{7,15},{8,0},{9,1},... | collective-permute-start | bytes 1622024 | tf_op jit(solution)/shard_map/ppermute | solution.py:414
  92.7 2.1 stack.6.refs_0_
  96.0 10.6 %collective-permute-done.27.refs_1_ = bf16[1,80,768]{2,1,0:T(8,128)(2,1)S(1)} collective-permute-done((bf16[1,80,768]{2,1,0:T(8,128)(2,1)S(1)}, bf16[1,80,768]{2,1,0:T(8,128)(2,1)S(1)}, u32[]{:S(2)}, u32[]{:S(2)}) %collective-permute-start.27) | collective-permute-done | bytes 122912 | tf_op jit(solution)/shard_map/ppermute | solution.py:414
  106.5 2.4 collective-permute-start.28
  108.9 12.5 %collective-permute-done.28.refs_2_ = bf16[1,80,768]{2,1,0:T(8,128)(2,1)S(1)} collective-permute-done((bf16[1,80,768]{2,1,0:T(8,128)(2,1)S(1)}, bf16[1,80,768]{2,1,0:T(8,128)(2,1)S(1)}, u32[]{:S(2)}, u32[]{:S(2)}) %collective-permute-start.28) | collective-permute-done | bytes 122912 | tf_op jit(solution)/shard_map/ppermute | solution.py:414
  122.8 5.3 %collective-permute-done.29.refs_3_ = bf16[1,80,768]{2,1,0:T(8,128)(2,1)S(1)} collective-permute-done((bf16[1,80,768]{2,1,0:T(8,128)(2,1)S(1)}, bf16[1,80,768]{2,1,0:T(8,128)(2,1)S(1)}, u32[]{:S(2)}, u32[]{:S(2)}) %collective-permute-start.29) | collective-permute-done | bytes 122912 | tf_op jit(solution)/shard_map/ppermute | solution.py:414
  130.2 13.1 %collective-permute-done.9.refs_1_ = bf16[4,528,128]{2,1,0:T(8,128)(2,1)S(1)} collective-permute-done((bf16[4,528,128]{2,1,0:T(8,128)(2,1)S(1)}, bf16[4,528,128]{2,1,0:T(8,128)(2,1)S(1)}, u32[]{:S(2)}, u32[]{:S(2)}) %collective-permute-start.9) | collective-permute-done | bytes 540704 | tf_op jit(solution)/shard_map/ppermute | solution.py:414
  146.5 5.9 %collective-permute-done.11.refs_3_ = bf16[4,528,128]{2,1,0:T(8,128)(2,1)S(1)} collective-permute-done((bf16[4,528,128]{2,1,0:T(8,128)(2,1)S(1)}, bf16[4,528,128]{2,1,0:T(8,128)(2,1)S(1)}, u32[]{:S(2)}, u32[]{:S(2)}) %collective-permute-start.11) | collective-permute-done | bytes 540704 | tf_op jit(solution)/shard_map/ppermute | solution.py:414
  155.7 6.4 %bias_order.1 = (f32[4,256,1024]{2,1,0:T(8,128)}, f32[8,1024]{1,0:T(8,128)}) custom-call(s32[1]{0:T(128)} %bitcast.4.me_ref, s32[16]{0:T(128)} %owner_ref.1, s32[16]{0:T(128)} %broadcast_xor_fusion.qsel_ref, bf16[4,528,128]{2,1,0:T(8,128)(2,1)} %stack.5.refs_0_, bf16[4,528,128]{2,1,0:T(8,128)(2,1)} %copy-done.23, bf16[4,528,128]{2,1,0:T(8,128)(2,1)} %copy-done.22, ...), custom_call_target="tpu_custom_call" | custom-call | flops 8388608 | bytes 6291456 | tf_op jit(solution)/shard_map/bias_order/pallas_call | solution.py:197
  163.8 2.2 copy-done.1
  168.1 12.1 %attend.3 = (bf16[3,64,192]{2,1,0:T(8,128)(2,1)S(1)}, bf16[3,64,192]{2,1,0:T(8,128)(2,1)S(1)}, bf16[3,64,192]{2,1,0:T(8,128)(2,1)S(1)}, bf16[3,64,192]{2,1,0:T(8,128)(2,1)S(1)}, f32[3,64,768]{2,1,0:T(8,128)S(1)}) custom-call(bf16[4,3,80,768]{3,2,1,0:T(8,128)(2,1)} %stack.4.refs_0_, bf16[4,3,80,768]{3,2,1,0:T(8,128)(2,1)} %collective-permute-done.3.refs_1_, ...), custom_call_target="tpu_custom_call" | custom-call | flops 5033164800 | bytes 8912896 | tf_op jit(solution)/shard_map/attend/pallas_call | solution.py:285
  180.8 8.6 %attend.4 = (bf16[2,64,192]{2,1,0:T(8,128)(2,1)S(1)}, bf16[2,64,192]{2,1,0:T(8,128)(2,1)S(1)}, bf16[2,64,192]{2,1,0:T(8,128)(2,1)S(1)}, bf16[2,64,192]{2,1,0:T(8,128)(2,1)S(1)}, f32[2,64,768]{2,1,0:T(8,128)S(1)}) custom-call(bf16[4,2,80,768]{3,2,1,0:T(8,128)(2,1)S(1)} %copy-done.8, bf16[4,2,80,768]{3,2,1,0:T(8,128)(2,1)} %collective-permute-done.18.refs_1_, ...), custom_call_target="tpu_custom_call" | custom-call | flops 3355443200 | bytes 7340032 | tf_op jit(solution)/shard_map/attend/pallas_call | solution.py:285
  196.8 3.5 %collective-permute-done.23.refs_7_ = bf16[2,64,192]{2,1,0:T(8,128)(2,1)S(1)} collective-permute-done((bf16[2,64,192]{2,1,0:T(8,128)(2,1)S(1)}, bf16[2,64,192]{2,1,0:T(8,128)(2,1)S(1)}, u32[]{:S(2)}, u32[]{:S(2)}) %collective-permute-start.23) | collective-permute-done | bytes 49184 | tf_op jit(solution)/shard_map/ppermute | solution.py:414
  201.0 3.4 %project.2 = (bf16[5,16,768]{2,1,0:T(8,128)(2,1)}, bf16[5,16,768]{2,1,0:T(8,128)(2,1)}, bf16[5,16,768]{2,1,0:T(8,128)(2,1)}, bf16[5,16,768]{2,1,0:T(8,128)(2,1)}) custom-call(s32[1]{0:T(128)} %bitcast.1.lane_ref, bf16[3,64,192]{2,1,0:T(8,128)(2,1)} %copy-done.16, bf16[3,64,192]{2,1,0:T(8,128)(2,1)} %copy-done.39, bf16[3,64,192]{2,1,0:T(8,128)(2,1)} %copy-done.40, ...), custom_call_target="tpu_custom_call" | custom-call | flops 377487360 | bytes 1179648 | tf_op jit(solution)/shard_map/project/pallas_call | solution.py:341
  206.3 2.5 %collective-permute-start.26 = (bf16[5,16,768]{2,1,0:T(8,128)(2,1)}, bf16[5,16,768]{2,1,0:T(8,128)(2,1)}, u32[]{:S(2)}, u32[]{:S(2)}) collective-permute-start(bf16[5,16,768]{2,1,0:T(8,128)(2,1)} %get-tuple-element.85), channel_id=1, source_target_pairs={{0,12},{1,13},{2,14},{3,15},{4,8},{5,9},{6,10},{7,11},{8,4},{9,5},... | collective-permute-start | bytes 368648 | tf_op jit(solution)/shard_map/ppermute | solution.py:414
  208.7 2.2 copy-done.3
  214.3 3.4 %attend.5 = (bf16[1,64,192]{2,1,0:T(8,128)(2,1)S(1)}, bf16[1,64,192]{2,1,0:T(8,128)(2,1)S(1)}, bf16[1,64,192]{2,1,0:T(8,128)(2,1)S(1)}, bf16[1,64,192]{2,1,0:T(8,128)(2,1)S(1)}, f32[1,64,768]{2,1,0:T(8,128)S(1)}) custom-call(bf16[4,1,80,768]{3,2,1,0:T(8,128)(2,1)S(1)} %copy-done.4, bf16[4,1,80,768]{3,2,1,0:T(8,128)(2,1)S(1)} %collective-permute-done.30.refs_1_, ...), custom_call_target="tpu_custom_call" | custom-call | flops 1677721600 | bytes 5767168 | tf_op jit(solution)/shard_map/attend/pallas_call | solution.py:285
  219.3 3.7 %collective-permute-done.33.refs_1_ = bf16[1,64,192]{2,1,0:T(8,128)(2,1)S(1)} collective-permute-done((bf16[1,64,192]{2,1,0:T(8,128)(2,1)S(1)}, bf16[1,64,192]{2,1,0:T(8,128)(2,1)S(1)}, u32[]{:S(2)}, u32[]{:S(2)}) %collective-permute-start.33) | collective-permute-done | bytes 24608 | tf_op jit(solution)/shard_map/ppermute | solution.py:414
  222.9 3.3 %collective-permute-done.35.refs_3_ = bf16[1,64,192]{2,1,0:T(8,128)(2,1)S(1)} collective-permute-done((bf16[1,64,192]{2,1,0:T(8,128)(2,1)S(1)}, bf16[1,64,192]{2,1,0:T(8,128)(2,1)S(1)}, u32[]{:S(2)}, u32[]{:S(2)}) %collective-permute-start.35) | collective-permute-done | bytes 24608 | tf_op jit(solution)/shard_map/ppermute | solution.py:414
  226.9 2.5 %project.3 = (bf16[1,16,768]{2,1,0:T(8,128)(2,1)}, bf16[1,16,768]{2,1,0:T(8,128)(2,1)}, bf16[1,16,768]{2,1,0:T(8,128)(2,1)}, bf16[1,16,768]{2,1,0:T(8,128)(2,1)}) custom-call(s32[1]{0:T(128)} %bitcast.1.lane_ref, bf16[1,64,192]{2,1,0:T(8,128)(2,1)} %copy-done.20, bf16[1,64,192]{2,1,0:T(8,128)(2,1)} %copy-done.45, bf16[1,64,192]{2,1,0:T(8,128)(2,1)} %copy-done.46, ...), custom_call_target="tpu_custom_call" | custom-call | flops 75497472 | bytes 1179648 | tf_op jit(solution)/shard_map/project/pallas_call | solution.py:341
  234.8 4.5 %collective-permute-done.38.refs_7_ = bf16[1,16,768]{2,1,0:T(8,128)(2,1)S(1)} collective-permute-done((bf16[1,16,768]{2,1,0:T(8,128)(2,1)}, bf16[1,16,768]{2,1,0:T(8,128)(2,1)S(1)}, u32[]{:S(2)}, u32[]{:S(2)}) %collective-permute-start.38) | collective-permute-done | bytes 24608 | tf_op jit(solution)/shard_map/ppermute | solution.py:414
  (190 shorter events, 50.0 us)
Async XLA Ops:
  3.5 19.1 %collective-permute-start = (bf16[3,80,768]{2,1,0:T(8,128)(2,1)}, bf16[3,80,768]{2,1,0:T(8,128)(2,1)S(1)}, u32[]{:S(2)}, u32[]{:S(2)}) collective-permute-start(bf16[3,80,768]{2,1,0:T(8,128)(2,1)} %get-tuple-element.55), channel_id=1, source_target_pairs={{0,4},{1,5},{2,6},{3,7},{4,0},{5,1},{6,2},{7,3},{8,12},{9,13},{10,... | collective-permute-start | bytes 1105928 | tf_op jit(solution)/shard_map/ppermute | solution.py:414
  6.6 28.4 %collective-permute-start.1 = (bf16[3,80,768]{2,1,0:T(8,128)(2,1)}, bf16[3,80,768]{2,1,0:T(8,128)(2,1)S(1)}, u32[]{:S(2)}, u32[]{:S(2)}) collective-permute-start(bf16[3,80,768]{2,1,0:T(8,128)(2,1)} %get-tuple-element.56), channel_id=1, source_target_pairs={{0,8},{1,9},{2,10},{3,11},{4,12},{5,13},{6,14},{7,15},{8,0},{9,1},... | collective-permute-start | bytes 1105928 | tf_op jit(solution)/shard_map/ppermute | solution.py:414
  9.2 25.8 %collective-permute-start.2 = (bf16[3,80,768]{2,1,0:T(8,128)(2,1)}, bf16[3,80,768]{2,1,0:T(8,128)(2,1)S(1)}, u32[]{:S(2)}, u32[]{:S(2)}) collective-permute-start(bf16[3,80,768]{2,1,0:T(8,128)(2,1)} %get-tuple-element.57), channel_id=1, source_target_pairs={{0,12},{1,13},{2,14},{3,15},{4,8},{5,9},{6,10},{7,11},{8,4},{9,5},... | collective-permute-start | bytes 1105928 | tf_op jit(solution)/shard_map/ppermute | solution.py:414
  39.3 56.2 %collective-permute-start.3 = (bf16[4,3,80,768]{3,2,1,0:T(8,128)(2,1)}, bf16[4,3,80,768]{3,2,1,0:T(8,128)(2,1)}, u32[]{:S(2)}, u32[]{:S(2)}) collective-permute-start(bf16[4,3,80,768]{3,2,1,0:T(8,128)(2,1)} %stack.4.refs_0_), channel_id=1, source_target_pairs={{0,2},{1,3},{2,0},{3,1},{4,6},{5,7},{6,4},{7,5},{8,10},{9,11},{10,... | collective-permute-start | bytes 4423688 | tf_op jit(solution)/shard_map/ppermute | solution.py:414
  51.9 12.1 %collective-permute-start.6 = (bf16[528,128]{1,0:T(8,128)(2,1)}, bf16[528,128]{1,0:T(8,128)(2,1)S(1)}, u32[]{:S(2)}, u32[]{:S(2)}) collective-permute-start(bf16[528,128]{1,0:T(8,128)(2,1)} %get-tuple-element.59), channel_id=1, source_target_pairs={{0,1},{1,0},{2,3},{3,2},{4,5},{5,4},{6,7},{7,6},{8,9},{9,8},{10,11... | collective-permute-start | bytes 405512 | tf_op jit(solution)/shard_map/ppermute | solution.py:414
  51.9 22.0 %collective-permute-start.7 = (bf16[528,128]{1,0:T(8,128)(2,1)}, bf16[528,128]{1,0:T(8,128)(2,1)S(1)}, u32[]{:S(2)}, u32[]{:S(2)}) collective-permute-start(bf16[528,128]{1,0:T(8,128)(2,1)} %get-tuple-element.60), channel_id=1, source_target_pairs={{0,2},{1,3},{2,0},{3,1},{4,6},{5,7},{6,4},{7,5},{8,10},{9,11},{10,... | collective-permute-start | bytes 405512 | tf_op jit(solution)/shard_map/ppermute | solution.py:414
  55.9 35.9 %collective-permute-start.15 = (bf16[2,80,768]{2,1,0:T(8,128)(2,1)}, bf16[2,80,768]{2,1,0:T(8,128)(2,1)S(1)}, u32[]{:S(2)}, u32[]{:S(2)}) collective-permute-start(bf16[2,80,768]{2,1,0:T(8,128)(2,1)} %get-tuple-element.69), channel_id=1, source_target_pairs={{0,4},{1,5},{2,6},{3,7},{4,0},{5,1},{6,2},{7,3},{8,12},{9,13},{10,... | collective-permute-start | bytes 737288 | tf_op jit(solution)/shard_map/ppermute | solution.py:414
  62.9 28.9 %collective-permute-start.16 = (bf16[2,80,768]{2,1,0:T(8,128)(2,1)}, bf16[2,80,768]{2,1,0:T(8,128)(2,1)S(1)}, u32[]{:S(2)}, u32[]{:S(2)}) collective-permute-start(bf16[2,80,768]{2,1,0:T(8,128)(2,1)} %get-tuple-element.70), channel_id=1, source_target_pairs={{0,8},{1,9},{2,10},{3,11},{4,12},{5,13},{6,14},{7,15},{8,0},{9,1},... | collective-permute-start | bytes 737288 | tf_op jit(solution)/shard_map/ppermute | solution.py:414
  64.0 27.8 %collective-permute-start.17 = (bf16[2,80,768]{2,1,0:T(8,128)(2,1)}, bf16[2,80,768]{2,1,0:T(8,128)(2,1)S(1)}, u32[]{:S(2)}, u32[]{:S(2)}) collective-permute-start(bf16[2,80,768]{2,1,0:T(8,128)(2,1)} %get-tuple-element.71), channel_id=1, source_target_pairs={{0,12},{1,13},{2,14},{3,15},{4,8},{5,9},{6,10},{7,11},{8,4},{9,5},... | collective-permute-start | bytes 737288 | tf_op jit(solution)/shard_map/ppermute | solution.py:414
  73.9 5.8 %collective-permute-start.8 = (bf16[528,128]{1,0:T(8,128)(2,1)S(1)}, bf16[528,128]{1,0:T(8,128)(2,1)S(1)}, u32[]{:S(2)}, u32[]{:S(2)}) collective-permute-start(bf16[528,128]{1,0:T(8,128)(2,1)S(1)} %copy-done.52), channel_id=1, source_target_pairs={{0,3},{1,2},{2,1},{3,0},{4,7},{5,6},{6,5},{7,4},{8,11},{9,10},{10,... | collective-permute-start | bytes 405512 | tf_op jit(solution)/shard_map/ppermute | solution.py:414
  82.3 45.9 %collective-permute-start.10 = (bf16[4,528,128]{2,1,0:T(8,128)(2,1)}, bf16[4,528,128]{2,1,0:T(8,128)(2,1)S(1)}, u32[]{:S(2)}, u32[]{:S(2)}) collective-permute-start(bf16[4,528,128]{2,1,0:T(8,128)(2,1)} %stack.5.refs_0_), channel_id=1, source_target_pairs={{0,8},{1,9},{2,10},{3,11},{4,12},{5,13},{6,14},{7,15},{8,0},{9,1},... | collective-permute-start | bytes 1622024 | tf_op jit(solution)/shard_map/ppermute | solution.py:414
  94.8 49.3 %collective-permute-start.18 = (bf16[4,2,80,768]{3,2,1,0:T(8,128)(2,1)}, bf16[4,2,80,768]{3,2,1,0:T(8,128)(2,1)}, u32[]{:S(2)}, u32[]{:S(2)}) collective-permute-start(bf16[4,2,80,768]{3,2,1,0:T(8,128)(2,1)} %stack.6.refs_0_), channel_id=1, source_target_pairs={{0,2},{1,3},{2,0},{3,1},{4,6},{5,7},{6,4},{7,5},{8,10},{9,11},{10,... | collective-permute-start | bytes 2949128 | tf_op jit(solution)/shard_map/ppermute | solution.py:414
  95.4 67.9 %collective-permute-start.4 = (bf16[4,3,80,768]{3,2,1,0:T(8,128)(2,1)}, bf16[4,3,80,768]{3,2,1,0:T(8,128)(2,1)}, u32[]{:S(2)}, u32[]{:S(2)}) collective-permute-start(bf16[4,3,80,768]{3,2,1,0:T(8,128)(2,1)} %stack.4.refs_0_), channel_id=1, source_target_pairs={{0,1},{1,0},{2,3},{3,2},{4,5},{5,4},{6,7},{7,6},{8,9},{9,8},{10,11... | collective-permute-start | bytes 4423688 | tf_op jit(solution)/shard_map/ppermute | solution.py:414
  95.4 68.4 %collective-permute-start.5 = (bf16[4,3,80,768]{3,2,1,0:T(8,128)(2,1)}, bf16[4,3,80,768]{3,2,1,0:T(8,128)(2,1)}, u32[]{:S(2)}, u32[]{:S(2)}) collective-permute-start(bf16[4,3,80,768]{3,2,1,0:T(8,128)(2,1)} %collective-permute-done.3.refs_1_), channel_id=1, source_target_pairs={{0,1},{1,0},{2,3},{3,2},{4,5},{5,4},{6,7},{7,6},{8,9},{9,8},{10,11... | collective-permute-start | bytes 4423688 | tf_op jit(solution)/shard_map/ppermute | solution.py:414
  95.9 10.6 %collective-permute-start.27 = (bf16[1,80,768]{2,1,0:T(8,128)(2,1)S(1)}, bf16[1,80,768]{2,1,0:T(8,128)(2,1)S(1)}, u32[]{:S(2)}, u32[]{:S(2)}) collective-permute-start(bf16[1,80,768]{2,1,0:T(8,128)(2,1)S(1)} %copy-done.55), channel_id=1, source_target_pairs={{0,4},{1,5},{2,6},{3,7},{4,0},{5,1},{6,2},{7,3},{8,12},{9,13},{10,... | collective-permute-start | bytes 368648 | tf_op jit(solution)/shard_map/ppermute | solution.py:414
  106.5 14.9 %collective-permute-start.28 = (bf16[1,80,768]{2,1,0:T(8,128)(2,1)S(1)}, bf16[1,80,768]{2,1,0:T(8,128)(2,1)S(1)}, u32[]{:S(2)}, u32[]{:S(2)}) collective-permute-start(bf16[1,80,768]{2,1,0:T(8,128)(2,1)S(1)} %copy-done.54), channel_id=1, source_target_pairs={{0,8},{1,9},{2,10},{3,11},{4,12},{5,13},{6,14},{7,15},{8,0},{9,1},... | collective-permute-start | bytes 368648 | tf_op jit(solution)/shard_map/ppermute | solution.py:414
  121.4 6.7 %collective-permute-start.29 = (bf16[1,80,768]{2,1,0:T(8,128)(2,1)S(1)}, bf16[1,80,768]{2,1,0:T(8,128)(2,1)S(1)}, u32[]{:S(2)}, u32[]{:S(2)}) collective-permute-start(bf16[1,80,768]{2,1,0:T(8,128)(2,1)S(1)} %copy-done.53), channel_id=1, source_target_pairs={{0,12},{1,13},{2,14},{3,15},{4,8},{5,9},{6,10},{7,11},{8,4},{9,5},... | collective-permute-start | bytes 368648 | tf_op jit(solution)/shard_map/ppermute | solution.py:414
  128.1 15.1 %collective-permute-start.9 = (bf16[4,528,128]{2,1,0:T(8,128)(2,1)S(1)}, bf16[4,528,128]{2,1,0:T(8,128)(2,1)S(1)}, u32[]{:S(2)}, u32[]{:S(2)}) collective-permute-start(bf16[4,528,128]{2,1,0:T(8,128)(2,1)S(1)} %copy-done.21), channel_id=1, source_target_pairs={{0,4},{1,5},{2,6},{3,7},{4,0},{5,1},{6,2},{7,3},{8,12},{9,13},{10,... | collective-permute-start | bytes 1622024 | tf_op jit(solution)/shard_map/ppermute | solution.py:414
  128.2 24.2 %collective-permute-start.11 = (bf16[4,528,128]{2,1,0:T(8,128)(2,1)S(1)}, bf16[4,528,128]{2,1,0:T(8,128)(2,1)S(1)}, u32[]{:S(2)}, u32[]{:S(2)}) collective-permute-start(bf16[4,528,128]{2,1,0:T(8,128)(2,1)S(1)} %collective-permute-done.10.refs_2_), channel_id=1, source_target_pairs={{0,4},{1,5},{2,6},{3,7},{4,0},{5,1},{6,2},{7,3},{8,12},{9,13},{10,... | collective-permute-start | bytes 1622024 | tf_op jit(solution)/shard_map/ppermute | solution.py:414
  144.1 36.7 %collective-permute-start.19 = (bf16[4,2,80,768]{3,2,1,0:T(8,128)(2,1)}, bf16[4,2,80,768]{3,2,1,0:T(8,128)(2,1)}, u32[]{:S(2)}, u32[]{:S(2)}) collective-permute-start(bf16[4,2,80,768]{3,2,1,0:T(8,128)(2,1)} %stack.6.refs_0_), channel_id=1, source_target_pairs={{0,1},{1,0},{2,3},{3,2},{4,5},{5,4},{6,7},{7,6},{8,9},{9,8},{10,11... | collective-permute-start | bytes 2949128 | tf_op jit(solution)/shard_map/ppermute | solution.py:414
  144.1 36.7 %collective-permute-start.20 = (bf16[4,2,80,768]{3,2,1,0:T(8,128)(2,1)}, bf16[4,2,80,768]{3,2,1,0:T(8,128)(2,1)}, u32[]{:S(2)}, u32[]{:S(2)}) collective-permute-start(bf16[4,2,80,768]{3,2,1,0:T(8,128)(2,1)} %collective-permute-done.18.refs_1_), channel_id=1, source_target_pairs={{0,1},{1,0},{2,3},{3,2},{4,5},{5,4},{6,7},{7,6},{8,9},{9,8},{10,11... | collective-permute-start | bytes 2949128 | tf_op jit(solution)/shard_map/ppermute | solution.py:414
  152.4 10.9 %collective-permute-start.30 = (bf16[4,1,80,768]{3,2,1,0:T(8,128)(2,1)}, bf16[4,1,80,768]{3,2,1,0:T(8,128)(2,1)S(1)}, u32[]{:S(2)}, u32[]{:S(2)}) collective-permute-start(bf16[4,1,80,768]{3,2,1,0:T(8,128)(2,1)} %stack.7.refs_0_), channel_id=1, source_target_pairs={{0,2},{1,3},{2,0},{3,1},{4,6},{5,7},{6,4},{7,5},{8,10},{9,11},{10,... | collective-permute-start | bytes 1474568 | tf_op jit(solution)/shard_map/ppermute | solution.py:414
  163.3 29.6 %collective-permute-start.31 = (bf16[4,1,80,768]{3,2,1,0:T(8,128)(2,1)S(1)}, bf16[4,1,80,768]{3,2,1,0:T(8,128)(2,1)S(1)}, u32[]{:S(2)}, u32[]{:S(2)}) collective-permute-start(bf16[4,1,80,768]{3,2,1,0:T(8,128)(2,1)S(1)} %copy-done.4), channel_id=1, source_target_pairs={{0,1},{1,0},{2,3},{3,2},{4,5},{5,4},{6,7},{7,6},{8,9},{9,8},{10,11... | collective-permute-start | bytes 1474568 | tf_op jit(solution)/shard_map/ppermute | solution.py:414
  163.3 30.8 %collective-permute-start.32 = (bf16[4,1,80,768]{3,2,1,0:T(8,128)(2,1)S(1)}, bf16[4,1,80,768]{3,2,1,0:T(8,128)(2,1)S(1)}, u32[]{:S(2)}, u32[]{:S(2)}) collective-permute-start(bf16[4,1,80,768]{3,2,1,0:T(8,128)(2,1)S(1)} %collective-permute-done.30.refs_1_), channel_id=1, source_target_pairs={{0,1},{1,0},{2,3},{3,2},{4,5},{5,4},{6,7},{7,6},{8,9},{9,8},{10,11... | collective-permute-start | bytes 1474568 | tf_op jit(solution)/shard_map/ppermute | solution.py:414
  191.2 9.1 %collective-permute-start.12 = (bf16[3,64,192]{2,1,0:T(8,128)(2,1)S(1)}, bf16[3,64,192]{2,1,0:T(8,128)(2,1)S(1)}, u32[]{:S(2)}, u32[]{:S(2)}) collective-permute-start(bf16[3,64,192]{2,1,0:T(8,128)(2,1)S(1)} %get-tuple-element.65), channel_id=1, source_target_pairs={{0,2},{1,3},{2,0},{3,1},{4,6},{5,7},{6,4},{7,5},{8,10},{9,11},{10,... | collective-permute-start | bytes 221192 | tf_op jit(solution)/shard_map/ppermute | solution.py:414
  192.9 7.3 %collective-permute-start.13 = (bf16[3,64,192]{2,1,0:T(8,128)(2,1)S(1)}, bf16[3,64,192]{2,1,0:T(8,128)(2,1)S(1)}, u32[]{:S(2)}, u32[]{:S(2)}) collective-permute-start(bf16[3,64,192]{2,1,0:T(8,128)(2,1)S(1)} %get-tuple-element.66), channel_id=1, source_target_pairs={{0,1},{1,0},{2,3},{3,2},{4,5},{5,4},{6,7},{7,6},{8,9},{9,8},{10,11... | collective-permute-start | bytes 221192 | tf_op jit(solution)/shard_map/ppermute | solution.py:414
  193.7 6.6 %collective-permute-start.14 = (bf16[3,64,192]{2,1,0:T(8,128)(2,1)S(1)}, bf16[3,64,192]{2,1,0:T(8,128)(2,1)S(1)}, u32[]{:S(2)}, u32[]{:S(2)}) collective-permute-start(bf16[3,64,192]{2,1,0:T(8,128)(2,1)S(1)} %get-tuple-element.67), channel_id=1, source_target_pairs={{0,3},{1,2},{2,1},{3,0},{4,7},{5,6},{6,5},{7,4},{8,11},{9,10},{10,... | collective-permute-start | bytes 221192 | tf_op jit(solution)/shard_map/ppermute | solution.py:414
  204.3 34.9 %collective-permute-start.24 = (bf16[5,16,768]{2,1,0:T(8,128)(2,1)}, bf16[5,16,768]{2,1,0:T(8,128)(2,1)S(1)}, u32[]{:S(2)}, u32[]{:S(2)}) collective-permute-start(bf16[5,16,768]{2,1,0:T(8,128)(2,1)} %get-tuple-element.83), channel_id=1, source_target_pairs={{0,4},{1,5},{2,6},{3,7},{4,0},{5,1},{6,2},{7,3},{8,12},{9,13},{10,... | collective-permute-start | bytes 368648 | tf_op jit(solution)/shard_map/ppermute | solution.py:414
  204.9 34.3 %collective-permute-start.25 = (bf16[5,16,768]{2,1,0:T(8,128)(2,1)}, bf16[5,16,768]{2,1,0:T(8,128)(2,1)S(1)}, u32[]{:S(2)}, u32[]{:S(2)}) collective-permute-start(bf16[5,16,768]{2,1,0:T(8,128)(2,1)} %get-tuple-element.84), channel_id=1, source_target_pairs={{0,8},{1,9},{2,10},{3,11},{4,12},{5,13},{6,14},{7,15},{8,0},{9,1},... | collective-permute-start | bytes 368648 | tf_op jit(solution)/shard_map/ppermute | solution.py:414
  206.3 33.0 %collective-permute-start.26 = (bf16[5,16,768]{2,1,0:T(8,128)(2,1)}, bf16[5,16,768]{2,1,0:T(8,128)(2,1)}, u32[]{:S(2)}, u32[]{:S(2)}) collective-permute-start(bf16[5,16,768]{2,1,0:T(8,128)(2,1)} %get-tuple-element.85), channel_id=1, source_target_pairs={{0,12},{1,13},{2,14},{3,15},{4,8},{5,9},{6,10},{7,11},{8,4},{9,5},... | collective-permute-start | bytes 368648 | tf_op jit(solution)/shard_map/ppermute | solution.py:414
  229.4 5.4 %collective-permute-start.37 = (bf16[1,16,768]{2,1,0:T(8,128)(2,1)}, bf16[1,16,768]{2,1,0:T(8,128)(2,1)S(1)}, u32[]{:S(2)}, u32[]{:S(2)}) collective-permute-start(bf16[1,16,768]{2,1,0:T(8,128)(2,1)} %get-tuple-element.101), channel_id=1, source_target_pairs={{0,8},{1,9},{2,10},{3,11},{4,12},{5,13},{6,14},{7,15},{8,0},{9,1},... | collective-permute-start | bytes 73736 | tf_op jit(solution)/shard_map/ppermute | solution.py:414
  233.4 5.8 %collective-permute-start.38 = (bf16[1,16,768]{2,1,0:T(8,128)(2,1)}, bf16[1,16,768]{2,1,0:T(8,128)(2,1)S(1)}, u32[]{:S(2)}, u32[]{:S(2)}) collective-permute-start(bf16[1,16,768]{2,1,0:T(8,128)(2,1)} %get-tuple-element.102), channel_id=1, source_target_pairs={{0,12},{1,13},{2,14},{3,15},{4,8},{5,9},{6,10},{7,11},{8,4},{9,5},... | collective-permute-start | bytes 73736 | tf_op jit(solution)/shard_map/ppermute | solution.py:414
  (65 other events, 587.8 us)
where the time goes:
time: 243 us; the launch traced here: 242 us
  waiting for transfers between devices  107 us (44%)
  Pallas kernels  63.6 us (26%)
  starting transfers between devices  46.1 us (19%)
  local copies, waits for them, and re-layouts  24 us (10%)
    ppermute x39, waiting for transfers between devices, across(): return lax.ppermute(x, 'key', [(i, i ^ code) for i in range(n)])  107 us
    ppermute x39, starting transfers between devices, across(): return lax.ppermute(x, 'key', [(i, i ^ code) for i in range(n)])  46.1 us
    pallas_call x3, Pallas kernels, attention(): pl.pallas_call(functools.partial(attention_kernel, pieces, hpg, direct, k...  24.2 us
    unnamed x117, local copies, waits for them, and re-layouts  20.8 us
    pallas_call x4, Pallas kernels, stacked(): pl.pallas_call(stack_kernel, grid=(steps,), in_specs=[pl.BlockSpec(block,...  9.34 us
    pallas_call x1, Pallas kernels, local_bias(): pl.pallas_call(functools.partial(bias_kernel, hpg), grid=(rows // tile,),...  9.01 us
    pallas_call x2, Pallas kernels, pack(): pl.pallas_call(functools.partial(pack_kernel, sizes, sg), grid_spec=pltpu...  6.92 us
    pallas_call x1, Pallas kernels, ordered_bias(): pl.pallas_call(functools.partial(order_kernel, hpg, keys, codes), in_spec...  6.36 us
  transfers between devices with their start and end apart: 39, of which 16 were waited for; matrix products, arithmetic and copies ran while one was open for 2% of the time, Pallas kernels for 21%

commit v1 on v0

--- a/solution.py
+++ b/solution.py
@@ -12,7 +12,7 @@
 H = 16
 LOG2E = 1.4426950408889634
 NEG = -1e9
-VMEM_LIMIT = 60 * 1024 * 1024
+MIB = 1024 * 1024
 F32 = jnp.float32
 BF16 = jnp.bfloat16
 
@@ -69,7 +69,7 @@
         cost_estimate=pl.CostEstimate(
             flops=2 * window * keys * c * 256, bytes_accessed=window * keys * c * 2, transcendentals=0
         ),
-        compiler_params=pltpu.CompilerParams(vmem_limit_bytes=VMEM_LIMIT),
+        compiler_params=pltpu.CompilerParams(vmem_limit_bytes=16 * MIB),
         name="bias_local",
     )(mask, pair.reshape(fold, rows, keys, c), pair_gain[None], proj_t)
 
@@ -116,6 +116,7 @@
         cost_estimate=pl.CostEstimate(
             flops=0, bytes_accessed=4 * sg * total * (keys + rows) * width, transcendentals=0
         ),
+        compiler_params=pltpu.CompilerParams(vmem_limit_bytes=12 * MIB),
         name="pack",
     )(group.reshape(1), *([key_groups] * sg), *([query_groups] * sg))
     return [outs[i * sg : (i + 1) * sg] for i in range(len(sizes))]
@@ -140,6 +141,7 @@
         cost_estimate=pl.CostEstimate(
             flops=0, bytes_accessed=4 * count * math.prod(shape), transcendentals=0
         ),
+        compiler_params=pltpu.CompilerParams(vmem_limit_bytes=8 * MIB),
         name="stack",
     )(*parts)
 
@@ -192,6 +194,7 @@
 
 def ordered_bias(parts, me, span_owner, qsel, hpg, keys, codes, window):
     n = len(codes)
+    limit = (40 if n * keys > 2048 else 14) * MIB
     smem = pl.BlockSpec(memory_space=pltpu.SMEM)
     vmem = pl.BlockSpec(memory_space=pltpu.VMEM)
     return pl.pallas_call(
@@ -209,7 +212,7 @@
         cost_estimate=pl.CostEstimate(
             flops=hpg * window * n * keys * 8, bytes_accessed=hpg * window * n * keys * 6, transcendentals=0
         ),
-        compiler_params=pltpu.CompilerParams(vmem_limit_bytes=VMEM_LIMIT),
+        compiler_params=pltpu.CompilerParams(vmem_limit_bytes=limit),
         name="bias_order",
     )(me.reshape(1), span_owner, qsel, *parts)
 
@@ -234,7 +237,7 @@
     for m in range(pieces):
         block = rows_of(token_refs[m], 0, keys)
         span = slice(m * sg * keys, (m + 1) * sg * keys)
-        k_t = nt_dot(wk_ref[...], block)
+        k_t = nn_dot(block, wk_ref[...]).T
         k_ref[:, span] = jnp.where(mask_ref[:1, span] > 0, k_t, 0.0).astype(BF16)
         v_ref[span, :] = nn_dot(block, wv_ref[...]).astype(BF16)
     if direct:
@@ -263,7 +266,7 @@
         out_refs[m][0] = total[m * rows : (m + 1) * rows].astype(BF16)
 
 
-def attention(arrays, queries, bias, mask, wq, wk_t, wv, w_gate, hpg, keys, query_rows):
+def attention(arrays, queries, bias, mask, wq, wk, wv, w_gate, hpg, keys, query_rows):
     pieces = len(arrays)
     sg, size, rows, width = arrays[0].shape
     window = bias.shape[1]
@@ -278,9 +281,9 @@
         specs.append(pl.BlockSpec((1, window, width), lambda s: (s, 0, 0)))
         args.append(queries)
         out_rows = [window]
-    consts = [bias, mask, wq, wk_t, wv, w_gate]
+    consts = [bias, mask, wq, wk, wv, w_gate]
     gate_rows = sg * query_rows
-    limit = VMEM_LIMIT if tokens > 2048 else 36 * 1024 * 1024
+    limit = (60 if tokens > 2048 else 26) * MIB
     flops = 2 * size * (tokens * width * feats * 2 + hpg * window * tokens * 512)
     return pl.pallas_call(
         functools.partial(attention_kernel, pieces, hpg, direct, keys),
@@ -347,6 +350,7 @@
         cost_estimate=pl.CostEstimate(
             flops=2 * sum(sizes) * rows * width * width, bytes_accessed=2 * width * width, transcendentals=0
         ),
+        compiler_params=pltpu.CompilerParams(vmem_limit_bytes=12 * MIB),
         name="project",
     )(lane.reshape(1), *flat, *gates, w_out)
 
@@ -366,6 +370,7 @@
         in_specs=[pl.BlockSpec(memory_space=pltpu.SMEM)] + [vmem] * len(parts),
         out_specs=vmem,
         out_shape=jax.ShapeDtypeStruct(shape, BF16),
+        compiler_params=pltpu.CompilerParams(vmem_limit_bytes=8 * MIB),
         name="assemble",
     )(group.reshape(1), *parts)
 
@@ -375,6 +380,12 @@
     while hg * hg < n or H % hg or samples % (n // hg):
         hg *= 2
     return hg
+
+
+def chunk_sizes(group_samples):
+    last = max(group_samples // 6, 1)
+    middle = max(group_samples // 3, 1)
+    return [group_samples - middle - last, middle, last]
 
 
 def local(
@@ -400,9 +411,7 @@
     hpg = H // hg
     feats = width // hg
     group_samples = samples // sg
-    last = max(group_samples // 6, 1)
-    middle = max(group_samples // 3, 1)
-    sizes = [group_samples - middle - last, middle, last]
+    sizes = chunk_sizes(group_samples)
     firsts = [sum(sizes[:c]) for c in range(len(sizes))]
     direct = query_rows % 16 == 0
     me = lax.axis_index("key")
@@ -452,7 +461,7 @@
     def own(w):
         return lax.dynamic_slice_in_dim(w, lane * feats, feats, 1)
 
-    wq, wk_t, wv = own(w_query), own(w_key).T, own(w_value)
+    wq, wk, wv = own(w_query), own(w_key), own(w_value)
 
     heads, gates = [], []
     previous = None
@@ -469,7 +478,7 @@
             queries = jnp.swapaxes(jnp.take(queries, order, axis=0), 0, 1).reshape(size, window, width)
         if previous is not None:
             arrays, previous = lax.optimization_barrier((arrays, previous))
-        results = attention(arrays, queries, bias, mask, wq, wk_t, wv, w_gate, hpg, keys, query_rows)
+        results = attention(arrays, queries, bias, mask, wq, wk, wv, w_gate, hpg, keys, query_rows)
         results, gate = results[:-1], results[-1]
         previous = gate
         if not direct:
@@ -482,11 +491,10 @@
         heads.append([across(r, m) for r, m in zip(results, labels)])
         gates.append(gate)
     outs = []
-    cut = len(sizes) - 1
-    for span in (slice(0, cut), slice(cut, cut + 1)):
+    for span in (slice(0, 1), slice(1, len(sizes))):
         back = projected(lane, heads[span], gates[span], w_out, labels, sg, query_rows)
         outs.extend(across(x, k * hg) for k, x in enumerate(back))
-    out = assembled(group, outs, [0, firsts[cut]], (sg, group_samples, query_rows, width))
+    out = assembled(group, outs, [0, sizes[0]], (sg, group_samples, query_rows, width))
     return out.reshape(samples, query_rows, width)
 
 

time: 243 us -> 209 us (0.86)
  Pallas kernels: 63.6 us -> 38.6 us
  local copies, waits for them, and re-layouts: 24 us -> 9.43 us
  waiting for transfers between devices: 107 us -> 111 us
    unnamed x117 -> x38, local copies, waits for them, and re-layouts: 20.8 us -> 6.7 us
    pallas_call x4, Pallas kernels: 9.34 us -> 1.95 us  [stacked(): pl.pallas_call(stack_kernel, grid=(steps,), in_specs=[pl.BlockSpec(block,...]
    pallas_call x2, Pallas kernels: 6.92 us -> 0.38 us  [pack(): pl.pallas_call(functools.partial(pack_kernel, sizes, sg), grid_spec=pltpu...]
    ppermute x39, waiting for transfers between devices: 107 us -> 111 us  [across(): return lax.ppermute(x, 'key', [(i, i ^ code) for i in range(n)])]
    pallas_call x2, Pallas kernels: 5.84 us -> 1.08 us  [projected(): pl.pallas_call(functools.partial(project_kernel, labels, sizes), in_specs...]
    pallas_call x1, Pallas kernels: 6.36 us -> 3.33 us  [ordered_bias(): pl.pallas_call(functools.partial(order_kernel, hpg, keys, codes), in_spec...]
    pallas_call x1, Pallas kernels: 9.01 us -> 6.51 us  [local_bias(): pl.pallas_call(functools.partial(bias_kernel, hpg), grid=(rows // tile,),...]
  transfers between devices with their start and end apart: 39 -> 39, of which waited for: 16 -> 15; matrix products, arithmetic and copies ran while one was open for 2% -> 1% of each run, Pallas kernels for 21% -> 15%
where the time goes in v1:
time: 209 us; the launch traced here: 208 us
  waiting for transfers between devices  111 us (53%)
  starting transfers between devices  48.5 us (23%)
  Pallas kernels  38.6 us (18%)
  local copies, waits for them, and re-layouts  9.43 us (5%)
    ppermute x39, waiting for transfers between devices, across(): return lax.ppermute(x, 'key', [(i, i ^ code) for i in range(n)])  111 us
    ppermute x39, starting transfers between devices, across(): return lax.ppermute(x, 'key', [(i, i ^ code) for i in range(n)])  48.5 us
    pallas_call x3, Pallas kernels, attention(): pl.pallas_call(functools.partial(attention_kernel, pieces, hpg, direct, k...  24.5 us
    unnamed x38, local copies, waits for them, and re-layouts  6.7 us
    pallas_call x1, Pallas kernels, local_bias(): pl.pallas_call(functools.partial(bias_kernel, hpg), grid=(rows // tile,),...  6.51 us
  transfers between devices with their start and end apart: 39, of which 15 were waited for; matrix products, arithmetic and copies ran while one was open for 1% of the time, Pallas kernels for 15%

profile of v1, /device:TPU:0, one launch (start us, length us, event | category | flops | bytes accessed | tf_op | source)
XLA Modules:
  0.0 208.4 jit_solution(14709454504557529309)
XLA Ops:
  0.0 1.8 copy-done.1
  3.0 3.1 %collective-permute-start = (bf16[3,80,768]{2,1,0:T(8,128)(2,1)S(1)}, bf16[3,80,768]{2,1,0:T(8,128)(2,1)S(1)}, u32[]{:S(2)}, u32[]{:S(2)}) collective-permute-start(bf16[3,80,768]{2,1,0:T(8,128)(2,1)S(1)} %get-tuple-element.55), channel_id=1, source_target_pairs={{0,4},{1,5},{2,6},{3,7},{4,0},{5,1},{6,2},{7,3},{8,12},{9,13},{10,... | collective-permute-start | bytes 1105928 | tf_op jit(solution)/shard_map/ppermute | solution.py:423
  6.1 2.6 %collective-permute-start.1 = (bf16[3,80,768]{2,1,0:T(8,128)(2,1)S(1)}, bf16[3,80,768]{2,1,0:T(8,128)(2,1)S(1)}, u32[]{:S(2)}, u32[]{:S(2)}) collective-permute-start(bf16[3,80,768]{2,1,0:T(8,128)(2,1)S(1)} %get-tuple-element.56), channel_id=1, source_target_pairs={{0,8},{1,9},{2,10},{3,11},{4,12},{5,13},{6,14},{7,15},{8,0},{9,1},... | collective-permute-start | bytes 1105928 | tf_op jit(solution)/shard_map/ppermute | solution.py:423
  8.7 13.2 %collective-permute-done.refs_1_ = bf16[3,80,768]{2,1,0:T(8,128)(2,1)S(1)} collective-permute-done((bf16[3,80,768]{2,1,0:T(8,128)(2,1)S(1)}, bf16[3,80,768]{2,1,0:T(8,128)(2,1)S(1)}, u32[]{:S(2)}, u32[]{:S(2)}) %collective-permute-start) | collective-permute-done | bytes 368672 | tf_op jit(solution)/shard_map/ppermute | solution.py:423
  21.9 12.4 %collective-permute-done.1.refs_2_ = bf16[3,80,768]{2,1,0:T(8,128)(2,1)S(1)} collective-permute-done((bf16[3,80,768]{2,1,0:T(8,128)(2,1)S(1)}, bf16[3,80,768]{2,1,0:T(8,128)(2,1)S(1)}, u32[]{:S(2)}, u32[]{:S(2)}) %collective-permute-start.1) | collective-permute-done | bytes 368672 | tf_op jit(solution)/shard_map/ppermute | solution.py:423
  34.3 1.7 stack.4.refs_0_
  36.0 1.5 collective-permute-start.3
  38.5 2.2 %copy-done.6 = bf16[256,64,128]{2,1,0:T(8,128)(2,1)S(1)} copy-done((bf16[256,64,128]{2,1,0:T(8,128)(2,1)S(1)}, bf16[256,64,128]{2,1,0:T(8,128)(2,1)}, u32[]{:S(2)}) %copy-start.6) | copy-done | bytes 4194328
  40.7 6.5 %bias_local.1 = (bf16[528,128]{1,0:T(8,128)(2,1)S(1)}, bf16[528,128]{1,0:T(8,128)(2,1)S(1)}, bf16[528,128]{1,0:T(8,128)(2,1)S(1)}, bf16[528,128]{1,0:T(8,128)(2,1)S(1)}) custom-call(f32[1,128]{1,0:T(1,128)S(1)} %broadcast_in_dim_tile.3.mask_ref, bf16[2,128,64,128]{3,2,1,0:T(8,128)(2,1)S(1)} %bitcast.30, f32[1,128]{1,0:T(1,128)S(1)} %bitcast.31, ...), custom_call_target="tpu_custom_call" | custom-call | flops 1073741824 | bytes 4194304 | tf_op jit(solution)/shard_map/bias_local/pallas_call | solution.py:58
  48.1 7.1 %collective-permute-start.18 = (bf16[2,80,768]{2,1,0:T(8,128)(2,1)S(1)}, bf16[2,80,768]{2,1,0:T(8,128)(2,1)S(1)}, u32[]{:S(2)}, u32[]{:S(2)}) collective-permute-start(bf16[2,80,768]{2,1,0:T(8,128)(2,1)S(1)} %get-tuple-element.74), channel_id=1, source_target_pairs={{0,4},{1,5},{2,6},{3,7},{4,0},{5,1},{6,2},{7,3},{8,12},{9,13},{10,... | collective-permute-start | bytes 737288 | tf_op jit(solution)/shard_map/ppermute | solution.py:423
  57.7 13.1 %collective-permute-done.7.refs_2_ = bf16[528,128]{1,0:T(8,128)(2,1)S(1)} collective-permute-done((bf16[528,128]{1,0:T(8,128)(2,1)S(1)}, bf16[528,128]{1,0:T(8,128)(2,1)S(1)}, u32[]{:S(2)}, u32[]{:S(2)}) %collective-permute-start.7) | collective-permute-done | bytes 135200 | tf_op jit(solution)/shard_map/ppermute | solution.py:423
  70.7 5.8 %collective-permute-done.8.refs_3_ = bf16[528,128]{1,0:T(8,128)(2,1)S(1)} collective-permute-done((bf16[528,128]{1,0:T(8,128)(2,1)S(1)}, bf16[528,128]{1,0:T(8,128)(2,1)S(1)}, u32[]{:S(2)}, u32[]{:S(2)}) %collective-permute-start.8) | collective-permute-done | bytes 135200 | tf_op jit(solution)/shard_map/ppermute | solution.py:423
  76.6 9.5 %collective-permute-start.10 = (bf16[4,528,128]{2,1,0:T(8,128)(2,1)S(1)}, bf16[4,528,128]{2,1,0:T(8,128)(2,1)S(1)}, u32[]{:S(2)}, u32[]{:S(2)}) collective-permute-start(bf16[4,528,128]{2,1,0:T(8,128)(2,1)S(1)} %stack.5.refs_0_), channel_id=1, source_target_pairs={{0,8},{1,9},{2,10},{3,11},{4,12},{5,13},{6,14},{7,15},{8,0},{9,1},... | collective-permute-start | bytes 1622024 | tf_op jit(solution)/shard_map/ppermute | solution.py:423
  87.5 13.0 %collective-permute-done.27.refs_1_ = bf16[1,80,768]{2,1,0:T(8,128)(2,1)S(1)} collective-permute-done((bf16[1,80,768]{2,1,0:T(8,128)(2,1)S(1)}, bf16[1,80,768]{2,1,0:T(8,128)(2,1)S(1)}, u32[]{:S(2)}, u32[]{:S(2)}) %collective-permute-start.27) | collective-permute-done | bytes 122912 | tf_op jit(solution)/shard_map/ppermute | solution.py:423
  100.6 2.4 %collective-permute-start.28 = (bf16[1,80,768]{2,1,0:T(8,128)(2,1)S(1)}, bf16[1,80,768]{2,1,0:T(8,128)(2,1)S(1)}, u32[]{:S(2)}, u32[]{:S(2)}) collective-permute-start(bf16[1,80,768]{2,1,0:T(8,128)(2,1)S(1)} %get-tuple-element.87), channel_id=1, source_target_pairs={{0,8},{1,9},{2,10},{3,11},{4,12},{5,13},{6,14},{7,15},{8,0},{9,1},... | collective-permute-start | bytes 368648 | tf_op jit(solution)/shard_map/ppermute | solution.py:423
  102.9 12.5 %collective-permute-done.28.refs_2_ = bf16[1,80,768]{2,1,0:T(8,128)(2,1)S(1)} collective-permute-done((bf16[1,80,768]{2,1,0:T(8,128)(2,1)S(1)}, bf16[1,80,768]{2,1,0:T(8,128)(2,1)S(1)}, u32[]{:S(2)}, u32[]{:S(2)}) %collective-permute-start.28) | collective-permute-done | bytes 122912 | tf_op jit(solution)/shard_map/ppermute | solution.py:423
  116.8 5.3 %collective-permute-done.29.refs_3_ = bf16[1,80,768]{2,1,0:T(8,128)(2,1)S(1)} collective-permute-done((bf16[1,80,768]{2,1,0:T(8,128)(2,1)S(1)}, bf16[1,80,768]{2,1,0:T(8,128)(2,1)S(1)}, u32[]{:S(2)}, u32[]{:S(2)}) %collective-permute-start.29) | collective-permute-done | bytes 122912 | tf_op jit(solution)/shard_map/ppermute | solution.py:423
  122.2 2.0 collective-permute-start.11
  124.2 13.1 %collective-permute-done.9.refs_1_ = bf16[4,528,128]{2,1,0:T(8,128)(2,1)S(1)} collective-permute-done((bf16[4,528,128]{2,1,0:T(8,128)(2,1)S(1)}, bf16[4,528,128]{2,1,0:T(8,128)(2,1)S(1)}, u32[]{:S(2)}, u32[]{:S(2)}) %collective-permute-start.9) | collective-permute-done | bytes 540704 | tf_op jit(solution)/shard_map/ppermute | solution.py:423
  138.7 7.6 %collective-permute-done.11.refs_3_ = bf16[4,528,128]{2,1,0:T(8,128)(2,1)S(1)} collective-permute-done((bf16[4,528,128]{2,1,0:T(8,128)(2,1)S(1)}, bf16[4,528,128]{2,1,0:T(8,128)(2,1)S(1)}, u32[]{:S(2)}, u32[]{:S(2)}) %collective-permute-start.11) | collective-permute-done | bytes 540704 | tf_op jit(solution)/shard_map/ppermute | solution.py:423
  147.4 1.7 constant_dynamic-slice_fusion
  149.2 3.3 %bias_order.1 = (f32[4,256,1024]{2,1,0:T(8,128)S(1)}, f32[8,1024]{1,0:T(8,128)S(1)}) custom-call(s32[1]{0:T(128)} %bitcast.4.me_ref, s32[16]{0:T(128)S(1)} %copy-done.14, s32[16]{0:T(128)S(1)} %broadcast_xor_fusion.qsel_ref, bf16[4,528,128]{2,1,0:T(8,128)(2,1)S(1)} %stack.5.refs_0_, bf16[4,528,128]{2,1,0:T(8,128)(2,1)S(1)} %copy-done.11, ...), custom_call_target="tpu_custom_call" | custom-call | flops 8388608 | bytes 6291456 | tf_op jit(solution)/shard_map/bias_order/pallas_call | solution.py:200
  152.5 5.4 %collective-permute-done.30.refs_1_ = bf16[4,1,80,768]{3,2,1,0:T(8,128)(2,1)} collective-permute-done((bf16[4,1,80,768]{3,2,1,0:T(8,128)(2,1)S(1)}, bf16[4,1,80,768]{3,2,1,0:T(8,128)(2,1)}, u32[]{:S(2)}, u32[]{:S(2)}) %collective-permute-start.30) | collective-permute-done | bytes 491552 | tf_op jit(solution)/shard_map/ppermute | solution.py:423
  158.4 11.7 %attend.3 = (bf16[3,64,192]{2,1,0:T(8,128)(2,1)S(1)}, bf16[3,64,192]{2,1,0:T(8,128)(2,1)S(1)}, bf16[3,64,192]{2,1,0:T(8,128)(2,1)S(1)}, bf16[3,64,192]{2,1,0:T(8,128)(2,1)S(1)}, f32[3,64,768]{2,1,0:T(8,128)S(1)}) custom-call(bf16[4,3,80,768]{3,2,1,0:T(8,128)(2,1)} %stack.4.refs_0_, bf16[4,3,80,768]{3,2,1,0:T(8,128)(2,1)} %collective-permute-done.3.refs_1_, ...), custom_call_target="tpu_custom_call" | custom-call | flops 5033164800 | bytes 8912896 | tf_op jit(solution)/shard_map/attend/pallas_call | solution.py:288
  170.1 8.3 %attend.4 = (bf16[2,64,192]{2,1,0:T(8,128)(2,1)S(1)}, bf16[2,64,192]{2,1,0:T(8,128)(2,1)S(1)}, bf16[2,64,192]{2,1,0:T(8,128)(2,1)S(1)}, bf16[2,64,192]{2,1,0:T(8,128)(2,1)S(1)}, f32[2,64,768]{2,1,0:T(8,128)S(1)}) custom-call(bf16[4,2,80,768]{3,2,1,0:T(8,128)(2,1)S(1)} %stack.6.refs_0_, bf16[4,2,80,768]{3,2,1,0:T(8,128)(2,1)} %collective-permute-done.21.refs_1_, ...), custom_call_target="tpu_custom_call" | custom-call | flops 3355443200 | bytes 7340032 | tf_op jit(solution)/shard_map/attend/pallas_call | solution.py:288
  178.5 4.5 %attend.5 = (bf16[1,64,192]{2,1,0:T(8,128)(2,1)S(1)}, bf16[1,64,192]{2,1,0:T(8,128)(2,1)S(1)}, bf16[1,64,192]{2,1,0:T(8,128)(2,1)S(1)}, bf16[1,64,192]{2,1,0:T(8,128)(2,1)S(1)}, f32[1,64,768]{2,1,0:T(8,128)S(1)}) custom-call(bf16[4,1,80,768]{3,2,1,0:T(8,128)(2,1)S(1)} %stack.7.refs_0_, bf16[4,1,80,768]{3,2,1,0:T(8,128)(2,1)} %collective-permute-done.30.refs_1_, ...), custom_call_target="tpu_custom_call" | custom-call | flops 1677721600 | bytes 5767168 | tf_op jit(solution)/shard_map/attend/pallas_call | solution.py:288
  183.3 1.7 collective-permute-start.24
  188.4 2.0 collective-permute-done.35.refs_7_
  193.7 2.4 %collective-permute-start.38 = (bf16[3,16,768]{2,1,0:T(8,128)(2,1)S(1)}, bf16[3,16,768]{2,1,0:T(8,128)(2,1)S(1)}, u32[]{:S(2)}, u32[]{:S(2)}) collective-permute-start(bf16[3,16,768]{2,1,0:T(8,128)(2,1)S(1)} %get-tuple-element.102), channel_id=1, source_target_pairs={{0,12},{1,13},{2,14},{3,15},{4,8},{5,9},{6,10},{7,11},{8,4},{9,5},... | collective-permute-start | bytes 221192 | tf_op jit(solution)/shard_map/ppermute | solution.py:423
  196.7 2.0 collective-permute-start.16
  198.7 2.4 %collective-permute-start.17 = (bf16[3,16,768]{2,1,0:T(8,128)(2,1)S(1)}, bf16[3,16,768]{2,1,0:T(8,128)(2,1)S(1)}, u32[]{:S(2)}, u32[]{:S(2)}) collective-permute-start(bf16[3,16,768]{2,1,0:T(8,128)(2,1)S(1)} %get-tuple-element.72), channel_id=1, source_target_pairs={{0,12},{1,13},{2,14},{3,15},{4,8},{5,9},{6,10},{7,11},{8,4},{9,5},... | collective-permute-start | bytes 221192 | tf_op jit(solution)/shard_map/ppermute | solution.py:423
  202.6 4.9 %collective-permute-done.16.refs_2_ = bf16[3,16,768]{2,1,0:T(8,128)(2,1)S(1)} collective-permute-done((bf16[3,16,768]{2,1,0:T(8,128)(2,1)S(1)}, bf16[3,16,768]{2,1,0:T(8,128)(2,1)S(1)}, u32[]{:S(2)}, u32[]{:S(2)}) %collective-permute-start.16) | collective-permute-done | bytes 73760 | tf_op jit(solution)/shard_map/ppermute | solution.py:423
  (111 shorter events, 21.3 us)
Async XLA Ops:
  3.0 18.9 %collective-permute-start = (bf16[3,80,768]{2,1,0:T(8,128)(2,1)S(1)}, bf16[3,80,768]{2,1,0:T(8,128)(2,1)S(1)}, u32[]{:S(2)}, u32[]{:S(2)}) collective-permute-start(bf16[3,80,768]{2,1,0:T(8,128)(2,1)S(1)} %get-tuple-element.55), channel_id=1, source_target_pairs={{0,4},{1,5},{2,6},{3,7},{4,0},{5,1},{6,2},{7,3},{8,12},{9,13},{10,... | collective-permute-start | bytes 1105928 | tf_op jit(solution)/shard_map/ppermute | solution.py:423
  6.1 28.2 %collective-permute-start.1 = (bf16[3,80,768]{2,1,0:T(8,128)(2,1)S(1)}, bf16[3,80,768]{2,1,0:T(8,128)(2,1)S(1)}, u32[]{:S(2)}, u32[]{:S(2)}) collective-permute-start(bf16[3,80,768]{2,1,0:T(8,128)(2,1)S(1)} %get-tuple-element.56), channel_id=1, source_target_pairs={{0,8},{1,9},{2,10},{3,11},{4,12},{5,13},{6,14},{7,15},{8,0},{9,1},... | collective-permute-start | bytes 1105928 | tf_op jit(solution)/shard_map/ppermute | solution.py:423
  8.7 25.6 %collective-permute-start.2 = (bf16[3,80,768]{2,1,0:T(8,128)(2,1)S(1)}, bf16[3,80,768]{2,1,0:T(8,128)(2,1)S(1)}, u32[]{:S(2)}, u32[]{:S(2)}) collective-permute-start(bf16[3,80,768]{2,1,0:T(8,128)(2,1)S(1)} %get-tuple-element.57), channel_id=1, source_target_pairs={{0,12},{1,13},{2,14},{3,15},{4,8},{5,9},{6,10},{7,11},{8,4},{9,5},... | collective-permute-start | bytes 1105928 | tf_op jit(solution)/shard_map/ppermute | solution.py:423
  36.0 51.0 %collective-permute-start.3 = (bf16[4,3,80,768]{3,2,1,0:T(8,128)(2,1)}, bf16[4,3,80,768]{3,2,1,0:T(8,128)(2,1)}, u32[]{:S(2)}, u32[]{:S(2)}) collective-permute-start(bf16[4,3,80,768]{3,2,1,0:T(8,128)(2,1)} %stack.4.refs_0_), channel_id=1, source_target_pairs={{0,2},{1,3},{2,0},{3,1},{4,6},{5,7},{6,4},{7,5},{8,10},{9,11},{10,... | collective-permute-start | bytes 4423688 | tf_op jit(solution)/shard_map/ppermute | solution.py:423
  47.2 9.1 %collective-permute-start.6 = (bf16[528,128]{1,0:T(8,128)(2,1)S(1)}, bf16[528,128]{1,0:T(8,128)(2,1)S(1)}, u32[]{:S(2)}, u32[]{:S(2)}) collective-permute-start(bf16[528,128]{1,0:T(8,128)(2,1)S(1)} %get-tuple-element.59), channel_id=1, source_target_pairs={{0,1},{1,0},{2,3},{3,2},{4,5},{5,4},{6,7},{7,6},{8,9},{9,8},{10,11... | collective-permute-start | bytes 405512 | tf_op jit(solution)/shard_map/ppermute | solution.py:423
  47.3 23.5 %collective-permute-start.7 = (bf16[528,128]{1,0:T(8,128)(2,1)S(1)}, bf16[528,128]{1,0:T(8,128)(2,1)S(1)}, u32[]{:S(2)}, u32[]{:S(2)}) collective-permute-start(bf16[528,128]{1,0:T(8,128)(2,1)S(1)} %get-tuple-element.60), channel_id=1, source_target_pairs={{0,2},{1,3},{2,0},{3,1},{4,6},{5,7},{6,4},{7,5},{8,10},{9,11},{10,... | collective-permute-start | bytes 405512 | tf_op jit(solution)/shard_map/ppermute | solution.py:423
  48.1 38.0 %collective-permute-start.18 = (bf16[2,80,768]{2,1,0:T(8,128)(2,1)S(1)}, bf16[2,80,768]{2,1,0:T(8,128)(2,1)S(1)}, u32[]{:S(2)}, u32[]{:S(2)}) collective-permute-start(bf16[2,80,768]{2,1,0:T(8,128)(2,1)S(1)} %get-tuple-element.74), channel_id=1, source_target_pairs={{0,4},{1,5},{2,6},{3,7},{4,0},{5,1},{6,2},{7,3},{8,12},{9,13},{10,... | collective-permute-start | bytes 737288 | tf_op jit(solution)/shard_map/ppermute | solution.py:423
  55.2 30.9 %collective-permute-start.19 = (bf16[2,80,768]{2,1,0:T(8,128)(2,1)S(1)}, bf16[2,80,768]{2,1,0:T(8,128)(2,1)S(1)}, u32[]{:S(2)}, u32[]{:S(2)}) collective-permute-start(bf16[2,80,768]{2,1,0:T(8,128)(2,1)S(1)} %get-tuple-element.75), channel_id=1, source_target_pairs={{0,8},{1,9},{2,10},{3,11},{4,12},{5,13},{6,14},{7,15},{8,0},{9,1},... | collective-permute-start | bytes 737288 | tf_op jit(solution)/shard_map/ppermute | solution.py:423
  56.3 29.8 %collective-permute-start.20 = (bf16[2,80,768]{2,1,0:T(8,128)(2,1)S(1)}, bf16[2,80,768]{2,1,0:T(8,128)(2,1)S(1)}, u32[]{:S(2)}, u32[]{:S(2)}) collective-permute-start(bf16[2,80,768]{2,1,0:T(8,128)(2,1)S(1)} %get-tuple-element.76), channel_id=1, source_target_pairs={{0,12},{1,13},{2,14},{3,15},{4,8},{5,9},{6,10},{7,11},{8,4},{9,5},... | collective-permute-start | bytes 737288 | tf_op jit(solution)/shard_map/ppermute | solution.py:423
  76.6 45.6 %collective-permute-start.10 = (bf16[4,528,128]{2,1,0:T(8,128)(2,1)S(1)}, bf16[4,528,128]{2,1,0:T(8,128)(2,1)S(1)}, u32[]{:S(2)}, u32[]{:S(2)}) collective-permute-start(bf16[4,528,128]{2,1,0:T(8,128)(2,1)S(1)} %stack.5.refs_0_), channel_id=1, source_target_pairs={{0,8},{1,9},{2,10},{3,11},{4,12},{5,13},{6,14},{7,15},{8,0},{9,1},... | collective-permute-start | bytes 1622024 | tf_op jit(solution)/shard_map/ppermute | solution.py:423
  86.3 51.8 %collective-permute-start.21 = (bf16[4,2,80,768]{3,2,1,0:T(8,128)(2,1)S(1)}, bf16[4,2,80,768]{3,2,1,0:T(8,128)(2,1)}, u32[]{:S(2)}, u32[]{:S(2)}) collective-permute-start(bf16[4,2,80,768]{3,2,1,0:T(8,128)(2,1)S(1)} %stack.6.refs_0_), channel_id=1, source_target_pairs={{0,2},{1,3},{2,0},{3,1},{4,6},{5,7},{6,4},{7,5},{8,10},{9,11},{10,... | collective-permute-start | bytes 2949128 | tf_op jit(solution)/shard_map/ppermute | solution.py:423
  87.0 70.9 %collective-permute-start.4 = (bf16[4,3,80,768]{3,2,1,0:T(8,128)(2,1)}, bf16[4,3,80,768]{3,2,1,0:T(8,128)(2,1)}, u32[]{:S(2)}, u32[]{:S(2)}) collective-permute-start(bf16[4,3,80,768]{3,2,1,0:T(8,128)(2,1)} %stack.4.refs_0_), channel_id=1, source_target_pairs={{0,1},{1,0},{2,3},{3,2},{4,5},{5,4},{6,7},{7,6},{8,9},{9,8},{10,11... | collective-permute-start | bytes 4423688 | tf_op jit(solution)/shard_map/ppermute | solution.py:423
  87.0 71.4 %collective-permute-start.5 = (bf16[4,3,80,768]{3,2,1,0:T(8,128)(2,1)}, bf16[4,3,80,768]{3,2,1,0:T(8,128)(2,1)}, u32[]{:S(2)}, u32[]{:S(2)}) collective-permute-start(bf16[4,3,80,768]{3,2,1,0:T(8,128)(2,1)} %collective-permute-done.3.refs_1_), channel_id=1, source_target_pairs={{0,1},{1,0},{2,3},{3,2},{4,5},{5,4},{6,7},{7,6},{8,9},{9,8},{10,11... | collective-permute-start | bytes 4423688 | tf_op jit(solution)/shard_map/ppermute | solution.py:423
  87.5 13.1 %collective-permute-start.27 = (bf16[1,80,768]{2,1,0:T(8,128)(2,1)S(1)}, bf16[1,80,768]{2,1,0:T(8,128)(2,1)S(1)}, u32[]{:S(2)}, u32[]{:S(2)}) collective-permute-start(bf16[1,80,768]{2,1,0:T(8,128)(2,1)S(1)} %get-tuple-element.86), channel_id=1, source_target_pairs={{0,4},{1,5},{2,6},{3,7},{4,0},{5,1},{6,2},{7,3},{8,12},{9,13},{10,... | collective-permute-start | bytes 368648 | tf_op jit(solution)/shard_map/ppermute | solution.py:423
  100.6 14.9 %collective-permute-start.28 = (bf16[1,80,768]{2,1,0:T(8,128)(2,1)S(1)}, bf16[1,80,768]{2,1,0:T(8,128)(2,1)S(1)}, u32[]{:S(2)}, u32[]{:S(2)}) collective-permute-start(bf16[1,80,768]{2,1,0:T(8,128)(2,1)S(1)} %get-tuple-element.87), channel_id=1, source_target_pairs={{0,8},{1,9},{2,10},{3,11},{4,12},{5,13},{6,14},{7,15},{8,0},{9,1},... | collective-permute-start | bytes 368648 | tf_op jit(solution)/shard_map/ppermute | solution.py:423
  115.5 6.7 %collective-permute-start.29 = (bf16[1,80,768]{2,1,0:T(8,128)(2,1)S(1)}, bf16[1,80,768]{2,1,0:T(8,128)(2,1)S(1)}, u32[]{:S(2)}, u32[]{:S(2)}) collective-permute-start(bf16[1,80,768]{2,1,0:T(8,128)(2,1)S(1)} %get-tuple-element.88), channel_id=1, source_target_pairs={{0,12},{1,13},{2,14},{3,15},{4,8},{5,9},{6,10},{7,11},{8,4},{9,5},... | collective-permute-start | bytes 368648 | tf_op jit(solution)/shard_map/ppermute | solution.py:423
  122.1 15.1 %collective-permute-start.9 = (bf16[4,528,128]{2,1,0:T(8,128)(2,1)S(1)}, bf16[4,528,128]{2,1,0:T(8,128)(2,1)S(1)}, u32[]{:S(2)}, u32[]{:S(2)}) collective-permute-start(bf16[4,528,128]{2,1,0:T(8,128)(2,1)S(1)} %stack.5.refs_0_), channel_id=1, source_target_pairs={{0,4},{1,5},{2,6},{3,7},{4,0},{5,1},{6,2},{7,3},{8,12},{9,13},{10,... | collective-permute-start | bytes 1622024 | tf_op jit(solution)/shard_map/ppermute | solution.py:423
  122.2 24.1 %collective-permute-start.11 = (bf16[4,528,128]{2,1,0:T(8,128)(2,1)S(1)}, bf16[4,528,128]{2,1,0:T(8,128)(2,1)S(1)}, u32[]{:S(2)}, u32[]{:S(2)}) collective-permute-start(bf16[4,528,128]{2,1,0:T(8,128)(2,1)S(1)} %collective-permute-done.10.refs_2_), channel_id=1, source_target_pairs={{0,4},{1,5},{2,6},{3,7},{4,0},{5,1},{6,2},{7,3},{8,12},{9,13},{10,... | collective-permute-start | bytes 1622024 | tf_op jit(solution)/shard_map/ppermute | solution.py:423
  138.1 32.0 %collective-permute-start.22 = (bf16[4,2,80,768]{3,2,1,0:T(8,128)(2,1)S(1)}, bf16[4,2,80,768]{3,2,1,0:T(8,128)(2,1)}, u32[]{:S(2)}, u32[]{:S(2)}) collective-permute-start(bf16[4,2,80,768]{3,2,1,0:T(8,128)(2,1)S(1)} %stack.6.refs_0_), channel_id=1, source_target_pairs={{0,1},{1,0},{2,3},{3,2},{4,5},{5,4},{6,7},{7,6},{8,9},{9,8},{10,11... | collective-permute-start | bytes 2949128 | tf_op jit(solution)/shard_map/ppermute | solution.py:423
  138.1 32.0 %collective-permute-start.23 = (bf16[4,2,80,768]{3,2,1,0:T(8,128)(2,1)}, bf16[4,2,80,768]{3,2,1,0:T(8,128)(2,1)}, u32[]{:S(2)}, u32[]{:S(2)}) collective-permute-start(bf16[4,2,80,768]{3,2,1,0:T(8,128)(2,1)} %collective-permute-done.21.refs_1_), channel_id=1, source_target_pairs={{0,1},{1,0},{2,3},{3,2},{4,5},{5,4},{6,7},{7,6},{8,9},{9,8},{10,11... | collective-permute-start | bytes 2949128 | tf_op jit(solution)/shard_map/ppermute | solution.py:423
  147.1 10.8 %collective-permute-start.30 = (bf16[4,1,80,768]{3,2,1,0:T(8,128)(2,1)S(1)}, bf16[4,1,80,768]{3,2,1,0:T(8,128)(2,1)}, u32[]{:S(2)}, u32[]{:S(2)}) collective-permute-start(bf16[4,1,80,768]{3,2,1,0:T(8,128)(2,1)S(1)} %stack.7.refs_0_), channel_id=1, source_target_pairs={{0,2},{1,3},{2,0},{3,1},{4,6},{5,7},{6,4},{7,5},{8,10},{9,11},{10,... | collective-permute-start | bytes 1474568 | tf_op jit(solution)/shard_map/ppermute | solution.py:423
  157.9 20.6 %collective-permute-start.31 = (bf16[4,1,80,768]{3,2,1,0:T(8,128)(2,1)S(1)}, bf16[4,1,80,768]{3,2,1,0:T(8,128)(2,1)S(1)}, u32[]{:S(2)}, u32[]{:S(2)}) collective-permute-start(bf16[4,1,80,768]{3,2,1,0:T(8,128)(2,1)S(1)} %stack.7.refs_0_), channel_id=1, source_target_pairs={{0,1},{1,0},{2,3},{3,2},{4,5},{5,4},{6,7},{7,6},{8,9},{9,8},{10,11... | collective-permute-start | bytes 1474568 | tf_op jit(solution)/shard_map/ppermute | solution.py:423
  157.9 20.6 %collective-permute-start.32 = (bf16[4,1,80,768]{3,2,1,0:T(8,128)(2,1)}, bf16[4,1,80,768]{3,2,1,0:T(8,128)(2,1)S(1)}, u32[]{:S(2)}, u32[]{:S(2)}) collective-permute-start(bf16[4,1,80,768]{3,2,1,0:T(8,128)(2,1)} %collective-permute-done.30.refs_1_), channel_id=1, source_target_pairs={{0,1},{1,0},{2,3},{3,2},{4,5},{5,4},{6,7},{7,6},{8,9},{9,8},{10,11... | collective-permute-start | bytes 1474568 | tf_op jit(solution)/shard_map/ppermute | solution.py:423
  183.3 7.1 %collective-permute-start.24 = (bf16[2,64,192]{2,1,0:T(8,128)(2,1)S(1)}, bf16[2,64,192]{2,1,0:T(8,128)(2,1)S(1)}, u32[]{:S(2)}, u32[]{:S(2)}) collective-permute-start(bf16[2,64,192]{2,1,0:T(8,128)(2,1)S(1)} %get-tuple-element.82), channel_id=1, source_target_pairs={{0,2},{1,3},{2,0},{3,1},{4,6},{5,7},{6,4},{7,5},{8,10},{9,11},{10,... | collective-permute-start | bytes 147464 | tf_op jit(solution)/shard_map/ppermute | solution.py:423
  185.1 6.0 %collective-permute-start.25 = (bf16[2,64,192]{2,1,0:T(8,128)(2,1)S(1)}, bf16[2,64,192]{2,1,0:T(8,128)(2,1)S(1)}, u32[]{:S(2)}, u32[]{:S(2)}) collective-permute-start(bf16[2,64,192]{2,1,0:T(8,128)(2,1)S(1)} %get-tuple-element.83), channel_id=1, source_target_pairs={{0,1},{1,0},{2,3},{3,2},{4,5},{5,4},{6,7},{7,6},{8,9},{9,8},{10,11... | collective-permute-start | bytes 147464 | tf_op jit(solution)/shard_map/ppermute | solution.py:423
  187.3 6.4 %collective-permute-start.12 = (bf16[3,64,192]{2,1,0:T(8,128)(2,1)S(1)}, bf16[3,64,192]{2,1,0:T(8,128)(2,1)S(1)}, u32[]{:S(2)}, u32[]{:S(2)}) collective-permute-start(bf16[3,64,192]{2,1,0:T(8,128)(2,1)S(1)} %get-tuple-element.65), channel_id=1, source_target_pairs={{0,2},{1,3},{2,0},{3,1},{4,6},{5,7},{6,4},{7,5},{8,10},{9,11},{10,... | collective-permute-start | bytes 221192 | tf_op jit(solution)/shard_map/ppermute | solution.py:423
  191.7 7.0 %collective-permute-start.36 = (bf16[3,16,768]{2,1,0:T(8,128)(2,1)S(1)}, bf16[3,16,768]{2,1,0:T(8,128)(2,1)S(1)}, u32[]{:S(2)}, u32[]{:S(2)}) collective-permute-start(bf16[3,16,768]{2,1,0:T(8,128)(2,1)S(1)} %get-tuple-element.100), channel_id=1, source_target_pairs={{0,4},{1,5},{2,6},{3,7},{4,0},{5,1},{6,2},{7,3},{8,12},{9,13},{10,... | collective-permute-start | bytes 221192 | tf_op jit(solution)/shard_map/ppermute | solution.py:423
  192.3 9.6 %collective-permute-start.37 = (bf16[3,16,768]{2,1,0:T(8,128)(2,1)S(1)}, bf16[3,16,768]{2,1,0:T(8,128)(2,1)S(1)}, u32[]{:S(2)}, u32[]{:S(2)}) collective-permute-start(bf16[3,16,768]{2,1,0:T(8,128)(2,1)S(1)} %get-tuple-element.101), channel_id=1, source_target_pairs={{0,8},{1,9},{2,10},{3,11},{4,12},{5,13},{6,14},{7,15},{8,0},{9,1},... | collective-permute-start | bytes 221192 | tf_op jit(solution)/shard_map/ppermute | solution.py:423
  193.7 8.2 %collective-permute-start.38 = (bf16[3,16,768]{2,1,0:T(8,128)(2,1)S(1)}, bf16[3,16,768]{2,1,0:T(8,128)(2,1)S(1)}, u32[]{:S(2)}, u32[]{:S(2)}) collective-permute-start(bf16[3,16,768]{2,1,0:T(8,128)(2,1)S(1)} %get-tuple-element.102), channel_id=1, source_target_pairs={{0,12},{1,13},{2,14},{3,15},{4,8},{5,9},{6,10},{7,11},{8,4},{9,5},... | collective-permute-start | bytes 221192 | tf_op jit(solution)/shard_map/ppermute | solution.py:423
  196.6 6.0 %collective-permute-start.15 = (bf16[3,16,768]{2,1,0:T(8,128)(2,1)S(1)}, bf16[3,16,768]{2,1,0:T(8,128)(2,1)S(1)}, u32[]{:S(2)}, u32[]{:S(2)}) collective-permute-start(bf16[3,16,768]{2,1,0:T(8,128)(2,1)S(1)} %get-tuple-element.70), channel_id=1, source_target_pairs={{0,4},{1,5},{2,6},{3,7},{4,0},{5,1},{6,2},{7,3},{8,12},{9,13},{10,... | collective-permute-start | bytes 221192 | tf_op jit(solution)/shard_map/ppermute | solution.py:423
  196.7 10.8 %collective-permute-start.16 = (bf16[3,16,768]{2,1,0:T(8,128)(2,1)S(1)}, bf16[3,16,768]{2,1,0:T(8,128)(2,1)S(1)}, u32[]{:S(2)}, u32[]{:S(2)}) collective-permute-start(bf16[3,16,768]{2,1,0:T(8,128)(2,1)S(1)} %get-tuple-element.71), channel_id=1, source_target_pairs={{0,8},{1,9},{2,10},{3,11},{4,12},{5,13},{6,14},{7,15},{8,0},{9,1},... | collective-permute-start | bytes 221192 | tf_op jit(solution)/shard_map/ppermute | solution.py:423
  198.7 8.8 %collective-permute-start.17 = (bf16[3,16,768]{2,1,0:T(8,128)(2,1)S(1)}, bf16[3,16,768]{2,1,0:T(8,128)(2,1)S(1)}, u32[]{:S(2)}, u32[]{:S(2)}) collective-permute-start(bf16[3,16,768]{2,1,0:T(8,128)(2,1)S(1)} %get-tuple-element.72), channel_id=1, source_target_pairs={{0,12},{1,13},{2,14},{3,15},{4,8},{5,9},{6,10},{7,11},{8,4},{9,5},... | collective-permute-start | bytes 221192 | tf_op jit(solution)/shard_map/ppermute | solution.py:423
  (26 other events, 260.0 us)

commit v2 on v1

--- a/solution.py
+++ b/solution.py
@@ -74,26 +74,27 @@
     )(mask, pair.reshape(fold, rows, keys, c), pair_gain[None], proj_t)
 
 
-def pack_kernel(sizes, sg, group_ref, *refs):
+def pack_kernel(sizes, count, group_ref, *refs):
     step = pl.program_id(0)
     start = 0
     for i, size in enumerate(sizes):
 
         @pl.when((step >= start) & (step < start + size))
         def _(i=i):
-            for k in range(sg):
-                out_ref = refs[(2 + i) * sg + k]
+            for k in range(count):
+                out_ref = refs[(2 + i) * count + k]
                 keys = refs[k].shape[2]
                 out_ref[0, :keys] = refs[k][0, 0]
-                out_ref[0, keys:] = refs[sg + k][0, 0]
+                out_ref[0, keys:] = refs[count + k][0, 0]
 
         start += size
 
 
-def pack(group, key_groups, query_groups, first, sizes):
-    sg, _, keys, width = key_groups.shape
+def pack(group, key_groups, query_groups, first, sizes, steps, limit):
+    _, _, keys, width = key_groups.shape
     rows = query_groups.shape[2]
     total = sum(sizes)
+    count = len(steps)
 
     def spec(length, k):
         return pl.BlockSpec((1, 1, length, width), lambda s, g: (g[0] ^ k, first + s, 0, 0))
@@ -105,21 +106,21 @@
         )
 
     outs = pl.pallas_call(
-        functools.partial(pack_kernel, sizes, sg),
+        functools.partial(pack_kernel, sizes, count),
         grid_spec=pltpu.PrefetchScalarGridSpec(
             num_scalar_prefetch=1,
             grid=(total,),
-            in_specs=[spec(keys, k) for k in range(sg)] + [spec(rows, k) for k in range(sg)],
-            out_specs=[out_spec(i) for i in range(len(sizes)) for _ in range(sg)],
-        ),
-        out_shape=[jax.ShapeDtypeStruct((size, keys + rows, width), BF16) for size in sizes for _ in range(sg)],
+            in_specs=[spec(keys, k) for k in steps] + [spec(rows, k) for k in steps],
+            out_specs=[out_spec(i) for i in range(len(sizes)) for _ in steps],
+        ),
+        out_shape=[jax.ShapeDtypeStruct((size, keys + rows, width), BF16) for size in sizes for _ in steps],
         cost_estimate=pl.CostEstimate(
-            flops=0, bytes_accessed=4 * sg * total * (keys + rows) * width, transcendentals=0
-        ),
-        compiler_params=pltpu.CompilerParams(vmem_limit_bytes=12 * MIB),
+            flops=0, bytes_accessed=4 * count * total * (keys + rows) * width, transcendentals=0
+        ),
+        compiler_params=pltpu.CompilerParams(vmem_limit_bytes=limit),
         name="pack",
-    )(group.reshape(1), *([key_groups] * sg), *([query_groups] * sg))
-    return [outs[i * sg : (i + 1) * sg] for i in range(len(sizes))]
+    )(group.reshape(1), *([key_groups] * count), *([query_groups] * count))
+    return [outs[i * count : (i + 1) * count] for i in range(len(sizes))]
 
 
 def stack_kernel(*refs):
@@ -218,35 +219,41 @@
 
 
 def attention_kernel(pieces, hpg, direct, keys, *refs):
-    token_refs, refs = refs[:pieces], refs[pieces:]
+    own_refs, far_refs, refs = refs[:pieces], refs[pieces : 2 * pieces], refs[2 * pieces :]
     if not direct:
         query_ref, refs = refs[0], refs[1:]
     count = pieces if direct else 1
     bias_ref, mask_ref, wq_ref, wk_ref, wv_ref, wg_ref = refs[:6]
     out_refs, gate_ref = refs[6 : 6 + count], refs[6 + count]
     q_ref, k_ref, v_ref = refs[7 + count :]
-    sg, _, _, width = token_refs[0].shape
+    total_rows, width = own_refs[0].shape[1:]
     feats = wq_ref.shape[1]
     head_size = feats // hpg
     scale = LOG2E / math.sqrt(head_size)
 
-    def rows_of(ref, start, stop):
+    def own_rows(start, stop):
+        return jnp.concatenate([ref[0, start:stop] for ref in own_refs], axis=0)
+
+    def far_rows(ref, start, stop):
         block = ref[:, 0, start:stop]
         return block.reshape(block.shape[0] * block.shape[1], width)
 
-    for m in range(pieces):
-        block = rows_of(token_refs[m], 0, keys)
-        span = slice(m * sg * keys, (m + 1) * sg * keys)
+    at = 0
+    for m in range(-1, pieces):
+        block = own_rows(0, keys) if m < 0 else far_rows(far_refs[m], 0, keys)
+        span = slice(at, at + block.shape[0])
         k_t = nn_dot(block, wk_ref[...]).T
         k_ref[:, span] = jnp.where(mask_ref[:1, span] > 0, k_t, 0.0).astype(BF16)
         v_ref[span, :] = nn_dot(block, wv_ref[...]).astype(BF16)
+        at += block.shape[0]
     if direct:
-        for m in range(pieces):
-            block = rows_of(token_refs[m], keys, token_refs[m].shape[2])
-            span = slice(m * block.shape[0], (m + 1) * block.shape[0])
-            q_ref[span, :] = nn_dot(block, wq_ref[...]).astype(BF16)
-            if m == 0:
-                gate_ref[0] = jax.nn.sigmoid(nn_dot(block, wg_ref[...]))
+        at = 0
+        for m in range(-1, pieces):
+            block = own_rows(keys, total_rows) if m < 0 else far_rows(far_refs[m], keys, total_rows)
+            q_ref[at : at + block.shape[0], :] = nn_dot(block, wq_ref[...]).astype(BF16)
+            at += block.shape[0]
+        block = jnp.concatenate([own_refs[0][0, keys:], far_rows(far_refs[0], keys, total_rows)], axis=0)
+        gate_ref[0] = jax.nn.sigmoid(nn_dot(block, wg_ref[...]))
     else:
         q_ref[...] = nn_dot(query_ref[0], wq_ref[...]).astype(BF16)
         gate_ref[...] = jnp.zeros_like(gate_ref)
@@ -261,28 +268,35 @@
         norm = 1.0 / jnp.sum(weights, axis=-1, keepdims=True)
         result = nn_dot((weights * norm).astype(BF16), v_ref[...])
         total = result if total is None else jnp.where(mine, result, total)
-    rows = total.shape[0] // count
-    for m in range(count):
-        out_refs[m][0] = total[m * rows : (m + 1) * rows].astype(BF16)
-
-
-def attention(arrays, queries, bias, mask, wq, wk, wv, w_gate, hpg, keys, query_rows):
-    pieces = len(arrays)
-    sg, size, rows, width = arrays[0].shape
+    total = total.astype(BF16)
+    if not direct:
+        out_refs[0][0] = total
+        return
+    own = total_rows - keys
+    far = out_refs[0].shape[1] - own
+    for m, out_ref in enumerate(out_refs):
+        out_ref[0, :own] = total[m * own : (m + 1) * own]
+        out_ref[0, own:] = total[pieces * own + m * far : pieces * own + (m + 1) * far]
+
+
+def attention(first, own, far, queries, bias, mask, wq, wk, wv, w_gate, hpg, keys, query_rows):
+    pieces = len(far)
+    others, size, rows, width = far[0].shape
     window = bias.shape[1]
     tokens = bias.shape[2]
     feats = wq.shape[1]
     direct = queries is None
     whole = pl.BlockSpec(memory_space=pltpu.VMEM)
-    specs = [pl.BlockSpec((sg, 1, rows, width), lambda s: (0, s, 0, 0))] * pieces
-    args = list(arrays)
-    out_rows = [sg * query_rows] * pieces
+    specs = [pl.BlockSpec((1, rows, width), lambda s: (first + s, 0, 0))] * pieces
+    specs += [pl.BlockSpec((others, 1, rows, width), lambda s: (0, s, 0, 0))] * pieces
+    args = list(own) + list(far)
+    gate_rows = (others + 1) * query_rows
+    out_rows = [gate_rows] * pieces
     if not direct:
         specs.append(pl.BlockSpec((1, window, width), lambda s: (s, 0, 0)))
         args.append(queries)
         out_rows = [window]
     consts = [bias, mask, wq, wk, wv, w_gate]
-    gate_rows = sg * query_rows
     limit = (60 if tokens > 2048 else 26) * MIB
     flops = 2 * size * (tokens * width * feats * 2 + hpg * window * tokens * 512)
     return pl.pallas_call(
@@ -427,7 +441,7 @@
     while bit:
         labels = labels + [m ^ bit for m in labels]
         bit //= 2
-    codes = [k * hg + m for m in labels for k in range(sg)]
+    codes = labels + [k * hg + m for m in labels for k in range(1, sg)]
     code_list = jnp.array(codes, jnp.int32)
     slot_of = [0] * n
     for p, code in enumerate(codes):
@@ -436,9 +450,20 @@
     key_groups = key_tokens.reshape(sg, group_samples, keys, width)
     query_groups = query_tokens.reshape(sg, group_samples, query_rows, width)
 
-    packed = pack(group, key_groups, query_groups, 0, sizes[:1])
-    packed = packed + pack(group, key_groups, query_groups, firsts[1], sizes[1:])
-    got = [[across(x, k * hg) for k, x in enumerate(sent)] for sent in packed]
+    others = range(1, sg)
+    packed = pack(group, key_groups, query_groups, 0, sizes[:1], others, 56 * MIB)
+    own_tokens = pack(group, key_groups, query_groups, 0, [group_samples], [0], 8 * MIB)[0]
+    packed = packed + pack(group, key_groups, query_groups, firsts[1], sizes[1:], others, 12 * MIB)
+    got = [[across(x, k * hg) for k, x in zip(others, sent)] for sent in packed]
+
+    def over_lanes(arrays):
+        bit = hg // 2
+        while bit:
+            arrays = arrays + [across(x, bit) for x in arrays]
+            bit //= 2
+        return arrays
+
+    own_tokens = over_lanes(list(own_tokens))
 
     relative = jnp.arange(hg) ^ lane
     proj_t = jnp.take(pair_proj.T.reshape(hg, hpg, -1), relative, axis=0).reshape(H, -1)
@@ -466,27 +491,29 @@
     heads, gates = [], []
     previous = None
     for c, size in enumerate(sizes):
-        arrays = [stacked(got[c])]
-        bit = hg // 2
-        while bit:
-            arrays = arrays + [across(x, bit) for x in arrays]
-            bit //= 2
+        far = [stacked(got[c])]
+        far = over_lanes(far)
         queries = None
         if not direct:
             order = jnp.array(slot_of, jnp.int32)[me ^ jnp.arange(n)]
-            queries = jnp.concatenate([x[:, :, keys:] for x in arrays], axis=0)
+            mine = [x[None, firsts[c] : firsts[c] + size, keys:] for x in own_tokens]
+            queries = jnp.concatenate(mine + [x[:, :, keys:] for x in far], axis=0)
             queries = jnp.swapaxes(jnp.take(queries, order, axis=0), 0, 1).reshape(size, window, width)
         if previous is not None:
-            arrays, previous = lax.optimization_barrier((arrays, previous))
-        results = attention(arrays, queries, bias, mask, wq, wk, wv, w_gate, hpg, keys, query_rows)
+            far, previous = lax.optimization_barrier((far, previous))
+        results = attention(firsts[c], own_tokens, far, queries, bias, mask, wq, wk, wv, w_gate, hpg, keys, query_rows)
         results, gate = results[:-1], results[-1]
         previous = gate
         if not direct:
             blocks = jnp.take(results[0].reshape(size, n, query_rows, feats), code_list ^ me, axis=1)
-            results = [
-                blocks[:, i * sg : (i + 1) * sg].reshape(size, sg * query_rows, feats) for i in range(hg)
-            ]
-            tokens = jnp.swapaxes(arrays[0][:, :, keys:], 0, 1).reshape(size, sg * query_rows, width)
+            results = []
+            for i in range(hg):
+                start = hg + i * (sg - 1)
+                part = jnp.concatenate([blocks[:, i : i + 1], blocks[:, start : start + sg - 1]], axis=1)
+                results.append(part.reshape(size, sg * query_rows, feats))
+            mine = own_tokens[0][None, firsts[c] : firsts[c] + size, keys:]
+            tokens = jnp.concatenate([mine, far[0][:, :, keys:]], axis=0)
+            tokens = jnp.swapaxes(tokens, 0, 1).reshape(size, sg * query_rows, width)
             gate = jax.nn.sigmoid(nn_dot(tokens, w_gate))
         heads.append([across(r, m) for r, m in zip(results, labels)])
         gates.append(gate)

time: 209 us -> 202 us (0.967)
  waiting for transfers between devices: 111 us -> 76.1 us
  starting transfers between devices: 48.5 us -> 68.9 us
  Pallas kernels: 38.6 us -> 45.9 us
    ppermute x39 -> x42, waiting for transfers between devices: 111 us -> 76.1 us  [across(): return lax.ppermute(x, 'key', [(i, i ^ code) for i in range(n)])]
    ppermute x39 -> x42, starting transfers between devices: 48.5 us -> 68.9 us  [across(): return lax.ppermute(x, 'key', [(i, i ^ code) for i in range(n)])]
    pallas_call x2 -> x3, Pallas kernels: 0.38 us -> 4.45 us  [pack(): pl.pallas_call(functools.partial(pack_kernel, sizes, count), grid_spec=pl...]
    pallas_call x4, Pallas kernels: 1.95 us -> 4.34 us  [stacked(): pl.pallas_call(stack_kernel, grid=(steps,), in_specs=[pl.BlockSpec(block,...]
    unnamed x38 -> x58, local copies, waits for them, and re-layouts: 6.7 us -> 6.76 us
  transfers between devices with their start and end apart: 39 -> 42, of which waited for: 15 -> 14; matrix products, arithmetic and copies ran while one was open for 1% -> 2% of each run, Pallas kernels for 15% -> 18%
where the time goes in v2:
time: 202 us
  waiting for transfers between devices  76.1 us (38%)
  starting transfers between devices  68.9 us (34%)
  Pallas kernels  45.9 us (23%)
  local copies, waits for them, and re-layouts  9.96 us (5%)
    ppermute x42, waiting for transfers between devices, across(): return lax.ppermute(x, 'key', [(i, i ^ code) for i in range(n)])  76.1 us
    ppermute x42, starting transfers between devices, across(): return lax.ppermute(x, 'key', [(i, i ^ code) for i in range(n)])  68.9 us
    pallas_call x3, Pallas kernels, attention(): pl.pallas_call(functools.partial(attention_kernel, pieces, hpg, direct, k...  24.5 us
    unnamed x58, local copies, waits for them, and re-layouts  6.76 us
    pallas_call x1, Pallas kernels, local_bias(): pl.pallas_call(functools.partial(bias_kernel, hpg), grid=(rows // tile,),...  6.51 us
    pallas_call x3, Pallas kernels, pack(): pl.pallas_call(functools.partial(pack_kernel, sizes, count), grid_spec=pl...  4.45 us
    pallas_call x4, Pallas kernels, stacked(): pl.pallas_call(stack_kernel, grid=(steps,), in_specs=[pl.BlockSpec(block,...  4.34 us
    pallas_call x1, Pallas kernels, ordered_bias(): pl.pallas_call(functools.partial(order_kernel, hpg, keys, codes), in_spec...  4.14 us
  transfers between devices with their start and end apart: 42, of which 14 were waited for; matrix products, arithmetic and copies ran while one was open for 2% of the time, Pallas kernels for 18%

profile of v2, /device:TPU:0, one launch (start us, length us, event | category | flops | bytes accessed | tf_op | source)
XLA Modules:
  0.0 202.1 jit_solution(4107811807045101007)
XLA Ops:
  0.0 3.4 %pack.4 = (bf16[3,80,768]{2,1,0:T(8,128)(2,1)}, bf16[3,80,768]{2,1,0:T(8,128)(2,1)}, bf16[3,80,768]{2,1,0:T(8,128)(2,1)}) custom-call(s32[1]{0:T(128)} %bitcast.group_ref, bf16[4,6,64,768]{3,2,1,0:T(8,128)(2,1)} %bitcast.14, bf16[4,6,64,768]{3,2,1,0:T(8,128)(2,1)} %bitcast.15, bf16[4,6,64,768]{3,2,1,0:T(8,128)(2,1)} %bitcast.16, ...), custom_call_target="tpu_custom_call" | custom-call | bytes 2211840 | tf_op jit(solution)/shard_map/pack/pallas_call | solution.py:108
  3.4 3.1 %collective-permute-start.3 = (bf16[3,80,768]{2,1,0:T(8,128)(2,1)}, bf16[3,80,768]{2,1,0:T(8,128)(2,1)}, u32[]{:S(2)}, u32[]{:S(2)}) collective-permute-start(bf16[3,80,768]{2,1,0:T(8,128)(2,1)} %get-tuple-element.51), channel_id=1, source_target_pairs={{0,4},{1,5},{2,6},{3,7},{4,0},{5,1},{6,2},{7,3},{8,12},{9,13},{10,... | collective-permute-start | bytes 1105928 | tf_op jit(solution)/shard_map/ppermute | solution.py:437
  6.4 2.6 %collective-permute-start.4 = (bf16[3,80,768]{2,1,0:T(8,128)(2,1)}, bf16[3,80,768]{2,1,0:T(8,128)(2,1)}, u32[]{:S(2)}, u32[]{:S(2)}) collective-permute-start(bf16[3,80,768]{2,1,0:T(8,128)(2,1)} %get-tuple-element.52), channel_id=1, source_target_pairs={{0,8},{1,9},{2,10},{3,11},{4,12},{5,13},{6,14},{7,15},{8,0},{9,1},... | collective-permute-start | bytes 1105928 | tf_op jit(solution)/shard_map/ppermute | solution.py:437
  13.5 3.5 %collective-permute-start.31 = (bf16[1,80,768]{2,1,0:T(8,128)(2,1)}, bf16[1,80,768]{2,1,0:T(8,128)(2,1)}, u32[]{:S(2)}, u32[]{:S(2)}) collective-permute-start(bf16[1,80,768]{2,1,0:T(8,128)(2,1)} %get-tuple-element.81), channel_id=1, source_target_pairs={{0,8},{1,9},{2,10},{3,11},{4,12},{5,13},{6,14},{7,15},{8,0},{9,1},... | collective-permute-start | bytes 368648 | tf_op jit(solution)/shard_map/ppermute | solution.py:437
  18.3 5.0 %collective-permute-done.3.refs_0_ = bf16[3,80,768]{2,1,0:T(8,128)(2,1)} collective-permute-done((bf16[3,80,768]{2,1,0:T(8,128)(2,1)}, bf16[3,80,768]{2,1,0:T(8,128)(2,1)}, u32[]{:S(2)}, u32[]{:S(2)}) %collective-permute-start.3) | collective-permute-done | bytes 368672 | tf_op jit(solution)/shard_map/ppermute | solution.py:437
  23.3 4.5 %collective-permute-start.32 = (bf16[1,80,768]{2,1,0:T(8,128)(2,1)}, bf16[1,80,768]{2,1,0:T(8,128)(2,1)}, u32[]{:S(2)}, u32[]{:S(2)}) collective-permute-start(bf16[1,80,768]{2,1,0:T(8,128)(2,1)} %copy-done.25), channel_id=1, source_target_pairs={{0,12},{1,13},{2,14},{3,15},{4,8},{5,9},{6,10},{7,11},{8,4},{9,5},... | collective-permute-start | bytes 368648 | tf_op jit(solution)/shard_map/ppermute | solution.py:437
  27.9 7.1 %collective-permute-done.4.refs_1_ = bf16[3,80,768]{2,1,0:T(8,128)(2,1)} collective-permute-done((bf16[3,80,768]{2,1,0:T(8,128)(2,1)}, bf16[3,80,768]{2,1,0:T(8,128)(2,1)}, u32[]{:S(2)}, u32[]{:S(2)}) %collective-permute-start.4) | collective-permute-done | bytes 368672 | tf_op jit(solution)/shard_map/ppermute | solution.py:437
  34.9 3.1 %stack.4.refs_4_ = bf16[3,3,80,768]{3,2,1,0:T(8,128)(2,1)} custom-call(bf16[3,80,768]{2,1,0:T(8,128)(2,1)} %collective-permute-done.3.refs_0_, bf16[3,80,768]{2,1,0:T(8,128)(2,1)} %collective-permute-done.4.refs_1_, bf16[3,80,768]{2,1,0:T(8,128)(2,1)} %collective-permute-done.5.refs_2_), custom_call_target="tpu_custom_call" | custom-call | bytes 2211840 | tf_op jit(solution)/shard_map/stack/pallas_call | solution.py:136
  38.1 1.5 collective-permute-start.6
  40.4 2.2 %copy-done.8 = bf16[256,64,128]{2,1,0:T(8,128)(2,1)S(1)} copy-done((bf16[256,64,128]{2,1,0:T(8,128)(2,1)S(1)}, bf16[256,64,128]{2,1,0:T(8,128)(2,1)}, u32[]{:S(2)}) %copy-start.8) | copy-done | bytes 4194328
  42.6 6.5 %bias_local.1 = (bf16[528,128]{1,0:T(8,128)(2,1)S(1)}, bf16[528,128]{1,0:T(8,128)(2,1)S(1)}, bf16[528,128]{1,0:T(8,128)(2,1)S(1)}, bf16[528,128]{1,0:T(8,128)(2,1)S(1)}) custom-call(f32[1,128]{1,0:T(1,128)S(1)} %broadcast_in_dim_tile.3.mask_ref, bf16[2,128,64,128]{3,2,1,0:T(8,128)(2,1)S(1)} %bitcast.28, f32[1,128]{1,0:T(1,128)S(1)} %bitcast.29, ...), custom_call_target="tpu_custom_call" | custom-call | flops 1073741824 | bytes 4194304 | tf_op jit(solution)/shard_map/bias_local/pallas_call | solution.py:58
  51.4 13.7 %collective-permute-start.21 = (bf16[2,80,768]{2,1,0:T(8,128)(2,1)S(1)}, bf16[2,80,768]{2,1,0:T(8,128)(2,1)S(1)}, u32[]{:S(2)}, u32[]{:S(2)}) collective-permute-start(bf16[2,80,768]{2,1,0:T(8,128)(2,1)S(1)} %copy-done.24), channel_id=1, source_target_pairs={{0,4},{1,5},{2,6},{3,7},{4,0},{5,1},{6,2},{7,3},{8,12},{9,13},{10,... | collective-permute-start | bytes 737288 | tf_op jit(solution)/shard_map/ppermute | solution.py:437
  66.3 14.7 %collective-permute-start.22 = (bf16[2,80,768]{2,1,0:T(8,128)(2,1)S(1)}, bf16[2,80,768]{2,1,0:T(8,128)(2,1)S(1)}, u32[]{:S(2)}, u32[]{:S(2)}) collective-permute-start(bf16[2,80,768]{2,1,0:T(8,128)(2,1)S(1)} %copy-done.22), channel_id=1, source_target_pairs={{0,8},{1,9},{2,10},{3,11},{4,12},{5,13},{6,14},{7,15},{8,0},{9,1},... | collective-permute-start | bytes 737288 | tf_op jit(solution)/shard_map/ppermute | solution.py:437
  83.4 1.6 collective-permute-start.33
  85.4 20.2 %collective-permute-done.22.refs_1_ = bf16[2,80,768]{2,1,0:T(8,128)(2,1)S(1)} collective-permute-done((bf16[2,80,768]{2,1,0:T(8,128)(2,1)S(1)}, bf16[2,80,768]{2,1,0:T(8,128)(2,1)S(1)}, u32[]{:S(2)}, u32[]{:S(2)}) %collective-permute-start.22) | collective-permute-done | bytes 245792 | tf_op jit(solution)/shard_map/ppermute | solution.py:437
  105.6 1.6 collective-permute-start
  108.1 13.4 %collective-permute-done.13.refs_2_ = bf16[4,528,128]{2,1,0:T(8,128)(2,1)} collective-permute-done((bf16[4,528,128]{2,1,0:T(8,128)(2,1)S(1)}, bf16[4,528,128]{2,1,0:T(8,128)(2,1)}, u32[]{:S(2)}, u32[]{:S(2)}) %collective-permute-start.13) | collective-permute-done | bytes 540704 | tf_op jit(solution)/shard_map/ppermute | solution.py:437
  122.2 7.1 %collective-permute-done.12.refs_1_ = bf16[4,528,128]{2,1,0:T(8,128)(2,1)S(1)} collective-permute-done((bf16[4,528,128]{2,1,0:T(8,128)(2,1)S(1)}, bf16[4,528,128]{2,1,0:T(8,128)(2,1)S(1)}, u32[]{:S(2)}, u32[]{:S(2)}) %collective-permute-start.12) | collective-permute-done | bytes 540704 | tf_op jit(solution)/shard_map/ppermute | solution.py:437
  130.1 1.5 collective-permute-start.24
  131.8 1.7 constant_dynamic-slice_fusion
  133.4 12.4 %collective-permute-done.24.refs_5_ = bf16[3,2,80,768]{3,2,1,0:T(8,128)(2,1)} collective-permute-done((bf16[3,2,80,768]{3,2,1,0:T(8,128)(2,1)S(1)}, bf16[3,2,80,768]{3,2,1,0:T(8,128)(2,1)}, u32[]{:S(2)}, u32[]{:S(2)}) %collective-permute-start.24) | collective-permute-done | bytes 737312 | tf_op jit(solution)/shard_map/ppermute | solution.py:437
  146.7 4.1 %bias_order.1 = (f32[4,256,1024]{2,1,0:T(8,128)S(1)}, f32[8,1024]{1,0:T(8,128)S(1)}) custom-call(s32[1]{0:T(128)} %bitcast.4.me_ref, s32[16]{0:T(128)S(1)} %copy-done.17, s32[16]{0:T(128)S(1)} %broadcast_xor_fusion.qsel_ref, bf16[4,528,128]{2,1,0:T(8,128)(2,1)S(1)} %copy-done.10, bf16[4,528,128]{2,1,0:T(8,128)(2,1)S(1)} %copy-done.14, ...), custom_call_target="tpu_custom_call" | custom-call | flops 8388608 | bytes 6291456 | tf_op jit(solution)/shard_map/bias_order/pallas_call | solution.py:201
  151.4 11.8 %attend.3 = (bf16[3,64,192]{2,1,0:T(8,128)(2,1)S(1)}, bf16[3,64,192]{2,1,0:T(8,128)(2,1)S(1)}, bf16[3,64,192]{2,1,0:T(8,128)(2,1)S(1)}, bf16[3,64,192]{2,1,0:T(8,128)(2,1)S(1)}, f32[3,64,768]{2,1,0:T(8,128)S(1)}) custom-call(bf16[6,80,768]{2,1,0:T(8,128)(2,1)S(1)} %copy-done.5, bf16[6,80,768]{2,1,0:T(8,128)(2,1)S(1)} %collective-permute-done.refs_1_, ...), custom_call_target="tpu_custom_call" | custom-call | flops 5033164800 | bytes 8912896 | tf_op jit(solution)/shard_map/attend/pallas_call | solution.py:302
  163.3 8.2 %attend.4 = (bf16[2,64,192]{2,1,0:T(8,128)(2,1)S(1)}, bf16[2,64,192]{2,1,0:T(8,128)(2,1)S(1)}, bf16[2,64,192]{2,1,0:T(8,128)(2,1)S(1)}, bf16[2,64,192]{2,1,0:T(8,128)(2,1)S(1)}, f32[2,64,768]{2,1,0:T(8,128)S(1)}) custom-call(bf16[6,80,768]{2,1,0:T(8,128)(2,1)S(1)} %copy-done.5, bf16[6,80,768]{2,1,0:T(8,128)(2,1)S(1)} %collective-permute-done.refs_1_, ...), custom_call_target="tpu_custom_call" | custom-call | flops 3355443200 | bytes 7340032 | tf_op jit(solution)/shard_map/attend/pallas_call | solution.py:302
  171.5 4.4 %attend.5 = (bf16[1,64,192]{2,1,0:T(8,128)(2,1)S(1)}, bf16[1,64,192]{2,1,0:T(8,128)(2,1)S(1)}, bf16[1,64,192]{2,1,0:T(8,128)(2,1)S(1)}, bf16[1,64,192]{2,1,0:T(8,128)(2,1)S(1)}, f32[1,64,768]{2,1,0:T(8,128)S(1)}) custom-call(bf16[6,80,768]{2,1,0:T(8,128)(2,1)S(1)} %copy-done.5, bf16[6,80,768]{2,1,0:T(8,128)(2,1)S(1)} %collective-permute-done.refs_1_, ...), custom_call_target="tpu_custom_call" | custom-call | flops 1677721600 | bytes 5767168 | tf_op jit(solution)/shard_map/attend/pallas_call | solution.py:302
  176.0 1.6 collective-permute-start.36
  178.1 1.6 collective-permute-start.29
  181.8 1.8 collective-permute-done.38.refs_7_
  187.2 3.0 %collective-permute-start.41 = (bf16[3,16,768]{2,1,0:T(8,128)(2,1)S(1)}, bf16[3,16,768]{2,1,0:T(8,128)(2,1)S(1)}, u32[]{:S(2)}, u32[]{:S(2)}) collective-permute-start(bf16[3,16,768]{2,1,0:T(8,128)(2,1)S(1)} %get-tuple-element.96), channel_id=1, source_target_pairs={{0,12},{1,13},{2,14},{3,15},{4,8},{5,9},{6,10},{7,11},{8,4},{9,5},... | collective-permute-start | bytes 221192 | tf_op jit(solution)/shard_map/ppermute | solution.py:437
  190.8 1.4 collective-permute-start.19
  192.2 3.0 %collective-permute-start.20 = (bf16[3,16,768]{2,1,0:T(8,128)(2,1)S(1)}, bf16[3,16,768]{2,1,0:T(8,128)(2,1)S(1)}, u32[]{:S(2)}, u32[]{:S(2)}) collective-permute-start(bf16[3,16,768]{2,1,0:T(8,128)(2,1)S(1)} %get-tuple-element.68), channel_id=1, source_target_pairs={{0,12},{1,13},{2,14},{3,15},{4,8},{5,9},{6,10},{7,11},{8,4},{9,5},... | collective-permute-start | bytes 221192 | tf_op jit(solution)/shard_map/ppermute | solution.py:437
  195.8 5.4 %collective-permute-done.19.refs_2_ = bf16[3,16,768]{2,1,0:T(8,128)(2,1)S(1)} collective-permute-done((bf16[3,16,768]{2,1,0:T(8,128)(2,1)S(1)}, bf16[3,16,768]{2,1,0:T(8,128)(2,1)S(1)}, u32[]{:S(2)}, u32[]{:S(2)}) %collective-permute-start.19) | collective-permute-done | bytes 73760 | tf_op jit(solution)/shard_map/ppermute | solution.py:437
  (138 shorter events, 24.9 us)
Async XLA Ops:
  3.4 20.0 %collective-permute-start.3 = (bf16[3,80,768]{2,1,0:T(8,128)(2,1)}, bf16[3,80,768]{2,1,0:T(8,128)(2,1)}, u32[]{:S(2)}, u32[]{:S(2)}) collective-permute-start(bf16[3,80,768]{2,1,0:T(8,128)(2,1)} %get-tuple-element.51), channel_id=1, source_target_pairs={{0,4},{1,5},{2,6},{3,7},{4,0},{5,1},{6,2},{7,3},{8,12},{9,13},{10,... | collective-permute-start | bytes 1105928 | tf_op jit(solution)/shard_map/ppermute | solution.py:437
  6.4 28.5 %collective-permute-start.4 = (bf16[3,80,768]{2,1,0:T(8,128)(2,1)}, bf16[3,80,768]{2,1,0:T(8,128)(2,1)}, u32[]{:S(2)}, u32[]{:S(2)}) collective-permute-start(bf16[3,80,768]{2,1,0:T(8,128)(2,1)} %get-tuple-element.52), channel_id=1, source_target_pairs={{0,8},{1,9},{2,10},{3,11},{4,12},{5,13},{6,14},{7,15},{8,0},{9,1},... | collective-permute-start | bytes 1105928 | tf_op jit(solution)/shard_map/ppermute | solution.py:437
  9.0 25.9 %collective-permute-start.5 = (bf16[3,80,768]{2,1,0:T(8,128)(2,1)}, bf16[3,80,768]{2,1,0:T(8,128)(2,1)}, u32[]{:S(2)}, u32[]{:S(2)}) collective-permute-start(bf16[3,80,768]{2,1,0:T(8,128)(2,1)} %get-tuple-element.53), channel_id=1, source_target_pairs={{0,12},{1,13},{2,14},{3,15},{4,8},{5,9},{6,10},{7,11},{8,4},{9,5},... | collective-permute-start | bytes 1105928 | tf_op jit(solution)/shard_map/ppermute | solution.py:437
  12.7 37.1 %collective-permute-start.30 = (bf16[1,80,768]{2,1,0:T(8,128)(2,1)}, bf16[1,80,768]{2,1,0:T(8,128)(2,1)}, u32[]{:S(2)}, u32[]{:S(2)}) collective-permute-start(bf16[1,80,768]{2,1,0:T(8,128)(2,1)} %get-tuple-element.80), channel_id=1, source_target_pairs={{0,4},{1,5},{2,6},{3,7},{4,0},{5,1},{6,2},{7,3},{8,12},{9,13},{10,... | collective-permute-start | bytes 368648 | tf_op jit(solution)/shard_map/ppermute | solution.py:437
  13.5 37.1 %collective-permute-start.31 = (bf16[1,80,768]{2,1,0:T(8,128)(2,1)}, bf16[1,80,768]{2,1,0:T(8,128)(2,1)}, u32[]{:S(2)}, u32[]{:S(2)}) collective-permute-start(bf16[1,80,768]{2,1,0:T(8,128)(2,1)} %get-tuple-element.81), channel_id=1, source_target_pairs={{0,8},{1,9},{2,10},{3,11},{4,12},{5,13},{6,14},{7,15},{8,0},{9,1},... | collective-permute-start | bytes 368648 | tf_op jit(solution)/shard_map/ppermute | solution.py:437
  23.3 28.0 %collective-permute-start.32 = (bf16[1,80,768]{2,1,0:T(8,128)(2,1)}, bf16[1,80,768]{2,1,0:T(8,128)(2,1)}, u32[]{:S(2)}, u32[]{:S(2)}) collective-permute-start(bf16[1,80,768]{2,1,0:T(8,128)(2,1)} %copy-done.25), channel_id=1, source_target_pairs={{0,12},{1,13},{2,14},{3,15},{4,8},{5,9},{6,10},{7,11},{8,4},{9,5},... | collective-permute-start | bytes 368648 | tf_op jit(solution)/shard_map/ppermute | solution.py:437
  38.1 83.5 %collective-permute-start.6 = (bf16[3,3,80,768]{3,2,1,0:T(8,128)(2,1)}, bf16[3,3,80,768]{3,2,1,0:T(8,128)(2,1)}, u32[]{:S(2)}, u32[]{:S(2)}) collective-permute-start(bf16[3,3,80,768]{3,2,1,0:T(8,128)(2,1)} %stack.4.refs_4_), channel_id=1, source_target_pairs={{0,2},{1,3},{2,0},{3,1},{4,6},{5,7},{6,4},{7,5},{8,10},{9,11},{10,... | collective-permute-start | bytes 3317768 | tf_op jit(solution)/shard_map/ppermute | solution.py:437
  49.2 17.2 %collective-permute-start.10 = (bf16[528,128]{1,0:T(8,128)(2,1)S(1)}, bf16[528,128]{1,0:T(8,128)(2,1)S(1)}, u32[]{:S(2)}, u32[]{:S(2)}) collective-permute-start(bf16[528,128]{1,0:T(8,128)(2,1)S(1)} %get-tuple-element.56), channel_id=1, source_target_pairs={{0,2},{1,3},{2,0},{3,1},{4,6},{5,7},{6,4},{7,5},{8,10},{9,11},{10,... | collective-permute-start | bytes 405512 | tf_op jit(solution)/shard_map/ppermute | solution.py:437
  49.7 31.3 %collective-permute-start.11 = (bf16[528,128]{1,0:T(8,128)(2,1)S(1)}, bf16[528,128]{1,0:T(8,128)(2,1)S(1)}, u32[]{:S(2)}, u32[]{:S(2)}) collective-permute-start(bf16[528,128]{1,0:T(8,128)(2,1)S(1)} %get-tuple-element.57), channel_id=1, source_target_pairs={{0,3},{1,2},{2,1},{3,0},{4,7},{5,6},{6,5},{7,4},{8,11},{9,10},{10,... | collective-permute-start | bytes 405512 | tf_op jit(solution)/shard_map/ppermute | solution.py:437
  50.7 32.8 %collective-permute-start.9 = (bf16[528,128]{1,0:T(8,128)(2,1)S(1)}, bf16[528,128]{1,0:T(8,128)(2,1)S(1)}, u32[]{:S(2)}, u32[]{:S(2)}) collective-permute-start(bf16[528,128]{1,0:T(8,128)(2,1)S(1)} %get-tuple-element.55), channel_id=1, source_target_pairs={{0,1},{1,0},{2,3},{3,2},{4,5},{5,4},{6,7},{7,6},{8,9},{9,8},{10,11... | collective-permute-start | bytes 405512 | tf_op jit(solution)/shard_map/ppermute | solution.py:437
  51.4 33.7 %collective-permute-start.21 = (bf16[2,80,768]{2,1,0:T(8,128)(2,1)S(1)}, bf16[2,80,768]{2,1,0:T(8,128)(2,1)S(1)}, u32[]{:S(2)}, u32[]{:S(2)}) collective-permute-start(bf16[2,80,768]{2,1,0:T(8,128)(2,1)S(1)} %copy-done.24), channel_id=1, source_target_pairs={{0,4},{1,5},{2,6},{3,7},{4,0},{5,1},{6,2},{7,3},{8,12},{9,13},{10,... | collective-permute-start | bytes 737288 | tf_op jit(solution)/shard_map/ppermute | solution.py:437
  66.3 39.3 %collective-permute-start.22 = (bf16[2,80,768]{2,1,0:T(8,128)(2,1)S(1)}, bf16[2,80,768]{2,1,0:T(8,128)(2,1)S(1)}, u32[]{:S(2)}, u32[]{:S(2)}) collective-permute-start(bf16[2,80,768]{2,1,0:T(8,128)(2,1)S(1)} %copy-done.22), channel_id=1, source_target_pairs={{0,8},{1,9},{2,10},{3,11},{4,12},{5,13},{6,14},{7,15},{8,0},{9,1},... | collective-permute-start | bytes 737288 | tf_op jit(solution)/shard_map/ppermute | solution.py:437
  81.1 24.5 %collective-permute-start.23 = (bf16[2,80,768]{2,1,0:T(8,128)(2,1)S(1)}, bf16[2,80,768]{2,1,0:T(8,128)(2,1)S(1)}, u32[]{:S(2)}, u32[]{:S(2)}) collective-permute-start(bf16[2,80,768]{2,1,0:T(8,128)(2,1)S(1)} %copy-done.20), channel_id=1, source_target_pairs={{0,12},{1,13},{2,14},{3,15},{4,8},{5,9},{6,10},{7,11},{8,4},{9,5},... | collective-permute-start | bytes 737288 | tf_op jit(solution)/shard_map/ppermute | solution.py:437
  83.4 23.8 %collective-permute-start.33 = (bf16[3,1,80,768]{3,2,1,0:T(8,128)(2,1)S(1)}, bf16[3,1,80,768]{3,2,1,0:T(8,128)(2,1)S(1)}, u32[]{:S(2)}, u32[]{:S(2)}) collective-permute-start(bf16[3,1,80,768]{3,2,1,0:T(8,128)(2,1)S(1)} %stack.7.refs_4_), channel_id=1, source_target_pairs={{0,2},{1,3},{2,0},{3,1},{4,6},{5,7},{6,4},{7,5},{8,10},{9,11},{10,... | collective-permute-start | bytes 1105928 | tf_op jit(solution)/shard_map/ppermute | solution.py:437
  85.1 36.4 %collective-permute-start.13 = (bf16[4,528,128]{2,1,0:T(8,128)(2,1)S(1)}, bf16[4,528,128]{2,1,0:T(8,128)(2,1)}, u32[]{:S(2)}, u32[]{:S(2)}) collective-permute-start(bf16[4,528,128]{2,1,0:T(8,128)(2,1)S(1)} %stack.5.refs_0_), channel_id=1, source_target_pairs={{0,8},{1,9},{2,10},{3,11},{4,12},{5,13},{6,14},{7,15},{8,0},{9,1},... | collective-permute-start | bytes 1622024 | tf_op jit(solution)/shard_map/ppermute | solution.py:437
  105.6 23.6 %collective-permute-start.12 = (bf16[4,528,128]{2,1,0:T(8,128)(2,1)S(1)}, bf16[4,528,128]{2,1,0:T(8,128)(2,1)S(1)}, u32[]{:S(2)}, u32[]{:S(2)}) collective-permute-start(bf16[4,528,128]{2,1,0:T(8,128)(2,1)S(1)} %stack.5.refs_0_), channel_id=1, source_target_pairs={{0,4},{1,5},{2,6},{3,7},{4,0},{5,1},{6,2},{7,3},{8,12},{9,13},{10,... | collective-permute-start | bytes 1622024 | tf_op jit(solution)/shard_map/ppermute | solution.py:437
  105.6 26.0 %collective-permute-start = (bf16[6,80,768]{2,1,0:T(8,128)(2,1)S(1)}, bf16[6,80,768]{2,1,0:T(8,128)(2,1)S(1)}, u32[]{:S(2)}, u32[]{:S(2)}) collective-permute-start(bf16[6,80,768]{2,1,0:T(8,128)(2,1)S(1)} %pack.3.refs_0_), channel_id=1, source_target_pairs={{0,2},{1,3},{2,0},{3,1},{4,6},{5,7},{6,4},{7,5},{8,10},{9,11},{10,... | collective-permute-start | bytes 2211848 | tf_op jit(solution)/shard_map/ppermute | solution.py:437
  107.2 24.4 %collective-permute-start.1 = (bf16[6,80,768]{2,1,0:T(8,128)(2,1)S(1)}, bf16[6,80,768]{2,1,0:T(8,128)(2,1)S(1)}, u32[]{:S(2)}, u32[]{:S(2)}) collective-permute-start(bf16[6,80,768]{2,1,0:T(8,128)(2,1)S(1)} %pack.3.refs_0_), channel_id=1, source_target_pairs={{0,1},{1,0},{2,3},{3,2},{4,5},{5,4},{6,7},{7,6},{8,9},{9,8},{10,11... | collective-permute-start | bytes 2211848 | tf_op jit(solution)/shard_map/ppermute | solution.py:437
  121.5 29.3 %collective-permute-start.7 = (bf16[3,3,80,768]{3,2,1,0:T(8,128)(2,1)}, bf16[3,3,80,768]{3,2,1,0:T(8,128)(2,1)}, u32[]{:S(2)}, u32[]{:S(2)}) collective-permute-start(bf16[3,3,80,768]{3,2,1,0:T(8,128)(2,1)} %stack.4.refs_4_), channel_id=1, source_target_pairs={{0,1},{1,0},{2,3},{3,2},{4,5},{5,4},{6,7},{7,6},{8,9},{9,8},{10,11... | collective-permute-start | bytes 3317768 | tf_op jit(solution)/shard_map/ppermute | solution.py:437
  121.5 29.9 %collective-permute-start.8 = (bf16[3,3,80,768]{3,2,1,0:T(8,128)(2,1)}, bf16[3,3,80,768]{3,2,1,0:T(8,128)(2,1)}, u32[]{:S(2)}, u32[]{:S(2)}) collective-permute-start(bf16[3,3,80,768]{3,2,1,0:T(8,128)(2,1)} %collective-permute-done.6.refs_5_), channel_id=1, source_target_pairs={{0,1},{1,0},{2,3},{3,2},{4,5},{5,4},{6,7},{7,6},{8,9},{9,8},{10,11... | collective-permute-start | bytes 3317768 | tf_op jit(solution)/shard_map/ppermute | solution.py:437
  130.1 15.8 %collective-permute-start.24 = (bf16[3,2,80,768]{3,2,1,0:T(8,128)(2,1)S(1)}, bf16[3,2,80,768]{3,2,1,0:T(8,128)(2,1)}, u32[]{:S(2)}, u32[]{:S(2)}) collective-permute-start(bf16[3,2,80,768]{3,2,1,0:T(8,128)(2,1)S(1)} %stack.6.refs_4_), channel_id=1, source_target_pairs={{0,2},{1,3},{2,0},{3,1},{4,6},{5,7},{6,4},{7,5},{8,10},{9,11},{10,... | collective-permute-start | bytes 2211848 | tf_op jit(solution)/shard_map/ppermute | solution.py:437
  131.6 14.3 %collective-permute-start.14 = (bf16[4,528,128]{2,1,0:T(8,128)(2,1)}, bf16[4,528,128]{2,1,0:T(8,128)(2,1)}, u32[]{:S(2)}, u32[]{:S(2)}) collective-permute-start(bf16[4,528,128]{2,1,0:T(8,128)(2,1)} %collective-permute-done.13.refs_2_), channel_id=1, source_target_pairs={{0,4},{1,5},{2,6},{3,7},{4,0},{5,1},{6,2},{7,3},{8,12},{9,13},{10,... | collective-permute-start | bytes 1622024 | tf_op jit(solution)/shard_map/ppermute | solution.py:437
  131.6 19.3 %collective-permute-start.2 = (bf16[6,80,768]{2,1,0:T(8,128)(2,1)S(1)}, bf16[6,80,768]{2,1,0:T(8,128)(2,1)}, u32[]{:S(2)}, u32[]{:S(2)}) collective-permute-start(bf16[6,80,768]{2,1,0:T(8,128)(2,1)S(1)} %collective-permute-done.refs_1_), channel_id=1, source_target_pairs={{0,1},{1,0},{2,3},{3,2},{4,5},{5,4},{6,7},{7,6},{8,9},{9,8},{10,11... | collective-permute-start | bytes 2211848 | tf_op jit(solution)/shard_map/ppermute | solution.py:437
  145.9 17.4 %collective-permute-start.25 = (bf16[3,2,80,768]{3,2,1,0:T(8,128)(2,1)S(1)}, bf16[3,2,80,768]{3,2,1,0:T(8,128)(2,1)S(1)}, u32[]{:S(2)}, u32[]{:S(2)}) collective-permute-start(bf16[3,2,80,768]{3,2,1,0:T(8,128)(2,1)S(1)} %stack.6.refs_4_), channel_id=1, source_target_pairs={{0,1},{1,0},{2,3},{3,2},{4,5},{5,4},{6,7},{7,6},{8,9},{9,8},{10,11... | collective-permute-start | bytes 2211848 | tf_op jit(solution)/shard_map/ppermute | solution.py:437
  145.9 17.4 %collective-permute-start.26 = (bf16[3,2,80,768]{3,2,1,0:T(8,128)(2,1)}, bf16[3,2,80,768]{3,2,1,0:T(8,128)(2,1)S(1)}, u32[]{:S(2)}, u32[]{:S(2)}) collective-permute-start(bf16[3,2,80,768]{3,2,1,0:T(8,128)(2,1)} %collective-permute-done.24.refs_5_), channel_id=1, source_target_pairs={{0,1},{1,0},{2,3},{3,2},{4,5},{5,4},{6,7},{7,6},{8,9},{9,8},{10,11... | collective-permute-start | bytes 2211848 | tf_op jit(solution)/shard_map/ppermute | solution.py:437
  150.8 20.7 %collective-permute-start.34 = (bf16[3,1,80,768]{3,2,1,0:T(8,128)(2,1)S(1)}, bf16[3,1,80,768]{3,2,1,0:T(8,128)(2,1)S(1)}, u32[]{:S(2)}, u32[]{:S(2)}) collective-permute-start(bf16[3,1,80,768]{3,2,1,0:T(8,128)(2,1)S(1)} %copy-done.12), channel_id=1, source_target_pairs={{0,1},{1,0},{2,3},{3,2},{4,5},{5,4},{6,7},{7,6},{8,9},{9,8},{10,11... | collective-permute-start | bytes 1105928 | tf_op jit(solution)/shard_map/ppermute | solution.py:437
  150.9 20.6 %collective-permute-start.35 = (bf16[3,1,80,768]{3,2,1,0:T(8,128)(2,1)S(1)}, bf16[3,1,80,768]{3,2,1,0:T(8,128)(2,1)S(1)}, u32[]{:S(2)}, u32[]{:S(2)}) collective-permute-start(bf16[3,1,80,768]{3,2,1,0:T(8,128)(2,1)S(1)} %copy-done.16), channel_id=1, source_target_pairs={{0,1},{1,0},{2,3},{3,2},{4,5},{5,4},{6,7},{7,6},{8,9},{9,8},{10,11... | collective-permute-start | bytes 1105928 | tf_op jit(solution)/shard_map/ppermute | solution.py:437
  178.1 7.1 %collective-permute-start.28 = (bf16[2,64,192]{2,1,0:T(8,128)(2,1)S(1)}, bf16[2,64,192]{2,1,0:T(8,128)(2,1)S(1)}, u32[]{:S(2)}, u32[]{:S(2)}) collective-permute-start(bf16[2,64,192]{2,1,0:T(8,128)(2,1)S(1)} %get-tuple-element.78), channel_id=1, source_target_pairs={{0,1},{1,0},{2,3},{3,2},{4,5},{5,4},{6,7},{7,6},{8,9},{9,8},{10,11... | collective-permute-start | bytes 147464 | tf_op jit(solution)/shard_map/ppermute | solution.py:437
  185.8 9.7 %collective-permute-start.40 = (bf16[3,16,768]{2,1,0:T(8,128)(2,1)S(1)}, bf16[3,16,768]{2,1,0:T(8,128)(2,1)S(1)}, u32[]{:S(2)}, u32[]{:S(2)}) collective-permute-start(bf16[3,16,768]{2,1,0:T(8,128)(2,1)S(1)} %get-tuple-element.95), channel_id=1, source_target_pairs={{0,8},{1,9},{2,10},{3,11},{4,12},{5,13},{6,14},{7,15},{8,0},{9,1},... | collective-permute-start | bytes 221192 | tf_op jit(solution)/shard_map/ppermute | solution.py:437
  187.2 8.3 %collective-permute-start.41 = (bf16[3,16,768]{2,1,0:T(8,128)(2,1)S(1)}, bf16[3,16,768]{2,1,0:T(8,128)(2,1)S(1)}, u32[]{:S(2)}, u32[]{:S(2)}) collective-permute-start(bf16[3,16,768]{2,1,0:T(8,128)(2,1)S(1)} %get-tuple-element.96), channel_id=1, source_target_pairs={{0,12},{1,13},{2,14},{3,15},{4,8},{5,9},{6,10},{7,11},{8,4},{9,5},... | collective-permute-start | bytes 221192 | tf_op jit(solution)/shard_map/ppermute | solution.py:437
  190.8 10.5 %collective-permute-start.19 = (bf16[3,16,768]{2,1,0:T(8,128)(2,1)S(1)}, bf16[3,16,768]{2,1,0:T(8,128)(2,1)S(1)}, u32[]{:S(2)}, u32[]{:S(2)}) collective-permute-start(bf16[3,16,768]{2,1,0:T(8,128)(2,1)S(1)} %get-tuple-element.67), channel_id=1, source_target_pairs={{0,8},{1,9},{2,10},{3,11},{4,12},{5,13},{6,14},{7,15},{8,0},{9,1},... | collective-permute-start | bytes 221192 | tf_op jit(solution)/shard_map/ppermute | solution.py:437
  192.2 9.1 %collective-permute-start.20 = (bf16[3,16,768]{2,1,0:T(8,128)(2,1)S(1)}, bf16[3,16,768]{2,1,0:T(8,128)(2,1)S(1)}, u32[]{:S(2)}, u32[]{:S(2)}) collective-permute-start(bf16[3,16,768]{2,1,0:T(8,128)(2,1)S(1)} %get-tuple-element.68), channel_id=1, source_target_pairs={{0,12},{1,13},{2,14},{3,15},{4,8},{5,9},{6,10},{7,11},{8,4},{9,5},... | collective-permute-start | bytes 221192 | tf_op jit(solution)/shard_map/ppermute | solution.py:437
  (39 other events, 527.4 us)

commit v3 on v2

--- a/solution.py
+++ b/solution.py
@@ -397,9 +397,8 @@
 
 
 def chunk_sizes(group_samples):
-    last = max(group_samples // 6, 1)
-    middle = max(group_samples // 3, 1)
-    return [group_samples - middle - last, middle, last]
+    last = max(group_samples // 3, 1)
+    return [group_samples - last, last]
 
 
 def local(

time: 202 us -> 230 us (1.14)
  waiting for transfers between devices: 76.1 us -> 134 us
  starting transfers between devices: 68.9 us -> 46.9 us
  Pallas kernels: 45.9 us -> 41.9 us
  local copies, waits for them, and re-layouts: 9.96 us -> 6.59 us
    ppermute x42 -> x33, waiting for transfers between devices: 76.1 us -> 134 us  [across(): return lax.ppermute(x, 'key', [(i, i ^ code) for i in range(n)])]
    ppermute x42 -> x33, starting transfers between devices: 68.9 us -> 46.9 us  [across(): return lax.ppermute(x, 'key', [(i, i ^ code) for i in range(n)])]
    unnamed x58 -> x30, local copies, waits for them, and re-layouts: 6.76 us -> 3.96 us
    pallas_call x4 -> x3, Pallas kernels: 4.34 us -> 1.86 us  [stacked(): pl.pallas_call(stack_kernel, grid=(steps,), in_specs=[pl.BlockSpec(block,...]
    pallas_call x3 -> x2, Pallas kernels: 24.5 us -> 23.6 us  [attention(): pl.pallas_call(functools.partial(attention_kernel, pieces, hpg, direct, k...]
  transfers between devices with their start and end apart: 42 -> 33, of which waited for: 14 -> 11; matrix products, arithmetic and copies ran while one was open for 2% -> 1% of each run, Pallas kernels for 18% -> 12%
where the time goes in v3:
time: 230 us
  waiting for transfers between devices  134 us (58%)
  starting transfers between devices  46.9 us (20%)
  Pallas kernels  41.9 us (18%)
  local copies, waits for them, and re-layouts  6.59 us (3%)
    ppermute x33, waiting for transfers between devices, across(): return lax.ppermute(x, 'key', [(i, i ^ code) for i in range(n)])  134 us
    ppermute x33, starting transfers between devices, across(): return lax.ppermute(x, 'key', [(i, i ^ code) for i in range(n)])  46.9 us
    pallas_call x2, Pallas kernels, attention(): pl.pallas_call(functools.partial(attention_kernel, pieces, hpg, direct, k...  23.6 us
    pallas_call x1, Pallas kernels, local_bias(): pl.pallas_call(functools.partial(bias_kernel, hpg), grid=(rows // tile,),...  6.51 us
  transfers between devices with their start and end apart: 33, of which 11 were waited for; matrix products, arithmetic and copies ran while one was open for 1% of the time, Pallas kernels for 12%

profile of v3, /device:TPU:0, one launch (start us, length us, event | category | flops | bytes accessed | tf_op | source)
XLA Modules:
  0.0 229.9 jit_solution(5551213326107296283)
XLA Ops:
  0.0 3.7 %pack.4 = (bf16[4,80,768]{2,1,0:T(8,128)(2,1)}, bf16[4,80,768]{2,1,0:T(8,128)(2,1)}, bf16[4,80,768]{2,1,0:T(8,128)(2,1)}) custom-call(s32[1]{0:T(128)} %bitcast.group_ref, bf16[4,6,64,768]{3,2,1,0:T(8,128)(2,1)} %bitcast.14, bf16[4,6,64,768]{3,2,1,0:T(8,128)(2,1)} %bitcast.15, bf16[4,6,64,768]{3,2,1,0:T(8,128)(2,1)} %bitcast.16, ...), custom_call_target="tpu_custom_call" | custom-call | bytes 2949120 | tf_op jit(solution)/shard_map/pack/pallas_call | solution.py:108
  3.7 3.1 %collective-permute-start.3 = (bf16[4,80,768]{2,1,0:T(8,128)(2,1)}, bf16[4,80,768]{2,1,0:T(8,128)(2,1)S(1)}, u32[]{:S(2)}, u32[]{:S(2)}) collective-permute-start(bf16[4,80,768]{2,1,0:T(8,128)(2,1)} %get-tuple-element.39), channel_id=1, source_target_pairs={{0,4},{1,5},{2,6},{3,7},{4,0},{5,1},{6,2},{7,3},{8,12},{9,13},{10,... | collective-permute-start | bytes 1474568 | tf_op jit(solution)/shard_map/ppermute | solution.py:436
  6.8 2.6 %collective-permute-start.4 = (bf16[4,80,768]{2,1,0:T(8,128)(2,1)}, bf16[4,80,768]{2,1,0:T(8,128)(2,1)S(1)}, u32[]{:S(2)}, u32[]{:S(2)}) collective-permute-start(bf16[4,80,768]{2,1,0:T(8,128)(2,1)} %get-tuple-element.40), channel_id=1, source_target_pairs={{0,8},{1,9},{2,10},{3,11},{4,12},{5,13},{6,14},{7,15},{8,0},{9,1},... | collective-permute-start | bytes 1474568 | tf_op jit(solution)/shard_map/ppermute | solution.py:436
  9.4 18.6 %collective-permute-done.3.refs_0_ = bf16[4,80,768]{2,1,0:T(8,128)(2,1)S(1)} collective-permute-done((bf16[4,80,768]{2,1,0:T(8,128)(2,1)}, bf16[4,80,768]{2,1,0:T(8,128)(2,1)S(1)}, u32[]{:S(2)}, u32[]{:S(2)}) %collective-permute-start.3) | collective-permute-done | bytes 491552 | tf_op jit(solution)/shard_map/ppermute | solution.py:436
  28.0 15.0 %collective-permute-done.4.refs_1_ = bf16[4,80,768]{2,1,0:T(8,128)(2,1)S(1)} collective-permute-done((bf16[4,80,768]{2,1,0:T(8,128)(2,1)}, bf16[4,80,768]{2,1,0:T(8,128)(2,1)S(1)}, u32[]{:S(2)}, u32[]{:S(2)}) %collective-permute-start.4) | collective-permute-done | bytes 491552 | tf_op jit(solution)/shard_map/ppermute | solution.py:436
  43.0 1.7 stack.3.refs_4_
  44.7 1.5 collective-permute-start.6
  47.2 2.2 copy-done.4
  49.4 6.5 %bias_local.1 = (bf16[528,128]{1,0:T(8,128)(2,1)S(1)}, bf16[528,128]{1,0:T(8,128)(2,1)S(1)}, bf16[528,128]{1,0:T(8,128)(2,1)S(1)}, bf16[528,128]{1,0:T(8,128)(2,1)S(1)}) custom-call(f32[1,128]{1,0:T(1,128)S(1)} %broadcast_in_dim_tile.3.mask_ref, bf16[2,128,64,128]{3,2,1,0:T(8,128)(2,1)S(1)} %bitcast.28, f32[1,128]{1,0:T(1,128)S(1)} %bitcast.29, ...), custom_call_target="tpu_custom_call" | custom-call | flops 1073741824 | bytes 4194304 | tf_op jit(solution)/shard_map/bias_local/pallas_call | solution.py:58
  56.5 1.6 collective-permute-start.9
  58.1 22.8 %collective-permute-done.10.refs_2_ = bf16[528,128]{1,0:T(8,128)(2,1)S(1)} collective-permute-done((bf16[528,128]{1,0:T(8,128)(2,1)S(1)}, bf16[528,128]{1,0:T(8,128)(2,1)S(1)}, u32[]{:S(2)}, u32[]{:S(2)}) %collective-permute-start.10) | collective-permute-done | bytes 135200 | tf_op jit(solution)/shard_map/ppermute | solution.py:436
  81.5 12.1 %collective-permute-start.13 = (bf16[4,528,128]{2,1,0:T(8,128)(2,1)S(1)}, bf16[4,528,128]{2,1,0:T(8,128)(2,1)}, u32[]{:S(2)}, u32[]{:S(2)}) collective-permute-start(bf16[4,528,128]{2,1,0:T(8,128)(2,1)S(1)} %stack.4.refs_0_), channel_id=1, source_target_pairs={{0,8},{1,9},{2,10},{3,11},{4,12},{5,13},{6,14},{7,15},{8,0},{9,1},... | collective-permute-start | bytes 1622024 | tf_op jit(solution)/shard_map/ppermute | solution.py:436
  93.8 1.9 collective-permute-start.22
  95.7 2.5 %collective-permute-start.23 = (bf16[2,80,768]{2,1,0:T(8,128)(2,1)S(1)}, bf16[2,80,768]{2,1,0:T(8,128)(2,1)S(1)}, u32[]{:S(2)}, u32[]{:S(2)}) collective-permute-start(bf16[2,80,768]{2,1,0:T(8,128)(2,1)S(1)} %get-tuple-element.59), channel_id=1, source_target_pairs={{0,12},{1,13},{2,14},{3,15},{4,8},{5,9},{6,10},{7,11},{8,4},{9,5},... | collective-permute-start | bytes 737288 | tf_op jit(solution)/shard_map/ppermute | solution.py:436
  98.3 13.2 %collective-permute-done.21.refs_0_ = bf16[2,80,768]{2,1,0:T(8,128)(2,1)S(1)} collective-permute-done((bf16[2,80,768]{2,1,0:T(8,128)(2,1)S(1)}, bf16[2,80,768]{2,1,0:T(8,128)(2,1)S(1)}, u32[]{:S(2)}, u32[]{:S(2)}) %collective-permute-start.21) | collective-permute-done | bytes 245792 | tf_op jit(solution)/shard_map/ppermute | solution.py:436
  112.3 21.7 %collective-permute-done.22.refs_1_ = bf16[2,80,768]{2,1,0:T(8,128)(2,1)S(1)} collective-permute-done((bf16[2,80,768]{2,1,0:T(8,128)(2,1)S(1)}, bf16[2,80,768]{2,1,0:T(8,128)(2,1)S(1)}, u32[]{:S(2)}, u32[]{:S(2)}) %collective-permute-start.22) | collective-permute-done | bytes 245792 | tf_op jit(solution)/shard_map/ppermute | solution.py:436
  134.5 5.3 %collective-permute-start.12 = (bf16[4,528,128]{2,1,0:T(8,128)(2,1)S(1)}, bf16[4,528,128]{2,1,0:T(8,128)(2,1)S(1)}, u32[]{:S(2)}, u32[]{:S(2)}) collective-permute-start(bf16[4,528,128]{2,1,0:T(8,128)(2,1)S(1)} %stack.4.refs_0_), channel_id=1, source_target_pairs={{0,4},{1,5},{2,6},{3,7},{4,0},{5,1},{6,2},{7,3},{8,12},{9,13},{10,... | collective-permute-start | bytes 1622024 | tf_op jit(solution)/shard_map/ppermute | solution.py:436
  140.0 12.4 %collective-permute-done.12.refs_1_ = bf16[4,528,128]{2,1,0:T(8,128)(2,1)S(1)} collective-permute-done((bf16[4,528,128]{2,1,0:T(8,128)(2,1)S(1)}, bf16[4,528,128]{2,1,0:T(8,128)(2,1)S(1)}, u32[]{:S(2)}, u32[]{:S(2)}) %collective-permute-start.12) | collective-permute-done | bytes 540704 | tf_op jit(solution)/shard_map/ppermute | solution.py:436
  154.9 1.7 collective-permute-start.14
  156.7 1.6 constant_dynamic-slice_fusion
  158.3 12.9 %collective-permute-done.24.refs_5_ = bf16[3,2,80,768]{3,2,1,0:T(8,128)(2,1)} collective-permute-done((bf16[3,2,80,768]{3,2,1,0:T(8,128)(2,1)S(1)}, bf16[3,2,80,768]{3,2,1,0:T(8,128)(2,1)}, u32[]{:S(2)}, u32[]{:S(2)}) %collective-permute-start.24) | collective-permute-done | bytes 737312 | tf_op jit(solution)/shard_map/ppermute | solution.py:436
  172.0 4.1 %bias_order.1 = (f32[4,256,1024]{2,1,0:T(8,128)S(1)}, f32[8,1024]{1,0:T(8,128)S(1)}) custom-call(s32[1]{0:T(128)} %bitcast.4.me_ref, s32[16]{0:T(128)S(1)} %copy-done.10, s32[16]{0:T(128)S(1)} %broadcast_xor_fusion.qsel_ref, bf16[4,528,128]{2,1,0:T(8,128)(2,1)S(1)} %stack.4.refs_0_, bf16[4,528,128]{2,1,0:T(8,128)(2,1)S(1)} %copy-done.9, ...), custom_call_target="tpu_custom_call" | custom-call | flops 8388608 | bytes 6291456 | tf_op jit(solution)/shard_map/bias_order/pallas_call | solution.py:201
  176.2 15.4 %attend.2 = (bf16[4,64,192]{2,1,0:T(8,128)(2,1)S(1)}, bf16[4,64,192]{2,1,0:T(8,128)(2,1)S(1)}, bf16[4,64,192]{2,1,0:T(8,128)(2,1)S(1)}, bf16[4,64,192]{2,1,0:T(8,128)(2,1)S(1)}, f32[4,64,768]{2,1,0:T(8,128)S(1)}) custom-call(bf16[6,80,768]{2,1,0:T(8,128)(2,1)S(1)} %pack.3.refs_0_, bf16[6,80,768]{2,1,0:T(8,128)(2,1)} %collective-permute-done.refs_1_, ...), custom_call_target="tpu_custom_call" | custom-call | flops 6710886400 | bytes 10485760 | tf_op jit(solution)/shard_map/attend/pallas_call | solution.py:302
  191.6 8.2 %attend.3 = (bf16[2,64,192]{2,1,0:T(8,128)(2,1)S(1)}, bf16[2,64,192]{2,1,0:T(8,128)(2,1)S(1)}, bf16[2,64,192]{2,1,0:T(8,128)(2,1)S(1)}, bf16[2,64,192]{2,1,0:T(8,128)(2,1)S(1)}, f32[2,64,768]{2,1,0:T(8,128)S(1)}) custom-call(bf16[6,80,768]{2,1,0:T(8,128)(2,1)S(1)} %pack.3.refs_0_, bf16[6,80,768]{2,1,0:T(8,128)(2,1)} %collective-permute-done.refs_1_, ...), custom_call_target="tpu_custom_call" | custom-call | flops 3355443200 | bytes 7340032 | tf_op jit(solution)/shard_map/attend/pallas_call | solution.py:302
  201.9 1.2 collective-permute-start.17
  203.1 1.7 collective-permute-done.27.refs_1_
  204.8 5.4 %collective-permute-done.29.refs_3_ = bf16[2,64,192]{2,1,0:T(8,128)(2,1)S(1)} collective-permute-done((bf16[2,64,192]{2,1,0:T(8,128)(2,1)S(1)}, bf16[2,64,192]{2,1,0:T(8,128)(2,1)S(1)}, u32[]{:S(2)}, u32[]{:S(2)}) %collective-permute-start.29) | collective-permute-done | bytes 49184 | tf_op jit(solution)/shard_map/ppermute | solution.py:436
  210.6 1.5 collective-permute-start.30
  213.4 1.4 collective-permute-start.19
  214.7 2.5 %collective-permute-start.20 = (bf16[4,16,768]{2,1,0:T(8,128)(2,1)S(1)}, bf16[4,16,768]{2,1,0:T(8,128)(2,1)S(1)}, u32[]{:S(2)}, u32[]{:S(2)}) collective-permute-start(bf16[4,16,768]{2,1,0:T(8,128)(2,1)S(1)} %get-tuple-element.56), channel_id=1, source_target_pairs={{0,12},{1,13},{2,14},{3,15},{4,8},{5,9},{6,10},{7,11},{8,4},{9,5},... | collective-permute-start | bytes 294920 | tf_op jit(solution)/shard_map/ppermute | solution.py:436
  217.2 2.0 collective-permute-start.32
  219.2 9.8 %collective-permute-done.31.refs_6_ = bf16[2,16,768]{2,1,0:T(8,128)(2,1)S(1)} collective-permute-done((bf16[2,16,768]{2,1,0:T(8,128)(2,1)S(1)}, bf16[2,16,768]{2,1,0:T(8,128)(2,1)S(1)}, u32[]{:S(2)}, u32[]{:S(2)}) %collective-permute-start.31) | collective-permute-done | bytes 49184 | tf_op jit(solution)/shard_map/ppermute | solution.py:436
  (90 shorter events, 11.7 us)
Async XLA Ops:
  3.7 24.3 %collective-permute-start.3 = (bf16[4,80,768]{2,1,0:T(8,128)(2,1)}, bf16[4,80,768]{2,1,0:T(8,128)(2,1)S(1)}, u32[]{:S(2)}, u32[]{:S(2)}) collective-permute-start(bf16[4,80,768]{2,1,0:T(8,128)(2,1)} %get-tuple-element.39), channel_id=1, source_target_pairs={{0,4},{1,5},{2,6},{3,7},{4,0},{5,1},{6,2},{7,3},{8,12},{9,13},{10,... | collective-permute-start | bytes 1474568 | tf_op jit(solution)/shard_map/ppermute | solution.py:436
  6.8 36.3 %collective-permute-start.4 = (bf16[4,80,768]{2,1,0:T(8,128)(2,1)}, bf16[4,80,768]{2,1,0:T(8,128)(2,1)S(1)}, u32[]{:S(2)}, u32[]{:S(2)}) collective-permute-start(bf16[4,80,768]{2,1,0:T(8,128)(2,1)} %get-tuple-element.40), channel_id=1, source_target_pairs={{0,8},{1,9},{2,10},{3,11},{4,12},{5,13},{6,14},{7,15},{8,0},{9,1},... | collective-permute-start | bytes 1474568 | tf_op jit(solution)/shard_map/ppermute | solution.py:436
  9.4 33.7 %collective-permute-start.5 = (bf16[4,80,768]{2,1,0:T(8,128)(2,1)}, bf16[4,80,768]{2,1,0:T(8,128)(2,1)S(1)}, u32[]{:S(2)}, u32[]{:S(2)}) collective-permute-start(bf16[4,80,768]{2,1,0:T(8,128)(2,1)} %get-tuple-element.41), channel_id=1, source_target_pairs={{0,12},{1,13},{2,14},{3,15},{4,8},{5,9},{6,10},{7,11},{8,4},{9,5},... | collective-permute-start | bytes 1474568 | tf_op jit(solution)/shard_map/ppermute | solution.py:436
  44.7 89.4 %collective-permute-start.6 = (bf16[3,4,80,768]{3,2,1,0:T(8,128)(2,1)}, bf16[3,4,80,768]{3,2,1,0:T(8,128)(2,1)}, u32[]{:S(2)}, u32[]{:S(2)}) collective-permute-start(bf16[3,4,80,768]{3,2,1,0:T(8,128)(2,1)} %stack.3.refs_4_), channel_id=1, source_target_pairs={{0,2},{1,3},{2,0},{3,1},{4,6},{5,7},{6,4},{7,5},{8,10},{9,11},{10,... | collective-permute-start | bytes 4423688 | tf_op jit(solution)/shard_map/ppermute | solution.py:436
  55.9 25.0 %collective-permute-start.10 = (bf16[528,128]{1,0:T(8,128)(2,1)S(1)}, bf16[528,128]{1,0:T(8,128)(2,1)S(1)}, u32[]{:S(2)}, u32[]{:S(2)}) collective-permute-start(bf16[528,128]{1,0:T(8,128)(2,1)S(1)} %get-tuple-element.44), channel_id=1, source_target_pairs={{0,2},{1,3},{2,0},{3,1},{4,6},{5,7},{6,4},{7,5},{8,10},{9,11},{10,... | collective-permute-start | bytes 405512 | tf_op jit(solution)/shard_map/ppermute | solution.py:436
  56.5 24.9 %collective-permute-start.11 = (bf16[528,128]{1,0:T(8,128)(2,1)S(1)}, bf16[528,128]{1,0:T(8,128)(2,1)S(1)}, u32[]{:S(2)}, u32[]{:S(2)}) collective-permute-start(bf16[528,128]{1,0:T(8,128)(2,1)S(1)} %get-tuple-element.45), channel_id=1, source_target_pairs={{0,3},{1,2},{2,1},{3,0},{4,7},{5,6},{6,5},{7,4},{8,11},{9,10},{10,... | collective-permute-start | bytes 405512 | tf_op jit(solution)/shard_map/ppermute | solution.py:436
  56.5 24.9 %collective-permute-start.9 = (bf16[528,128]{1,0:T(8,128)(2,1)S(1)}, bf16[528,128]{1,0:T(8,128)(2,1)S(1)}, u32[]{:S(2)}, u32[]{:S(2)}) collective-permute-start(bf16[528,128]{1,0:T(8,128)(2,1)S(1)} %get-tuple-element.43), channel_id=1, source_target_pairs={{0,1},{1,0},{2,3},{3,2},{4,5},{5,4},{6,7},{7,6},{8,9},{9,8},{10,11... | collective-permute-start | bytes 405512 | tf_op jit(solution)/shard_map/ppermute | solution.py:436
  81.5 58.4 %collective-permute-start.13 = (bf16[4,528,128]{2,1,0:T(8,128)(2,1)S(1)}, bf16[4,528,128]{2,1,0:T(8,128)(2,1)}, u32[]{:S(2)}, u32[]{:S(2)}) collective-permute-start(bf16[4,528,128]{2,1,0:T(8,128)(2,1)S(1)} %stack.4.refs_0_), channel_id=1, source_target_pairs={{0,8},{1,9},{2,10},{3,11},{4,12},{5,13},{6,14},{7,15},{8,0},{9,1},... | collective-permute-start | bytes 1622024 | tf_op jit(solution)/shard_map/ppermute | solution.py:436
  93.7 17.9 %collective-permute-start.21 = (bf16[2,80,768]{2,1,0:T(8,128)(2,1)S(1)}, bf16[2,80,768]{2,1,0:T(8,128)(2,1)S(1)}, u32[]{:S(2)}, u32[]{:S(2)}) collective-permute-start(bf16[2,80,768]{2,1,0:T(8,128)(2,1)S(1)} %get-tuple-element.57), channel_id=1, source_target_pairs={{0,4},{1,5},{2,6},{3,7},{4,0},{5,1},{6,2},{7,3},{8,12},{9,13},{10,... | collective-permute-start | bytes 737288 | tf_op jit(solution)/shard_map/ppermute | solution.py:436
  93.8 40.2 %collective-permute-start.22 = (bf16[2,80,768]{2,1,0:T(8,128)(2,1)S(1)}, bf16[2,80,768]{2,1,0:T(8,128)(2,1)S(1)}, u32[]{:S(2)}, u32[]{:S(2)}) collective-permute-start(bf16[2,80,768]{2,1,0:T(8,128)(2,1)S(1)} %get-tuple-element.58), channel_id=1, source_target_pairs={{0,8},{1,9},{2,10},{3,11},{4,12},{5,13},{6,14},{7,15},{8,0},{9,1},... | collective-permute-start | bytes 737288 | tf_op jit(solution)/shard_map/ppermute | solution.py:436
  95.7 38.8 %collective-permute-start.23 = (bf16[2,80,768]{2,1,0:T(8,128)(2,1)S(1)}, bf16[2,80,768]{2,1,0:T(8,128)(2,1)S(1)}, u32[]{:S(2)}, u32[]{:S(2)}) collective-permute-start(bf16[2,80,768]{2,1,0:T(8,128)(2,1)S(1)} %get-tuple-element.59), channel_id=1, source_target_pairs={{0,12},{1,13},{2,14},{3,15},{4,8},{5,9},{6,10},{7,11},{8,4},{9,5},... | collective-permute-start | bytes 737288 | tf_op jit(solution)/shard_map/ppermute | solution.py:436
  111.6 42.5 %collective-permute-start = (bf16[6,80,768]{2,1,0:T(8,128)(2,1)S(1)}, bf16[6,80,768]{2,1,0:T(8,128)(2,1)}, u32[]{:S(2)}, u32[]{:S(2)}) collective-permute-start(bf16[6,80,768]{2,1,0:T(8,128)(2,1)S(1)} %pack.3.refs_0_), channel_id=1, source_target_pairs={{0,2},{1,3},{2,0},{3,1},{4,6},{5,7},{6,4},{7,5},{8,10},{9,11},{10,... | collective-permute-start | bytes 2211848 | tf_op jit(solution)/shard_map/ppermute | solution.py:436
  134.0 42.1 %collective-permute-start.7 = (bf16[3,4,80,768]{3,2,1,0:T(8,128)(2,1)}, bf16[3,4,80,768]{3,2,1,0:T(8,128)(2,1)}, u32[]{:S(2)}, u32[]{:S(2)}) collective-permute-start(bf16[3,4,80,768]{3,2,1,0:T(8,128)(2,1)} %stack.3.refs_4_), channel_id=1, source_target_pairs={{0,1},{1,0},{2,3},{3,2},{4,5},{5,4},{6,7},{7,6},{8,9},{9,8},{10,11... | collective-permute-start | bytes 4423688 | tf_op jit(solution)/shard_map/ppermute | solution.py:436
  134.1 42.0 %collective-permute-start.8 = (bf16[3,4,80,768]{3,2,1,0:T(8,128)(2,1)}, bf16[3,4,80,768]{3,2,1,0:T(8,128)(2,1)}, u32[]{:S(2)}, u32[]{:S(2)}) collective-permute-start(bf16[3,4,80,768]{3,2,1,0:T(8,128)(2,1)} %collective-permute-done.6.refs_5_), channel_id=1, source_target_pairs={{0,1},{1,0},{2,3},{3,2},{4,5},{5,4},{6,7},{7,6},{8,9},{9,8},{10,11... | collective-permute-start | bytes 4423688 | tf_op jit(solution)/shard_map/ppermute | solution.py:436
  134.5 17.9 %collective-permute-start.12 = (bf16[4,528,128]{2,1,0:T(8,128)(2,1)S(1)}, bf16[4,528,128]{2,1,0:T(8,128)(2,1)S(1)}, u32[]{:S(2)}, u32[]{:S(2)}) collective-permute-start(bf16[4,528,128]{2,1,0:T(8,128)(2,1)S(1)} %stack.4.refs_0_), channel_id=1, source_target_pairs={{0,4},{1,5},{2,6},{3,7},{4,0},{5,1},{6,2},{7,3},{8,12},{9,13},{10,... | collective-permute-start | bytes 1622024 | tf_op jit(solution)/shard_map/ppermute | solution.py:436
  139.8 14.2 %collective-permute-start.1 = (bf16[6,80,768]{2,1,0:T(8,128)(2,1)S(1)}, bf16[6,80,768]{2,1,0:T(8,128)(2,1)S(1)}, u32[]{:S(2)}, u32[]{:S(2)}) collective-permute-start(bf16[6,80,768]{2,1,0:T(8,128)(2,1)S(1)} %pack.3.refs_0_), channel_id=1, source_target_pairs={{0,1},{1,0},{2,3},{3,2},{4,5},{5,4},{6,7},{7,6},{8,9},{9,8},{10,11... | collective-permute-start | bytes 2211848 | tf_op jit(solution)/shard_map/ppermute | solution.py:436
  153.2 18.0 %collective-permute-start.24 = (bf16[3,2,80,768]{3,2,1,0:T(8,128)(2,1)S(1)}, bf16[3,2,80,768]{3,2,1,0:T(8,128)(2,1)}, u32[]{:S(2)}, u32[]{:S(2)}) collective-permute-start(bf16[3,2,80,768]{3,2,1,0:T(8,128)(2,1)S(1)} %stack.5.refs_4_), channel_id=1, source_target_pairs={{0,2},{1,3},{2,0},{3,1},{4,6},{5,7},{6,4},{7,5},{8,10},{9,11},{10,... | collective-permute-start | bytes 2211848 | tf_op jit(solution)/shard_map/ppermute | solution.py:436
  154.0 22.1 %collective-permute-start.2 = (bf16[6,80,768]{2,1,0:T(8,128)(2,1)}, bf16[6,80,768]{2,1,0:T(8,128)(2,1)}, u32[]{:S(2)}, u32[]{:S(2)}) collective-permute-start(bf16[6,80,768]{2,1,0:T(8,128)(2,1)} %collective-permute-done.refs_1_), channel_id=1, source_target_pairs={{0,1},{1,0},{2,3},{3,2},{4,5},{5,4},{6,7},{7,6},{8,9},{9,8},{10,11... | collective-permute-start | bytes 2211848 | tf_op jit(solution)/shard_map/ppermute | solution.py:436
  154.9 16.3 %collective-permute-start.14 = (bf16[4,528,128]{2,1,0:T(8,128)(2,1)}, bf16[4,528,128]{2,1,0:T(8,128)(2,1)}, u32[]{:S(2)}, u32[]{:S(2)}) collective-permute-start(bf16[4,528,128]{2,1,0:T(8,128)(2,1)} %collective-permute-done.13.refs_2_), channel_id=1, source_target_pairs={{0,4},{1,5},{2,6},{3,7},{4,0},{5,1},{6,2},{7,3},{8,12},{9,13},{10,... | collective-permute-start | bytes 1622024 | tf_op jit(solution)/shard_map/ppermute | solution.py:436
  171.2 20.3 %collective-permute-start.25 = (bf16[3,2,80,768]{3,2,1,0:T(8,128)(2,1)S(1)}, bf16[3,2,80,768]{3,2,1,0:T(8,128)(2,1)S(1)}, u32[]{:S(2)}, u32[]{:S(2)}) collective-permute-start(bf16[3,2,80,768]{3,2,1,0:T(8,128)(2,1)S(1)} %stack.5.refs_4_), channel_id=1, source_target_pairs={{0,1},{1,0},{2,3},{3,2},{4,5},{5,4},{6,7},{7,6},{8,9},{9,8},{10,11... | collective-permute-start | bytes 2211848 | tf_op jit(solution)/shard_map/ppermute | solution.py:436
  171.2 20.3 %collective-permute-start.26 = (bf16[3,2,80,768]{3,2,1,0:T(8,128)(2,1)}, bf16[3,2,80,768]{3,2,1,0:T(8,128)(2,1)S(1)}, u32[]{:S(2)}, u32[]{:S(2)}) collective-permute-start(bf16[3,2,80,768]{3,2,1,0:T(8,128)(2,1)} %collective-permute-done.24.refs_5_), channel_id=1, source_target_pairs={{0,1},{1,0},{2,3},{3,2},{4,5},{5,4},{6,7},{7,6},{8,9},{9,8},{10,11... | collective-permute-start | bytes 2211848 | tf_op jit(solution)/shard_map/ppermute | solution.py:436
  199.8 5.0 %collective-permute-start.27 = (bf16[2,64,192]{2,1,0:T(8,128)(2,1)S(1)}, bf16[2,64,192]{2,1,0:T(8,128)(2,1)S(1)}, u32[]{:S(2)}, u32[]{:S(2)}) collective-permute-start(bf16[2,64,192]{2,1,0:T(8,128)(2,1)S(1)} %get-tuple-element.65), channel_id=1, source_target_pairs={{0,2},{1,3},{2,0},{3,1},{4,6},{5,7},{6,4},{7,5},{8,10},{9,11},{10,... | collective-permute-start | bytes 147464 | tf_op jit(solution)/shard_map/ppermute | solution.py:436
  201.0 11.1 %collective-permute-start.15 = (bf16[4,64,192]{2,1,0:T(8,128)(2,1)S(1)}, bf16[4,64,192]{2,1,0:T(8,128)(2,1)S(1)}, u32[]{:S(2)}, u32[]{:S(2)}) collective-permute-start(bf16[4,64,192]{2,1,0:T(8,128)(2,1)S(1)} %get-tuple-element.49), channel_id=1, source_target_pairs={{0,2},{1,3},{2,0},{3,1},{4,6},{5,7},{6,4},{7,5},{8,10},{9,11},{10,... | collective-permute-start | bytes 294920 | tf_op jit(solution)/shard_map/ppermute | solution.py:436
  201.9 10.2 %collective-permute-start.16 = (bf16[4,64,192]{2,1,0:T(8,128)(2,1)S(1)}, bf16[4,64,192]{2,1,0:T(8,128)(2,1)S(1)}, u32[]{:S(2)}, u32[]{:S(2)}) collective-permute-start(bf16[4,64,192]{2,1,0:T(8,128)(2,1)S(1)} %get-tuple-element.50), channel_id=1, source_target_pairs={{0,1},{1,0},{2,3},{3,2},{4,5},{5,4},{6,7},{7,6},{8,9},{9,8},{10,11... | collective-permute-start | bytes 294920 | tf_op jit(solution)/shard_map/ppermute | solution.py:436
  201.9 10.2 %collective-permute-start.17 = (bf16[4,64,192]{2,1,0:T(8,128)(2,1)S(1)}, bf16[4,64,192]{2,1,0:T(8,128)(2,1)S(1)}, u32[]{:S(2)}, u32[]{:S(2)}) collective-permute-start(bf16[4,64,192]{2,1,0:T(8,128)(2,1)S(1)} %get-tuple-element.51), channel_id=1, source_target_pairs={{0,3},{1,2},{2,1},{3,0},{4,7},{5,6},{6,5},{7,4},{8,11},{9,10},{10,... | collective-permute-start | bytes 294920 | tf_op jit(solution)/shard_map/ppermute | solution.py:436
  204.8 5.4 %collective-permute-start.29 = (bf16[2,64,192]{2,1,0:T(8,128)(2,1)S(1)}, bf16[2,64,192]{2,1,0:T(8,128)(2,1)S(1)}, u32[]{:S(2)}, u32[]{:S(2)}) collective-permute-start(bf16[2,64,192]{2,1,0:T(8,128)(2,1)S(1)} %get-tuple-element.67), channel_id=1, source_target_pairs={{0,3},{1,2},{2,1},{3,0},{4,7},{5,6},{6,5},{7,4},{8,11},{9,10},{10,... | collective-permute-start | bytes 147464 | tf_op jit(solution)/shard_map/ppermute | solution.py:436
  210.6 6.6 %collective-permute-start.30 = (bf16[2,16,768]{2,1,0:T(8,128)(2,1)S(1)}, bf16[2,16,768]{2,1,0:T(8,128)(2,1)S(1)}, u32[]{:S(2)}, u32[]{:S(2)}) collective-permute-start(bf16[2,16,768]{2,1,0:T(8,128)(2,1)S(1)} %get-tuple-element.70), channel_id=1, source_target_pairs={{0,4},{1,5},{2,6},{3,7},{4,0},{5,1},{6,2},{7,3},{8,12},{9,13},{10,... | collective-permute-start | bytes 147464 | tf_op jit(solution)/shard_map/ppermute | solution.py:436
  212.7 16.3 %collective-permute-start.18 = (bf16[4,16,768]{2,1,0:T(8,128)(2,1)S(1)}, bf16[4,16,768]{2,1,0:T(8,128)(2,1)S(1)}, u32[]{:S(2)}, u32[]{:S(2)}) collective-permute-start(bf16[4,16,768]{2,1,0:T(8,128)(2,1)S(1)} %get-tuple-element.54), channel_id=1, source_target_pairs={{0,4},{1,5},{2,6},{3,7},{4,0},{5,1},{6,2},{7,3},{8,12},{9,13},{10,... | collective-permute-start | bytes 294920 | tf_op jit(solution)/shard_map/ppermute | solution.py:436
  213.4 15.7 %collective-permute-start.19 = (bf16[4,16,768]{2,1,0:T(8,128)(2,1)S(1)}, bf16[4,16,768]{2,1,0:T(8,128)(2,1)S(1)}, u32[]{:S(2)}, u32[]{:S(2)}) collective-permute-start(bf16[4,16,768]{2,1,0:T(8,128)(2,1)S(1)} %get-tuple-element.55), channel_id=1, source_target_pairs={{0,8},{1,9},{2,10},{3,11},{4,12},{5,13},{6,14},{7,15},{8,0},{9,1},... | collective-permute-start | bytes 294920 | tf_op jit(solution)/shard_map/ppermute | solution.py:436
  214.7 14.4 %collective-permute-start.20 = (bf16[4,16,768]{2,1,0:T(8,128)(2,1)S(1)}, bf16[4,16,768]{2,1,0:T(8,128)(2,1)S(1)}, u32[]{:S(2)}, u32[]{:S(2)}) collective-permute-start(bf16[4,16,768]{2,1,0:T(8,128)(2,1)S(1)} %get-tuple-element.56), channel_id=1, source_target_pairs={{0,12},{1,13},{2,14},{3,15},{4,8},{5,9},{6,10},{7,11},{8,4},{9,5},... | collective-permute-start | bytes 294920 | tf_op jit(solution)/shard_map/ppermute | solution.py:436
  217.2 11.9 %collective-permute-start.31 = (bf16[2,16,768]{2,1,0:T(8,128)(2,1)S(1)}, bf16[2,16,768]{2,1,0:T(8,128)(2,1)S(1)}, u32[]{:S(2)}, u32[]{:S(2)}) collective-permute-start(bf16[2,16,768]{2,1,0:T(8,128)(2,1)S(1)} %get-tuple-element.71), channel_id=1, source_target_pairs={{0,8},{1,9},{2,10},{3,11},{4,12},{5,13},{6,14},{7,15},{8,0},{9,1},... | collective-permute-start | bytes 147464 | tf_op jit(solution)/shard_map/ppermute | solution.py:436
  217.2 11.9 %collective-permute-start.32 = (bf16[2,16,768]{2,1,0:T(8,128)(2,1)S(1)}, bf16[2,16,768]{2,1,0:T(8,128)(2,1)S(1)}, u32[]{:S(2)}, u32[]{:S(2)}) collective-permute-start(bf16[2,16,768]{2,1,0:T(8,128)(2,1)S(1)} %get-tuple-element.72), channel_id=1, source_target_pairs={{0,12},{1,13},{2,14},{3,15},{4,8},{5,9},{6,10},{7,11},{8,4},{9,5},... | collective-permute-start | bytes 147464 | tf_op jit(solution)/shard_map/ppermute | solution.py:436
  (16 other events, 488.9 us)

commit v4 on v3

--- a/solution.py
+++ b/solution.py
@@ -218,18 +218,12 @@
     )(me.reshape(1), span_owner, qsel, *parts)
 
 
-def attention_kernel(pieces, hpg, direct, keys, *refs):
+def heads_kernel(pieces, direct, keys, *refs):
     own_refs, far_refs, refs = refs[:pieces], refs[pieces : 2 * pieces], refs[2 * pieces :]
     if not direct:
         query_ref, refs = refs[0], refs[1:]
-    count = pieces if direct else 1
-    bias_ref, mask_ref, wq_ref, wk_ref, wv_ref, wg_ref = refs[:6]
-    out_refs, gate_ref = refs[6 : 6 + count], refs[6 + count]
-    q_ref, k_ref, v_ref = refs[7 + count :]
+    wq_ref, wk_ref, wv_ref, wg_ref, q_ref, k_ref, v_ref, gate_ref = refs
     total_rows, width = own_refs[0].shape[1:]
-    feats = wq_ref.shape[1]
-    head_size = feats // hpg
-    scale = LOG2E / math.sqrt(head_size)
 
     def own_rows(start, stop):
         return jnp.concatenate([ref[0, start:stop] for ref in own_refs], axis=0)
@@ -242,48 +236,25 @@
     for m in range(-1, pieces):
         block = own_rows(0, keys) if m < 0 else far_rows(far_refs[m], 0, keys)
         span = slice(at, at + block.shape[0])
-        k_t = nn_dot(block, wk_ref[...]).T
-        k_ref[:, span] = jnp.where(mask_ref[:1, span] > 0, k_t, 0.0).astype(BF16)
-        v_ref[span, :] = nn_dot(block, wv_ref[...]).astype(BF16)
+        k_ref[0, :, span] = nn_dot(block, wk_ref[...]).T.astype(BF16)
+        v_ref[0, span, :] = nn_dot(block, wv_ref[...]).astype(BF16)
         at += block.shape[0]
     if direct:
         at = 0
         for m in range(-1, pieces):
             block = own_rows(keys, total_rows) if m < 0 else far_rows(far_refs[m], keys, total_rows)
-            q_ref[at : at + block.shape[0], :] = nn_dot(block, wq_ref[...]).astype(BF16)
+            q_ref[0, at : at + block.shape[0], :] = nn_dot(block, wq_ref[...]).astype(BF16)
             at += block.shape[0]
         block = jnp.concatenate([own_refs[0][0, keys:], far_rows(far_refs[0], keys, total_rows)], axis=0)
         gate_ref[0] = jax.nn.sigmoid(nn_dot(block, wg_ref[...]))
     else:
-        q_ref[...] = nn_dot(query_ref[0], wq_ref[...]).astype(BF16)
+        q_ref[0] = nn_dot(query_ref[0], wq_ref[...]).astype(BF16)
         gate_ref[...] = jnp.zeros_like(gate_ref)
-    q = q_ref[...]
-    owner = lax.broadcasted_iota(jnp.int32, q.shape, 1) // head_size
-    total = None
-    for h in range(hpg):
-        mine = owner == h
-        scores = nn_dot(jnp.where(mine, q, jnp.zeros_like(q)), k_ref[...])
-        scores = scores * scale + bias_ref[h]
-        weights = jnp.exp2(scores - jnp.max(scores, axis=-1, keepdims=True))
-        norm = 1.0 / jnp.sum(weights, axis=-1, keepdims=True)
-        result = nn_dot((weights * norm).astype(BF16), v_ref[...])
-        total = result if total is None else jnp.where(mine, result, total)
-    total = total.astype(BF16)
-    if not direct:
-        out_refs[0][0] = total
-        return
-    own = total_rows - keys
-    far = out_refs[0].shape[1] - own
-    for m, out_ref in enumerate(out_refs):
-        out_ref[0, :own] = total[m * own : (m + 1) * own]
-        out_ref[0, own:] = total[pieces * own + m * far : pieces * own + (m + 1) * far]
-
-
-def attention(first, own, far, queries, bias, mask, wq, wk, wv, w_gate, hpg, keys, query_rows):
+
+
+def projections(first, own, far, queries, wq, wk, wv, w_gate, keys, query_rows, window, tokens):
     pieces = len(far)
     others, size, rows, width = far[0].shape
-    window = bias.shape[1]
-    tokens = bias.shape[2]
     feats = wq.shape[1]
     direct = queries is None
     whole = pl.BlockSpec(memory_space=pltpu.VMEM)
@@ -291,35 +262,72 @@
     specs += [pl.BlockSpec((others, 1, rows, width), lambda s: (0, s, 0, 0))] * pieces
     args = list(own) + list(far)
     gate_rows = (others + 1) * query_rows
-    out_rows = [gate_rows] * pieces
     if not direct:
         specs.append(pl.BlockSpec((1, window, width), lambda s: (s, 0, 0)))
         args.append(queries)
-        out_rows = [window]
-    consts = [bias, mask, wq, wk, wv, w_gate]
-    limit = (60 if tokens > 2048 else 26) * MIB
-    flops = 2 * size * (tokens * width * feats * 2 + hpg * window * tokens * 512)
-    return pl.pallas_call(
-        functools.partial(attention_kernel, pieces, hpg, direct, keys),
+    consts = [wq, wk, wv, w_gate]
+    shapes = [(window, feats), (feats, tokens), (tokens, feats), (gate_rows, width)]
+    return pl.pallas_call(
+        functools.partial(heads_kernel, pieces, direct, keys),
         grid=(size,),
         in_specs=specs + [whole] * len(consts),
-        out_specs=[pl.BlockSpec((1, r, feats), lambda s: (s, 0, 0)) for r in out_rows]
-        + [pl.BlockSpec((1, gate_rows, width), lambda s: (s, 0, 0))],
-        out_shape=[jax.ShapeDtypeStruct((size, r, feats), BF16) for r in out_rows]
-        + [jax.ShapeDtypeStruct((size, gate_rows, width), F32)],
-        scratch_shapes=[
-            pltpu.VMEM((window, feats), BF16),
-            pltpu.VMEM((feats, tokens), BF16),
-            pltpu.VMEM((tokens, feats), BF16),
+        out_specs=[pl.BlockSpec((1,) + x, lambda s: (s, 0, 0)) for x in shapes],
+        out_shape=[
+            jax.ShapeDtypeStruct((size,) + x, F32 if i == 3 else BF16) for i, x in enumerate(shapes)
         ],
         cost_estimate=pl.CostEstimate(
-            flops=flops,
-            bytes_accessed=size * tokens * width * 2 + hpg * window * tokens * 4,
+            flops=4 * size * tokens * width * feats, bytes_accessed=size * tokens * width * 3, transcendentals=0
+        ),
+        compiler_params=pltpu.CompilerParams(vmem_limit_bytes=(48 if tokens > 2048 else 16) * MIB),
+        name="heads",
+    )(*args, *consts)
+
+
+def attention_kernel(hpg, splits, q_ref, k_ref, v_ref, bias_ref, mask_ref, *out_refs):
+    q = q_ref[0]
+    k = k_ref[0] * mask_ref[:1].astype(BF16)
+    head_size = q.shape[1] // hpg
+    scale = LOG2E / math.sqrt(head_size)
+    owner = lax.broadcasted_iota(jnp.int32, q.shape, 1) // head_size
+    total = None
+    for h in range(hpg):
+        mine = owner == h
+        scores = nn_dot(jnp.where(mine, q, jnp.zeros_like(q)), k)
+        scores = scores * scale + bias_ref[h]
+        weights = jnp.exp2(scores - jnp.max(scores, axis=-1, keepdims=True))
+        norm = 1.0 / jnp.sum(weights, axis=-1, keepdims=True)
+        result = nn_dot((weights * norm).astype(BF16), v_ref[0])
+        total = result if total is None else jnp.where(mine, result, total)
+    total = total.astype(BF16)
+    if splits is None:
+        out_refs[0][0] = total
+        return
+    own, far = splits
+    pieces = len(out_refs)
+    for m, out_ref in enumerate(out_refs):
+        out_ref[0, :own] = total[m * own : (m + 1) * own]
+        out_ref[0, own:] = total[pieces * own + m * far : pieces * own + (m + 1) * far]
+
+
+def attention(q, k, v, bias, mask, hpg, splits, pieces):
+    size, window, feats = q.shape
+    tokens = k.shape[2]
+    out_rows = [window] if splits is None else [sum(splits)] * pieces
+    return pl.pallas_call(
+        functools.partial(attention_kernel, hpg, splits),
+        grid=(size,),
+        in_specs=[pl.BlockSpec((1,) + x.shape[1:], lambda s: (s, 0, 0)) for x in (q, k, v)]
+        + [pl.BlockSpec(memory_space=pltpu.VMEM)] * 2,
+        out_specs=[pl.BlockSpec((1, r, feats), lambda s: (s, 0, 0)) for r in out_rows],
+        out_shape=[jax.ShapeDtypeStruct((size, r, feats), BF16) for r in out_rows],
+        cost_estimate=pl.CostEstimate(
+            flops=2 * size * hpg * window * tokens * 512,
+            bytes_accessed=size * tokens * feats * 4 + hpg * window * tokens * 4,
             transcendentals=size * hpg * window * tokens,
         ),
-        compiler_params=pltpu.CompilerParams(vmem_limit_bytes=limit),
+        compiler_params=pltpu.CompilerParams(vmem_limit_bytes=(58 if tokens > 2048 else 20) * MIB),
         name="attend",
-    )(*args, *consts)
+    )(q, k, v, bias, mask)
 
 
 def project_kernel(labels, sizes, lane_ref, *refs):
@@ -488,7 +496,6 @@
     wq, wk, wv = own(w_query), own(w_key), own(w_value)
 
     heads, gates = [], []
-    previous = None
     for c, size in enumerate(sizes):
         far = [stacked(got[c])]
         far = over_lanes(far)
@@ -498,11 +505,14 @@
             mine = [x[None, firsts[c] : firsts[c] + size, keys:] for x in own_tokens]
             queries = jnp.concatenate(mine + [x[:, :, keys:] for x in far], axis=0)
             queries = jnp.swapaxes(jnp.take(queries, order, axis=0), 0, 1).reshape(size, window, width)
-        if previous is not None:
+        if c:
             far, previous = lax.optimization_barrier((far, previous))
-        results = attention(firsts[c], own_tokens, far, queries, bias, mask, wq, wk, wv, w_gate, hpg, keys, query_rows)
-        results, gate = results[:-1], results[-1]
-        previous = gate
+        q, k, v, gate = projections(
+            firsts[c], own_tokens, far, queries, wq, wk, wv, w_gate, keys, query_rows, window, n * keys
+        )
+        splits = (query_rows, (sg - 1) * query_rows) if direct else None
+        results = attention(q, k, v, bias, mask, hpg, splits, hg)
+        previous = results[0]
         if not direct:
             blocks = jnp.take(results[0].reshape(size, n, query_rows, feats), code_list ^ me, axis=1)
             results = []

time: 230 us -> 228 us (level)
  starting transfers between devices: 46.9 us -> 38.8 us
  waiting for transfers between devices: 134 us -> 139 us
    ppermute x33, starting transfers between devices: 46.9 us -> 38.8 us  [across(): return lax.ppermute(x, 'key', [(i, i ^ code) for i in range(n)])]
    ppermute x33, waiting for transfers between devices: 134 us -> 139 us  [across(): return lax.ppermute(x, 'key', [(i, i ^ code) for i in range(n)])]
    pallas_call x2 -> x4, Pallas kernels: 23.6 us -> 25.8 us  [the longest x2 14 us: attention(): pl.pallas_call(functools.partial(attention_kernel, hpg, splits), grid=(si...]
  transfers between devices with their start and end apart: 33 -> 33, of which waited for: 11 -> 11; matrix products, arithmetic and copies ran while one was open for 1% -> 1% of each run, Pallas kernels for 12% -> 13%
where the time goes in v4:
time: 228 us; the launch traced here: 227 us
  waiting for transfers between devices  139 us (61%)
  Pallas kernels  43.3 us (19%)
  starting transfers between devices  38.8 us (17%)
  local copies, waits for them, and re-layouts  5.85 us (3%)
    ppermute x33, waiting for transfers between devices, across(): return lax.ppermute(x, 'key', [(i, i ^ code) for i in range(n)])  139 us
    ppermute x33, starting transfers between devices, across(): return lax.ppermute(x, 'key', [(i, i ^ code) for i in range(n)])  38.8 us
    pallas_call x2, Pallas kernels, attention(): pl.pallas_call(functools.partial(attention_kernel, hpg, splits), grid=(si...  14 us
    pallas_call x2, Pallas kernels, projections(): pl.pallas_call(functools.partial(heads_kernel, pieces, direct, keys), gri...  11.8 us
    pallas_call x1, Pallas kernels, local_bias(): pl.pallas_call(functools.partial(bias_kernel, hpg), grid=(rows // tile,),...  6.5 us
  transfers between devices with their start and end apart: 33, of which 11 were waited for; matrix products, arithmetic and copies ran while one was open for 1% of the time, Pallas kernels for 13%

profile of v4, /device:TPU:0, one launch (start us, length us, event | category | flops | bytes accessed | tf_op | source)
XLA Modules:
  0.0 227.2 jit_solution(17581831592664912401)
XLA Ops:
  0.0 3.7 %pack.4 = (bf16[4,80,768]{2,1,0:T(8,128)(2,1)}, bf16[4,80,768]{2,1,0:T(8,128)(2,1)}, bf16[4,80,768]{2,1,0:T(8,128)(2,1)}) custom-call(s32[1]{0:T(128)} %bitcast.group_ref, bf16[4,6,64,768]{3,2,1,0:T(8,128)(2,1)} %bitcast.14, bf16[4,6,64,768]{3,2,1,0:T(8,128)(2,1)} %bitcast.15, bf16[4,6,64,768]{3,2,1,0:T(8,128)(2,1)} %bitcast.16, ...), custom_call_target="tpu_custom_call" | custom-call | bytes 2949120 | tf_op jit(solution)/shard_map/pack/pallas_call | solution.py:108
  3.7 3.1 %collective-permute-start.3 = (bf16[4,80,768]{2,1,0:T(8,128)(2,1)}, bf16[4,80,768]{2,1,0:T(8,128)(2,1)S(1)}, u32[]{:S(2)}, u32[]{:S(2)}) collective-permute-start(bf16[4,80,768]{2,1,0:T(8,128)(2,1)} %get-tuple-element.45), channel_id=1, source_target_pairs={{0,4},{1,5},{2,6},{3,7},{4,0},{5,1},{6,2},{7,3},{8,12},{9,13},{10,... | collective-permute-start | bytes 1474568 | tf_op jit(solution)/shard_map/ppermute | solution.py:444
  6.8 2.6 %collective-permute-start.4 = (bf16[4,80,768]{2,1,0:T(8,128)(2,1)}, bf16[4,80,768]{2,1,0:T(8,128)(2,1)S(1)}, u32[]{:S(2)}, u32[]{:S(2)}) collective-permute-start(bf16[4,80,768]{2,1,0:T(8,128)(2,1)} %get-tuple-element.46), channel_id=1, source_target_pairs={{0,8},{1,9},{2,10},{3,11},{4,12},{5,13},{6,14},{7,15},{8,0},{9,1},... | collective-permute-start | bytes 1474568 | tf_op jit(solution)/shard_map/ppermute | solution.py:444
  9.4 18.6 %collective-permute-done.3.refs_0_ = bf16[4,80,768]{2,1,0:T(8,128)(2,1)S(1)} collective-permute-done((bf16[4,80,768]{2,1,0:T(8,128)(2,1)}, bf16[4,80,768]{2,1,0:T(8,128)(2,1)S(1)}, u32[]{:S(2)}, u32[]{:S(2)}) %collective-permute-start.3) | collective-permute-done | bytes 491552 | tf_op jit(solution)/shard_map/ppermute | solution.py:444
  28.0 15.0 %collective-permute-done.4.refs_1_ = bf16[4,80,768]{2,1,0:T(8,128)(2,1)S(1)} collective-permute-done((bf16[4,80,768]{2,1,0:T(8,128)(2,1)}, bf16[4,80,768]{2,1,0:T(8,128)(2,1)S(1)}, u32[]{:S(2)}, u32[]{:S(2)}) %collective-permute-start.4) | collective-permute-done | bytes 491552 | tf_op jit(solution)/shard_map/ppermute | solution.py:444
  43.3 1.6 collective-permute-start.6
  45.8 2.2 copy-done.5
  48.0 6.5 %bias_local.1 = (bf16[528,128]{1,0:T(8,128)(2,1)S(1)}, bf16[528,128]{1,0:T(8,128)(2,1)S(1)}, bf16[528,128]{1,0:T(8,128)(2,1)S(1)}, bf16[528,128]{1,0:T(8,128)(2,1)S(1)}) custom-call(f32[1,128]{1,0:T(1,128)S(1)} %broadcast_in_dim_tile.3.mask_ref, bf16[2,128,64,128]{3,2,1,0:T(8,128)(2,1)S(1)} %bitcast.28, f32[1,128]{1,0:T(1,128)S(1)} %bitcast.29, ...), custom_call_target="tpu_custom_call" | custom-call | flops 1073741824 | bytes 4194304 | tf_op jit(solution)/shard_map/bias_local/pallas_call | solution.py:58
  55.2 1.3 collective-permute-start.11
  56.5 22.9 %collective-permute-done.10.refs_2_ = bf16[528,128]{1,0:T(8,128)(2,1)S(1)} collective-permute-done((bf16[528,128]{1,0:T(8,128)(2,1)S(1)}, bf16[528,128]{1,0:T(8,128)(2,1)S(1)}, u32[]{:S(2)}, u32[]{:S(2)}) %collective-permute-start.10) | collective-permute-done | bytes 135200 | tf_op jit(solution)/shard_map/ppermute | solution.py:444
  79.9 11.1 %collective-permute-start.12 = (bf16[4,528,128]{2,1,0:T(8,128)(2,1)S(1)}, bf16[4,528,128]{2,1,0:T(8,128)(2,1)S(1)}, u32[]{:S(2)}, u32[]{:S(2)}) collective-permute-start(bf16[4,528,128]{2,1,0:T(8,128)(2,1)S(1)} %stack.4.refs_0_), channel_id=1, source_target_pairs={{0,4},{1,5},{2,6},{3,7},{4,0},{5,1},{6,2},{7,3},{8,12},{9,13},{10,... | collective-permute-start | bytes 1622024 | tf_op jit(solution)/shard_map/ppermute | solution.py:444
  91.2 3.0 %collective-permute-start.22 = (bf16[2,80,768]{2,1,0:T(8,128)(2,1)S(1)}, bf16[2,80,768]{2,1,0:T(8,128)(2,1)S(1)}, u32[]{:S(2)}, u32[]{:S(2)}) collective-permute-start(bf16[2,80,768]{2,1,0:T(8,128)(2,1)S(1)} %get-tuple-element.67), channel_id=1, source_target_pairs={{0,8},{1,9},{2,10},{3,11},{4,12},{5,13},{6,14},{7,15},{8,0},{9,1},... | collective-permute-start | bytes 737288 | tf_op jit(solution)/shard_map/ppermute | solution.py:444
  94.2 1.4 collective-permute-start.23
  95.7 18.8 %collective-permute-done.21.refs_0_ = bf16[2,80,768]{2,1,0:T(8,128)(2,1)S(1)} collective-permute-done((bf16[2,80,768]{2,1,0:T(8,128)(2,1)S(1)}, bf16[2,80,768]{2,1,0:T(8,128)(2,1)S(1)}, u32[]{:S(2)}, u32[]{:S(2)}) %collective-permute-start.21) | collective-permute-done | bytes 245792 | tf_op jit(solution)/shard_map/ppermute | solution.py:444
  115.6 6.6 %collective-permute-done.23.refs_2_ = bf16[2,80,768]{2,1,0:T(8,128)(2,1)S(1)} collective-permute-done((bf16[2,80,768]{2,1,0:T(8,128)(2,1)S(1)}, bf16[2,80,768]{2,1,0:T(8,128)(2,1)S(1)}, u32[]{:S(2)}, u32[]{:S(2)}) %collective-permute-start.23) | collective-permute-done | bytes 245792 | tf_op jit(solution)/shard_map/ppermute | solution.py:444
  123.2 24.3 %collective-permute-done.13.refs_2_ = bf16[4,528,128]{2,1,0:T(8,128)(2,1)} collective-permute-done((bf16[4,528,128]{2,1,0:T(8,128)(2,1)S(1)}, bf16[4,528,128]{2,1,0:T(8,128)(2,1)}, u32[]{:S(2)}, u32[]{:S(2)}) %collective-permute-start.13) | collective-permute-done | bytes 540704 | tf_op jit(solution)/shard_map/ppermute | solution.py:444
  149.7 1.7 constant_dynamic-slice_fusion
  151.4 14.9 %collective-permute-done.24.refs_5_ = bf16[3,2,80,768]{3,2,1,0:T(8,128)(2,1)} collective-permute-done((bf16[3,2,80,768]{3,2,1,0:T(8,128)(2,1)}, bf16[3,2,80,768]{3,2,1,0:T(8,128)(2,1)}, u32[]{:S(2)}, u32[]{:S(2)}) %collective-permute-start.24) | collective-permute-done | bytes 737312 | tf_op jit(solution)/shard_map/ppermute | solution.py:444
  167.0 4.0 %bias_order.1 = (f32[4,256,1024]{2,1,0:T(8,128)S(1)}, f32[8,1024]{1,0:T(8,128)S(1)}) custom-call(s32[1]{0:T(128)} %bitcast.4.me_ref, s32[16]{0:T(128)S(1)} %copy-done.12, s32[16]{0:T(128)S(1)} %broadcast_xor_fusion.qsel_ref, bf16[4,528,128]{2,1,0:T(8,128)(2,1)S(1)} %copy-done.9, bf16[4,528,128]{2,1,0:T(8,128)(2,1)S(1)} %copy-done.11, ...), custom_call_target="tpu_custom_call" | custom-call | flops 8388608 | bytes 6291456 | tf_op jit(solution)/shard_map/bias_order/pallas_call | solution.py:201
  171.1 7.5 %heads.2 = (bf16[4,256,192]{2,1,0:T(8,128)(2,1)S(1)}, bf16[4,192,1024]{2,1,0:T(8,128)(2,1)S(1)}, bf16[4,1024,192]{2,1,0:T(8,128)(2,1)S(1)}, f32[4,64,768]{2,1,0:T(8,128)S(1)}) custom-call(bf16[6,80,768]{2,1,0:T(8,128)(2,1)S(1)} %pack.3.refs_0_, bf16[6,80,768]{2,1,0:T(8,128)(2,1)} %collective-permute-done.refs_1_, bf16[6,80,768]{2,1,0:T(8,128)(2,1)S(1)} %copy-done.7, ...), custom_call_target="tpu_custom_call" | custom-call | flops 2415919104 | bytes 9437184 | tf_op jit(solution)/shard_map/heads/pallas_call | solution.py:270
  178.6 9.3 %attend.2 = (bf16[4,64,192]{2,1,0:T(8,128)(2,1)S(1)}, bf16[4,64,192]{2,1,0:T(8,128)(2,1)S(1)}, bf16[4,64,192]{2,1,0:T(8,128)(2,1)S(1)}, bf16[4,64,192]{2,1,0:T(8,128)(2,1)S(1)}) custom-call(bf16[4,256,192]{2,1,0:T(8,128)(2,1)S(1)} %get-tuple-element.48.q_ref, bf16[4,192,1024]{2,1,0:T(8,128)(2,1)S(1)} %get-tuple-element.49.k_ref, ...), custom_call_target="tpu_custom_call" | custom-call | flops 4294967296 | bytes 7340032 | tf_op jit(solution)/shard_map/attend/pallas_call | solution.py:316
  188.0 4.3 %heads.3 = (bf16[2,256,192]{2,1,0:T(8,128)(2,1)S(1)}, bf16[2,192,1024]{2,1,0:T(8,128)(2,1)S(1)}, bf16[2,1024,192]{2,1,0:T(8,128)(2,1)S(1)}, f32[2,64,768]{2,1,0:T(8,128)S(1)}) custom-call(bf16[6,80,768]{2,1,0:T(8,128)(2,1)S(1)} %pack.3.refs_0_, bf16[6,80,768]{2,1,0:T(8,128)(2,1)} %collective-permute-done.refs_1_, bf16[6,80,768]{2,1,0:T(8,128)(2,1)S(1)} %copy-done.7, ...), custom_call_target="tpu_custom_call" | custom-call | flops 1207959552 | bytes 4718592 | tf_op jit(solution)/shard_map/heads/pallas_call | solution.py:270
  192.3 4.7 %attend.3 = (bf16[2,64,192]{2,1,0:T(8,128)(2,1)S(1)}, bf16[2,64,192]{2,1,0:T(8,128)(2,1)S(1)}, bf16[2,64,192]{2,1,0:T(8,128)(2,1)S(1)}, bf16[2,64,192]{2,1,0:T(8,128)(2,1)S(1)}) custom-call(bf16[2,256,192]{2,1,0:T(8,128)(2,1)S(1)} %get-tuple-element.73.q_ref, bf16[2,192,1024]{2,1,0:T(8,128)(2,1)S(1)} %get-tuple-element.74.k_ref, ...), custom_call_target="tpu_custom_call" | custom-call | flops 2147483648 | bytes 5767168 | tf_op jit(solution)/shard_map/attend/pallas_call | solution.py:316
  197.0 1.2 collective-permute-start.27
  199.1 1.3 collective-permute-start.17
  200.3 1.7 collective-permute-done.27.refs_1_
  202.0 5.4 %collective-permute-done.29.refs_3_ = bf16[2,64,192]{2,1,0:T(8,128)(2,1)S(1)} collective-permute-done((bf16[2,64,192]{2,1,0:T(8,128)(2,1)S(1)}, bf16[2,64,192]{2,1,0:T(8,128)(2,1)S(1)}, u32[]{:S(2)}, u32[]{:S(2)}) %collective-permute-start.29) | collective-permute-done | bytes 49184 | tf_op jit(solution)/shard_map/ppermute | solution.py:444
  208.6 2.1 collective-permute-start.18
  211.7 1.4 collective-permute-start.20
  213.1 2.0 collective-permute-start.31
  215.1 1.4 collective-permute-start.32
  216.5 9.8 %collective-permute-done.31.refs_6_ = bf16[2,16,768]{2,1,0:T(8,128)(2,1)S(1)} collective-permute-done((bf16[2,16,768]{2,1,0:T(8,128)(2,1)S(1)}, bf16[2,16,768]{2,1,0:T(8,128)(2,1)S(1)}, u32[]{:S(2)}, u32[]{:S(2)}) %collective-permute-start.31) | collective-permute-done | bytes 49184 | tf_op jit(solution)/shard_map/ppermute | solution.py:444
  (96 shorter events, 11.6 us)
Async XLA Ops:
  3.7 24.3 %collective-permute-start.3 = (bf16[4,80,768]{2,1,0:T(8,128)(2,1)}, bf16[4,80,768]{2,1,0:T(8,128)(2,1)S(1)}, u32[]{:S(2)}, u32[]{:S(2)}) collective-permute-start(bf16[4,80,768]{2,1,0:T(8,128)(2,1)} %get-tuple-element.45), channel_id=1, source_target_pairs={{0,4},{1,5},{2,6},{3,7},{4,0},{5,1},{6,2},{7,3},{8,12},{9,13},{10,... | collective-permute-start | bytes 1474568 | tf_op jit(solution)/shard_map/ppermute | solution.py:444
  6.8 36.3 %collective-permute-start.4 = (bf16[4,80,768]{2,1,0:T(8,128)(2,1)}, bf16[4,80,768]{2,1,0:T(8,128)(2,1)S(1)}, u32[]{:S(2)}, u32[]{:S(2)}) collective-permute-start(bf16[4,80,768]{2,1,0:T(8,128)(2,1)} %get-tuple-element.46), channel_id=1, source_target_pairs={{0,8},{1,9},{2,10},{3,11},{4,12},{5,13},{6,14},{7,15},{8,0},{9,1},... | collective-permute-start | bytes 1474568 | tf_op jit(solution)/shard_map/ppermute | solution.py:444
  9.4 33.7 %collective-permute-start.5 = (bf16[4,80,768]{2,1,0:T(8,128)(2,1)}, bf16[4,80,768]{2,1,0:T(8,128)(2,1)S(1)}, u32[]{:S(2)}, u32[]{:S(2)}) collective-permute-start(bf16[4,80,768]{2,1,0:T(8,128)(2,1)} %get-tuple-element.47), channel_id=1, source_target_pairs={{0,12},{1,13},{2,14},{3,15},{4,8},{5,9},{6,10},{7,11},{8,4},{9,5},... | collective-permute-start | bytes 1474568 | tf_op jit(solution)/shard_map/ppermute | solution.py:444
  43.3 71.9 %collective-permute-start.6 = (bf16[3,4,80,768]{3,2,1,0:T(8,128)(2,1)S(1)}, bf16[3,4,80,768]{3,2,1,0:T(8,128)(2,1)}, u32[]{:S(2)}, u32[]{:S(2)}) collective-permute-start(bf16[3,4,80,768]{3,2,1,0:T(8,128)(2,1)S(1)} %stack.3.refs_4_), channel_id=1, source_target_pairs={{0,2},{1,3},{2,0},{3,1},{4,6},{5,7},{6,4},{7,5},{8,10},{9,11},{10,... | collective-permute-start | bytes 4423688 | tf_op jit(solution)/shard_map/ppermute | solution.py:444
  54.5 1.9 collective-permute-start.9
  54.6 24.7 %collective-permute-start.10 = (bf16[528,128]{1,0:T(8,128)(2,1)S(1)}, bf16[528,128]{1,0:T(8,128)(2,1)S(1)}, u32[]{:S(2)}, u32[]{:S(2)}) collective-permute-start(bf16[528,128]{1,0:T(8,128)(2,1)S(1)} %get-tuple-element.53), channel_id=1, source_target_pairs={{0,2},{1,3},{2,0},{3,1},{4,6},{5,7},{6,4},{7,5},{8,10},{9,11},{10,... | collective-permute-start | bytes 405512 | tf_op jit(solution)/shard_map/ppermute | solution.py:444
  55.2 24.6 %collective-permute-start.11 = (bf16[528,128]{1,0:T(8,128)(2,1)S(1)}, bf16[528,128]{1,0:T(8,128)(2,1)S(1)}, u32[]{:S(2)}, u32[]{:S(2)}) collective-permute-start(bf16[528,128]{1,0:T(8,128)(2,1)S(1)} %get-tuple-element.54), channel_id=1, source_target_pairs={{0,3},{1,2},{2,1},{3,0},{4,7},{5,6},{6,5},{7,4},{8,11},{9,10},{10,... | collective-permute-start | bytes 405512 | tf_op jit(solution)/shard_map/ppermute | solution.py:444
  79.9 42.3 %collective-permute-start.12 = (bf16[4,528,128]{2,1,0:T(8,128)(2,1)S(1)}, bf16[4,528,128]{2,1,0:T(8,128)(2,1)S(1)}, u32[]{:S(2)}, u32[]{:S(2)}) collective-permute-start(bf16[4,528,128]{2,1,0:T(8,128)(2,1)S(1)} %stack.4.refs_0_), channel_id=1, source_target_pairs={{0,4},{1,5},{2,6},{3,7},{4,0},{5,1},{6,2},{7,3},{8,12},{9,13},{10,... | collective-permute-start | bytes 1622024 | tf_op jit(solution)/shard_map/ppermute | solution.py:444
  91.1 23.5 %collective-permute-start.21 = (bf16[2,80,768]{2,1,0:T(8,128)(2,1)S(1)}, bf16[2,80,768]{2,1,0:T(8,128)(2,1)S(1)}, u32[]{:S(2)}, u32[]{:S(2)}) collective-permute-start(bf16[2,80,768]{2,1,0:T(8,128)(2,1)S(1)} %get-tuple-element.66), channel_id=1, source_target_pairs={{0,4},{1,5},{2,6},{3,7},{4,0},{5,1},{6,2},{7,3},{8,12},{9,13},{10,... | collective-permute-start | bytes 737288 | tf_op jit(solution)/shard_map/ppermute | solution.py:444
  91.2 23.9 %collective-permute-start.22 = (bf16[2,80,768]{2,1,0:T(8,128)(2,1)S(1)}, bf16[2,80,768]{2,1,0:T(8,128)(2,1)S(1)}, u32[]{:S(2)}, u32[]{:S(2)}) collective-permute-start(bf16[2,80,768]{2,1,0:T(8,128)(2,1)S(1)} %get-tuple-element.67), channel_id=1, source_target_pairs={{0,8},{1,9},{2,10},{3,11},{4,12},{5,13},{6,14},{7,15},{8,0},{9,1},... | collective-permute-start | bytes 737288 | tf_op jit(solution)/shard_map/ppermute | solution.py:444
  94.2 28.0 %collective-permute-start.23 = (bf16[2,80,768]{2,1,0:T(8,128)(2,1)S(1)}, bf16[2,80,768]{2,1,0:T(8,128)(2,1)S(1)}, u32[]{:S(2)}, u32[]{:S(2)}) collective-permute-start(bf16[2,80,768]{2,1,0:T(8,128)(2,1)S(1)} %get-tuple-element.68), channel_id=1, source_target_pairs={{0,12},{1,13},{2,14},{3,15},{4,8},{5,9},{6,10},{7,11},{8,4},{9,5},... | collective-permute-start | bytes 737288 | tf_op jit(solution)/shard_map/ppermute | solution.py:444
  114.5 34.2 %collective-permute-start = (bf16[6,80,768]{2,1,0:T(8,128)(2,1)S(1)}, bf16[6,80,768]{2,1,0:T(8,128)(2,1)}, u32[]{:S(2)}, u32[]{:S(2)}) collective-permute-start(bf16[6,80,768]{2,1,0:T(8,128)(2,1)S(1)} %pack.3.refs_0_), channel_id=1, source_target_pairs={{0,2},{1,3},{2,0},{3,1},{4,6},{5,7},{6,4},{7,5},{8,10},{9,11},{10,... | collective-permute-start | bytes 2211848 | tf_op jit(solution)/shard_map/ppermute | solution.py:444
  115.1 56.0 %collective-permute-start.7 = (bf16[3,4,80,768]{3,2,1,0:T(8,128)(2,1)S(1)}, bf16[3,4,80,768]{3,2,1,0:T(8,128)(2,1)}, u32[]{:S(2)}, u32[]{:S(2)}) collective-permute-start(bf16[3,4,80,768]{3,2,1,0:T(8,128)(2,1)S(1)} %stack.3.refs_4_), channel_id=1, source_target_pairs={{0,1},{1,0},{2,3},{3,2},{4,5},{5,4},{6,7},{7,6},{8,9},{9,8},{10,11... | collective-permute-start | bytes 4423688 | tf_op jit(solution)/shard_map/ppermute | solution.py:444
  115.2 55.9 %collective-permute-start.8 = (bf16[3,4,80,768]{3,2,1,0:T(8,128)(2,1)}, bf16[3,4,80,768]{3,2,1,0:T(8,128)(2,1)}, u32[]{:S(2)}, u32[]{:S(2)}) collective-permute-start(bf16[3,4,80,768]{3,2,1,0:T(8,128)(2,1)} %collective-permute-done.6.refs_5_), channel_id=1, source_target_pairs={{0,1},{1,0},{2,3},{3,2},{4,5},{5,4},{6,7},{7,6},{8,9},{9,8},{10,11... | collective-permute-start | bytes 4423688 | tf_op jit(solution)/shard_map/ppermute | solution.py:444
  122.2 25.4 %collective-permute-start.13 = (bf16[4,528,128]{2,1,0:T(8,128)(2,1)S(1)}, bf16[4,528,128]{2,1,0:T(8,128)(2,1)}, u32[]{:S(2)}, u32[]{:S(2)}) collective-permute-start(bf16[4,528,128]{2,1,0:T(8,128)(2,1)S(1)} %stack.4.refs_0_), channel_id=1, source_target_pairs={{0,8},{1,9},{2,10},{3,11},{4,12},{5,13},{6,14},{7,15},{8,0},{9,1},... | collective-permute-start | bytes 1622024 | tf_op jit(solution)/shard_map/ppermute | solution.py:444
  122.2 26.5 %collective-permute-start.1 = (bf16[6,80,768]{2,1,0:T(8,128)(2,1)S(1)}, bf16[6,80,768]{2,1,0:T(8,128)(2,1)S(1)}, u32[]{:S(2)}, u32[]{:S(2)}) collective-permute-start(bf16[6,80,768]{2,1,0:T(8,128)(2,1)S(1)} %pack.3.refs_0_), channel_id=1, source_target_pairs={{0,1},{1,0},{2,3},{3,2},{4,5},{5,4},{6,7},{7,6},{8,9},{9,8},{10,11... | collective-permute-start | bytes 2211848 | tf_op jit(solution)/shard_map/ppermute | solution.py:444
  147.6 18.7 %collective-permute-start.24 = (bf16[3,2,80,768]{3,2,1,0:T(8,128)(2,1)}, bf16[3,2,80,768]{3,2,1,0:T(8,128)(2,1)}, u32[]{:S(2)}, u32[]{:S(2)}) collective-permute-start(bf16[3,2,80,768]{3,2,1,0:T(8,128)(2,1)} %stack.5.refs_4_), channel_id=1, source_target_pairs={{0,2},{1,3},{2,0},{3,1},{4,6},{5,7},{6,4},{7,5},{8,10},{9,11},{10,... | collective-permute-start | bytes 2211848 | tf_op jit(solution)/shard_map/ppermute | solution.py:444
  148.7 22.4 %collective-permute-start.2 = (bf16[6,80,768]{2,1,0:T(8,128)(2,1)}, bf16[6,80,768]{2,1,0:T(8,128)(2,1)}, u32[]{:S(2)}, u32[]{:S(2)}) collective-permute-start(bf16[6,80,768]{2,1,0:T(8,128)(2,1)} %collective-permute-done.refs_1_), channel_id=1, source_target_pairs={{0,1},{1,0},{2,3},{3,2},{4,5},{5,4},{6,7},{7,6},{8,9},{9,8},{10,11... | collective-permute-start | bytes 2211848 | tf_op jit(solution)/shard_map/ppermute | solution.py:444
  149.7 16.7 %collective-permute-start.14 = (bf16[4,528,128]{2,1,0:T(8,128)(2,1)}, bf16[4,528,128]{2,1,0:T(8,128)(2,1)}, u32[]{:S(2)}, u32[]{:S(2)}) collective-permute-start(bf16[4,528,128]{2,1,0:T(8,128)(2,1)} %collective-permute-done.13.refs_2_), channel_id=1, source_target_pairs={{0,4},{1,5},{2,6},{3,7},{4,0},{5,1},{6,2},{7,3},{8,12},{9,13},{10,... | collective-permute-start | bytes 1622024 | tf_op jit(solution)/shard_map/ppermute | solution.py:444
  166.3 21.6 %collective-permute-start.25 = (bf16[3,2,80,768]{3,2,1,0:T(8,128)(2,1)}, bf16[3,2,80,768]{3,2,1,0:T(8,128)(2,1)S(1)}, u32[]{:S(2)}, u32[]{:S(2)}) collective-permute-start(bf16[3,2,80,768]{3,2,1,0:T(8,128)(2,1)} %stack.5.refs_4_), channel_id=1, source_target_pairs={{0,1},{1,0},{2,3},{3,2},{4,5},{5,4},{6,7},{7,6},{8,9},{9,8},{10,11... | collective-permute-start | bytes 2211848 | tf_op jit(solution)/shard_map/ppermute | solution.py:444
  166.3 21.6 %collective-permute-start.26 = (bf16[3,2,80,768]{3,2,1,0:T(8,128)(2,1)}, bf16[3,2,80,768]{3,2,1,0:T(8,128)(2,1)S(1)}, u32[]{:S(2)}, u32[]{:S(2)}) collective-permute-start(bf16[3,2,80,768]{3,2,1,0:T(8,128)(2,1)} %collective-permute-done.24.refs_5_), channel_id=1, source_target_pairs={{0,1},{1,0},{2,3},{3,2},{4,5},{5,4},{6,7},{7,6},{8,9},{9,8},{10,11... | collective-permute-start | bytes 2211848 | tf_op jit(solution)/shard_map/ppermute | solution.py:444
  197.0 5.0 %collective-permute-start.27 = (bf16[2,64,192]{2,1,0:T(8,128)(2,1)S(1)}, bf16[2,64,192]{2,1,0:T(8,128)(2,1)S(1)}, u32[]{:S(2)}, u32[]{:S(2)}) collective-permute-start(bf16[2,64,192]{2,1,0:T(8,128)(2,1)S(1)} %get-tuple-element.77), channel_id=1, source_target_pairs={{0,2},{1,3},{2,0},{3,1},{4,6},{5,7},{6,4},{7,5},{8,10},{9,11},{10,... | collective-permute-start | bytes 147464 | tf_op jit(solution)/shard_map/ppermute | solution.py:444
  198.2 9.7 %collective-permute-start.15 = (bf16[4,64,192]{2,1,0:T(8,128)(2,1)S(1)}, bf16[4,64,192]{2,1,0:T(8,128)(2,1)S(1)}, u32[]{:S(2)}, u32[]{:S(2)}) collective-permute-start(bf16[4,64,192]{2,1,0:T(8,128)(2,1)S(1)} %get-tuple-element.58), channel_id=1, source_target_pairs={{0,2},{1,3},{2,0},{3,1},{4,6},{5,7},{6,4},{7,5},{8,10},{9,11},{10,... | collective-permute-start | bytes 294920 | tf_op jit(solution)/shard_map/ppermute | solution.py:444
  199.1 8.9 %collective-permute-start.16 = (bf16[4,64,192]{2,1,0:T(8,128)(2,1)S(1)}, bf16[4,64,192]{2,1,0:T(8,128)(2,1)S(1)}, u32[]{:S(2)}, u32[]{:S(2)}) collective-permute-start(bf16[4,64,192]{2,1,0:T(8,128)(2,1)S(1)} %get-tuple-element.59), channel_id=1, source_target_pairs={{0,1},{1,0},{2,3},{3,2},{4,5},{5,4},{6,7},{7,6},{8,9},{9,8},{10,11... | collective-permute-start | bytes 294920 | tf_op jit(solution)/shard_map/ppermute | solution.py:444
  199.1 8.9 %collective-permute-start.17 = (bf16[4,64,192]{2,1,0:T(8,128)(2,1)S(1)}, bf16[4,64,192]{2,1,0:T(8,128)(2,1)S(1)}, u32[]{:S(2)}, u32[]{:S(2)}) collective-permute-start(bf16[4,64,192]{2,1,0:T(8,128)(2,1)S(1)} %get-tuple-element.60), channel_id=1, source_target_pairs={{0,3},{1,2},{2,1},{3,0},{4,7},{5,6},{6,5},{7,4},{8,11},{9,10},{10,... | collective-permute-start | bytes 294920 | tf_op jit(solution)/shard_map/ppermute | solution.py:444
  202.0 5.4 %collective-permute-start.29 = (bf16[2,64,192]{2,1,0:T(8,128)(2,1)S(1)}, bf16[2,64,192]{2,1,0:T(8,128)(2,1)S(1)}, u32[]{:S(2)}, u32[]{:S(2)}) collective-permute-start(bf16[2,64,192]{2,1,0:T(8,128)(2,1)S(1)} %get-tuple-element.79), channel_id=1, source_target_pairs={{0,3},{1,2},{2,1},{3,0},{4,7},{5,6},{6,5},{7,4},{8,11},{9,10},{10,... | collective-permute-start | bytes 147464 | tf_op jit(solution)/shard_map/ppermute | solution.py:444
  207.8 7.3 %collective-permute-start.30 = (bf16[2,16,768]{2,1,0:T(8,128)(2,1)S(1)}, bf16[2,16,768]{2,1,0:T(8,128)(2,1)S(1)}, u32[]{:S(2)}, u32[]{:S(2)}) collective-permute-start(bf16[2,16,768]{2,1,0:T(8,128)(2,1)S(1)} %get-tuple-element.82), channel_id=1, source_target_pairs={{0,4},{1,5},{2,6},{3,7},{4,0},{5,1},{6,2},{7,3},{8,12},{9,13},{10,... | collective-permute-start | bytes 147464 | tf_op jit(solution)/shard_map/ppermute | solution.py:444
  208.6 17.8 %collective-permute-start.18 = (bf16[4,16,768]{2,1,0:T(8,128)(2,1)S(1)}, bf16[4,16,768]{2,1,0:T(8,128)(2,1)S(1)}, u32[]{:S(2)}, u32[]{:S(2)}) collective-permute-start(bf16[4,16,768]{2,1,0:T(8,128)(2,1)S(1)} %get-tuple-element.63), channel_id=1, source_target_pairs={{0,4},{1,5},{2,6},{3,7},{4,0},{5,1},{6,2},{7,3},{8,12},{9,13},{10,... | collective-permute-start | bytes 294920 | tf_op jit(solution)/shard_map/ppermute | solution.py:444
  210.6 15.7 %collective-permute-start.19 = (bf16[4,16,768]{2,1,0:T(8,128)(2,1)S(1)}, bf16[4,16,768]{2,1,0:T(8,128)(2,1)S(1)}, u32[]{:S(2)}, u32[]{:S(2)}) collective-permute-start(bf16[4,16,768]{2,1,0:T(8,128)(2,1)S(1)} %get-tuple-element.64), channel_id=1, source_target_pairs={{0,8},{1,9},{2,10},{3,11},{4,12},{5,13},{6,14},{7,15},{8,0},{9,1},... | collective-permute-start | bytes 294920 | tf_op jit(solution)/shard_map/ppermute | solution.py:444
  211.7 14.7 %collective-permute-start.20 = (bf16[4,16,768]{2,1,0:T(8,128)(2,1)S(1)}, bf16[4,16,768]{2,1,0:T(8,128)(2,1)S(1)}, u32[]{:S(2)}, u32[]{:S(2)}) collective-permute-start(bf16[4,16,768]{2,1,0:T(8,128)(2,1)S(1)} %get-tuple-element.65), channel_id=1, source_target_pairs={{0,12},{1,13},{2,14},{3,15},{4,8},{5,9},{6,10},{7,11},{8,4},{9,5},... | collective-permute-start | bytes 294920 | tf_op jit(solution)/shard_map/ppermute | solution.py:444
  213.1 13.2 %collective-permute-start.31 = (bf16[2,16,768]{2,1,0:T(8,128)(2,1)S(1)}, bf16[2,16,768]{2,1,0:T(8,128)(2,1)S(1)}, u32[]{:S(2)}, u32[]{:S(2)}) collective-permute-start(bf16[2,16,768]{2,1,0:T(8,128)(2,1)S(1)} %get-tuple-element.83), channel_id=1, source_target_pairs={{0,8},{1,9},{2,10},{3,11},{4,12},{5,13},{6,14},{7,15},{8,0},{9,1},... | collective-permute-start | bytes 147464 | tf_op jit(solution)/shard_map/ppermute | solution.py:444
  215.1 11.2 %collective-permute-start.32 = (bf16[2,16,768]{2,1,0:T(8,128)(2,1)S(1)}, bf16[2,16,768]{2,1,0:T(8,128)(2,1)S(1)}, u32[]{:S(2)}, u32[]{:S(2)}) collective-permute-start(bf16[2,16,768]{2,1,0:T(8,128)(2,1)S(1)} %get-tuple-element.84), channel_id=1, source_target_pairs={{0,12},{1,13},{2,14},{3,15},{4,8},{5,9},{6,10},{7,11},{8,4},{9,5},... | collective-permute-start | bytes 147464 | tf_op jit(solution)/shard_map/ppermute | solution.py:444
  (18 other events, 616.5 us)

commit v5 on v4

--- a/solution.py
+++ b/solution.py
@@ -25,16 +25,18 @@
     return jnp.dot(a, b, preferred_element_type=F32)
 
 
-def bias_kernel(hpg, mask_ref, pair_ref, gain_ref, proj_ref, *out_refs):
+def bias_kernel(hpg, lane_ref, mask_ref, pair_ref, gain_ref, proj_ref, *out_refs):
     fold, rows, keys, c = pair_ref.shape
-    heads = proj_ref.shape[0]
+    groups = proj_ref.shape[0]
+    heads = groups * hpg
     step = pl.program_id(0)
+    proj = jnp.concatenate([proj_ref[lane_ref[0] ^ m] for m in range(groups)], axis=0).astype(BF16)
     total_rows = (out_refs[0].shape[0] - 16) // hpg
     x = jnp.swapaxes(pair_ref[...], 0, 1).reshape(rows * fold * keys, c).astype(F32)
     center = x - jnp.mean(x, axis=-1, keepdims=True)
     spread = jnp.mean(center * center, axis=-1, keepdims=True)
     normed = (center * lax.rsqrt(spread + 1e-5) * gain_ref[...]).astype(BF16)
-    bias = nt_dot(proj_ref[...], normed)
+    bias = nt_dot(proj, normed)
     bias = bias.reshape(heads, rows, fold * keys).astype(BF16)
     for h in range(heads):
         start = pl.multiple_of((h % hpg) * total_rows + step * rows, 16)
@@ -42,36 +44,38 @@
 
     @pl.when(step == 0)
     def _():
-        row = jnp.broadcast_to(mask_ref[...], (16, fold * keys)).astype(BF16)
+        row = jnp.concatenate([mask_ref[...].astype(F32)] * fold, axis=1)
+        row = jnp.broadcast_to(row, (16, fold * keys)).astype(BF16)
         for out_ref in out_refs:
             out_ref[hpg * total_rows :, :] = row
 
 
-def local_bias(pair, key_mask, pair_gain, proj_t, hpg):
+def local_bias(lane, pair, key_mask, pair_gain, pair_proj, hpg):
     window, keys, c = pair.shape
-    heads = proj_t.shape[0]
+    groups = pair_proj.shape[1] // hpg
     fold = 128 // keys
     rows = window // fold
     tile = 16
-    mask = jnp.tile(key_mask.astype(F32), fold)[None]
+    proj = pair_proj.T.reshape(groups, hpg, c).astype(F32)
     shape = (hpg * rows + 16, 128)
     return pl.pallas_call(
         functools.partial(bias_kernel, hpg),
         grid=(rows // tile,),
         in_specs=[
-            pl.BlockSpec((1, 128), lambda i: (0, 0)),
+            pl.BlockSpec(memory_space=pltpu.SMEM),
+            pl.BlockSpec((1, keys), lambda i: (0, 0)),
             pl.BlockSpec((fold, tile, keys, c), lambda i: (0, i, 0, 0)),
             pl.BlockSpec((1, c), lambda i: (0, 0)),
-            pl.BlockSpec((heads, c), lambda i: (0, 0)),
+            pl.BlockSpec((groups, hpg, c), lambda i: (0, 0, 0)),
         ],
-        out_specs=[pl.BlockSpec(shape, lambda i: (0, 0))] * (heads // hpg),
-        out_shape=[jax.ShapeDtypeStruct(shape, BF16)] * (heads // hpg),
+        out_specs=[pl.BlockSpec(shape, lambda i: (0, 0))] * groups,
+        out_shape=[jax.ShapeDtypeStruct(shape, BF16)] * groups,
         cost_estimate=pl.CostEstimate(
             flops=2 * window * keys * c * 256, bytes_accessed=window * keys * c * 2, transcendentals=0
         ),
-        compiler_params=pltpu.CompilerParams(vmem_limit_bytes=16 * MIB),
+        compiler_params=pltpu.CompilerParams(vmem_limit_bytes=56 * MIB),
         name="bias_local",
-    )(mask, pair.reshape(fold, rows, keys, c), pair_gain[None], proj_t)
+    )(lane.reshape(1), key_mask[None], pair.reshape(fold, rows, keys, c), pair_gain[None], proj)
 
 
 def pack_kernel(sizes, count, group_ref, *refs):
@@ -405,8 +409,10 @@
 
 
 def chunk_sizes(group_samples):
-    last = max(group_samples // 3, 1)
-    return [group_samples - last, last]
+    if group_samples < 4:
+        return [1] * group_samples
+    first = group_samples - 2
+    return [first - first // 2, first // 2, 1, 1]
 
 
 def local(
@@ -472,9 +478,7 @@
 
     own_tokens = over_lanes(list(own_tokens))
 
-    relative = jnp.arange(hg) ^ lane
-    proj_t = jnp.take(pair_proj.T.reshape(hg, hpg, -1), relative, axis=0).reshape(H, -1)
-    pieces = local_bias(pair, key_mask, pair_gain, proj_t, hpg)
+    pieces = local_bias(lane, pair, key_mask, pair_gain, pair_proj, hpg)
     pieces = [across(x, m) for m, x in enumerate(pieces)]
     parts = {0: stacked(pieces)}
     bit = sg // 2
@@ -527,10 +531,11 @@
         heads.append([across(r, m) for r, m in zip(results, labels)])
         gates.append(gate)
     outs = []
-    for span in (slice(0, 1), slice(1, len(sizes))):
+    cut = (len(sizes) + 1) // 2
+    for span in (slice(0, cut), slice(cut, len(sizes))):
         back = projected(lane, heads[span], gates[span], w_out, labels, sg, query_rows)
         outs.extend(across(x, k * hg) for k, x in enumerate(back))
-    out = assembled(group, outs, [0, sizes[0]], (sg, group_samples, query_rows, width))
+    out = assembled(group, outs, [0, firsts[cut]], (sg, group_samples, query_rows, width))
     return out.reshape(samples, query_rows, width)
 
 

time: 228 us -> 210 us (0.921)
  waiting for transfers between devices: 139 us -> 107 us
  starting transfers between devices: 38.8 us -> 47 us
  Pallas kernels: 43.3 us -> 48.4 us
    ppermute x33 -> x51, waiting for transfers between devices: 139 us -> 107 us  [across(): return lax.ppermute(x, 'key', [(i, i ^ code) for i in range(n)])]
    ppermute x33 -> x51, starting transfers between devices: 38.8 us -> 47 us  [across(): return lax.ppermute(x, 'key', [(i, i ^ code) for i in range(n)])]
    pallas_call x1, Pallas kernels: 6.5 us -> 9.06 us  [local_bias(): pl.pallas_call(functools.partial(bias_kernel, hpg), grid=(rows // tile,),...]
    pallas_call x2 -> x4, Pallas kernels: 11.8 us -> 13.4 us  [projections(): pl.pallas_call(functools.partial(heads_kernel, pieces, direct, keys), gri...]
    pallas_call x2 -> x4, Pallas kernels: 14 us -> 15.1 us  [attention(): pl.pallas_call(functools.partial(attention_kernel, hpg, splits), grid=(si...]
  transfers between devices with their start and end apart: 33 -> 51, of which waited for: 11 -> 13; matrix products, arithmetic and copies ran while one was open for 1% -> 1% of each run, Pallas kernels for 13% -> 23%
where the time goes in v5:
time: 210 us
  waiting for transfers between devices  107 us (51%)
  Pallas kernels  48.4 us (23%)
  starting transfers between devices  47 us (22%)
  local copies, waits for them, and re-layouts  6.12 us (3%)
    ppermute x51, waiting for transfers between devices, across(): return lax.ppermute(x, 'key', [(i, i ^ code) for i in range(n)])  107 us
    ppermute x51, starting transfers between devices, across(): return lax.ppermute(x, 'key', [(i, i ^ code) for i in range(n)])  47 us
    pallas_call x4, Pallas kernels, attention(): pl.pallas_call(functools.partial(attention_kernel, hpg, splits), grid=(si...  15.1 us
    pallas_call x4, Pallas kernels, projections(): pl.pallas_call(functools.partial(heads_kernel, pieces, direct, keys), gri...  13.4 us
    pallas_call x1, Pallas kernels, local_bias(): pl.pallas_call(functools.partial(bias_kernel, hpg), grid=(rows // tile,),...  9.06 us
    unnamed x48, local copies, waits for them, and re-layouts  4.37 us
  transfers between devices with their start and end apart: 51, of which 13 were waited for; matrix products, arithmetic and copies ran while one was open for 1% of the time, Pallas kernels for 23%

profile of v5, /device:TPU:0, one launch (start us, length us, event | category | flops | bytes accessed | tf_op | source)
XLA Modules:
  0.0 209.9 jit_solution(10147398511394976371)
XLA Ops:
  0.0 1.8 copy-done.1
  3.1 3.1 %collective-permute-start.30 = (bf16[1,80,768]{2,1,0:T(8,128)(2,1)S(1)}, bf16[1,80,768]{2,1,0:T(8,128)(2,1)S(1)}, u32[]{:S(2)}, u32[]{:S(2)}) collective-permute-start(bf16[1,80,768]{2,1,0:T(8,128)(2,1)S(1)} %get-tuple-element.111), channel_id=1, source_target_pairs={{0,4},{1,5},{2,6},{3,7},{4,0},{5,1},{6,2},{7,3},{8,12},{9,13},{10,... | collective-permute-start | bytes 368648 | tf_op jit(solution)/shard_map/ppermute | solution.py:450
  6.2 2.6 %collective-permute-start.31 = (bf16[1,80,768]{2,1,0:T(8,128)(2,1)S(1)}, bf16[1,80,768]{2,1,0:T(8,128)(2,1)S(1)}, u32[]{:S(2)}, u32[]{:S(2)}) collective-permute-start(bf16[1,80,768]{2,1,0:T(8,128)(2,1)S(1)} %get-tuple-element.112), channel_id=1, source_target_pairs={{0,8},{1,9},{2,10},{3,11},{4,12},{5,13},{6,14},{7,15},{8,0},{9,1},... | collective-permute-start | bytes 368648 | tf_op jit(solution)/shard_map/ppermute | solution.py:450
  9.7 3.5 %collective-permute-start.40 = (bf16[1,80,768]{2,1,0:T(8,128)(2,1)S(1)}, bf16[1,80,768]{2,1,0:T(8,128)(2,1)S(1)}, u32[]{:S(2)}, u32[]{:S(2)}) collective-permute-start(bf16[1,80,768]{2,1,0:T(8,128)(2,1)S(1)} %get-tuple-element.126), channel_id=1, source_target_pairs={{0,8},{1,9},{2,10},{3,11},{4,12},{5,13},{6,14},{7,15},{8,0},{9,1},... | collective-permute-start | bytes 368648 | tf_op jit(solution)/shard_map/ppermute | solution.py:450
  13.8 9.1 %bias_local.1 = (bf16[528,128]{1,0:T(8,128)(2,1)}, bf16[528,128]{1,0:T(8,128)(2,1)}, bf16[528,128]{1,0:T(8,128)(2,1)}, bf16[528,128]{1,0:T(8,128)(2,1)}) custom-call(s32[1]{0:T(128)} %bitcast.1.lane_ref, s32[1,64]{1,0:T(1,128)} %bitcast.28, bf16[2,128,64,128]{3,2,1,0:T(8,128)(2,1)} %bitcast.26, f32[1,128]{1,0:T(1,128)} %bitcast.29, f32[4,4,128]{2,1,0:T(4,128)} %bitcast.27), custom_call_target="tpu_custom_call" | custom-call | flops 1073741824 | bytes 4194304 | tf_op jit(solution)/shard_map/bias_local/pallas_call | solution.py:61
  23.0 1.7 collective-permute-start.10
  24.7 2.1 %pack.4 = (bf16[2,80,768]{2,1,0:T(8,128)(2,1)}, bf16[2,80,768]{2,1,0:T(8,128)(2,1)}, bf16[2,80,768]{2,1,0:T(8,128)(2,1)}) custom-call(s32[1]{0:T(128)} %bitcast.group_ref, bf16[4,6,64,768]{3,2,1,0:T(8,128)(2,1)} %bitcast.12, bf16[4,6,64,768]{3,2,1,0:T(8,128)(2,1)} %bitcast.13, bf16[4,6,64,768]{3,2,1,0:T(8,128)(2,1)} %bitcast.14, ...), custom_call_target="tpu_custom_call" | custom-call | bytes 1474560 | tf_op jit(solution)/shard_map/pack/pallas_call | solution.py:112
  28.1 3.0 %collective-permute-start.4 = (bf16[2,80,768]{2,1,0:T(8,128)(2,1)}, bf16[2,80,768]{2,1,0:T(8,128)(2,1)S(1)}, u32[]{:S(2)}, u32[]{:S(2)}) collective-permute-start(bf16[2,80,768]{2,1,0:T(8,128)(2,1)} %get-tuple-element.76), channel_id=1, source_target_pairs={{0,8},{1,9},{2,10},{3,11},{4,12},{5,13},{6,14},{7,15},{8,0},{9,1},... | collective-permute-start | bytes 737288 | tf_op jit(solution)/shard_map/ppermute | solution.py:450
  33.2 5.8 %collective-permute-done.11.refs_3_ = bf16[528,128]{1,0:T(8,128)(2,1)S(1)} collective-permute-done((bf16[528,128]{1,0:T(8,128)(2,1)S(1)}, bf16[528,128]{1,0:T(8,128)(2,1)S(1)}, u32[]{:S(2)}, u32[]{:S(2)}) %collective-permute-start.11) | collective-permute-done | bytes 135200 | tf_op jit(solution)/shard_map/ppermute | solution.py:450
  40.6 8.1 %collective-permute-done.4.refs_1_ = bf16[2,80,768]{2,1,0:T(8,128)(2,1)S(1)} collective-permute-done((bf16[2,80,768]{2,1,0:T(8,128)(2,1)}, bf16[2,80,768]{2,1,0:T(8,128)(2,1)S(1)}, u32[]{:S(2)}, u32[]{:S(2)}) %collective-permute-start.4) | collective-permute-done | bytes 245792 | tf_op jit(solution)/shard_map/ppermute | solution.py:450
  48.7 7.0 %collective-permute-start.19 = (bf16[2,80,768]{2,1,0:T(8,128)(2,1)S(1)}, bf16[2,80,768]{2,1,0:T(8,128)(2,1)S(1)}, u32[]{:S(2)}, u32[]{:S(2)}) collective-permute-start(bf16[2,80,768]{2,1,0:T(8,128)(2,1)S(1)} %get-tuple-element.92), channel_id=1, source_target_pairs={{0,8},{1,9},{2,10},{3,11},{4,12},{5,13},{6,14},{7,15},{8,0},{9,1},... | collective-permute-start | bytes 737288 | tf_op jit(solution)/shard_map/ppermute | solution.py:450
  58.0 35.0 %collective-permute-done.19.refs_1_ = bf16[2,80,768]{2,1,0:T(8,128)(2,1)S(1)} collective-permute-done((bf16[2,80,768]{2,1,0:T(8,128)(2,1)S(1)}, bf16[2,80,768]{2,1,0:T(8,128)(2,1)S(1)}, u32[]{:S(2)}, u32[]{:S(2)}) %collective-permute-start.19) | collective-permute-done | bytes 245792 | tf_op jit(solution)/shard_map/ppermute | solution.py:450
  97.7 14.6 %collective-permute-done.refs_1_ = bf16[6,80,768]{2,1,0:T(8,128)(2,1)S(1)} collective-permute-done((bf16[6,80,768]{2,1,0:T(8,128)(2,1)S(1)}, bf16[6,80,768]{2,1,0:T(8,128)(2,1)S(1)}, u32[]{:S(2)}, u32[]{:S(2)}) %collective-permute-start) | collective-permute-done | bytes 737312 | tf_op jit(solution)/shard_map/ppermute | solution.py:450
  112.3 15.9 %collective-permute-done.6.refs_5_ = bf16[3,2,80,768]{3,2,1,0:T(8,128)(2,1)} collective-permute-done((bf16[3,2,80,768]{3,2,1,0:T(8,128)(2,1)}, bf16[3,2,80,768]{3,2,1,0:T(8,128)(2,1)}, u32[]{:S(2)}, u32[]{:S(2)}) %collective-permute-start.6) | collective-permute-done | bytes 737312 | tf_op jit(solution)/shard_map/ppermute | solution.py:450
  128.9 12.2 %collective-permute-done.21.refs_5_ = bf16[3,2,80,768]{3,2,1,0:T(8,128)(2,1)} collective-permute-done((bf16[3,2,80,768]{3,2,1,0:T(8,128)(2,1)}, bf16[3,2,80,768]{3,2,1,0:T(8,128)(2,1)}, u32[]{:S(2)}, u32[]{:S(2)}) %collective-permute-start.21) | collective-permute-done | bytes 737312 | tf_op jit(solution)/shard_map/ppermute | solution.py:450
  141.0 1.6 constant_dynamic-slice_fusion
  144.0 4.1 %bias_order.1 = (f32[4,256,1024]{2,1,0:T(8,128)S(1)}, f32[8,1024]{1,0:T(8,128)S(1)}) custom-call(s32[1]{0:T(128)} %bitcast.4.me_ref, s32[16]{0:T(128)S(1)} %copy-done.20, s32[16]{0:T(128)S(1)} %broadcast_xor_fusion.qsel_ref, bf16[4,528,128]{2,1,0:T(8,128)(2,1)S(1)} %copy-done.8, bf16[4,528,128]{2,1,0:T(8,128)(2,1)S(1)} %copy-done.12, ...), custom_call_target="tpu_custom_call" | custom-call | flops 8388608 | bytes 6291456 | tf_op jit(solution)/shard_map/bias_order/pallas_call | solution.py:205
  148.7 4.4 %heads.4 = (bf16[2,256,192]{2,1,0:T(8,128)(2,1)S(1)}, bf16[2,192,1024]{2,1,0:T(8,128)(2,1)S(1)}, bf16[2,1024,192]{2,1,0:T(8,128)(2,1)S(1)}, f32[2,64,768]{2,1,0:T(8,128)S(1)}) custom-call(bf16[6,80,768]{2,1,0:T(8,128)(2,1)S(1)} %pack.3.refs_0_, bf16[6,80,768]{2,1,0:T(8,128)(2,1)S(1)} %collective-permute-done.refs_1_, ...), custom_call_target="tpu_custom_call" | custom-call | flops 1207959552 | bytes 4718592 | tf_op jit(solution)/shard_map/heads/pallas_call | solution.py:274
  153.1 5.0 %attend.4 = (bf16[2,64,192]{2,1,0:T(8,128)(2,1)S(1)}, bf16[2,64,192]{2,1,0:T(8,128)(2,1)S(1)}, bf16[2,64,192]{2,1,0:T(8,128)(2,1)S(1)}, bf16[2,64,192]{2,1,0:T(8,128)(2,1)S(1)}) custom-call(bf16[2,256,192]{2,1,0:T(8,128)(2,1)S(1)} %get-tuple-element.78.q_ref, bf16[2,192,1024]{2,1,0:T(8,128)(2,1)S(1)} %get-tuple-element.79.k_ref, ...), custom_call_target="tpu_custom_call" | custom-call | flops 2147483648 | bytes 5767168 | tf_op jit(solution)/shard_map/attend/pallas_call | solution.py:320
  160.3 4.2 %heads.5 = (bf16[2,256,192]{2,1,0:T(8,128)(2,1)S(1)}, bf16[2,192,1024]{2,1,0:T(8,128)(2,1)S(1)}, bf16[2,1024,192]{2,1,0:T(8,128)(2,1)S(1)}, f32[2,64,768]{2,1,0:T(8,128)S(1)}) custom-call(bf16[6,80,768]{2,1,0:T(8,128)(2,1)S(1)} %pack.3.refs_0_, bf16[6,80,768]{2,1,0:T(8,128)(2,1)S(1)} %collective-permute-done.refs_1_, ...), custom_call_target="tpu_custom_call" | custom-call | flops 1207959552 | bytes 4718592 | tf_op jit(solution)/shard_map/heads/pallas_call | solution.py:274
  164.5 5.2 %attend.5 = (bf16[2,64,192]{2,1,0:T(8,128)(2,1)S(1)}, bf16[2,64,192]{2,1,0:T(8,128)(2,1)S(1)}, bf16[2,64,192]{2,1,0:T(8,128)(2,1)S(1)}, bf16[2,64,192]{2,1,0:T(8,128)(2,1)S(1)}) custom-call(bf16[2,256,192]{2,1,0:T(8,128)(2,1)S(1)} %get-tuple-element.98.q_ref, bf16[2,192,1024]{2,1,0:T(8,128)(2,1)S(1)} %get-tuple-element.99.k_ref, ...), custom_call_target="tpu_custom_call" | custom-call | flops 2147483648 | bytes 5767168 | tf_op jit(solution)/shard_map/attend/pallas_call | solution.py:320
  169.6 2.4 %heads.6 = (bf16[1,256,192]{2,1,0:T(8,128)(2,1)S(1)}, bf16[1,192,1024]{2,1,0:T(8,128)(2,1)S(1)}, bf16[1,1024,192]{2,1,0:T(8,128)(2,1)S(1)}, f32[1,64,768]{2,1,0:T(8,128)S(1)}) custom-call(bf16[6,80,768]{2,1,0:T(8,128)(2,1)S(1)} %pack.3.refs_0_, bf16[6,80,768]{2,1,0:T(8,128)(2,1)S(1)} %collective-permute-done.refs_1_, ...), custom_call_target="tpu_custom_call" | custom-call | flops 603979776 | bytes 2359296 | tf_op jit(solution)/shard_map/heads/pallas_call | solution.py:274
  172.0 2.5 %attend.6 = (bf16[1,64,192]{2,1,0:T(8,128)(2,1)S(1)}, bf16[1,64,192]{2,1,0:T(8,128)(2,1)S(1)}, bf16[1,64,192]{2,1,0:T(8,128)(2,1)S(1)}, bf16[1,64,192]{2,1,0:T(8,128)(2,1)S(1)}) custom-call(bf16[1,256,192]{2,1,0:T(8,128)(2,1)S(1)} %get-tuple-element.118.q_ref, bf16[1,192,1024]{2,1,0:T(8,128)(2,1)S(1)} %get-tuple-element.119.k_ref, ...), custom_call_target="tpu_custom_call" | custom-call | flops 1073741824 | bytes 4980736 | tf_op jit(solution)/shard_map/attend/pallas_call | solution.py:320
  175.1 1.6 collective-permute-start.38
  176.7 2.4 %heads.7 = (bf16[1,256,192]{2,1,0:T(8,128)(2,1)S(1)}, bf16[1,192,1024]{2,1,0:T(8,128)(2,1)S(1)}, bf16[1,1024,192]{2,1,0:T(8,128)(2,1)S(1)}, f32[1,64,768]{2,1,0:T(8,128)S(1)}) custom-call(bf16[6,80,768]{2,1,0:T(8,128)(2,1)S(1)} %pack.3.refs_0_, bf16[6,80,768]{2,1,0:T(8,128)(2,1)S(1)} %collective-permute-done.refs_1_, ...), custom_call_target="tpu_custom_call" | custom-call | flops 603979776 | bytes 2359296 | tf_op jit(solution)/shard_map/heads/pallas_call | solution.py:274
  179.1 2.5 %attend.7 = (bf16[1,64,192]{2,1,0:T(8,128)(2,1)S(1)}, bf16[1,64,192]{2,1,0:T(8,128)(2,1)S(1)}, bf16[1,64,192]{2,1,0:T(8,128)(2,1)S(1)}, bf16[1,64,192]{2,1,0:T(8,128)(2,1)S(1)}) custom-call(bf16[1,256,192]{2,1,0:T(8,128)(2,1)S(1)} %get-tuple-element.132.q_ref, bf16[1,192,1024]{2,1,0:T(8,128)(2,1)S(1)} %get-tuple-element.133.k_ref, ...), custom_call_target="tpu_custom_call" | custom-call | flops 1073741824 | bytes 4980736 | tf_op jit(solution)/shard_map/attend/pallas_call | solution.py:320
  182.2 1.6 collective-permute-start.47
  183.9 2.0 collective-permute-done.45.refs_5_
  186.1 1.7 collective-permute-start.25
  193.5 2.8 %collective-permute-start.28 = (bf16[4,16,768]{2,1,0:T(8,128)(2,1)S(1)}, bf16[4,16,768]{2,1,0:T(8,128)(2,1)S(1)}, u32[]{:S(2)}, u32[]{:S(2)}) collective-permute-start(bf16[4,16,768]{2,1,0:T(8,128)(2,1)S(1)} %get-tuple-element.109), channel_id=1, source_target_pairs={{0,8},{1,9},{2,10},{3,11},{4,12},{5,13},{6,14},{7,15},{8,0},{9,1},... | collective-permute-start | bytes 294920 | tf_op jit(solution)/shard_map/ppermute | solution.py:450
  198.0 2.1 collective-permute-start.50
  200.1 8.9 %collective-permute-done.49.refs_6_ = bf16[2,16,768]{2,1,0:T(8,128)(2,1)S(1)} collective-permute-done((bf16[2,16,768]{2,1,0:T(8,128)(2,1)S(1)}, bf16[2,16,768]{2,1,0:T(8,128)(2,1)S(1)}, u32[]{:S(2)}, u32[]{:S(2)}) %collective-permute-start.49) | collective-permute-done | bytes 49184 | tf_op jit(solution)/shard_map/ppermute | solution.py:450
  (143 shorter events, 29.2 us)
Async XLA Ops:
  3.1 19.8 %collective-permute-start.30 = (bf16[1,80,768]{2,1,0:T(8,128)(2,1)S(1)}, bf16[1,80,768]{2,1,0:T(8,128)(2,1)S(1)}, u32[]{:S(2)}, u32[]{:S(2)}) collective-permute-start(bf16[1,80,768]{2,1,0:T(8,128)(2,1)S(1)} %get-tuple-element.111), channel_id=1, source_target_pairs={{0,4},{1,5},{2,6},{3,7},{4,0},{5,1},{6,2},{7,3},{8,12},{9,13},{10,... | collective-permute-start | bytes 368648 | tf_op jit(solution)/shard_map/ppermute | solution.py:450
  6.2 16.7 %collective-permute-start.31 = (bf16[1,80,768]{2,1,0:T(8,128)(2,1)S(1)}, bf16[1,80,768]{2,1,0:T(8,128)(2,1)S(1)}, u32[]{:S(2)}, u32[]{:S(2)}) collective-permute-start(bf16[1,80,768]{2,1,0:T(8,128)(2,1)S(1)} %get-tuple-element.112), channel_id=1, source_target_pairs={{0,8},{1,9},{2,10},{3,11},{4,12},{5,13},{6,14},{7,15},{8,0},{9,1},... | collective-permute-start | bytes 368648 | tf_op jit(solution)/shard_map/ppermute | solution.py:450
  8.8 14.2 %collective-permute-start.32 = (bf16[1,80,768]{2,1,0:T(8,128)(2,1)S(1)}, bf16[1,80,768]{2,1,0:T(8,128)(2,1)S(1)}, u32[]{:S(2)}, u32[]{:S(2)}) collective-permute-start(bf16[1,80,768]{2,1,0:T(8,128)(2,1)S(1)} %get-tuple-element.113), channel_id=1, source_target_pairs={{0,12},{1,13},{2,14},{3,15},{4,8},{5,9},{6,10},{7,11},{8,4},{9,5},... | collective-permute-start | bytes 368648 | tf_op jit(solution)/shard_map/ppermute | solution.py:450
  8.8 18.0 %collective-permute-start.39 = (bf16[1,80,768]{2,1,0:T(8,128)(2,1)S(1)}, bf16[1,80,768]{2,1,0:T(8,128)(2,1)S(1)}, u32[]{:S(2)}, u32[]{:S(2)}) collective-permute-start(bf16[1,80,768]{2,1,0:T(8,128)(2,1)S(1)} %get-tuple-element.125), channel_id=1, source_target_pairs={{0,4},{1,5},{2,6},{3,7},{4,0},{5,1},{6,2},{7,3},{8,12},{9,13},{10,... | collective-permute-start | bytes 368648 | tf_op jit(solution)/shard_map/ppermute | solution.py:450
  9.7 18.4 %collective-permute-start.40 = (bf16[1,80,768]{2,1,0:T(8,128)(2,1)S(1)}, bf16[1,80,768]{2,1,0:T(8,128)(2,1)S(1)}, u32[]{:S(2)}, u32[]{:S(2)}) collective-permute-start(bf16[1,80,768]{2,1,0:T(8,128)(2,1)S(1)} %get-tuple-element.126), channel_id=1, source_target_pairs={{0,8},{1,9},{2,10},{3,11},{4,12},{5,13},{6,14},{7,15},{8,0},{9,1},... | collective-permute-start | bytes 368648 | tf_op jit(solution)/shard_map/ppermute | solution.py:450
  26.9 13.7 %collective-permute-start.3 = (bf16[2,80,768]{2,1,0:T(8,128)(2,1)}, bf16[2,80,768]{2,1,0:T(8,128)(2,1)S(1)}, u32[]{:S(2)}, u32[]{:S(2)}) collective-permute-start(bf16[2,80,768]{2,1,0:T(8,128)(2,1)} %get-tuple-element.75), channel_id=1, source_target_pairs={{0,4},{1,5},{2,6},{3,7},{4,0},{5,1},{6,2},{7,3},{8,12},{9,13},{10,... | collective-permute-start | bytes 737288 | tf_op jit(solution)/shard_map/ppermute | solution.py:450
  28.1 20.6 %collective-permute-start.4 = (bf16[2,80,768]{2,1,0:T(8,128)(2,1)}, bf16[2,80,768]{2,1,0:T(8,128)(2,1)S(1)}, u32[]{:S(2)}, u32[]{:S(2)}) collective-permute-start(bf16[2,80,768]{2,1,0:T(8,128)(2,1)} %get-tuple-element.76), channel_id=1, source_target_pairs={{0,8},{1,9},{2,10},{3,11},{4,12},{5,13},{6,14},{7,15},{8,0},{9,1},... | collective-permute-start | bytes 737288 | tf_op jit(solution)/shard_map/ppermute | solution.py:450
  31.7 16.9 %collective-permute-start.5 = (bf16[2,80,768]{2,1,0:T(8,128)(2,1)}, bf16[2,80,768]{2,1,0:T(8,128)(2,1)S(1)}, u32[]{:S(2)}, u32[]{:S(2)}) collective-permute-start(bf16[2,80,768]{2,1,0:T(8,128)(2,1)} %get-tuple-element.77), channel_id=1, source_target_pairs={{0,12},{1,13},{2,14},{3,15},{4,8},{5,9},{6,10},{7,11},{8,4},{9,5},... | collective-permute-start | bytes 737288 | tf_op jit(solution)/shard_map/ppermute | solution.py:450
  32.0 23.7 %collective-permute-start.18 = (bf16[2,80,768]{2,1,0:T(8,128)(2,1)S(1)}, bf16[2,80,768]{2,1,0:T(8,128)(2,1)S(1)}, u32[]{:S(2)}, u32[]{:S(2)}) collective-permute-start(bf16[2,80,768]{2,1,0:T(8,128)(2,1)S(1)} %get-tuple-element.91), channel_id=1, source_target_pairs={{0,4},{1,5},{2,6},{3,7},{4,0},{5,1},{6,2},{7,3},{8,12},{9,13},{10,... | collective-permute-start | bytes 737288 | tf_op jit(solution)/shard_map/ppermute | solution.py:450
  39.0 56.0 %collective-permute-start.33 = (bf16[3,1,80,768]{3,2,1,0:T(8,128)(2,1)S(1)}, bf16[3,1,80,768]{3,2,1,0:T(8,128)(2,1)S(1)}, u32[]{:S(2)}, u32[]{:S(2)}) collective-permute-start(bf16[3,1,80,768]{3,2,1,0:T(8,128)(2,1)S(1)} %stack.8.refs_4_), channel_id=1, source_target_pairs={{0,2},{1,3},{2,0},{3,1},{4,6},{5,7},{6,4},{7,5},{8,10},{9,11},{10,... | collective-permute-start | bytes 1105928 | tf_op jit(solution)/shard_map/ppermute | solution.py:450
  40.6 55.5 %collective-permute-start.12 = (bf16[4,528,128]{2,1,0:T(8,128)(2,1)S(1)}, bf16[4,528,128]{2,1,0:T(8,128)(2,1)S(1)}, u32[]{:S(2)}, u32[]{:S(2)}) collective-permute-start(bf16[4,528,128]{2,1,0:T(8,128)(2,1)S(1)} %stack.6.refs_0_), channel_id=1, source_target_pairs={{0,4},{1,5},{2,6},{3,7},{4,0},{5,1},{6,2},{7,3},{8,12},{9,13},{10,... | collective-permute-start | bytes 1622024 | tf_op jit(solution)/shard_map/ppermute | solution.py:450
  48.7 48.6 %collective-permute-start.13 = (bf16[4,528,128]{2,1,0:T(8,128)(2,1)S(1)}, bf16[4,528,128]{2,1,0:T(8,128)(2,1)}, u32[]{:S(2)}, u32[]{:S(2)}) collective-permute-start(bf16[4,528,128]{2,1,0:T(8,128)(2,1)S(1)} %stack.6.refs_0_), channel_id=1, source_target_pairs={{0,8},{1,9},{2,10},{3,11},{4,12},{5,13},{6,14},{7,15},{8,0},{9,1},... | collective-permute-start | bytes 1622024 | tf_op jit(solution)/shard_map/ppermute | solution.py:450
  48.7 44.3 %collective-permute-start.19 = (bf16[2,80,768]{2,1,0:T(8,128)(2,1)S(1)}, bf16[2,80,768]{2,1,0:T(8,128)(2,1)S(1)}, u32[]{:S(2)}, u32[]{:S(2)}) collective-permute-start(bf16[2,80,768]{2,1,0:T(8,128)(2,1)S(1)} %get-tuple-element.92), channel_id=1, source_target_pairs={{0,8},{1,9},{2,10},{3,11},{4,12},{5,13},{6,14},{7,15},{8,0},{9,1},... | collective-permute-start | bytes 737288 | tf_op jit(solution)/shard_map/ppermute | solution.py:450
  55.6 37.8 %collective-permute-start.20 = (bf16[2,80,768]{2,1,0:T(8,128)(2,1)S(1)}, bf16[2,80,768]{2,1,0:T(8,128)(2,1)S(1)}, u32[]{:S(2)}, u32[]{:S(2)}) collective-permute-start(bf16[2,80,768]{2,1,0:T(8,128)(2,1)S(1)} %get-tuple-element.93), channel_id=1, source_target_pairs={{0,12},{1,13},{2,14},{3,15},{4,8},{5,9},{6,10},{7,11},{8,4},{9,5},... | collective-permute-start | bytes 737288 | tf_op jit(solution)/shard_map/ppermute | solution.py:450
  93.0 19.4 %collective-permute-start = (bf16[6,80,768]{2,1,0:T(8,128)(2,1)S(1)}, bf16[6,80,768]{2,1,0:T(8,128)(2,1)S(1)}, u32[]{:S(2)}, u32[]{:S(2)}) collective-permute-start(bf16[6,80,768]{2,1,0:T(8,128)(2,1)S(1)} %pack.3.refs_0_), channel_id=1, source_target_pairs={{0,2},{1,3},{2,0},{3,1},{4,6},{5,7},{6,4},{7,5},{8,10},{9,11},{10,... | collective-permute-start | bytes 2211848 | tf_op jit(solution)/shard_map/ppermute | solution.py:450
  93.5 34.8 %collective-permute-start.6 = (bf16[3,2,80,768]{3,2,1,0:T(8,128)(2,1)}, bf16[3,2,80,768]{3,2,1,0:T(8,128)(2,1)}, u32[]{:S(2)}, u32[]{:S(2)}) collective-permute-start(bf16[3,2,80,768]{3,2,1,0:T(8,128)(2,1)} %stack.5.refs_4_), channel_id=1, source_target_pairs={{0,2},{1,3},{2,0},{3,1},{4,6},{5,7},{6,4},{7,5},{8,10},{9,11},{10,... | collective-permute-start | bytes 2211848 | tf_op jit(solution)/shard_map/ppermute | solution.py:450
  95.0 33.2 %collective-permute-start.1 = (bf16[6,80,768]{2,1,0:T(8,128)(2,1)S(1)}, bf16[6,80,768]{2,1,0:T(8,128)(2,1)S(1)}, u32[]{:S(2)}, u32[]{:S(2)}) collective-permute-start(bf16[6,80,768]{2,1,0:T(8,128)(2,1)S(1)} %pack.3.refs_0_), channel_id=1, source_target_pairs={{0,1},{1,0},{2,3},{3,2},{4,5},{5,4},{6,7},{7,6},{8,9},{9,8},{10,11... | collective-permute-start | bytes 2211848 | tf_op jit(solution)/shard_map/ppermute | solution.py:450
  96.8 31.5 %collective-permute-start.7 = (bf16[3,2,80,768]{3,2,1,0:T(8,128)(2,1)}, bf16[3,2,80,768]{3,2,1,0:T(8,128)(2,1)}, u32[]{:S(2)}, u32[]{:S(2)}) collective-permute-start(bf16[3,2,80,768]{3,2,1,0:T(8,128)(2,1)} %stack.5.refs_4_), channel_id=1, source_target_pairs={{0,1},{1,0},{2,3},{3,2},{4,5},{5,4},{6,7},{7,6},{8,9},{9,8},{10,11... | collective-permute-start | bytes 2211848 | tf_op jit(solution)/shard_map/ppermute | solution.py:450
  97.2 43.8 %collective-permute-start.21 = (bf16[3,2,80,768]{3,2,1,0:T(8,128)(2,1)}, bf16[3,2,80,768]{3,2,1,0:T(8,128)(2,1)}, u32[]{:S(2)}, u32[]{:S(2)}) collective-permute-start(bf16[3,2,80,768]{3,2,1,0:T(8,128)(2,1)} %stack.7.refs_4_), channel_id=1, source_target_pairs={{0,2},{1,3},{2,0},{3,1},{4,6},{5,7},{6,4},{7,5},{8,10},{9,11},{10,... | collective-permute-start | bytes 2211848 | tf_op jit(solution)/shard_map/ppermute | solution.py:450
  112.3 35.8 %collective-permute-start.2 = (bf16[6,80,768]{2,1,0:T(8,128)(2,1)S(1)}, bf16[6,80,768]{2,1,0:T(8,128)(2,1)}, u32[]{:S(2)}, u32[]{:S(2)}) collective-permute-start(bf16[6,80,768]{2,1,0:T(8,128)(2,1)S(1)} %collective-permute-done.refs_1_), channel_id=1, source_target_pairs={{0,1},{1,0},{2,3},{3,2},{4,5},{5,4},{6,7},{7,6},{8,9},{9,8},{10,11... | collective-permute-start | bytes 2211848 | tf_op jit(solution)/shard_map/ppermute | solution.py:450
  128.2 20.0 %collective-permute-start.8 = (bf16[3,2,80,768]{3,2,1,0:T(8,128)(2,1)}, bf16[3,2,80,768]{3,2,1,0:T(8,128)(2,1)}, u32[]{:S(2)}, u32[]{:S(2)}) collective-permute-start(bf16[3,2,80,768]{3,2,1,0:T(8,128)(2,1)} %collective-permute-done.6.refs_5_), channel_id=1, source_target_pairs={{0,1},{1,0},{2,3},{3,2},{4,5},{5,4},{6,7},{7,6},{8,9},{9,8},{10,11... | collective-permute-start | bytes 2211848 | tf_op jit(solution)/shard_map/ppermute | solution.py:450
  128.2 15.0 %collective-permute-start.14 = (bf16[4,528,128]{2,1,0:T(8,128)(2,1)}, bf16[4,528,128]{2,1,0:T(8,128)(2,1)}, u32[]{:S(2)}, u32[]{:S(2)}) collective-permute-start(bf16[4,528,128]{2,1,0:T(8,128)(2,1)} %collective-permute-done.13.refs_2_), channel_id=1, source_target_pairs={{0,4},{1,5},{2,6},{3,7},{4,0},{5,1},{6,2},{7,3},{8,12},{9,13},{10,... | collective-permute-start | bytes 1622024 | tf_op jit(solution)/shard_map/ppermute | solution.py:450
  128.4 29.9 %collective-permute-start.22 = (bf16[3,2,80,768]{3,2,1,0:T(8,128)(2,1)}, bf16[3,2,80,768]{3,2,1,0:T(8,128)(2,1)S(1)}, u32[]{:S(2)}, u32[]{:S(2)}) collective-permute-start(bf16[3,2,80,768]{3,2,1,0:T(8,128)(2,1)} %stack.7.refs_4_), channel_id=1, source_target_pairs={{0,1},{1,0},{2,3},{3,2},{4,5},{5,4},{6,7},{7,6},{8,9},{9,8},{10,11... | collective-permute-start | bytes 2211848 | tf_op jit(solution)/shard_map/ppermute | solution.py:450
  141.0 17.7 %collective-permute-start.23 = (bf16[3,2,80,768]{3,2,1,0:T(8,128)(2,1)}, bf16[3,2,80,768]{3,2,1,0:T(8,128)(2,1)S(1)}, u32[]{:S(2)}, u32[]{:S(2)}) collective-permute-start(bf16[3,2,80,768]{3,2,1,0:T(8,128)(2,1)} %collective-permute-done.21.refs_5_), channel_id=1, source_target_pairs={{0,1},{1,0},{2,3},{3,2},{4,5},{5,4},{6,7},{7,6},{8,9},{9,8},{10,11... | collective-permute-start | bytes 2211848 | tf_op jit(solution)/shard_map/ppermute | solution.py:450
  143.2 14.9 %collective-permute-start.42 = (bf16[3,1,80,768]{3,2,1,0:T(8,128)(2,1)S(1)}, bf16[3,1,80,768]{3,2,1,0:T(8,128)(2,1)S(1)}, u32[]{:S(2)}, u32[]{:S(2)}) collective-permute-start(bf16[3,1,80,768]{3,2,1,0:T(8,128)(2,1)S(1)} %stack.9.refs_4_), channel_id=1, source_target_pairs={{0,2},{1,3},{2,0},{3,1},{4,6},{5,7},{6,4},{7,5},{8,10},{9,11},{10,... | collective-permute-start | bytes 1105928 | tf_op jit(solution)/shard_map/ppermute | solution.py:450
  148.1 21.5 %collective-permute-start.34 = (bf16[3,1,80,768]{3,2,1,0:T(8,128)(2,1)S(1)}, bf16[3,1,80,768]{3,2,1,0:T(8,128)(2,1)S(1)}, u32[]{:S(2)}, u32[]{:S(2)}) collective-permute-start(bf16[3,1,80,768]{3,2,1,0:T(8,128)(2,1)S(1)} %copy-done.10), channel_id=1, source_target_pairs={{0,1},{1,0},{2,3},{3,2},{4,5},{5,4},{6,7},{7,6},{8,9},{9,8},{10,11... | collective-permute-start | bytes 1105928 | tf_op jit(solution)/shard_map/ppermute | solution.py:450
  148.2 21.4 %collective-permute-start.35 = (bf16[3,1,80,768]{3,2,1,0:T(8,128)(2,1)S(1)}, bf16[3,1,80,768]{3,2,1,0:T(8,128)(2,1)S(1)}, u32[]{:S(2)}, u32[]{:S(2)}) collective-permute-start(bf16[3,1,80,768]{3,2,1,0:T(8,128)(2,1)S(1)} %copy-done.14), channel_id=1, source_target_pairs={{0,1},{1,0},{2,3},{3,2},{4,5},{5,4},{6,7},{7,6},{8,9},{9,8},{10,11... | collective-permute-start | bytes 1105928 | tf_op jit(solution)/shard_map/ppermute | solution.py:450
  158.1 16.9 %collective-permute-start.43 = (bf16[3,1,80,768]{3,2,1,0:T(8,128)(2,1)S(1)}, bf16[3,1,80,768]{3,2,1,0:T(8,128)(2,1)S(1)}, u32[]{:S(2)}, u32[]{:S(2)}) collective-permute-start(bf16[3,1,80,768]{3,2,1,0:T(8,128)(2,1)S(1)} %stack.9.refs_4_), channel_id=1, source_target_pairs={{0,1},{1,0},{2,3},{3,2},{4,5},{5,4},{6,7},{7,6},{8,9},{9,8},{10,11... | collective-permute-start | bytes 1105928 | tf_op jit(solution)/shard_map/ppermute | solution.py:450
  158.3 18.4 %collective-permute-start.44 = (bf16[3,1,80,768]{3,2,1,0:T(8,128)(2,1)S(1)}, bf16[3,1,80,768]{3,2,1,0:T(8,128)(2,1)S(1)}, u32[]{:S(2)}, u32[]{:S(2)}) collective-permute-start(bf16[3,1,80,768]{3,2,1,0:T(8,128)(2,1)S(1)} %collective-permute-done.42.refs_5_), channel_id=1, source_target_pairs={{0,1},{1,0},{2,3},{3,2},{4,5},{5,4},{6,7},{7,6},{8,9},{9,8},{10,11... | collective-permute-start | bytes 1105928 | tf_op jit(solution)/shard_map/ppermute | solution.py:450
  158.7 29.1 %collective-permute-start.15 = (bf16[2,64,192]{2,1,0:T(8,128)(2,1)S(1)}, bf16[2,64,192]{2,1,0:T(8,128)(2,1)S(1)}, u32[]{:S(2)}, u32[]{:S(2)}) collective-permute-start(bf16[2,64,192]{2,1,0:T(8,128)(2,1)S(1)} %get-tuple-element.88), channel_id=1, source_target_pairs={{0,2},{1,3},{2,0},{3,1},{4,6},{5,7},{6,4},{7,5},{8,10},{9,11},{10,... | collective-permute-start | bytes 147464 | tf_op jit(solution)/shard_map/ppermute | solution.py:450
  193.1 15.9 %collective-permute-start.27 = (bf16[4,16,768]{2,1,0:T(8,128)(2,1)S(1)}, bf16[4,16,768]{2,1,0:T(8,128)(2,1)S(1)}, u32[]{:S(2)}, u32[]{:S(2)}) collective-permute-start(bf16[4,16,768]{2,1,0:T(8,128)(2,1)S(1)} %get-tuple-element.108), channel_id=1, source_target_pairs={{0,4},{1,5},{2,6},{3,7},{4,0},{5,1},{6,2},{7,3},{8,12},{9,13},{10,... | collective-permute-start | bytes 294920 | tf_op jit(solution)/shard_map/ppermute | solution.py:450
  193.5 15.6 %collective-permute-start.28 = (bf16[4,16,768]{2,1,0:T(8,128)(2,1)S(1)}, bf16[4,16,768]{2,1,0:T(8,128)(2,1)S(1)}, u32[]{:S(2)}, u32[]{:S(2)}) collective-permute-start(bf16[4,16,768]{2,1,0:T(8,128)(2,1)S(1)} %get-tuple-element.109), channel_id=1, source_target_pairs={{0,8},{1,9},{2,10},{3,11},{4,12},{5,13},{6,14},{7,15},{8,0},{9,1},... | collective-permute-start | bytes 294920 | tf_op jit(solution)/shard_map/ppermute | solution.py:450
  (43 other events, 668.3 us)

commit v6 on v5

--- a/solution.py
+++ b/solution.py
@@ -409,10 +409,9 @@
 
 
 def chunk_sizes(group_samples):
-    if group_samples < 4:
-        return [1] * group_samples
-    first = group_samples - 2
-    return [first - first // 2, first // 2, 1, 1]
+    last = max(group_samples // 6, 1)
+    middle = max(group_samples // 3, 1)
+    return [group_samples - middle - last, middle, last]
 
 
 def local(

time: 210 us -> 192 us (0.914)
  waiting for transfers between devices: 107 us -> 92.4 us
  starting transfers between devices: 47 us -> 43.8 us
    ppermute x51 -> x42, waiting for transfers between devices: 107 us -> 92.4 us  [across(): return lax.ppermute(x, 'key', [(i, i ^ code) for i in range(n)])]
    ppermute x51 -> x42, starting transfers between devices: 47 us -> 43.8 us  [across(): return lax.ppermute(x, 'key', [(i, i ^ code) for i in range(n)])]
    pallas_call x4 -> x3, Pallas kernels: 13.4 us -> 11.5 us  [projections(): pl.pallas_call(functools.partial(heads_kernel, pieces, direct, keys), gri...]
    pallas_call x4 -> x3, Pallas kernels: 15.1 us -> 14.2 us  [attention(): pl.pallas_call(functools.partial(attention_kernel, hpg, splits), grid=(si...]
    unnamed x48 -> x52, local copies, waits for them, and re-layouts: 4.37 us -> 3.96 us
  transfers between devices with their start and end apart: 51 -> 42, of which waited for: 13 -> 14; matrix products, arithmetic and copies ran while one was open for 1% -> 1% of each run, Pallas kernels for 23% -> 22%
where the time goes in v6:
time: 192 us
  waiting for transfers between devices  92.4 us (48%)
  Pallas kernels  48.9 us (25%)
  starting transfers between devices  43.8 us (23%)
  local copies, waits for them, and re-layouts  5.8 us (3%)
    ppermute x42, waiting for transfers between devices, across(): return lax.ppermute(x, 'key', [(i, i ^ code) for i in range(n)])  92.4 us
    ppermute x42, starting transfers between devices, across(): return lax.ppermute(x, 'key', [(i, i ^ code) for i in range(n)])  43.8 us
    pallas_call x3, Pallas kernels, attention(): pl.pallas_call(functools.partial(attention_kernel, hpg, splits), grid=(si...  14.2 us
    pallas_call x3, Pallas kernels, projections(): pl.pallas_call(functools.partial(heads_kernel, pieces, direct, keys), gri...  11.5 us
    pallas_call x1, Pallas kernels, local_bias(): pl.pallas_call(functools.partial(bias_kernel, hpg), grid=(rows // tile,),...  9.15 us
    pallas_call x3, Pallas kernels, pack(): pl.pallas_call(functools.partial(pack_kernel, sizes, count), grid_spec=pl...  4.4 us
    pallas_call x1, Pallas kernels, ordered_bias(): pl.pallas_call(functools.partial(order_kernel, hpg, keys, codes), in_spec...  4.14 us
    unnamed x52, local copies, waits for them, and re-layouts  3.96 us
  transfers between devices with their start and end apart: 42, of which 14 were waited for; matrix products, arithmetic and copies ran while one was open for 1% of the time, Pallas kernels for 22%

profile of v6, /device:TPU:0, one launch (start us, length us, event | category | flops | bytes accessed | tf_op | source)
XLA Modules:
  0.0 191.9 jit_solution(16563233709119105489)
XLA Ops:
  0.0 3.3 %pack.4 = (bf16[3,80,768]{2,1,0:T(8,128)(2,1)}, bf16[3,80,768]{2,1,0:T(8,128)(2,1)}, bf16[3,80,768]{2,1,0:T(8,128)(2,1)}) custom-call(s32[1]{0:T(128)} %bitcast.group_ref, bf16[4,6,64,768]{3,2,1,0:T(8,128)(2,1)} %bitcast.12, bf16[4,6,64,768]{3,2,1,0:T(8,128)(2,1)} %bitcast.13, bf16[4,6,64,768]{3,2,1,0:T(8,128)(2,1)} %bitcast.14, ...), custom_call_target="tpu_custom_call" | custom-call | bytes 2211840 | tf_op jit(solution)/shard_map/pack/pallas_call | solution.py:112
  3.3 3.1 %collective-permute-start.3 = (bf16[3,80,768]{2,1,0:T(8,128)(2,1)}, bf16[3,80,768]{2,1,0:T(8,128)(2,1)S(1)}, u32[]{:S(2)}, u32[]{:S(2)}) collective-permute-start(bf16[3,80,768]{2,1,0:T(8,128)(2,1)} %get-tuple-element.60), channel_id=1, source_target_pairs={{0,4},{1,5},{2,6},{3,7},{4,0},{5,1},{6,2},{7,3},{8,12},{9,13},{10,... | collective-permute-start | bytes 1105928 | tf_op jit(solution)/shard_map/ppermute | solution.py:449
  6.4 2.6 %collective-permute-start.4 = (bf16[3,80,768]{2,1,0:T(8,128)(2,1)}, bf16[3,80,768]{2,1,0:T(8,128)(2,1)S(1)}, u32[]{:S(2)}, u32[]{:S(2)}) collective-permute-start(bf16[3,80,768]{2,1,0:T(8,128)(2,1)} %get-tuple-element.61), channel_id=1, source_target_pairs={{0,8},{1,9},{2,10},{3,11},{4,12},{5,13},{6,14},{7,15},{8,0},{9,1},... | collective-permute-start | bytes 1105928 | tf_op jit(solution)/shard_map/ppermute | solution.py:449
  9.0 13.4 %collective-permute-done.3.refs_0_ = bf16[3,80,768]{2,1,0:T(8,128)(2,1)S(1)} collective-permute-done((bf16[3,80,768]{2,1,0:T(8,128)(2,1)}, bf16[3,80,768]{2,1,0:T(8,128)(2,1)S(1)}, u32[]{:S(2)}, u32[]{:S(2)}) %collective-permute-start.3) | collective-permute-done | bytes 368672 | tf_op jit(solution)/shard_map/ppermute | solution.py:449
  22.4 12.4 %collective-permute-done.4.refs_1_ = bf16[3,80,768]{2,1,0:T(8,128)(2,1)S(1)} collective-permute-done((bf16[3,80,768]{2,1,0:T(8,128)(2,1)}, bf16[3,80,768]{2,1,0:T(8,128)(2,1)S(1)}, u32[]{:S(2)}, u32[]{:S(2)}) %collective-permute-start.4) | collective-permute-done | bytes 368672 | tf_op jit(solution)/shard_map/ppermute | solution.py:449
  40.9 7.1 %collective-permute-start.30 = (bf16[1,80,768]{2,1,0:T(8,128)(2,1)}, bf16[1,80,768]{2,1,0:T(8,128)(2,1)}, u32[]{:S(2)}, u32[]{:S(2)}) collective-permute-start(bf16[1,80,768]{2,1,0:T(8,128)(2,1)} %get-tuple-element.96), channel_id=1, source_target_pairs={{0,4},{1,5},{2,6},{3,7},{4,0},{5,1},{6,2},{7,3},{8,12},{9,13},{10,... | collective-permute-start | bytes 368648 | tf_op jit(solution)/shard_map/ppermute | solution.py:449
  51.0 9.2 %bias_local.1 = (bf16[528,128]{1,0:T(8,128)(2,1)}, bf16[528,128]{1,0:T(8,128)(2,1)}, bf16[528,128]{1,0:T(8,128)(2,1)}, bf16[528,128]{1,0:T(8,128)(2,1)}) custom-call(s32[1]{0:T(128)} %bitcast.1.lane_ref, s32[1,64]{1,0:T(1,128)} %bitcast.28, bf16[2,128,64,128]{3,2,1,0:T(8,128)(2,1)} %bitcast.26, f32[1,128]{1,0:T(1,128)} %bitcast.29, f32[4,4,128]{2,1,0:T(4,128)} %bitcast.27), custom_call_target="tpu_custom_call" | custom-call | flops 1073741824 | bytes 4194304 | tf_op jit(solution)/shard_map/bias_local/pallas_call | solution.py:61
  63.1 1.9 collective-permute-start.19
  65.0 1.9 %collective-permute-done.10.refs_2_ = bf16[528,128]{1,0:T(8,128)(2,1)S(1)} collective-permute-done((bf16[528,128]{1,0:T(8,128)(2,1)}, bf16[528,128]{1,0:T(8,128)(2,1)S(1)}, u32[]{:S(2)}, u32[]{:S(2)}) %collective-permute-start.10) | collective-permute-done | bytes 135200 | tf_op jit(solution)/shard_map/ppermute | solution.py:449
  67.0 2.4 %collective-permute-start.20 = (bf16[2,80,768]{2,1,0:T(8,128)(2,1)S(1)}, bf16[2,80,768]{2,1,0:T(8,128)(2,1)S(1)}, u32[]{:S(2)}, u32[]{:S(2)}) collective-permute-start(bf16[2,80,768]{2,1,0:T(8,128)(2,1)S(1)} %copy-done.19), channel_id=1, source_target_pairs={{0,12},{1,13},{2,14},{3,15},{4,8},{5,9},{6,10},{7,11},{8,4},{9,5},... | collective-permute-start | bytes 737288 | tf_op jit(solution)/shard_map/ppermute | solution.py:449
  71.9 3.3 %collective-permute-done.18.refs_0_ = bf16[2,80,768]{2,1,0:T(8,128)(2,1)S(1)} collective-permute-done((bf16[2,80,768]{2,1,0:T(8,128)(2,1)S(1)}, bf16[2,80,768]{2,1,0:T(8,128)(2,1)S(1)}, u32[]{:S(2)}, u32[]{:S(2)}) %collective-permute-start.18) | collective-permute-done | bytes 245792 | tf_op jit(solution)/shard_map/ppermute | solution.py:449
  75.2 3.1 %collective-permute-start.12 = (bf16[4,528,128]{2,1,0:T(8,128)(2,1)S(1)}, bf16[4,528,128]{2,1,0:T(8,128)(2,1)S(1)}, u32[]{:S(2)}, u32[]{:S(2)}) collective-permute-start(bf16[4,528,128]{2,1,0:T(8,128)(2,1)S(1)} %stack.5.refs_0_), channel_id=1, source_target_pairs={{0,4},{1,5},{2,6},{3,7},{4,0},{5,1},{6,2},{7,3},{8,12},{9,13},{10,... | collective-permute-start | bytes 1622024 | tf_op jit(solution)/shard_map/ppermute | solution.py:449
  78.5 4.7 %collective-permute-done.19.refs_1_ = bf16[2,80,768]{2,1,0:T(8,128)(2,1)S(1)} collective-permute-done((bf16[2,80,768]{2,1,0:T(8,128)(2,1)S(1)}, bf16[2,80,768]{2,1,0:T(8,128)(2,1)S(1)}, u32[]{:S(2)}, u32[]{:S(2)}) %collective-permute-start.19) | collective-permute-done | bytes 245792 | tf_op jit(solution)/shard_map/ppermute | solution.py:449
  84.4 16.1 %collective-permute-done.12.refs_1_ = bf16[4,528,128]{2,1,0:T(8,128)(2,1)S(1)} collective-permute-done((bf16[4,528,128]{2,1,0:T(8,128)(2,1)S(1)}, bf16[4,528,128]{2,1,0:T(8,128)(2,1)S(1)}, u32[]{:S(2)}, u32[]{:S(2)}) %collective-permute-start.12) | collective-permute-done | bytes 540704 | tf_op jit(solution)/shard_map/ppermute | solution.py:449
  102.0 9.2 %collective-permute-done.13.refs_2_ = bf16[4,528,128]{2,1,0:T(8,128)(2,1)} collective-permute-done((bf16[4,528,128]{2,1,0:T(8,128)(2,1)S(1)}, bf16[4,528,128]{2,1,0:T(8,128)(2,1)}, u32[]{:S(2)}, u32[]{:S(2)}) %collective-permute-start.13) | collective-permute-done | bytes 540704 | tf_op jit(solution)/shard_map/ppermute | solution.py:449
  111.8 1.7 constant_dynamic-slice_fusion
  113.5 15.9 %collective-permute-done.21.refs_5_ = bf16[3,2,80,768]{3,2,1,0:T(8,128)(2,1)} collective-permute-done((bf16[3,2,80,768]{3,2,1,0:T(8,128)(2,1)}, bf16[3,2,80,768]{3,2,1,0:T(8,128)(2,1)}, u32[]{:S(2)}, u32[]{:S(2)}) %collective-permute-start.21) | collective-permute-done | bytes 737312 | tf_op jit(solution)/shard_map/ppermute | solution.py:449
  130.1 4.1 %bias_order.1 = (f32[4,256,1024]{2,1,0:T(8,128)S(1)}, f32[8,1024]{1,0:T(8,128)S(1)}) custom-call(s32[1]{0:T(128)} %bitcast.4.me_ref, s32[16]{0:T(128)S(1)} %copy-done.17, s32[16]{0:T(128)S(1)} %broadcast_xor_fusion.qsel_ref, bf16[4,528,128]{2,1,0:T(8,128)(2,1)S(1)} %copy-done.9, bf16[4,528,128]{2,1,0:T(8,128)(2,1)S(1)} %copy-done.13, ...), custom_call_target="tpu_custom_call" | custom-call | flops 8388608 | bytes 6291456 | tf_op jit(solution)/shard_map/bias_order/pallas_call | solution.py:205
  134.9 5.9 %heads.3 = (bf16[3,256,192]{2,1,0:T(8,128)(2,1)S(1)}, bf16[3,192,1024]{2,1,0:T(8,128)(2,1)S(1)}, bf16[3,1024,192]{2,1,0:T(8,128)(2,1)S(1)}, f32[3,64,768]{2,1,0:T(8,128)S(1)}) custom-call(bf16[6,80,768]{2,1,0:T(8,128)(2,1)S(1)} %copy-done.5, bf16[6,80,768]{2,1,0:T(8,128)(2,1)S(1)} %collective-permute-done.refs_1_, ...), custom_call_target="tpu_custom_call" | custom-call | flops 1811939328 | bytes 7077888 | tf_op jit(solution)/shard_map/heads/pallas_call | solution.py:274
  140.8 7.0 %attend.3 = (bf16[3,64,192]{2,1,0:T(8,128)(2,1)S(1)}, bf16[3,64,192]{2,1,0:T(8,128)(2,1)S(1)}, bf16[3,64,192]{2,1,0:T(8,128)(2,1)S(1)}, bf16[3,64,192]{2,1,0:T(8,128)(2,1)S(1)}) custom-call(bf16[3,256,192]{2,1,0:T(8,128)(2,1)S(1)} %get-tuple-element.63.q_ref, bf16[3,192,1024]{2,1,0:T(8,128)(2,1)S(1)} %get-tuple-element.64.k_ref, ...), custom_call_target="tpu_custom_call" | custom-call | flops 3221225472 | bytes 6553600 | tf_op jit(solution)/shard_map/attend/pallas_call | solution.py:320
  147.8 4.1 %heads.4 = (bf16[2,256,192]{2,1,0:T(8,128)(2,1)S(1)}, bf16[2,192,1024]{2,1,0:T(8,128)(2,1)S(1)}, bf16[2,1024,192]{2,1,0:T(8,128)(2,1)S(1)}, f32[2,64,768]{2,1,0:T(8,128)S(1)}) custom-call(bf16[6,80,768]{2,1,0:T(8,128)(2,1)S(1)} %copy-done.5, bf16[6,80,768]{2,1,0:T(8,128)(2,1)S(1)} %collective-permute-done.refs_1_, ...), custom_call_target="tpu_custom_call" | custom-call | flops 1207959552 | bytes 4718592 | tf_op jit(solution)/shard_map/heads/pallas_call | solution.py:274
  152.0 4.9 %attend.4 = (bf16[2,64,192]{2,1,0:T(8,128)(2,1)S(1)}, bf16[2,64,192]{2,1,0:T(8,128)(2,1)S(1)}, bf16[2,64,192]{2,1,0:T(8,128)(2,1)S(1)}, bf16[2,64,192]{2,1,0:T(8,128)(2,1)S(1)}) custom-call(bf16[2,256,192]{2,1,0:T(8,128)(2,1)S(1)} %get-tuple-element.83.q_ref, bf16[2,192,1024]{2,1,0:T(8,128)(2,1)S(1)} %get-tuple-element.84.k_ref, ...), custom_call_target="tpu_custom_call" | custom-call | flops 2147483648 | bytes 5767168 | tf_op jit(solution)/shard_map/attend/pallas_call | solution.py:320
  160.1 1.8 collective-permute-done.24.refs_5_
  163.4 2.9 %collective-permute-done.26.refs_7_ = bf16[2,64,192]{2,1,0:T(8,128)(2,1)S(1)} collective-permute-done((bf16[2,64,192]{2,1,0:T(8,128)(2,1)S(1)}, bf16[2,64,192]{2,1,0:T(8,128)(2,1)S(1)}, u32[]{:S(2)}, u32[]{:S(2)}) %collective-permute-start.26) | collective-permute-done | bytes 49184 | tf_op jit(solution)/shard_map/ppermute | solution.py:449
  167.1 2.7 %collective-permute-start.28 = (bf16[5,16,768]{2,1,0:T(8,128)(2,1)S(1)}, bf16[5,16,768]{2,1,0:T(8,128)(2,1)S(1)}, u32[]{:S(2)}, u32[]{:S(2)}) collective-permute-start(bf16[5,16,768]{2,1,0:T(8,128)(2,1)S(1)} %get-tuple-element.94), channel_id=1, source_target_pairs={{0,8},{1,9},{2,10},{3,11},{4,12},{5,13},{6,14},{7,15},{8,0},{9,1},... | collective-permute-start | bytes 368648 | tf_op jit(solution)/shard_map/ppermute | solution.py:449
  169.8 1.6 collective-permute-start.29
  171.5 2.3 %attend.5 = (bf16[1,64,192]{2,1,0:T(8,128)(2,1)S(1)}, bf16[1,64,192]{2,1,0:T(8,128)(2,1)S(1)}, bf16[1,64,192]{2,1,0:T(8,128)(2,1)S(1)}, bf16[1,64,192]{2,1,0:T(8,128)(2,1)S(1)}) custom-call(bf16[1,256,192]{2,1,0:T(8,128)(2,1)S(1)} %get-tuple-element.103.q_ref, bf16[1,192,1024]{2,1,0:T(8,128)(2,1)S(1)} %get-tuple-element.104.k_ref, ...), custom_call_target="tpu_custom_call" | custom-call | flops 1073741824 | bytes 4980736 | tf_op jit(solution)/shard_map/attend/pallas_call | solution.py:320
  174.9 2.9 %collective-permute-done.36.refs_1_ = bf16[1,64,192]{2,1,0:T(8,128)(2,1)S(1)} collective-permute-done((bf16[1,64,192]{2,1,0:T(8,128)(2,1)S(1)}, bf16[1,64,192]{2,1,0:T(8,128)(2,1)S(1)}, u32[]{:S(2)}, u32[]{:S(2)}) %collective-permute-start.36) | collective-permute-done | bytes 24608 | tf_op jit(solution)/shard_map/ppermute | solution.py:449
  177.8 3.3 %collective-permute-done.38.refs_3_ = bf16[1,64,192]{2,1,0:T(8,128)(2,1)S(1)} collective-permute-done((bf16[1,64,192]{2,1,0:T(8,128)(2,1)S(1)}, bf16[1,64,192]{2,1,0:T(8,128)(2,1)S(1)}, u32[]{:S(2)}, u32[]{:S(2)}) %collective-permute-start.38) | collective-permute-done | bytes 24608 | tf_op jit(solution)/shard_map/ppermute | solution.py:449
  181.6 2.7 %collective-permute-start.40 = (bf16[1,16,768]{2,1,0:T(8,128)(2,1)S(1)}, bf16[1,16,768]{2,1,0:T(8,128)(2,1)S(1)}, u32[]{:S(2)}, u32[]{:S(2)}) collective-permute-start(bf16[1,16,768]{2,1,0:T(8,128)(2,1)S(1)} %get-tuple-element.113), channel_id=1, source_target_pairs={{0,8},{1,9},{2,10},{3,11},{4,12},{5,13},{6,14},{7,15},{8,0},{9,1},... | collective-permute-start | bytes 73736 | tf_op jit(solution)/shard_map/ppermute | solution.py:449
  185.4 2.2 %collective-permute-start.41 = (bf16[1,16,768]{2,1,0:T(8,128)(2,1)S(1)}, bf16[1,16,768]{2,1,0:T(8,128)(2,1)S(1)}, u32[]{:S(2)}, u32[]{:S(2)}) collective-permute-start(bf16[1,16,768]{2,1,0:T(8,128)(2,1)S(1)} %get-tuple-element.114), channel_id=1, source_target_pairs={{0,12},{1,13},{2,14},{3,15},{4,8},{5,9},{6,10},{7,11},{8,4},{9,5},... | collective-permute-start | bytes 73736 | tf_op jit(solution)/shard_map/ppermute | solution.py:449
  187.6 3.4 %collective-permute-done.41.refs_7_ = bf16[1,16,768]{2,1,0:T(8,128)(2,1)S(1)} collective-permute-done((bf16[1,16,768]{2,1,0:T(8,128)(2,1)S(1)}, bf16[1,16,768]{2,1,0:T(8,128)(2,1)S(1)}, u32[]{:S(2)}, u32[]{:S(2)}) %collective-permute-start.41) | collective-permute-done | bytes 24608 | tf_op jit(solution)/shard_map/ppermute | solution.py:449
  (126 shorter events, 28.2 us)
Async XLA Ops:
  3.3 19.1 %collective-permute-start.3 = (bf16[3,80,768]{2,1,0:T(8,128)(2,1)}, bf16[3,80,768]{2,1,0:T(8,128)(2,1)S(1)}, u32[]{:S(2)}, u32[]{:S(2)}) collective-permute-start(bf16[3,80,768]{2,1,0:T(8,128)(2,1)} %get-tuple-element.60), channel_id=1, source_target_pairs={{0,4},{1,5},{2,6},{3,7},{4,0},{5,1},{6,2},{7,3},{8,12},{9,13},{10,... | collective-permute-start | bytes 1105928 | tf_op jit(solution)/shard_map/ppermute | solution.py:449
  6.4 28.4 %collective-permute-start.4 = (bf16[3,80,768]{2,1,0:T(8,128)(2,1)}, bf16[3,80,768]{2,1,0:T(8,128)(2,1)S(1)}, u32[]{:S(2)}, u32[]{:S(2)}) collective-permute-start(bf16[3,80,768]{2,1,0:T(8,128)(2,1)} %get-tuple-element.61), channel_id=1, source_target_pairs={{0,8},{1,9},{2,10},{3,11},{4,12},{5,13},{6,14},{7,15},{8,0},{9,1},... | collective-permute-start | bytes 1105928 | tf_op jit(solution)/shard_map/ppermute | solution.py:449
  9.0 25.8 %collective-permute-start.5 = (bf16[3,80,768]{2,1,0:T(8,128)(2,1)}, bf16[3,80,768]{2,1,0:T(8,128)(2,1)S(1)}, u32[]{:S(2)}, u32[]{:S(2)}) collective-permute-start(bf16[3,80,768]{2,1,0:T(8,128)(2,1)} %get-tuple-element.62), channel_id=1, source_target_pairs={{0,12},{1,13},{2,14},{3,15},{4,8},{5,9},{6,10},{7,11},{8,4},{9,5},... | collective-permute-start | bytes 1105928 | tf_op jit(solution)/shard_map/ppermute | solution.py:449
  36.4 64.3 %collective-permute-start.6 = (bf16[3,3,80,768]{3,2,1,0:T(8,128)(2,1)}, bf16[3,3,80,768]{3,2,1,0:T(8,128)(2,1)}, u32[]{:S(2)}, u32[]{:S(2)}) collective-permute-start(bf16[3,3,80,768]{3,2,1,0:T(8,128)(2,1)} %stack.4.refs_4_), channel_id=1, source_target_pairs={{0,2},{1,3},{2,0},{3,1},{4,6},{5,7},{6,4},{7,5},{8,10},{9,11},{10,... | collective-permute-start | bytes 3317768 | tf_op jit(solution)/shard_map/ppermute | solution.py:449
  40.9 19.3 %collective-permute-start.30 = (bf16[1,80,768]{2,1,0:T(8,128)(2,1)}, bf16[1,80,768]{2,1,0:T(8,128)(2,1)}, u32[]{:S(2)}, u32[]{:S(2)}) collective-permute-start(bf16[1,80,768]{2,1,0:T(8,128)(2,1)} %get-tuple-element.96), channel_id=1, source_target_pairs={{0,4},{1,5},{2,6},{3,7},{4,0},{5,1},{6,2},{7,3},{8,12},{9,13},{10,... | collective-permute-start | bytes 368648 | tf_op jit(solution)/shard_map/ppermute | solution.py:449
  48.0 12.8 %collective-permute-start.31 = (bf16[1,80,768]{2,1,0:T(8,128)(2,1)}, bf16[1,80,768]{2,1,0:T(8,128)(2,1)}, u32[]{:S(2)}, u32[]{:S(2)}) collective-permute-start(bf16[1,80,768]{2,1,0:T(8,128)(2,1)} %get-tuple-element.97), channel_id=1, source_target_pairs={{0,8},{1,9},{2,10},{3,11},{4,12},{5,13},{6,14},{7,15},{8,0},{9,1},... | collective-permute-start | bytes 368648 | tf_op jit(solution)/shard_map/ppermute | solution.py:449
  49.0 13.1 %collective-permute-start.32 = (bf16[1,80,768]{2,1,0:T(8,128)(2,1)}, bf16[1,80,768]{2,1,0:T(8,128)(2,1)}, u32[]{:S(2)}, u32[]{:S(2)}) collective-permute-start(bf16[1,80,768]{2,1,0:T(8,128)(2,1)} %get-tuple-element.98), channel_id=1, source_target_pairs={{0,12},{1,13},{2,14},{3,15},{4,8},{5,9},{6,10},{7,11},{8,4},{9,5},... | collective-permute-start | bytes 368648 | tf_op jit(solution)/shard_map/ppermute | solution.py:449
  60.2 6.7 %collective-permute-start.10 = (bf16[528,128]{1,0:T(8,128)(2,1)}, bf16[528,128]{1,0:T(8,128)(2,1)S(1)}, u32[]{:S(2)}, u32[]{:S(2)}) collective-permute-start(bf16[528,128]{1,0:T(8,128)(2,1)} %get-tuple-element.68), channel_id=1, source_target_pairs={{0,2},{1,3},{2,0},{3,1},{4,6},{5,7},{6,4},{7,5},{8,10},{9,11},{10,... | collective-permute-start | bytes 405512 | tf_op jit(solution)/shard_map/ppermute | solution.py:449
  60.8 9.6 %collective-permute-start.11 = (bf16[528,128]{1,0:T(8,128)(2,1)}, bf16[528,128]{1,0:T(8,128)(2,1)S(1)}, u32[]{:S(2)}, u32[]{:S(2)}) collective-permute-start(bf16[528,128]{1,0:T(8,128)(2,1)} %get-tuple-element.69), channel_id=1, source_target_pairs={{0,3},{1,2},{2,1},{3,0},{4,7},{5,6},{6,5},{7,4},{8,11},{9,10},{10,... | collective-permute-start | bytes 405512 | tf_op jit(solution)/shard_map/ppermute | solution.py:449
  62.1 13.1 %collective-permute-start.18 = (bf16[2,80,768]{2,1,0:T(8,128)(2,1)S(1)}, bf16[2,80,768]{2,1,0:T(8,128)(2,1)S(1)}, u32[]{:S(2)}, u32[]{:S(2)}) collective-permute-start(bf16[2,80,768]{2,1,0:T(8,128)(2,1)S(1)} %copy-done.23), channel_id=1, source_target_pairs={{0,4},{1,5},{2,6},{3,7},{4,0},{5,1},{6,2},{7,3},{8,12},{9,13},{10,... | collective-permute-start | bytes 737288 | tf_op jit(solution)/shard_map/ppermute | solution.py:449
  63.1 20.1 %collective-permute-start.19 = (bf16[2,80,768]{2,1,0:T(8,128)(2,1)S(1)}, bf16[2,80,768]{2,1,0:T(8,128)(2,1)S(1)}, u32[]{:S(2)}, u32[]{:S(2)}) collective-permute-start(bf16[2,80,768]{2,1,0:T(8,128)(2,1)S(1)} %copy-done.21), channel_id=1, source_target_pairs={{0,8},{1,9},{2,10},{3,11},{4,12},{5,13},{6,14},{7,15},{8,0},{9,1},... | collective-permute-start | bytes 737288 | tf_op jit(solution)/shard_map/ppermute | solution.py:449
  67.0 16.2 %collective-permute-start.20 = (bf16[2,80,768]{2,1,0:T(8,128)(2,1)S(1)}, bf16[2,80,768]{2,1,0:T(8,128)(2,1)S(1)}, u32[]{:S(2)}, u32[]{:S(2)}) collective-permute-start(bf16[2,80,768]{2,1,0:T(8,128)(2,1)S(1)} %copy-done.19), channel_id=1, source_target_pairs={{0,12},{1,13},{2,14},{3,15},{4,8},{5,9},{6,10},{7,11},{8,4},{9,5},... | collective-permute-start | bytes 737288 | tf_op jit(solution)/shard_map/ppermute | solution.py:449
  70.4 13.1 %collective-permute-start.33 = (bf16[3,1,80,768]{3,2,1,0:T(8,128)(2,1)S(1)}, bf16[3,1,80,768]{3,2,1,0:T(8,128)(2,1)S(1)}, u32[]{:S(2)}, u32[]{:S(2)}) collective-permute-start(bf16[3,1,80,768]{3,2,1,0:T(8,128)(2,1)S(1)} %stack.7.refs_4_), channel_id=1, source_target_pairs={{0,2},{1,3},{2,0},{3,1},{4,6},{5,7},{6,4},{7,5},{8,10},{9,11},{10,... | collective-permute-start | bytes 1105928 | tf_op jit(solution)/shard_map/ppermute | solution.py:449
  75.2 25.3 %collective-permute-start.12 = (bf16[4,528,128]{2,1,0:T(8,128)(2,1)S(1)}, bf16[4,528,128]{2,1,0:T(8,128)(2,1)S(1)}, u32[]{:S(2)}, u32[]{:S(2)}) collective-permute-start(bf16[4,528,128]{2,1,0:T(8,128)(2,1)S(1)} %stack.5.refs_0_), channel_id=1, source_target_pairs={{0,4},{1,5},{2,6},{3,7},{4,0},{5,1},{6,2},{7,3},{8,12},{9,13},{10,... | collective-permute-start | bytes 1622024 | tf_op jit(solution)/shard_map/ppermute | solution.py:449
  83.2 28.0 %collective-permute-start.13 = (bf16[4,528,128]{2,1,0:T(8,128)(2,1)S(1)}, bf16[4,528,128]{2,1,0:T(8,128)(2,1)}, u32[]{:S(2)}, u32[]{:S(2)}) collective-permute-start(bf16[4,528,128]{2,1,0:T(8,128)(2,1)S(1)} %stack.5.refs_0_), channel_id=1, source_target_pairs={{0,8},{1,9},{2,10},{3,11},{4,12},{5,13},{6,14},{7,15},{8,0},{9,1},... | collective-permute-start | bytes 1622024 | tf_op jit(solution)/shard_map/ppermute | solution.py:449
  83.2 28.5 %collective-permute-start = (bf16[6,80,768]{2,1,0:T(8,128)(2,1)S(1)}, bf16[6,80,768]{2,1,0:T(8,128)(2,1)S(1)}, u32[]{:S(2)}, u32[]{:S(2)}) collective-permute-start(bf16[6,80,768]{2,1,0:T(8,128)(2,1)S(1)} %pack.3.refs_0_), channel_id=1, source_target_pairs={{0,2},{1,3},{2,0},{3,1},{4,6},{5,7},{6,4},{7,5},{8,10},{9,11},{10,... | collective-permute-start | bytes 2211848 | tf_op jit(solution)/shard_map/ppermute | solution.py:449
  83.5 28.2 %collective-permute-start.1 = (bf16[6,80,768]{2,1,0:T(8,128)(2,1)S(1)}, bf16[6,80,768]{2,1,0:T(8,128)(2,1)S(1)}, u32[]{:S(2)}, u32[]{:S(2)}) collective-permute-start(bf16[6,80,768]{2,1,0:T(8,128)(2,1)S(1)} %pack.3.refs_0_), channel_id=1, source_target_pairs={{0,1},{1,0},{2,3},{3,2},{4,5},{5,4},{6,7},{7,6},{8,9},{9,8},{10,11... | collective-permute-start | bytes 2211848 | tf_op jit(solution)/shard_map/ppermute | solution.py:449
  100.5 33.9 %collective-permute-start.7 = (bf16[3,3,80,768]{3,2,1,0:T(8,128)(2,1)}, bf16[3,3,80,768]{3,2,1,0:T(8,128)(2,1)}, u32[]{:S(2)}, u32[]{:S(2)}) collective-permute-start(bf16[3,3,80,768]{3,2,1,0:T(8,128)(2,1)} %stack.4.refs_4_), channel_id=1, source_target_pairs={{0,1},{1,0},{2,3},{3,2},{4,5},{5,4},{6,7},{7,6},{8,9},{9,8},{10,11... | collective-permute-start | bytes 3317768 | tf_op jit(solution)/shard_map/ppermute | solution.py:449
  100.7 34.2 %collective-permute-start.8 = (bf16[3,3,80,768]{3,2,1,0:T(8,128)(2,1)}, bf16[3,3,80,768]{3,2,1,0:T(8,128)(2,1)}, u32[]{:S(2)}, u32[]{:S(2)}) collective-permute-start(bf16[3,3,80,768]{3,2,1,0:T(8,128)(2,1)} %collective-permute-done.6.refs_5_), channel_id=1, source_target_pairs={{0,1},{1,0},{2,3},{3,2},{4,5},{5,4},{6,7},{7,6},{8,9},{9,8},{10,11... | collective-permute-start | bytes 3317768 | tf_op jit(solution)/shard_map/ppermute | solution.py:449
  111.2 18.2 %collective-permute-start.21 = (bf16[3,2,80,768]{3,2,1,0:T(8,128)(2,1)}, bf16[3,2,80,768]{3,2,1,0:T(8,128)(2,1)}, u32[]{:S(2)}, u32[]{:S(2)}) collective-permute-start(bf16[3,2,80,768]{3,2,1,0:T(8,128)(2,1)} %stack.6.refs_4_), channel_id=1, source_target_pairs={{0,2},{1,3},{2,0},{3,1},{4,6},{5,7},{6,4},{7,5},{8,10},{9,11},{10,... | collective-permute-start | bytes 2211848 | tf_op jit(solution)/shard_map/ppermute | solution.py:449
  111.7 17.7 %collective-permute-start.14 = (bf16[4,528,128]{2,1,0:T(8,128)(2,1)}, bf16[4,528,128]{2,1,0:T(8,128)(2,1)}, u32[]{:S(2)}, u32[]{:S(2)}) collective-permute-start(bf16[4,528,128]{2,1,0:T(8,128)(2,1)} %collective-permute-done.13.refs_2_), channel_id=1, source_target_pairs={{0,4},{1,5},{2,6},{3,7},{4,0},{5,1},{6,2},{7,3},{8,12},{9,13},{10,... | collective-permute-start | bytes 1622024 | tf_op jit(solution)/shard_map/ppermute | solution.py:449
  111.7 22.6 %collective-permute-start.2 = (bf16[6,80,768]{2,1,0:T(8,128)(2,1)S(1)}, bf16[6,80,768]{2,1,0:T(8,128)(2,1)S(1)}, u32[]{:S(2)}, u32[]{:S(2)}) collective-permute-start(bf16[6,80,768]{2,1,0:T(8,128)(2,1)S(1)} %collective-permute-done.refs_1_), channel_id=1, source_target_pairs={{0,1},{1,0},{2,3},{3,2},{4,5},{5,4},{6,7},{7,6},{8,9},{9,8},{10,11... | collective-permute-start | bytes 2211848 | tf_op jit(solution)/shard_map/ppermute | solution.py:449
  129.4 18.5 %collective-permute-start.22 = (bf16[3,2,80,768]{3,2,1,0:T(8,128)(2,1)}, bf16[3,2,80,768]{3,2,1,0:T(8,128)(2,1)S(1)}, u32[]{:S(2)}, u32[]{:S(2)}) collective-permute-start(bf16[3,2,80,768]{3,2,1,0:T(8,128)(2,1)} %stack.6.refs_4_), channel_id=1, source_target_pairs={{0,1},{1,0},{2,3},{3,2},{4,5},{5,4},{6,7},{7,6},{8,9},{9,8},{10,11... | collective-permute-start | bytes 2211848 | tf_op jit(solution)/shard_map/ppermute | solution.py:449
  129.4 18.5 %collective-permute-start.23 = (bf16[3,2,80,768]{3,2,1,0:T(8,128)(2,1)}, bf16[3,2,80,768]{3,2,1,0:T(8,128)(2,1)S(1)}, u32[]{:S(2)}, u32[]{:S(2)}) collective-permute-start(bf16[3,2,80,768]{3,2,1,0:T(8,128)(2,1)} %collective-permute-done.21.refs_5_), channel_id=1, source_target_pairs={{0,1},{1,0},{2,3},{3,2},{4,5},{5,4},{6,7},{7,6},{8,9},{9,8},{10,11... | collective-permute-start | bytes 2211848 | tf_op jit(solution)/shard_map/ppermute | solution.py:449
  134.3 24.6 %collective-permute-start.34 = (bf16[3,1,80,768]{3,2,1,0:T(8,128)(2,1)S(1)}, bf16[3,1,80,768]{3,2,1,0:T(8,128)(2,1)S(1)}, u32[]{:S(2)}, u32[]{:S(2)}) collective-permute-start(bf16[3,1,80,768]{3,2,1,0:T(8,128)(2,1)S(1)} %copy-done.11), channel_id=1, source_target_pairs={{0,1},{1,0},{2,3},{3,2},{4,5},{5,4},{6,7},{7,6},{8,9},{9,8},{10,11... | collective-permute-start | bytes 1105928 | tf_op jit(solution)/shard_map/ppermute | solution.py:449
  134.4 25.7 %collective-permute-start.35 = (bf16[3,1,80,768]{3,2,1,0:T(8,128)(2,1)S(1)}, bf16[3,1,80,768]{3,2,1,0:T(8,128)(2,1)S(1)}, u32[]{:S(2)}, u32[]{:S(2)}) collective-permute-start(bf16[3,1,80,768]{3,2,1,0:T(8,128)(2,1)S(1)} %copy-done.15), channel_id=1, source_target_pairs={{0,1},{1,0},{2,3},{3,2},{4,5},{5,4},{6,7},{7,6},{8,9},{9,8},{10,11... | collective-permute-start | bytes 1105928 | tf_op jit(solution)/shard_map/ppermute | solution.py:449
  157.9 8.4 %collective-permute-start.15 = (bf16[3,64,192]{2,1,0:T(8,128)(2,1)S(1)}, bf16[3,64,192]{2,1,0:T(8,128)(2,1)S(1)}, u32[]{:S(2)}, u32[]{:S(2)}) collective-permute-start(bf16[3,64,192]{2,1,0:T(8,128)(2,1)S(1)} %get-tuple-element.73), channel_id=1, source_target_pairs={{0,2},{1,3},{2,0},{3,1},{4,6},{5,7},{6,4},{7,5},{8,10},{9,11},{10,... | collective-permute-start | bytes 221192 | tf_op jit(solution)/shard_map/ppermute | solution.py:449
  158.9 7.3 %collective-permute-start.16 = (bf16[3,64,192]{2,1,0:T(8,128)(2,1)S(1)}, bf16[3,64,192]{2,1,0:T(8,128)(2,1)S(1)}, u32[]{:S(2)}, u32[]{:S(2)}) collective-permute-start(bf16[3,64,192]{2,1,0:T(8,128)(2,1)S(1)} %get-tuple-element.74), channel_id=1, source_target_pairs={{0,1},{1,0},{2,3},{3,2},{4,5},{5,4},{6,7},{7,6},{8,9},{9,8},{10,11... | collective-permute-start | bytes 221192 | tf_op jit(solution)/shard_map/ppermute | solution.py:449
  159.0 7.3 %collective-permute-start.17 = (bf16[3,64,192]{2,1,0:T(8,128)(2,1)S(1)}, bf16[3,64,192]{2,1,0:T(8,128)(2,1)S(1)}, u32[]{:S(2)}, u32[]{:S(2)}) collective-permute-start(bf16[3,64,192]{2,1,0:T(8,128)(2,1)S(1)} %get-tuple-element.75), channel_id=1, source_target_pairs={{0,3},{1,2},{2,1},{3,0},{4,7},{5,6},{6,5},{7,4},{8,11},{9,10},{10,... | collective-permute-start | bytes 221192 | tf_op jit(solution)/shard_map/ppermute | solution.py:449
  167.0 24.0 %collective-permute-start.27 = (bf16[5,16,768]{2,1,0:T(8,128)(2,1)S(1)}, bf16[5,16,768]{2,1,0:T(8,128)(2,1)S(1)}, u32[]{:S(2)}, u32[]{:S(2)}) collective-permute-start(bf16[5,16,768]{2,1,0:T(8,128)(2,1)S(1)} %get-tuple-element.93), channel_id=1, source_target_pairs={{0,4},{1,5},{2,6},{3,7},{4,0},{5,1},{6,2},{7,3},{8,12},{9,13},{10,... | collective-permute-start | bytes 368648 | tf_op jit(solution)/shard_map/ppermute | solution.py:449
  167.1 23.9 %collective-permute-start.28 = (bf16[5,16,768]{2,1,0:T(8,128)(2,1)S(1)}, bf16[5,16,768]{2,1,0:T(8,128)(2,1)S(1)}, u32[]{:S(2)}, u32[]{:S(2)}) collective-permute-start(bf16[5,16,768]{2,1,0:T(8,128)(2,1)S(1)} %get-tuple-element.94), channel_id=1, source_target_pairs={{0,8},{1,9},{2,10},{3,11},{4,12},{5,13},{6,14},{7,15},{8,0},{9,1},... | collective-permute-start | bytes 368648 | tf_op jit(solution)/shard_map/ppermute | solution.py:449
  169.8 21.2 %collective-permute-start.29 = (bf16[5,16,768]{2,1,0:T(8,128)(2,1)S(1)}, bf16[5,16,768]{2,1,0:T(8,128)(2,1)S(1)}, u32[]{:S(2)}, u32[]{:S(2)}) collective-permute-start(bf16[5,16,768]{2,1,0:T(8,128)(2,1)S(1)} %get-tuple-element.95), channel_id=1, source_target_pairs={{0,12},{1,13},{2,14},{3,15},{4,8},{5,9},{6,10},{7,11},{8,4},{9,5},... | collective-permute-start | bytes 368648 | tf_op jit(solution)/shard_map/ppermute | solution.py:449
  (36 other events, 473.8 us)

commit v7 on v4

--- a/solution.py
+++ b/solution.py
@@ -222,7 +222,8 @@
     own_refs, far_refs, refs = refs[:pieces], refs[pieces : 2 * pieces], refs[2 * pieces :]
     if not direct:
         query_ref, refs = refs[0], refs[1:]
-    wq_ref, wk_ref, wv_ref, wg_ref, q_ref, k_ref, v_ref, gate_ref = refs
+    wq_ref, wk_ref, wv_ref, wg_ref = refs[:4]
+    q_ref, k_ref, v_ref, gate_ref = refs[-4:]
     total_rows, width = own_refs[0].shape[1:]
 
     def own_rows(start, stop):
@@ -252,7 +253,7 @@
         gate_ref[...] = jnp.zeros_like(gate_ref)
 
 
-def projections(first, own, far, queries, wq, wk, wv, w_gate, keys, query_rows, window, tokens):
+def projections(first, total, offset, filled, own, far, queries, wq, wk, wv, w_gate, keys, query_rows, window, tokens):
     pieces = len(far)
     others, size, rows, width = far[0].shape
     feats = wq.shape[1]
@@ -267,20 +268,22 @@
         args.append(queries)
     consts = [wq, wk, wv, w_gate]
     shapes = [(window, feats), (feats, tokens), (tokens, feats), (gate_rows, width)]
+    before = len(args) + len(consts)
     return pl.pallas_call(
         functools.partial(heads_kernel, pieces, direct, keys),
         grid=(size,),
-        in_specs=specs + [whole] * len(consts),
-        out_specs=[pl.BlockSpec((1,) + x, lambda s: (s, 0, 0)) for x in shapes],
+        in_specs=specs + [whole] * len(consts) + [pl.BlockSpec(memory_space=pl.ANY)] * len(filled),
+        out_specs=[pl.BlockSpec((1,) + x, lambda s: (offset + s, 0, 0)) for x in shapes],
         out_shape=[
-            jax.ShapeDtypeStruct((size,) + x, F32 if i == 3 else BF16) for i, x in enumerate(shapes)
+            jax.ShapeDtypeStruct((total,) + x, F32 if i == 3 else BF16) for i, x in enumerate(shapes)
         ],
+        input_output_aliases={before + i: i for i in range(len(filled))},
         cost_estimate=pl.CostEstimate(
             flops=4 * size * tokens * width * feats, bytes_accessed=size * tokens * width * 3, transcendentals=0
         ),
         compiler_params=pltpu.CompilerParams(vmem_limit_bytes=(48 if tokens > 2048 else 16) * MIB),
         name="heads",
-    )(*args, *consts)
+    )(*args, *consts, *filled)
 
 
 def attention_kernel(hpg, splits, q_ref, k_ref, v_ref, bias_ref, mask_ref, *out_refs):
@@ -405,8 +408,8 @@
 
 
 def chunk_sizes(group_samples):
-    last = max(group_samples // 3, 1)
-    return [group_samples - last, last]
+    size = max(group_samples // 3, 1)
+    return [group_samples - 2 * size, size, size]
 
 
 def local(
@@ -496,41 +499,48 @@
     wq, wk, wv = own(w_query), own(w_key), own(w_value)
 
     heads, gates = [], []
-    for c, size in enumerate(sizes):
-        far = [stacked(got[c])]
-        far = over_lanes(far)
-        queries = None
-        if not direct:
-            order = jnp.array(slot_of, jnp.int32)[me ^ jnp.arange(n)]
-            mine = [x[None, firsts[c] : firsts[c] + size, keys:] for x in own_tokens]
-            queries = jnp.concatenate(mine + [x[:, :, keys:] for x in far], axis=0)
-            queries = jnp.swapaxes(jnp.take(queries, order, axis=0), 0, 1).reshape(size, window, width)
-        if c:
-            far, previous = lax.optimization_barrier((far, previous))
-        q, k, v, gate = projections(
-            firsts[c], own_tokens, far, queries, wq, wk, wv, w_gate, keys, query_rows, window, n * keys
-        )
+    groups = [[0, 1], [2]]
+    for g, members in enumerate(groups):
+        total = sum(sizes[c] for c in members)
+        filled = ()
+        rows = []
+        for c in members:
+            size = sizes[c]
+            far = [stacked(got[c])]
+            far = over_lanes(far)
+            queries = None
+            if not direct:
+                slots = jnp.array(slot_of, jnp.int32)[me ^ jnp.arange(n)]
+                mine = [x[None, firsts[c] : firsts[c] + size, keys:] for x in own_tokens]
+                queries = jnp.concatenate(mine + [x[:, :, keys:] for x in far], axis=0)
+                queries = jnp.swapaxes(jnp.take(queries, slots, axis=0), 0, 1).reshape(size, window, width)
+                tokens = jnp.concatenate([mine[0], far[0][:, :, keys:]], axis=0)
+                rows.append(jnp.swapaxes(tokens, 0, 1).reshape(size, sg * query_rows, width))
+            if g:
+                far, _ = lax.optimization_barrier((far, heads[-1][0]))
+            offset = firsts[c] - firsts[members[0]]
+            filled = projections(
+                firsts[c], total, offset, filled, own_tokens, far, queries,
+                wq, wk, wv, w_gate, keys, query_rows, window, n * keys,
+            )
+        q, k, v, gate = filled
         splits = (query_rows, (sg - 1) * query_rows) if direct else None
         results = attention(q, k, v, bias, mask, hpg, splits, hg)
-        previous = results[0]
         if not direct:
-            blocks = jnp.take(results[0].reshape(size, n, query_rows, feats), code_list ^ me, axis=1)
+            blocks = jnp.take(results[0].reshape(total, n, query_rows, feats), code_list ^ me, axis=1)
             results = []
             for i in range(hg):
                 start = hg + i * (sg - 1)
                 part = jnp.concatenate([blocks[:, i : i + 1], blocks[:, start : start + sg - 1]], axis=1)
-                results.append(part.reshape(size, sg * query_rows, feats))
-            mine = own_tokens[0][None, firsts[c] : firsts[c] + size, keys:]
-            tokens = jnp.concatenate([mine, far[0][:, :, keys:]], axis=0)
-            tokens = jnp.swapaxes(tokens, 0, 1).reshape(size, sg * query_rows, width)
-            gate = jax.nn.sigmoid(nn_dot(tokens, w_gate))
+                results.append(part.reshape(total, sg * query_rows, feats))
+            gate = jax.nn.sigmoid(nn_dot(jnp.concatenate(rows, axis=0), w_gate))
         heads.append([across(r, m) for r, m in zip(results, labels)])
         gates.append(gate)
     outs = []
-    for span in (slice(0, 1), slice(1, len(sizes))):
-        back = projected(lane, heads[span], gates[span], w_out, labels, sg, query_rows)
+    for g in range(len(groups)):
+        back = projected(lane, heads[g : g + 1], gates[g : g + 1], w_out, labels, sg, query_rows)
         outs.extend(across(x, k * hg) for k, x in enumerate(back))
-    out = assembled(group, outs, [0, sizes[0]], (sg, group_samples, query_rows, width))
+    out = assembled(group, outs, [0, firsts[2]], (sg, group_samples, query_rows, width))
     return out.reshape(samples, query_rows, width)
 
 

time: 228 us -> 222 us (0.974)
  waiting for transfers between devices: 139 us -> 101 us
  starting transfers between devices: 38.8 us -> 66.8 us
  local copies, waits for them, and re-layouts: 5.85 us -> 8.96 us
    ppermute x33 -> x39, waiting for transfers between devices: 139 us -> 101 us  [across(): return lax.ppermute(x, 'key', [(i, i ^ code) for i in range(n)])]
    ppermute x33 -> x39, starting transfers between devices: 38.8 us -> 66.8 us  [across(): return lax.ppermute(x, 'key', [(i, i ^ code) for i in range(n)])]
    unnamed x34 -> x42, local copies, waits for them, and re-layouts: 3.18 us -> 5.57 us
    pallas_call x2 -> x3, Pallas kernels: 11.8 us -> 12.6 us  [projections(): pl.pallas_call(functools.partial(heads_kernel, pieces, direct, keys), gri...]
  transfers between devices with their start and end apart: 33 -> 39, of which waited for: 11 -> 12; matrix products, arithmetic and copies ran while one was open for 1% -> 1% of each run, Pallas kernels for 13% -> 12%
where the time goes in v7:
time: 222 us; the launch traced here: 221 us
  waiting for transfers between devices  101 us (45%)
  starting transfers between devices  66.8 us (30%)
  Pallas kernels  43 us (19%)
  local copies, waits for them, and re-layouts  8.96 us (4%)
    ppermute x39, waiting for transfers between devices, across(): return lax.ppermute(x, 'key', [(i, i ^ code) for i in range(n)])  101 us
    ppermute x39, starting transfers between devices, across(): return lax.ppermute(x, 'key', [(i, i ^ code) for i in range(n)])  66.8 us
    pallas_call x2, Pallas kernels, attention(): pl.pallas_call(functools.partial(attention_kernel, hpg, splits), grid=(si...  14.2 us
    pallas_call x3, Pallas kernels, projections(): pl.pallas_call(functools.partial(heads_kernel, pieces, direct, keys), gri...  12.6 us
    pallas_call x1, Pallas kernels, local_bias(): pl.pallas_call(functools.partial(bias_kernel, hpg), grid=(rows // tile,),...  6.51 us
    unnamed x42, local copies, waits for them, and re-layouts  5.57 us
  transfers between devices with their start and end apart: 39, of which 12 were waited for; matrix products, arithmetic and copies ran while one was open for 1% of the time, Pallas kernels for 12%

profile of v7, /device:TPU:0, one launch (start us, length us, event | category | flops | bytes accessed | tf_op | source)
XLA Modules:
  0.0 221.3 jit_solution(5837455399652590392)
XLA Ops:
  2.4 2.2 copy-done.5
  5.2 6.5 %bias_local.1 = (bf16[528,128]{1,0:T(8,128)(2,1)S(1)}, bf16[528,128]{1,0:T(8,128)(2,1)S(1)}, bf16[528,128]{1,0:T(8,128)(2,1)S(1)}, bf16[528,128]{1,0:T(8,128)(2,1)S(1)}) custom-call(f32[1,128]{1,0:T(1,128)S(1)} %broadcast_in_dim_tile.3.mask_ref, bf16[2,128,64,128]{3,2,1,0:T(8,128)(2,1)S(1)} %bitcast.28, f32[1,128]{1,0:T(1,128)S(1)} %bitcast.29, ...), custom_call_target="tpu_custom_call" | custom-call | flops 1073741824 | bytes 4194304 | tf_op jit(solution)/shard_map/bias_local/pallas_call | solution.py:58
  12.3 2.1 pack.5
  14.4 3.7 %collective-permute-start.10 = (bf16[2,80,768]{2,1,0:T(8,128)(2,1)}, bf16[2,80,768]{2,1,0:T(8,128)(2,1)S(1)}, u32[]{:S(2)}, u32[]{:S(2)}) collective-permute-start(bf16[2,80,768]{2,1,0:T(8,128)(2,1)} %get-tuple-element.56), channel_id=1, source_target_pairs={{0,8},{1,9},{2,10},{3,11},{4,12},{5,13},{6,14},{7,15},{8,0},{9,1},... | collective-permute-start | bytes 737288 | tf_op jit(solution)/shard_map/ppermute | solution.py:447
  21.4 4.3 %collective-permute-done.16.refs_2_ = bf16[528,128]{1,0:T(8,128)(2,1)S(1)} collective-permute-done((bf16[528,128]{1,0:T(8,128)(2,1)S(1)}, bf16[528,128]{1,0:T(8,128)(2,1)S(1)}, u32[]{:S(2)}, u32[]{:S(2)}) %collective-permute-start.16) | collective-permute-done | bytes 135200 | tf_op jit(solution)/shard_map/ppermute | solution.py:447
  26.8 1.9 collective-permute-start.4
  28.9 6.8 %collective-permute-done.10.refs_1_ = bf16[2,80,768]{2,1,0:T(8,128)(2,1)S(1)} collective-permute-done((bf16[2,80,768]{2,1,0:T(8,128)(2,1)}, bf16[2,80,768]{2,1,0:T(8,128)(2,1)S(1)}, u32[]{:S(2)}, u32[]{:S(2)}) %collective-permute-start.10) | collective-permute-done | bytes 245792 | tf_op jit(solution)/shard_map/ppermute | solution.py:447
  35.7 1.8 collective-permute-start
  37.5 3.0 %collective-permute-start.5 = (bf16[2,80,768]{2,1,0:T(8,128)(2,1)S(1)}, bf16[2,80,768]{2,1,0:T(8,128)(2,1)S(1)}, u32[]{:S(2)}, u32[]{:S(2)}) collective-permute-start(bf16[2,80,768]{2,1,0:T(8,128)(2,1)S(1)} %get-tuple-element.54), channel_id=1, source_target_pairs={{0,12},{1,13},{2,14},{3,15},{4,8},{5,9},{6,10},{7,11},{8,4},{9,5},... | collective-permute-start | bytes 737288 | tf_op jit(solution)/shard_map/ppermute | solution.py:447
  40.6 3.9 %collective-permute-start.27 = (bf16[2,80,768]{2,1,0:T(8,128)(2,1)S(1)}, bf16[2,80,768]{2,1,0:T(8,128)(2,1)S(1)}, u32[]{:S(2)}, u32[]{:S(2)}) collective-permute-start(bf16[2,80,768]{2,1,0:T(8,128)(2,1)S(1)} %get-tuple-element.80), channel_id=1, source_target_pairs={{0,4},{1,5},{2,6},{3,7},{4,0},{5,1},{6,2},{7,3},{8,12},{9,13},{10,... | collective-permute-start | bytes 737288 | tf_op jit(solution)/shard_map/ppermute | solution.py:447
  46.4 10.4 %collective-permute-done.4.refs_1_ = bf16[2,80,768]{2,1,0:T(8,128)(2,1)S(1)} collective-permute-done((bf16[2,80,768]{2,1,0:T(8,128)(2,1)S(1)}, bf16[2,80,768]{2,1,0:T(8,128)(2,1)S(1)}, u32[]{:S(2)}, u32[]{:S(2)}) %collective-permute-start.4) | collective-permute-done | bytes 245792 | tf_op jit(solution)/shard_map/ppermute | solution.py:447
  57.6 18.5 %collective-permute-start.28 = (bf16[2,80,768]{2,1,0:T(8,128)(2,1)S(1)}, bf16[2,80,768]{2,1,0:T(8,128)(2,1)S(1)}, u32[]{:S(2)}, u32[]{:S(2)}) collective-permute-start(bf16[2,80,768]{2,1,0:T(8,128)(2,1)S(1)} %get-tuple-element.81), channel_id=1, source_target_pairs={{0,8},{1,9},{2,10},{3,11},{4,12},{5,13},{6,14},{7,15},{8,0},{9,1},... | collective-permute-start | bytes 737288 | tf_op jit(solution)/shard_map/ppermute | solution.py:447
  76.6 24.5 %collective-permute-done.28.refs_1_ = bf16[2,80,768]{2,1,0:T(8,128)(2,1)S(1)} collective-permute-done((bf16[2,80,768]{2,1,0:T(8,128)(2,1)S(1)}, bf16[2,80,768]{2,1,0:T(8,128)(2,1)S(1)}, u32[]{:S(2)}, u32[]{:S(2)}) %collective-permute-start.28) | collective-permute-done | bytes 245792 | tf_op jit(solution)/shard_map/ppermute | solution.py:447
  101.2 1.9 collective-permute-start.12
  107.3 13.4 %collective-permute-done.12.refs_5_ = bf16[3,2,80,768]{3,2,1,0:T(8,128)(2,1)} collective-permute-done((bf16[3,2,80,768]{3,2,1,0:T(8,128)(2,1)S(1)}, bf16[3,2,80,768]{3,2,1,0:T(8,128)(2,1)}, u32[]{:S(2)}, u32[]{:S(2)}) %collective-permute-start.12) | collective-permute-done | bytes 737312 | tf_op jit(solution)/shard_map/ppermute | solution.py:447
  121.7 5.5 %collective-permute-start.20 = (bf16[4,528,128]{2,1,0:T(8,128)(2,1)}, bf16[4,528,128]{2,1,0:T(8,128)(2,1)}, u32[]{:S(2)}, u32[]{:S(2)}) collective-permute-start(bf16[4,528,128]{2,1,0:T(8,128)(2,1)} %collective-permute-done.19.refs_2_), channel_id=1, source_target_pairs={{0,4},{1,5},{2,6},{3,7},{4,0},{5,1},{6,2},{7,3},{8,12},{9,13},{10,... | collective-permute-start | bytes 1622024 | tf_op jit(solution)/shard_map/ppermute | solution.py:447
  127.2 9.3 %collective-permute-done.6.refs_5_ = bf16[3,2,80,768]{3,2,1,0:T(8,128)(2,1)} collective-permute-done((bf16[3,2,80,768]{3,2,1,0:T(8,128)(2,1)}, bf16[3,2,80,768]{3,2,1,0:T(8,128)(2,1)}, u32[]{:S(2)}, u32[]{:S(2)}) %collective-permute-start.6) | collective-permute-done | bytes 737312 | tf_op jit(solution)/shard_map/ppermute | solution.py:447
  136.5 15.3 %collective-permute-done.30.refs_5_ = bf16[3,2,80,768]{3,2,1,0:T(8,128)(2,1)S(1)} collective-permute-done((bf16[3,2,80,768]{3,2,1,0:T(8,128)(2,1)S(1)}, bf16[3,2,80,768]{3,2,1,0:T(8,128)(2,1)S(1)}, u32[]{:S(2)}, u32[]{:S(2)}) %collective-permute-start.30) | collective-permute-done | bytes 737312 | tf_op jit(solution)/shard_map/ppermute | solution.py:447
  152.8 1.7 constant_dynamic-slice_fusion
  155.4 4.1 %bias_order.1 = (f32[4,256,1024]{2,1,0:T(8,128)S(1)}, f32[8,1024]{1,0:T(8,128)S(1)}) custom-call(s32[1]{0:T(128)} %bitcast.4.me_ref, s32[16]{0:T(128)S(1)} %copy-done.18, s32[16]{0:T(128)S(1)} %broadcast_xor_fusion.qsel_ref, bf16[4,528,128]{2,1,0:T(8,128)(2,1)S(1)} %copy-done.11, bf16[4,528,128]{2,1,0:T(8,128)(2,1)S(1)} %copy-done.17, ...), custom_call_target="tpu_custom_call" | custom-call | flops 8388608 | bytes 6291456 | tf_op jit(solution)/shard_map/bias_order/pallas_call | solution.py:201
  159.6 4.2 %heads.3 = (bf16[4,256,192]{2,1,0:T(8,128)(2,1)S(1)}, bf16[4,192,1024]{2,1,0:T(8,128)(2,1)S(1)}, bf16[4,1024,192]{2,1,0:T(8,128)(2,1)S(1)}, f32[4,64,768]{2,1,0:T(8,128)S(1)}) custom-call(bf16[6,80,768]{2,1,0:T(8,128)(2,1)S(1)} %pack.3.refs_0_, bf16[6,80,768]{2,1,0:T(8,128)(2,1)S(1)} %collective-permute-done.refs_1_, ...), custom_call_target="tpu_custom_call" | custom-call | flops 1207959552 | bytes 4718592 | tf_op jit(solution)/shard_map/heads/pallas_call | solution.py:272
  163.9 4.4 %heads.4 = (bf16[4,256,192]{2,1,0:T(8,128)(2,1)S(1)}, bf16[4,192,1024]{2,1,0:T(8,128)(2,1)S(1)}, bf16[4,1024,192]{2,1,0:T(8,128)(2,1)S(1)}, f32[4,64,768]{2,1,0:T(8,128)S(1)}) custom-call(bf16[6,80,768]{2,1,0:T(8,128)(2,1)S(1)} %pack.3.refs_0_, ...), custom_call_target="tpu_custom_call", output_to_operand_aliasing={{0}: (12, {}), {1}: (13, {}), {2}: (14, {}), {3}: (15, {})} | custom-call | flops 1207959552 | bytes 4718592 | tf_op jit(solution)/shard_map/heads/pallas_call | solution.py:272
  168.3 9.3 %attend.2 = (bf16[4,64,192]{2,1,0:T(8,128)(2,1)S(1)}, bf16[4,64,192]{2,1,0:T(8,128)(2,1)S(1)}, bf16[4,64,192]{2,1,0:T(8,128)(2,1)S(1)}, bf16[4,64,192]{2,1,0:T(8,128)(2,1)S(1)}) custom-call(bf16[4,256,192]{2,1,0:T(8,128)(2,1)S(1)} %get-tuple-element.62.q_ref, bf16[4,192,1024]{2,1,0:T(8,128)(2,1)S(1)} %get-tuple-element.63.k_ref, ...), custom_call_target="tpu_custom_call" | custom-call | flops 4294967296 | bytes 7340032 | tf_op jit(solution)/shard_map/attend/pallas_call | solution.py:319
  177.7 3.9 %heads.5 = (bf16[2,256,192]{2,1,0:T(8,128)(2,1)S(1)}, bf16[2,192,1024]{2,1,0:T(8,128)(2,1)S(1)}, bf16[2,1024,192]{2,1,0:T(8,128)(2,1)S(1)}, f32[2,64,768]{2,1,0:T(8,128)S(1)}) custom-call(bf16[6,80,768]{2,1,0:T(8,128)(2,1)S(1)} %pack.3.refs_0_, bf16[6,80,768]{2,1,0:T(8,128)(2,1)S(1)} %collective-permute-done.refs_1_, ...), custom_call_target="tpu_custom_call" | custom-call | flops 1207959552 | bytes 4718592 | tf_op jit(solution)/shard_map/heads/pallas_call | solution.py:272
  181.6 4.9 %attend.3 = (bf16[2,64,192]{2,1,0:T(8,128)(2,1)S(1)}, bf16[2,64,192]{2,1,0:T(8,128)(2,1)S(1)}, bf16[2,64,192]{2,1,0:T(8,128)(2,1)S(1)}, bf16[2,64,192]{2,1,0:T(8,128)(2,1)S(1)}) custom-call(bf16[2,256,192]{2,1,0:T(8,128)(2,1)S(1)} %get-tuple-element.87.q_ref, bf16[2,192,1024]{2,1,0:T(8,128)(2,1)S(1)} %get-tuple-element.88.k_ref, ...), custom_call_target="tpu_custom_call" | custom-call | flops 2147483648 | bytes 5767168 | tf_op jit(solution)/shard_map/attend/pallas_call | solution.py:319
  186.5 1.8 collective-permute-start.33
  188.6 1.8 collective-permute-start.23
  191.7 5.4 %collective-permute-done.35.refs_3_ = bf16[2,64,192]{2,1,0:T(8,128)(2,1)S(1)} collective-permute-done((bf16[2,64,192]{2,1,0:T(8,128)(2,1)S(1)}, bf16[2,64,192]{2,1,0:T(8,128)(2,1)S(1)}, u32[]{:S(2)}, u32[]{:S(2)}) %collective-permute-start.35) | collective-permute-done | bytes 49184 | tf_op jit(solution)/shard_map/ppermute | solution.py:447
  197.6 5.2 %collective-permute-start.36 = (bf16[2,16,768]{2,1,0:T(8,128)(2,1)S(1)}, bf16[2,16,768]{2,1,0:T(8,128)(2,1)S(1)}, u32[]{:S(2)}, u32[]{:S(2)}) collective-permute-start(bf16[2,16,768]{2,1,0:T(8,128)(2,1)S(1)} %get-tuple-element.96), channel_id=1, source_target_pairs={{0,4},{1,5},{2,6},{3,7},{4,0},{5,1},{6,2},{7,3},{8,12},{9,13},{10,... | collective-permute-start | bytes 147464 | tf_op jit(solution)/shard_map/ppermute | solution.py:447
  203.6 4.0 %collective-permute-start.25 = (bf16[4,16,768]{2,1,0:T(8,128)(2,1)S(1)}, bf16[4,16,768]{2,1,0:T(8,128)(2,1)S(1)}, u32[]{:S(2)}, u32[]{:S(2)}) collective-permute-start(bf16[4,16,768]{2,1,0:T(8,128)(2,1)S(1)} %get-tuple-element.78), channel_id=1, source_target_pairs={{0,8},{1,9},{2,10},{3,11},{4,12},{5,13},{6,14},{7,15},{8,0},{9,1},... | collective-permute-start | bytes 294920 | tf_op jit(solution)/shard_map/ppermute | solution.py:447
  209.1 2.3 %collective-permute-start.38 = (bf16[2,16,768]{2,1,0:T(8,128)(2,1)S(1)}, bf16[2,16,768]{2,1,0:T(8,128)(2,1)S(1)}, u32[]{:S(2)}, u32[]{:S(2)}) collective-permute-start(bf16[2,16,768]{2,1,0:T(8,128)(2,1)S(1)} %get-tuple-element.98), channel_id=1, source_target_pairs={{0,12},{1,13},{2,14},{3,15},{4,8},{5,9},{6,10},{7,11},{8,4},{9,5},... | collective-permute-start | bytes 147464 | tf_op jit(solution)/shard_map/ppermute | solution.py:447
  211.4 9.0 %collective-permute-done.37.refs_6_ = bf16[2,16,768]{2,1,0:T(8,128)(2,1)S(1)} collective-permute-done((bf16[2,16,768]{2,1,0:T(8,128)(2,1)S(1)}, bf16[2,16,768]{2,1,0:T(8,128)(2,1)S(1)}, u32[]{:S(2)}, u32[]{:S(2)}) %collective-permute-start.37) | collective-permute-done | bytes 49184 | tf_op jit(solution)/shard_map/ppermute | solution.py:447
  (118 shorter events, 23.6 us)
Async XLA Ops:
  14.4 21.3 %collective-permute-start.10 = (bf16[2,80,768]{2,1,0:T(8,128)(2,1)}, bf16[2,80,768]{2,1,0:T(8,128)(2,1)S(1)}, u32[]{:S(2)}, u32[]{:S(2)}) collective-permute-start(bf16[2,80,768]{2,1,0:T(8,128)(2,1)} %get-tuple-element.56), channel_id=1, source_target_pairs={{0,8},{1,9},{2,10},{3,11},{4,12},{5,13},{6,14},{7,15},{8,0},{9,1},... | collective-permute-start | bytes 737288 | tf_op jit(solution)/shard_map/ppermute | solution.py:447
  18.1 19.4 %collective-permute-start.11 = (bf16[2,80,768]{2,1,0:T(8,128)(2,1)}, bf16[2,80,768]{2,1,0:T(8,128)(2,1)S(1)}, u32[]{:S(2)}, u32[]{:S(2)}) collective-permute-start(bf16[2,80,768]{2,1,0:T(8,128)(2,1)} %get-tuple-element.57), channel_id=1, source_target_pairs={{0,12},{1,13},{2,14},{3,15},{4,8},{5,9},{6,10},{7,11},{8,4},{9,5},... | collective-permute-start | bytes 737288 | tf_op jit(solution)/shard_map/ppermute | solution.py:447
  21.0 19.6 %collective-permute-start.9 = (bf16[2,80,768]{2,1,0:T(8,128)(2,1)}, bf16[2,80,768]{2,1,0:T(8,128)(2,1)S(1)}, u32[]{:S(2)}, u32[]{:S(2)}) collective-permute-start(bf16[2,80,768]{2,1,0:T(8,128)(2,1)} %get-tuple-element.55), channel_id=1, source_target_pairs={{0,4},{1,5},{2,6},{3,7},{4,0},{5,1},{6,2},{7,3},{8,12},{9,13},{10,... | collective-permute-start | bytes 737288 | tf_op jit(solution)/shard_map/ppermute | solution.py:447
  25.7 20.1 %collective-permute-start.3 = (bf16[2,80,768]{2,1,0:T(8,128)(2,1)S(1)}, bf16[2,80,768]{2,1,0:T(8,128)(2,1)S(1)}, u32[]{:S(2)}, u32[]{:S(2)}) collective-permute-start(bf16[2,80,768]{2,1,0:T(8,128)(2,1)S(1)} %get-tuple-element.52), channel_id=1, source_target_pairs={{0,4},{1,5},{2,6},{3,7},{4,0},{5,1},{6,2},{7,3},{8,12},{9,13},{10,... | collective-permute-start | bytes 737288 | tf_op jit(solution)/shard_map/ppermute | solution.py:447
  26.8 30.0 %collective-permute-start.4 = (bf16[2,80,768]{2,1,0:T(8,128)(2,1)S(1)}, bf16[2,80,768]{2,1,0:T(8,128)(2,1)S(1)}, u32[]{:S(2)}, u32[]{:S(2)}) collective-permute-start(bf16[2,80,768]{2,1,0:T(8,128)(2,1)S(1)} %get-tuple-element.53), channel_id=1, source_target_pairs={{0,8},{1,9},{2,10},{3,11},{4,12},{5,13},{6,14},{7,15},{8,0},{9,1},... | collective-permute-start | bytes 737288 | tf_op jit(solution)/shard_map/ppermute | solution.py:447
  35.7 69.9 %collective-permute-start = (bf16[6,80,768]{2,1,0:T(8,128)(2,1)S(1)}, bf16[6,80,768]{2,1,0:T(8,128)(2,1)S(1)}, u32[]{:S(2)}, u32[]{:S(2)}) collective-permute-start(bf16[6,80,768]{2,1,0:T(8,128)(2,1)S(1)} %pack.3.refs_0_), channel_id=1, source_target_pairs={{0,2},{1,3},{2,0},{3,1},{4,6},{5,7},{6,4},{7,5},{8,10},{9,11},{10,... | collective-permute-start | bytes 2211848 | tf_op jit(solution)/shard_map/ppermute | solution.py:447
  37.5 20.0 %collective-permute-start.5 = (bf16[2,80,768]{2,1,0:T(8,128)(2,1)S(1)}, bf16[2,80,768]{2,1,0:T(8,128)(2,1)S(1)}, u32[]{:S(2)}, u32[]{:S(2)}) collective-permute-start(bf16[2,80,768]{2,1,0:T(8,128)(2,1)S(1)} %get-tuple-element.54), channel_id=1, source_target_pairs={{0,12},{1,13},{2,14},{3,15},{4,8},{5,9},{6,10},{7,11},{8,4},{9,5},... | collective-permute-start | bytes 737288 | tf_op jit(solution)/shard_map/ppermute | solution.py:447
  40.6 35.5 %collective-permute-start.27 = (bf16[2,80,768]{2,1,0:T(8,128)(2,1)S(1)}, bf16[2,80,768]{2,1,0:T(8,128)(2,1)S(1)}, u32[]{:S(2)}, u32[]{:S(2)}) collective-permute-start(bf16[2,80,768]{2,1,0:T(8,128)(2,1)S(1)} %get-tuple-element.80), channel_id=1, source_target_pairs={{0,4},{1,5},{2,6},{3,7},{4,0},{5,1},{6,2},{7,3},{8,12},{9,13},{10,... | collective-permute-start | bytes 737288 | tf_op jit(solution)/shard_map/ppermute | solution.py:447
  45.9 57.3 %collective-permute-start.19 = (bf16[4,528,128]{2,1,0:T(8,128)(2,1)S(1)}, bf16[4,528,128]{2,1,0:T(8,128)(2,1)}, u32[]{:S(2)}, u32[]{:S(2)}) collective-permute-start(bf16[4,528,128]{2,1,0:T(8,128)(2,1)S(1)} %stack.6.refs_0_), channel_id=1, source_target_pairs={{0,8},{1,9},{2,10},{3,11},{4,12},{5,13},{6,14},{7,15},{8,0},{9,1},... | collective-permute-start | bytes 1622024 | tf_op jit(solution)/shard_map/ppermute | solution.py:447
  56.8 47.6 %collective-permute-start.18 = (bf16[4,528,128]{2,1,0:T(8,128)(2,1)S(1)}, bf16[4,528,128]{2,1,0:T(8,128)(2,1)S(1)}, u32[]{:S(2)}, u32[]{:S(2)}) collective-permute-start(bf16[4,528,128]{2,1,0:T(8,128)(2,1)S(1)} %stack.6.refs_0_), channel_id=1, source_target_pairs={{0,4},{1,5},{2,6},{3,7},{4,0},{5,1},{6,2},{7,3},{8,12},{9,13},{10,... | collective-permute-start | bytes 1622024 | tf_op jit(solution)/shard_map/ppermute | solution.py:447
  57.6 43.5 %collective-permute-start.28 = (bf16[2,80,768]{2,1,0:T(8,128)(2,1)S(1)}, bf16[2,80,768]{2,1,0:T(8,128)(2,1)S(1)}, u32[]{:S(2)}, u32[]{:S(2)}) collective-permute-start(bf16[2,80,768]{2,1,0:T(8,128)(2,1)S(1)} %get-tuple-element.81), channel_id=1, source_target_pairs={{0,8},{1,9},{2,10},{3,11},{4,12},{5,13},{6,14},{7,15},{8,0},{9,1},... | collective-permute-start | bytes 737288 | tf_op jit(solution)/shard_map/ppermute | solution.py:447
  76.1 25.1 %collective-permute-start.29 = (bf16[2,80,768]{2,1,0:T(8,128)(2,1)S(1)}, bf16[2,80,768]{2,1,0:T(8,128)(2,1)S(1)}, u32[]{:S(2)}, u32[]{:S(2)}) collective-permute-start(bf16[2,80,768]{2,1,0:T(8,128)(2,1)S(1)} %get-tuple-element.82), channel_id=1, source_target_pairs={{0,12},{1,13},{2,14},{3,15},{4,8},{5,9},{6,10},{7,11},{8,4},{9,5},... | collective-permute-start | bytes 737288 | tf_op jit(solution)/shard_map/ppermute | solution.py:447
  101.2 19.5 %collective-permute-start.12 = (bf16[3,2,80,768]{3,2,1,0:T(8,128)(2,1)S(1)}, bf16[3,2,80,768]{3,2,1,0:T(8,128)(2,1)}, u32[]{:S(2)}, u32[]{:S(2)}) collective-permute-start(bf16[3,2,80,768]{3,2,1,0:T(8,128)(2,1)S(1)} %stack.5.refs_4_), channel_id=1, source_target_pairs={{0,2},{1,3},{2,0},{3,1},{4,6},{5,7},{6,4},{7,5},{8,10},{9,11},{10,... | collective-permute-start | bytes 2211848 | tf_op jit(solution)/shard_map/ppermute | solution.py:447
  103.1 17.6 %collective-permute-start.13 = (bf16[3,2,80,768]{3,2,1,0:T(8,128)(2,1)S(1)}, bf16[3,2,80,768]{3,2,1,0:T(8,128)(2,1)S(1)}, u32[]{:S(2)}, u32[]{:S(2)}) collective-permute-start(bf16[3,2,80,768]{3,2,1,0:T(8,128)(2,1)S(1)} %stack.5.refs_4_), channel_id=1, source_target_pairs={{0,1},{1,0},{2,3},{3,2},{4,5},{5,4},{6,7},{7,6},{8,9},{9,8},{10,11... | collective-permute-start | bytes 2211848 | tf_op jit(solution)/shard_map/ppermute | solution.py:447
  105.3 31.3 %collective-permute-start.6 = (bf16[3,2,80,768]{3,2,1,0:T(8,128)(2,1)}, bf16[3,2,80,768]{3,2,1,0:T(8,128)(2,1)}, u32[]{:S(2)}, u32[]{:S(2)}) collective-permute-start(bf16[3,2,80,768]{3,2,1,0:T(8,128)(2,1)} %stack.4.refs_4_), channel_id=1, source_target_pairs={{0,2},{1,3},{2,0},{3,1},{4,6},{5,7},{6,4},{7,5},{8,10},{9,11},{10,... | collective-permute-start | bytes 2211848 | tf_op jit(solution)/shard_map/ppermute | solution.py:447
  105.6 46.2 %collective-permute-start.30 = (bf16[3,2,80,768]{3,2,1,0:T(8,128)(2,1)S(1)}, bf16[3,2,80,768]{3,2,1,0:T(8,128)(2,1)S(1)}, u32[]{:S(2)}, u32[]{:S(2)}) collective-permute-start(bf16[3,2,80,768]{3,2,1,0:T(8,128)(2,1)S(1)} %stack.7.refs_4_), channel_id=1, source_target_pairs={{0,2},{1,3},{2,0},{3,1},{4,6},{5,7},{6,4},{7,5},{8,10},{9,11},{10,... | collective-permute-start | bytes 2211848 | tf_op jit(solution)/shard_map/ppermute | solution.py:447
  107.3 47.8 %collective-permute-start.2 = (bf16[6,80,768]{2,1,0:T(8,128)(2,1)S(1)}, bf16[6,80,768]{2,1,0:T(8,128)(2,1)}, u32[]{:S(2)}, u32[]{:S(2)}) collective-permute-start(bf16[6,80,768]{2,1,0:T(8,128)(2,1)S(1)} %collective-permute-done.refs_1_), channel_id=1, source_target_pairs={{0,1},{1,0},{2,3},{3,2},{4,5},{5,4},{6,7},{7,6},{8,9},{9,8},{10,11... | collective-permute-start | bytes 2211848 | tf_op jit(solution)/shard_map/ppermute | solution.py:447
  120.7 38.9 %collective-permute-start.14 = (bf16[3,2,80,768]{3,2,1,0:T(8,128)(2,1)}, bf16[3,2,80,768]{3,2,1,0:T(8,128)(2,1)}, u32[]{:S(2)}, u32[]{:S(2)}) collective-permute-start(bf16[3,2,80,768]{3,2,1,0:T(8,128)(2,1)} %collective-permute-done.12.refs_5_), channel_id=1, source_target_pairs={{0,1},{1,0},{2,3},{3,2},{4,5},{5,4},{6,7},{7,6},{8,9},{9,8},{10,11... | collective-permute-start | bytes 2211848 | tf_op jit(solution)/shard_map/ppermute | solution.py:447
  121.7 32.9 %collective-permute-start.20 = (bf16[4,528,128]{2,1,0:T(8,128)(2,1)}, bf16[4,528,128]{2,1,0:T(8,128)(2,1)}, u32[]{:S(2)}, u32[]{:S(2)}) collective-permute-start(bf16[4,528,128]{2,1,0:T(8,128)(2,1)} %collective-permute-done.19.refs_2_), channel_id=1, source_target_pairs={{0,4},{1,5},{2,6},{3,7},{4,0},{5,1},{6,2},{7,3},{8,12},{9,13},{10,... | collective-permute-start | bytes 1622024 | tf_op jit(solution)/shard_map/ppermute | solution.py:447
  136.5 27.3 %collective-permute-start.7 = (bf16[3,2,80,768]{3,2,1,0:T(8,128)(2,1)}, bf16[3,2,80,768]{3,2,1,0:T(8,128)(2,1)}, u32[]{:S(2)}, u32[]{:S(2)}) collective-permute-start(bf16[3,2,80,768]{3,2,1,0:T(8,128)(2,1)} %stack.4.refs_4_), channel_id=1, source_target_pairs={{0,1},{1,0},{2,3},{3,2},{4,5},{5,4},{6,7},{7,6},{8,9},{9,8},{10,11... | collective-permute-start | bytes 2211848 | tf_op jit(solution)/shard_map/ppermute | solution.py:447
  152.8 11.1 %collective-permute-start.8 = (bf16[3,2,80,768]{3,2,1,0:T(8,128)(2,1)}, bf16[3,2,80,768]{3,2,1,0:T(8,128)(2,1)}, u32[]{:S(2)}, u32[]{:S(2)}) collective-permute-start(bf16[3,2,80,768]{3,2,1,0:T(8,128)(2,1)} %collective-permute-done.6.refs_5_), channel_id=1, source_target_pairs={{0,1},{1,0},{2,3},{3,2},{4,5},{5,4},{6,7},{7,6},{8,9},{9,8},{10,11... | collective-permute-start | bytes 2211848 | tf_op jit(solution)/shard_map/ppermute | solution.py:447
  154.5 23.1 %collective-permute-start.31 = (bf16[3,2,80,768]{3,2,1,0:T(8,128)(2,1)S(1)}, bf16[3,2,80,768]{3,2,1,0:T(8,128)(2,1)S(1)}, u32[]{:S(2)}, u32[]{:S(2)}) collective-permute-start(bf16[3,2,80,768]{3,2,1,0:T(8,128)(2,1)S(1)} %copy-done.7), channel_id=1, source_target_pairs={{0,1},{1,0},{2,3},{3,2},{4,5},{5,4},{6,7},{7,6},{8,9},{9,8},{10,11... | collective-permute-start | bytes 2211848 | tf_op jit(solution)/shard_map/ppermute | solution.py:447
  155.1 22.6 %collective-permute-start.32 = (bf16[3,2,80,768]{3,2,1,0:T(8,128)(2,1)}, bf16[3,2,80,768]{3,2,1,0:T(8,128)(2,1)S(1)}, u32[]{:S(2)}, u32[]{:S(2)}) collective-permute-start(bf16[3,2,80,768]{3,2,1,0:T(8,128)(2,1)} %copy-done.12), channel_id=1, source_target_pairs={{0,1},{1,0},{2,3},{3,2},{4,5},{5,4},{6,7},{7,6},{8,9},{9,8},{10,11... | collective-permute-start | bytes 2211848 | tf_op jit(solution)/shard_map/ppermute | solution.py:447
  188.3 14.6 %collective-permute-start.21 = (bf16[4,64,192]{2,1,0:T(8,128)(2,1)S(1)}, bf16[4,64,192]{2,1,0:T(8,128)(2,1)S(1)}, u32[]{:S(2)}, u32[]{:S(2)}) collective-permute-start(bf16[4,64,192]{2,1,0:T(8,128)(2,1)S(1)} %get-tuple-element.72), channel_id=1, source_target_pairs={{0,2},{1,3},{2,0},{3,1},{4,6},{5,7},{6,4},{7,5},{8,10},{9,11},{10,... | collective-permute-start | bytes 294920 | tf_op jit(solution)/shard_map/ppermute | solution.py:447
  188.6 14.2 %collective-permute-start.22 = (bf16[4,64,192]{2,1,0:T(8,128)(2,1)S(1)}, bf16[4,64,192]{2,1,0:T(8,128)(2,1)S(1)}, u32[]{:S(2)}, u32[]{:S(2)}) collective-permute-start(bf16[4,64,192]{2,1,0:T(8,128)(2,1)S(1)} %get-tuple-element.73), channel_id=1, source_target_pairs={{0,1},{1,0},{2,3},{3,2},{4,5},{5,4},{6,7},{7,6},{8,9},{9,8},{10,11... | collective-permute-start | bytes 294920 | tf_op jit(solution)/shard_map/ppermute | solution.py:447
  188.6 14.2 %collective-permute-start.23 = (bf16[4,64,192]{2,1,0:T(8,128)(2,1)S(1)}, bf16[4,64,192]{2,1,0:T(8,128)(2,1)S(1)}, u32[]{:S(2)}, u32[]{:S(2)}) collective-permute-start(bf16[4,64,192]{2,1,0:T(8,128)(2,1)S(1)} %get-tuple-element.74), channel_id=1, source_target_pairs={{0,3},{1,2},{2,1},{3,0},{4,7},{5,6},{6,5},{7,4},{8,11},{9,10},{10,... | collective-permute-start | bytes 294920 | tf_op jit(solution)/shard_map/ppermute | solution.py:447
  197.6 11.5 %collective-permute-start.36 = (bf16[2,16,768]{2,1,0:T(8,128)(2,1)S(1)}, bf16[2,16,768]{2,1,0:T(8,128)(2,1)S(1)}, u32[]{:S(2)}, u32[]{:S(2)}) collective-permute-start(bf16[2,16,768]{2,1,0:T(8,128)(2,1)S(1)} %get-tuple-element.96), channel_id=1, source_target_pairs={{0,4},{1,5},{2,6},{3,7},{4,0},{5,1},{6,2},{7,3},{8,12},{9,13},{10,... | collective-permute-start | bytes 147464 | tf_op jit(solution)/shard_map/ppermute | solution.py:447
  203.5 16.9 %collective-permute-start.24 = (bf16[4,16,768]{2,1,0:T(8,128)(2,1)S(1)}, bf16[4,16,768]{2,1,0:T(8,128)(2,1)S(1)}, u32[]{:S(2)}, u32[]{:S(2)}) collective-permute-start(bf16[4,16,768]{2,1,0:T(8,128)(2,1)S(1)} %get-tuple-element.77), channel_id=1, source_target_pairs={{0,4},{1,5},{2,6},{3,7},{4,0},{5,1},{6,2},{7,3},{8,12},{9,13},{10,... | collective-permute-start | bytes 294920 | tf_op jit(solution)/shard_map/ppermute | solution.py:447
  203.6 16.8 %collective-permute-start.25 = (bf16[4,16,768]{2,1,0:T(8,128)(2,1)S(1)}, bf16[4,16,768]{2,1,0:T(8,128)(2,1)S(1)}, u32[]{:S(2)}, u32[]{:S(2)}) collective-permute-start(bf16[4,16,768]{2,1,0:T(8,128)(2,1)S(1)} %get-tuple-element.78), channel_id=1, source_target_pairs={{0,8},{1,9},{2,10},{3,11},{4,12},{5,13},{6,14},{7,15},{8,0},{9,1},... | collective-permute-start | bytes 294920 | tf_op jit(solution)/shard_map/ppermute | solution.py:447
  207.5 12.9 %collective-permute-start.26 = (bf16[4,16,768]{2,1,0:T(8,128)(2,1)S(1)}, bf16[4,16,768]{2,1,0:T(8,128)(2,1)S(1)}, u32[]{:S(2)}, u32[]{:S(2)}) collective-permute-start(bf16[4,16,768]{2,1,0:T(8,128)(2,1)S(1)} %get-tuple-element.79), channel_id=1, source_target_pairs={{0,12},{1,13},{2,14},{3,15},{4,8},{5,9},{6,10},{7,11},{8,4},{9,5},... | collective-permute-start | bytes 294920 | tf_op jit(solution)/shard_map/ppermute | solution.py:447
  207.9 12.5 %collective-permute-start.37 = (bf16[2,16,768]{2,1,0:T(8,128)(2,1)S(1)}, bf16[2,16,768]{2,1,0:T(8,128)(2,1)S(1)}, u32[]{:S(2)}, u32[]{:S(2)}) collective-permute-start(bf16[2,16,768]{2,1,0:T(8,128)(2,1)S(1)} %get-tuple-element.97), channel_id=1, source_target_pairs={{0,8},{1,9},{2,10},{3,11},{4,12},{5,13},{6,14},{7,15},{8,0},{9,1},... | collective-permute-start | bytes 147464 | tf_op jit(solution)/shard_map/ppermute | solution.py:447
  209.1 11.3 %collective-permute-start.38 = (bf16[2,16,768]{2,1,0:T(8,128)(2,1)S(1)}, bf16[2,16,768]{2,1,0:T(8,128)(2,1)S(1)}, u32[]{:S(2)}, u32[]{:S(2)}) collective-permute-start(bf16[2,16,768]{2,1,0:T(8,128)(2,1)S(1)} %get-tuple-element.98), channel_id=1, source_target_pairs={{0,12},{1,13},{2,14},{3,15},{4,8},{5,9},{6,10},{7,11},{8,4},{9,5},... | collective-permute-start | bytes 147464 | tf_op jit(solution)/shard_map/ppermute | solution.py:447
  (28 other events, 381.8 us)

commit v8 on v7

--- a/solution.py
+++ b/solution.py
@@ -291,16 +291,22 @@
     k = k_ref[0] * mask_ref[:1].astype(BF16)
     head_size = q.shape[1] // hpg
     scale = LOG2E / math.sqrt(head_size)
-    owner = lax.broadcasted_iota(jnp.int32, q.shape, 1) // head_size
-    total = None
-    for h in range(hpg):
-        mine = owner == h
-        scores = nn_dot(jnp.where(mine, q, jnp.zeros_like(q)), k)
-        scores = scores * scale + bias_ref[h]
-        weights = jnp.exp2(scores - jnp.max(scores, axis=-1, keepdims=True))
-        norm = 1.0 / jnp.sum(weights, axis=-1, keepdims=True)
-        result = nn_dot((weights * norm).astype(BF16), v_ref[0])
-        total = result if total is None else jnp.where(mine, result, total)
+    tile = min(128, q.shape[0])
+    parts = []
+    for r in range(0, q.shape[0], tile):
+        rows = q[r : r + tile]
+        owner = lax.broadcasted_iota(jnp.int32, rows.shape, 1) // head_size
+        part = None
+        for h in range(hpg):
+            mine = owner == h
+            scores = nn_dot(jnp.where(mine, rows, jnp.zeros_like(rows)), k)
+            scores = scores * scale + bias_ref[h, r : r + tile]
+            weights = jnp.exp2(scores - jnp.max(scores, axis=-1, keepdims=True))
+            norm = 1.0 / jnp.sum(weights, axis=-1, keepdims=True)
+            result = nn_dot(weights.astype(BF16), v_ref[0]) * norm
+            part = result if part is None else jnp.where(mine, result, part)
+        parts.append(part)
+    total = jnp.concatenate(parts, axis=0)
     total = total.astype(BF16)
     if splits is None:
         out_refs[0][0] = total

time: 222 us -> 219 us (0.986)
  no operation moved by 1% of the time
where the time goes in v8:
time: 219 us
  waiting for transfers between devices  101 us (46%)
  starting transfers between devices  66.7 us (30%)
  Pallas kernels  40.9 us (19%)
  local copies, waits for them, and re-layouts  8.96 us (4%)
    ppermute x39, waiting for transfers between devices, across(): return lax.ppermute(x, 'key', [(i, i ^ code) for i in range(n)])  101 us
    ppermute x39, starting transfers between devices, across(): return lax.ppermute(x, 'key', [(i, i ^ code) for i in range(n)])  66.7 us
    pallas_call x3, Pallas kernels, projections(): pl.pallas_call(functools.partial(heads_kernel, pieces, direct, keys), gri...  12.6 us
    pallas_call x2, Pallas kernels, attention(): pl.pallas_call(functools.partial(attention_kernel, hpg, splits), grid=(si...  12.1 us
    pallas_call x1, Pallas kernels, local_bias(): pl.pallas_call(functools.partial(bias_kernel, hpg), grid=(rows // tile,),...  6.51 us
    unnamed x42, local copies, waits for them, and re-layouts  5.57 us
  transfers between devices with their start and end apart: 39, of which 12 were waited for; matrix products, arithmetic and copies ran while one was open for 1% of the time, Pallas kernels for 12%

profile of v8, /device:TPU:0, one launch (start us, length us, event | category | flops | bytes accessed | tf_op | source)
XLA Modules:
  0.0 219.1 jit_solution(16117426602488459310)
XLA Ops:
  2.4 2.2 copy-done.5
  5.2 6.5 %bias_local.1 = (bf16[528,128]{1,0:T(8,128)(2,1)S(1)}, bf16[528,128]{1,0:T(8,128)(2,1)S(1)}, bf16[528,128]{1,0:T(8,128)(2,1)S(1)}, bf16[528,128]{1,0:T(8,128)(2,1)S(1)}) custom-call(f32[1,128]{1,0:T(1,128)S(1)} %broadcast_in_dim_tile.3.mask_ref, bf16[2,128,64,128]{3,2,1,0:T(8,128)(2,1)S(1)} %bitcast.28, f32[1,128]{1,0:T(1,128)S(1)} %bitcast.29, ...), custom_call_target="tpu_custom_call" | custom-call | flops 1073741824 | bytes 4194304 | tf_op jit(solution)/shard_map/bias_local/pallas_call | solution.py:58
  12.3 2.1 pack.5
  14.4 3.7 %collective-permute-start.10 = (bf16[2,80,768]{2,1,0:T(8,128)(2,1)}, bf16[2,80,768]{2,1,0:T(8,128)(2,1)S(1)}, u32[]{:S(2)}, u32[]{:S(2)}) collective-permute-start(bf16[2,80,768]{2,1,0:T(8,128)(2,1)} %get-tuple-element.56), channel_id=1, source_target_pairs={{0,8},{1,9},{2,10},{3,11},{4,12},{5,13},{6,14},{7,15},{8,0},{9,1},... | collective-permute-start | bytes 737288 | tf_op jit(solution)/shard_map/ppermute | solution.py:453
  21.4 4.3 %collective-permute-done.16.refs_2_ = bf16[528,128]{1,0:T(8,128)(2,1)S(1)} collective-permute-done((bf16[528,128]{1,0:T(8,128)(2,1)S(1)}, bf16[528,128]{1,0:T(8,128)(2,1)S(1)}, u32[]{:S(2)}, u32[]{:S(2)}) %collective-permute-start.16) | collective-permute-done | bytes 135200 | tf_op jit(solution)/shard_map/ppermute | solution.py:453
  26.8 1.9 collective-permute-start.4
  28.9 6.8 %collective-permute-done.10.refs_1_ = bf16[2,80,768]{2,1,0:T(8,128)(2,1)S(1)} collective-permute-done((bf16[2,80,768]{2,1,0:T(8,128)(2,1)}, bf16[2,80,768]{2,1,0:T(8,128)(2,1)S(1)}, u32[]{:S(2)}, u32[]{:S(2)}) %collective-permute-start.10) | collective-permute-done | bytes 245792 | tf_op jit(solution)/shard_map/ppermute | solution.py:453
  35.7 1.8 collective-permute-start
  37.5 3.0 %collective-permute-start.5 = (bf16[2,80,768]{2,1,0:T(8,128)(2,1)S(1)}, bf16[2,80,768]{2,1,0:T(8,128)(2,1)S(1)}, u32[]{:S(2)}, u32[]{:S(2)}) collective-permute-start(bf16[2,80,768]{2,1,0:T(8,128)(2,1)S(1)} %get-tuple-element.54), channel_id=1, source_target_pairs={{0,12},{1,13},{2,14},{3,15},{4,8},{5,9},{6,10},{7,11},{8,4},{9,5},... | collective-permute-start | bytes 737288 | tf_op jit(solution)/shard_map/ppermute | solution.py:453
  40.6 3.9 %collective-permute-start.27 = (bf16[2,80,768]{2,1,0:T(8,128)(2,1)S(1)}, bf16[2,80,768]{2,1,0:T(8,128)(2,1)S(1)}, u32[]{:S(2)}, u32[]{:S(2)}) collective-permute-start(bf16[2,80,768]{2,1,0:T(8,128)(2,1)S(1)} %get-tuple-element.80), channel_id=1, source_target_pairs={{0,4},{1,5},{2,6},{3,7},{4,0},{5,1},{6,2},{7,3},{8,12},{9,13},{10,... | collective-permute-start | bytes 737288 | tf_op jit(solution)/shard_map/ppermute | solution.py:453
  46.4 10.4 %collective-permute-done.4.refs_1_ = bf16[2,80,768]{2,1,0:T(8,128)(2,1)S(1)} collective-permute-done((bf16[2,80,768]{2,1,0:T(8,128)(2,1)S(1)}, bf16[2,80,768]{2,1,0:T(8,128)(2,1)S(1)}, u32[]{:S(2)}, u32[]{:S(2)}) %collective-permute-start.4) | collective-permute-done | bytes 245792 | tf_op jit(solution)/shard_map/ppermute | solution.py:453
  57.6 18.5 %collective-permute-start.28 = (bf16[2,80,768]{2,1,0:T(8,128)(2,1)S(1)}, bf16[2,80,768]{2,1,0:T(8,128)(2,1)S(1)}, u32[]{:S(2)}, u32[]{:S(2)}) collective-permute-start(bf16[2,80,768]{2,1,0:T(8,128)(2,1)S(1)} %get-tuple-element.81), channel_id=1, source_target_pairs={{0,8},{1,9},{2,10},{3,11},{4,12},{5,13},{6,14},{7,15},{8,0},{9,1},... | collective-permute-start | bytes 737288 | tf_op jit(solution)/shard_map/ppermute | solution.py:453
  76.6 24.5 %collective-permute-done.28.refs_1_ = bf16[2,80,768]{2,1,0:T(8,128)(2,1)S(1)} collective-permute-done((bf16[2,80,768]{2,1,0:T(8,128)(2,1)S(1)}, bf16[2,80,768]{2,1,0:T(8,128)(2,1)S(1)}, u32[]{:S(2)}, u32[]{:S(2)}) %collective-permute-start.28) | collective-permute-done | bytes 245792 | tf_op jit(solution)/shard_map/ppermute | solution.py:453
  101.2 1.9 collective-permute-start.12
  107.3 13.4 %collective-permute-done.12.refs_5_ = bf16[3,2,80,768]{3,2,1,0:T(8,128)(2,1)} collective-permute-done((bf16[3,2,80,768]{3,2,1,0:T(8,128)(2,1)S(1)}, bf16[3,2,80,768]{3,2,1,0:T(8,128)(2,1)}, u32[]{:S(2)}, u32[]{:S(2)}) %collective-permute-start.12) | collective-permute-done | bytes 737312 | tf_op jit(solution)/shard_map/ppermute | solution.py:453
  121.7 5.5 %collective-permute-start.20 = (bf16[4,528,128]{2,1,0:T(8,128)(2,1)}, bf16[4,528,128]{2,1,0:T(8,128)(2,1)}, u32[]{:S(2)}, u32[]{:S(2)}) collective-permute-start(bf16[4,528,128]{2,1,0:T(8,128)(2,1)} %collective-permute-done.19.refs_2_), channel_id=1, source_target_pairs={{0,4},{1,5},{2,6},{3,7},{4,0},{5,1},{6,2},{7,3},{8,12},{9,13},{10,... | collective-permute-start | bytes 1622024 | tf_op jit(solution)/shard_map/ppermute | solution.py:453
  127.2 9.3 %collective-permute-done.6.refs_5_ = bf16[3,2,80,768]{3,2,1,0:T(8,128)(2,1)} collective-permute-done((bf16[3,2,80,768]{3,2,1,0:T(8,128)(2,1)}, bf16[3,2,80,768]{3,2,1,0:T(8,128)(2,1)}, u32[]{:S(2)}, u32[]{:S(2)}) %collective-permute-start.6) | collective-permute-done | bytes 737312 | tf_op jit(solution)/shard_map/ppermute | solution.py:453
  136.5 15.3 %collective-permute-done.30.refs_5_ = bf16[3,2,80,768]{3,2,1,0:T(8,128)(2,1)S(1)} collective-permute-done((bf16[3,2,80,768]{3,2,1,0:T(8,128)(2,1)S(1)}, bf16[3,2,80,768]{3,2,1,0:T(8,128)(2,1)S(1)}, u32[]{:S(2)}, u32[]{:S(2)}) %collective-permute-start.30) | collective-permute-done | bytes 737312 | tf_op jit(solution)/shard_map/ppermute | solution.py:453
  152.8 1.7 constant_dynamic-slice_fusion
  155.4 4.1 %bias_order.1 = (f32[4,256,1024]{2,1,0:T(8,128)S(1)}, f32[8,1024]{1,0:T(8,128)S(1)}) custom-call(s32[1]{0:T(128)} %bitcast.4.me_ref, s32[16]{0:T(128)S(1)} %copy-done.18, s32[16]{0:T(128)S(1)} %broadcast_xor_fusion.qsel_ref, bf16[4,528,128]{2,1,0:T(8,128)(2,1)S(1)} %copy-done.11, bf16[4,528,128]{2,1,0:T(8,128)(2,1)S(1)} %copy-done.17, ...), custom_call_target="tpu_custom_call" | custom-call | flops 8388608 | bytes 6291456 | tf_op jit(solution)/shard_map/bias_order/pallas_call | solution.py:201
  159.6 4.2 %heads.3 = (bf16[4,256,192]{2,1,0:T(8,128)(2,1)S(1)}, bf16[4,192,1024]{2,1,0:T(8,128)(2,1)S(1)}, bf16[4,1024,192]{2,1,0:T(8,128)(2,1)S(1)}, f32[4,64,768]{2,1,0:T(8,128)S(1)}) custom-call(bf16[6,80,768]{2,1,0:T(8,128)(2,1)S(1)} %pack.3.refs_0_, bf16[6,80,768]{2,1,0:T(8,128)(2,1)S(1)} %collective-permute-done.refs_1_, ...), custom_call_target="tpu_custom_call" | custom-call | flops 1207959552 | bytes 4718592 | tf_op jit(solution)/shard_map/heads/pallas_call | solution.py:272
  163.9 4.4 %heads.4 = (bf16[4,256,192]{2,1,0:T(8,128)(2,1)S(1)}, bf16[4,192,1024]{2,1,0:T(8,128)(2,1)S(1)}, bf16[4,1024,192]{2,1,0:T(8,128)(2,1)S(1)}, f32[4,64,768]{2,1,0:T(8,128)S(1)}) custom-call(bf16[6,80,768]{2,1,0:T(8,128)(2,1)S(1)} %pack.3.refs_0_, ...), custom_call_target="tpu_custom_call", output_to_operand_aliasing={{0}: (12, {}), {1}: (13, {}), {2}: (14, {}), {3}: (15, {})} | custom-call | flops 1207959552 | bytes 4718592 | tf_op jit(solution)/shard_map/heads/pallas_call | solution.py:272
  168.3 8.0 %attend.2 = (bf16[4,64,192]{2,1,0:T(8,128)(2,1)S(1)}, bf16[4,64,192]{2,1,0:T(8,128)(2,1)S(1)}, bf16[4,64,192]{2,1,0:T(8,128)(2,1)S(1)}, bf16[4,64,192]{2,1,0:T(8,128)(2,1)S(1)}) custom-call(bf16[4,256,192]{2,1,0:T(8,128)(2,1)S(1)} %get-tuple-element.62.q_ref, bf16[4,192,1024]{2,1,0:T(8,128)(2,1)S(1)} %get-tuple-element.63.k_ref, ...), custom_call_target="tpu_custom_call" | custom-call | flops 4294967296 | bytes 7340032 | tf_op jit(solution)/shard_map/attend/pallas_call | solution.py:325
  176.4 3.9 %heads.5 = (bf16[2,256,192]{2,1,0:T(8,128)(2,1)S(1)}, bf16[2,192,1024]{2,1,0:T(8,128)(2,1)S(1)}, bf16[2,1024,192]{2,1,0:T(8,128)(2,1)S(1)}, f32[2,64,768]{2,1,0:T(8,128)S(1)}) custom-call(bf16[6,80,768]{2,1,0:T(8,128)(2,1)S(1)} %pack.3.refs_0_, bf16[6,80,768]{2,1,0:T(8,128)(2,1)S(1)} %collective-permute-done.refs_1_, ...), custom_call_target="tpu_custom_call" | custom-call | flops 1207959552 | bytes 4718592 | tf_op jit(solution)/shard_map/heads/pallas_call | solution.py:272
  180.4 4.0 %attend.3 = (bf16[2,64,192]{2,1,0:T(8,128)(2,1)S(1)}, bf16[2,64,192]{2,1,0:T(8,128)(2,1)S(1)}, bf16[2,64,192]{2,1,0:T(8,128)(2,1)S(1)}, bf16[2,64,192]{2,1,0:T(8,128)(2,1)S(1)}) custom-call(bf16[2,256,192]{2,1,0:T(8,128)(2,1)S(1)} %get-tuple-element.87.q_ref, bf16[2,192,1024]{2,1,0:T(8,128)(2,1)S(1)} %get-tuple-element.88.k_ref, ...), custom_call_target="tpu_custom_call" | custom-call | flops 2147483648 | bytes 5767168 | tf_op jit(solution)/shard_map/attend/pallas_call | solution.py:325
  184.4 1.7 collective-permute-start.33
  186.5 1.8 collective-permute-start.23
  189.6 5.5 %collective-permute-done.35.refs_3_ = bf16[2,64,192]{2,1,0:T(8,128)(2,1)S(1)} collective-permute-done((bf16[2,64,192]{2,1,0:T(8,128)(2,1)S(1)}, bf16[2,64,192]{2,1,0:T(8,128)(2,1)S(1)}, u32[]{:S(2)}, u32[]{:S(2)}) %collective-permute-start.35) | collective-permute-done | bytes 49184 | tf_op jit(solution)/shard_map/ppermute | solution.py:453
  195.5 5.2 %collective-permute-start.36 = (bf16[2,16,768]{2,1,0:T(8,128)(2,1)S(1)}, bf16[2,16,768]{2,1,0:T(8,128)(2,1)S(1)}, u32[]{:S(2)}, u32[]{:S(2)}) collective-permute-start(bf16[2,16,768]{2,1,0:T(8,128)(2,1)S(1)} %get-tuple-element.96), channel_id=1, source_target_pairs={{0,4},{1,5},{2,6},{3,7},{4,0},{5,1},{6,2},{7,3},{8,12},{9,13},{10,... | collective-permute-start | bytes 147464 | tf_op jit(solution)/shard_map/ppermute | solution.py:453
  201.5 3.9 %collective-permute-start.25 = (bf16[4,16,768]{2,1,0:T(8,128)(2,1)S(1)}, bf16[4,16,768]{2,1,0:T(8,128)(2,1)S(1)}, u32[]{:S(2)}, u32[]{:S(2)}) collective-permute-start(bf16[4,16,768]{2,1,0:T(8,128)(2,1)S(1)} %get-tuple-element.78), channel_id=1, source_target_pairs={{0,8},{1,9},{2,10},{3,11},{4,12},{5,13},{6,14},{7,15},{8,0},{9,1},... | collective-permute-start | bytes 294920 | tf_op jit(solution)/shard_map/ppermute | solution.py:453
  206.9 2.3 %collective-permute-start.38 = (bf16[2,16,768]{2,1,0:T(8,128)(2,1)S(1)}, bf16[2,16,768]{2,1,0:T(8,128)(2,1)S(1)}, u32[]{:S(2)}, u32[]{:S(2)}) collective-permute-start(bf16[2,16,768]{2,1,0:T(8,128)(2,1)S(1)} %get-tuple-element.98), channel_id=1, source_target_pairs={{0,12},{1,13},{2,14},{3,15},{4,8},{5,9},{6,10},{7,11},{8,4},{9,5},... | collective-permute-start | bytes 147464 | tf_op jit(solution)/shard_map/ppermute | solution.py:453
  209.2 9.1 %collective-permute-done.37.refs_6_ = bf16[2,16,768]{2,1,0:T(8,128)(2,1)S(1)} collective-permute-done((bf16[2,16,768]{2,1,0:T(8,128)(2,1)S(1)}, bf16[2,16,768]{2,1,0:T(8,128)(2,1)S(1)}, u32[]{:S(2)}, u32[]{:S(2)}) %collective-permute-start.37) | collective-permute-done | bytes 49184 | tf_op jit(solution)/shard_map/ppermute | solution.py:453
  (118 shorter events, 23.6 us)
Async XLA Ops:
  14.4 21.3 %collective-permute-start.10 = (bf16[2,80,768]{2,1,0:T(8,128)(2,1)}, bf16[2,80,768]{2,1,0:T(8,128)(2,1)S(1)}, u32[]{:S(2)}, u32[]{:S(2)}) collective-permute-start(bf16[2,80,768]{2,1,0:T(8,128)(2,1)} %get-tuple-element.56), channel_id=1, source_target_pairs={{0,8},{1,9},{2,10},{3,11},{4,12},{5,13},{6,14},{7,15},{8,0},{9,1},... | collective-permute-start | bytes 737288 | tf_op jit(solution)/shard_map/ppermute | solution.py:453
  18.1 19.4 %collective-permute-start.11 = (bf16[2,80,768]{2,1,0:T(8,128)(2,1)}, bf16[2,80,768]{2,1,0:T(8,128)(2,1)S(1)}, u32[]{:S(2)}, u32[]{:S(2)}) collective-permute-start(bf16[2,80,768]{2,1,0:T(8,128)(2,1)} %get-tuple-element.57), channel_id=1, source_target_pairs={{0,12},{1,13},{2,14},{3,15},{4,8},{5,9},{6,10},{7,11},{8,4},{9,5},... | collective-permute-start | bytes 737288 | tf_op jit(solution)/shard_map/ppermute | solution.py:453
  21.0 19.6 %collective-permute-start.9 = (bf16[2,80,768]{2,1,0:T(8,128)(2,1)}, bf16[2,80,768]{2,1,0:T(8,128)(2,1)S(1)}, u32[]{:S(2)}, u32[]{:S(2)}) collective-permute-start(bf16[2,80,768]{2,1,0:T(8,128)(2,1)} %get-tuple-element.55), channel_id=1, source_target_pairs={{0,4},{1,5},{2,6},{3,7},{4,0},{5,1},{6,2},{7,3},{8,12},{9,13},{10,... | collective-permute-start | bytes 737288 | tf_op jit(solution)/shard_map/ppermute | solution.py:453
  25.7 20.1 %collective-permute-start.3 = (bf16[2,80,768]{2,1,0:T(8,128)(2,1)S(1)}, bf16[2,80,768]{2,1,0:T(8,128)(2,1)S(1)}, u32[]{:S(2)}, u32[]{:S(2)}) collective-permute-start(bf16[2,80,768]{2,1,0:T(8,128)(2,1)S(1)} %get-tuple-element.52), channel_id=1, source_target_pairs={{0,4},{1,5},{2,6},{3,7},{4,0},{5,1},{6,2},{7,3},{8,12},{9,13},{10,... | collective-permute-start | bytes 737288 | tf_op jit(solution)/shard_map/ppermute | solution.py:453
  26.8 30.0 %collective-permute-start.4 = (bf16[2,80,768]{2,1,0:T(8,128)(2,1)S(1)}, bf16[2,80,768]{2,1,0:T(8,128)(2,1)S(1)}, u32[]{:S(2)}, u32[]{:S(2)}) collective-permute-start(bf16[2,80,768]{2,1,0:T(8,128)(2,1)S(1)} %get-tuple-element.53), channel_id=1, source_target_pairs={{0,8},{1,9},{2,10},{3,11},{4,12},{5,13},{6,14},{7,15},{8,0},{9,1},... | collective-permute-start | bytes 737288 | tf_op jit(solution)/shard_map/ppermute | solution.py:453
  35.7 69.9 %collective-permute-start = (bf16[6,80,768]{2,1,0:T(8,128)(2,1)S(1)}, bf16[6,80,768]{2,1,0:T(8,128)(2,1)S(1)}, u32[]{:S(2)}, u32[]{:S(2)}) collective-permute-start(bf16[6,80,768]{2,1,0:T(8,128)(2,1)S(1)} %pack.3.refs_0_), channel_id=1, source_target_pairs={{0,2},{1,3},{2,0},{3,1},{4,6},{5,7},{6,4},{7,5},{8,10},{9,11},{10,... | collective-permute-start | bytes 2211848 | tf_op jit(solution)/shard_map/ppermute | solution.py:453
  37.5 20.0 %collective-permute-start.5 = (bf16[2,80,768]{2,1,0:T(8,128)(2,1)S(1)}, bf16[2,80,768]{2,1,0:T(8,128)(2,1)S(1)}, u32[]{:S(2)}, u32[]{:S(2)}) collective-permute-start(bf16[2,80,768]{2,1,0:T(8,128)(2,1)S(1)} %get-tuple-element.54), channel_id=1, source_target_pairs={{0,12},{1,13},{2,14},{3,15},{4,8},{5,9},{6,10},{7,11},{8,4},{9,5},... | collective-permute-start | bytes 737288 | tf_op jit(solution)/shard_map/ppermute | solution.py:453
  40.6 35.5 %collective-permute-start.27 = (bf16[2,80,768]{2,1,0:T(8,128)(2,1)S(1)}, bf16[2,80,768]{2,1,0:T(8,128)(2,1)S(1)}, u32[]{:S(2)}, u32[]{:S(2)}) collective-permute-start(bf16[2,80,768]{2,1,0:T(8,128)(2,1)S(1)} %get-tuple-element.80), channel_id=1, source_target_pairs={{0,4},{1,5},{2,6},{3,7},{4,0},{5,1},{6,2},{7,3},{8,12},{9,13},{10,... | collective-permute-start | bytes 737288 | tf_op jit(solution)/shard_map/ppermute | solution.py:453
  45.9 57.3 %collective-permute-start.19 = (bf16[4,528,128]{2,1,0:T(8,128)(2,1)S(1)}, bf16[4,528,128]{2,1,0:T(8,128)(2,1)}, u32[]{:S(2)}, u32[]{:S(2)}) collective-permute-start(bf16[4,528,128]{2,1,0:T(8,128)(2,1)S(1)} %stack.6.refs_0_), channel_id=1, source_target_pairs={{0,8},{1,9},{2,10},{3,11},{4,12},{5,13},{6,14},{7,15},{8,0},{9,1},... | collective-permute-start | bytes 1622024 | tf_op jit(solution)/shard_map/ppermute | solution.py:453
  56.8 47.6 %collective-permute-start.18 = (bf16[4,528,128]{2,1,0:T(8,128)(2,1)S(1)}, bf16[4,528,128]{2,1,0:T(8,128)(2,1)S(1)}, u32[]{:S(2)}, u32[]{:S(2)}) collective-permute-start(bf16[4,528,128]{2,1,0:T(8,128)(2,1)S(1)} %stack.6.refs_0_), channel_id=1, source_target_pairs={{0,4},{1,5},{2,6},{3,7},{4,0},{5,1},{6,2},{7,3},{8,12},{9,13},{10,... | collective-permute-start | bytes 1622024 | tf_op jit(solution)/shard_map/ppermute | solution.py:453
  57.6 43.5 %collective-permute-start.28 = (bf16[2,80,768]{2,1,0:T(8,128)(2,1)S(1)}, bf16[2,80,768]{2,1,0:T(8,128)(2,1)S(1)}, u32[]{:S(2)}, u32[]{:S(2)}) collective-permute-start(bf16[2,80,768]{2,1,0:T(8,128)(2,1)S(1)} %get-tuple-element.81), channel_id=1, source_target_pairs={{0,8},{1,9},{2,10},{3,11},{4,12},{5,13},{6,14},{7,15},{8,0},{9,1},... | collective-permute-start | bytes 737288 | tf_op jit(solution)/shard_map/ppermute | solution.py:453
  76.1 25.1 %collective-permute-start.29 = (bf16[2,80,768]{2,1,0:T(8,128)(2,1)S(1)}, bf16[2,80,768]{2,1,0:T(8,128)(2,1)S(1)}, u32[]{:S(2)}, u32[]{:S(2)}) collective-permute-start(bf16[2,80,768]{2,1,0:T(8,128)(2,1)S(1)} %get-tuple-element.82), channel_id=1, source_target_pairs={{0,12},{1,13},{2,14},{3,15},{4,8},{5,9},{6,10},{7,11},{8,4},{9,5},... | collective-permute-start | bytes 737288 | tf_op jit(solution)/shard_map/ppermute | solution.py:453
  101.2 19.5 %collective-permute-start.12 = (bf16[3,2,80,768]{3,2,1,0:T(8,128)(2,1)S(1)}, bf16[3,2,80,768]{3,2,1,0:T(8,128)(2,1)}, u32[]{:S(2)}, u32[]{:S(2)}) collective-permute-start(bf16[3,2,80,768]{3,2,1,0:T(8,128)(2,1)S(1)} %stack.5.refs_4_), channel_id=1, source_target_pairs={{0,2},{1,3},{2,0},{3,1},{4,6},{5,7},{6,4},{7,5},{8,10},{9,11},{10,... | collective-permute-start | bytes 2211848 | tf_op jit(solution)/shard_map/ppermute | solution.py:453
  103.1 17.6 %collective-permute-start.13 = (bf16[3,2,80,768]{3,2,1,0:T(8,128)(2,1)S(1)}, bf16[3,2,80,768]{3,2,1,0:T(8,128)(2,1)S(1)}, u32[]{:S(2)}, u32[]{:S(2)}) collective-permute-start(bf16[3,2,80,768]{3,2,1,0:T(8,128)(2,1)S(1)} %stack.5.refs_4_), channel_id=1, source_target_pairs={{0,1},{1,0},{2,3},{3,2},{4,5},{5,4},{6,7},{7,6},{8,9},{9,8},{10,11... | collective-permute-start | bytes 2211848 | tf_op jit(solution)/shard_map/ppermute | solution.py:453
  105.3 31.3 %collective-permute-start.6 = (bf16[3,2,80,768]{3,2,1,0:T(8,128)(2,1)}, bf16[3,2,80,768]{3,2,1,0:T(8,128)(2,1)}, u32[]{:S(2)}, u32[]{:S(2)}) collective-permute-start(bf16[3,2,80,768]{3,2,1,0:T(8,128)(2,1)} %stack.4.refs_4_), channel_id=1, source_target_pairs={{0,2},{1,3},{2,0},{3,1},{4,6},{5,7},{6,4},{7,5},{8,10},{9,11},{10,... | collective-permute-start | bytes 2211848 | tf_op jit(solution)/shard_map/ppermute | solution.py:453
  105.6 46.2 %collective-permute-start.30 = (bf16[3,2,80,768]{3,2,1,0:T(8,128)(2,1)S(1)}, bf16[3,2,80,768]{3,2,1,0:T(8,128)(2,1)S(1)}, u32[]{:S(2)}, u32[]{:S(2)}) collective-permute-start(bf16[3,2,80,768]{3,2,1,0:T(8,128)(2,1)S(1)} %stack.7.refs_4_), channel_id=1, source_target_pairs={{0,2},{1,3},{2,0},{3,1},{4,6},{5,7},{6,4},{7,5},{8,10},{9,11},{10,... | collective-permute-start | bytes 2211848 | tf_op jit(solution)/shard_map/ppermute | solution.py:453
  107.3 47.8 %collective-permute-start.2 = (bf16[6,80,768]{2,1,0:T(8,128)(2,1)S(1)}, bf16[6,80,768]{2,1,0:T(8,128)(2,1)}, u32[]{:S(2)}, u32[]{:S(2)}) collective-permute-start(bf16[6,80,768]{2,1,0:T(8,128)(2,1)S(1)} %collective-permute-done.refs_1_), channel_id=1, source_target_pairs={{0,1},{1,0},{2,3},{3,2},{4,5},{5,4},{6,7},{7,6},{8,9},{9,8},{10,11... | collective-permute-start | bytes 2211848 | tf_op jit(solution)/shard_map/ppermute | solution.py:453
  120.7 38.9 %collective-permute-start.14 = (bf16[3,2,80,768]{3,2,1,0:T(8,128)(2,1)}, bf16[3,2,80,768]{3,2,1,0:T(8,128)(2,1)}, u32[]{:S(2)}, u32[]{:S(2)}) collective-permute-start(bf16[3,2,80,768]{3,2,1,0:T(8,128)(2,1)} %collective-permute-done.12.refs_5_), channel_id=1, source_target_pairs={{0,1},{1,0},{2,3},{3,2},{4,5},{5,4},{6,7},{7,6},{8,9},{9,8},{10,11... | collective-permute-start | bytes 2211848 | tf_op jit(solution)/shard_map/ppermute | solution.py:453
  121.7 32.9 %collective-permute-start.20 = (bf16[4,528,128]{2,1,0:T(8,128)(2,1)}, bf16[4,528,128]{2,1,0:T(8,128)(2,1)}, u32[]{:S(2)}, u32[]{:S(2)}) collective-permute-start(bf16[4,528,128]{2,1,0:T(8,128)(2,1)} %collective-permute-done.19.refs_2_), channel_id=1, source_target_pairs={{0,4},{1,5},{2,6},{3,7},{4,0},{5,1},{6,2},{7,3},{8,12},{9,13},{10,... | collective-permute-start | bytes 1622024 | tf_op jit(solution)/shard_map/ppermute | solution.py:453
  136.5 27.3 %collective-permute-start.7 = (bf16[3,2,80,768]{3,2,1,0:T(8,128)(2,1)}, bf16[3,2,80,768]{3,2,1,0:T(8,128)(2,1)}, u32[]{:S(2)}, u32[]{:S(2)}) collective-permute-start(bf16[3,2,80,768]{3,2,1,0:T(8,128)(2,1)} %stack.4.refs_4_), channel_id=1, source_target_pairs={{0,1},{1,0},{2,3},{3,2},{4,5},{5,4},{6,7},{7,6},{8,9},{9,8},{10,11... | collective-permute-start | bytes 2211848 | tf_op jit(solution)/shard_map/ppermute | solution.py:453
  152.8 11.1 %collective-permute-start.8 = (bf16[3,2,80,768]{3,2,1,0:T(8,128)(2,1)}, bf16[3,2,80,768]{3,2,1,0:T(8,128)(2,1)}, u32[]{:S(2)}, u32[]{:S(2)}) collective-permute-start(bf16[3,2,80,768]{3,2,1,0:T(8,128)(2,1)} %collective-permute-done.6.refs_5_), channel_id=1, source_target_pairs={{0,1},{1,0},{2,3},{3,2},{4,5},{5,4},{6,7},{7,6},{8,9},{9,8},{10,11... | collective-permute-start | bytes 2211848 | tf_op jit(solution)/shard_map/ppermute | solution.py:453
  154.5 21.8 %collective-permute-start.31 = (bf16[3,2,80,768]{3,2,1,0:T(8,128)(2,1)S(1)}, bf16[3,2,80,768]{3,2,1,0:T(8,128)(2,1)S(1)}, u32[]{:S(2)}, u32[]{:S(2)}) collective-permute-start(bf16[3,2,80,768]{3,2,1,0:T(8,128)(2,1)S(1)} %copy-done.7), channel_id=1, source_target_pairs={{0,1},{1,0},{2,3},{3,2},{4,5},{5,4},{6,7},{7,6},{8,9},{9,8},{10,11... | collective-permute-start | bytes 2211848 | tf_op jit(solution)/shard_map/ppermute | solution.py:453
  155.1 21.3 %collective-permute-start.32 = (bf16[3,2,80,768]{3,2,1,0:T(8,128)(2,1)}, bf16[3,2,80,768]{3,2,1,0:T(8,128)(2,1)S(1)}, u32[]{:S(2)}, u32[]{:S(2)}) collective-permute-start(bf16[3,2,80,768]{3,2,1,0:T(8,128)(2,1)} %copy-done.12), channel_id=1, source_target_pairs={{0,1},{1,0},{2,3},{3,2},{4,5},{5,4},{6,7},{7,6},{8,9},{9,8},{10,11... | collective-permute-start | bytes 2211848 | tf_op jit(solution)/shard_map/ppermute | solution.py:453
  186.1 14.6 %collective-permute-start.21 = (bf16[4,64,192]{2,1,0:T(8,128)(2,1)S(1)}, bf16[4,64,192]{2,1,0:T(8,128)(2,1)S(1)}, u32[]{:S(2)}, u32[]{:S(2)}) collective-permute-start(bf16[4,64,192]{2,1,0:T(8,128)(2,1)S(1)} %get-tuple-element.72), channel_id=1, source_target_pairs={{0,2},{1,3},{2,0},{3,1},{4,6},{5,7},{6,4},{7,5},{8,10},{9,11},{10,... | collective-permute-start | bytes 294920 | tf_op jit(solution)/shard_map/ppermute | solution.py:453
  186.5 14.2 %collective-permute-start.22 = (bf16[4,64,192]{2,1,0:T(8,128)(2,1)S(1)}, bf16[4,64,192]{2,1,0:T(8,128)(2,1)S(1)}, u32[]{:S(2)}, u32[]{:S(2)}) collective-permute-start(bf16[4,64,192]{2,1,0:T(8,128)(2,1)S(1)} %get-tuple-element.73), channel_id=1, source_target_pairs={{0,1},{1,0},{2,3},{3,2},{4,5},{5,4},{6,7},{7,6},{8,9},{9,8},{10,11... | collective-permute-start | bytes 294920 | tf_op jit(solution)/shard_map/ppermute | solution.py:453
  186.5 14.2 %collective-permute-start.23 = (bf16[4,64,192]{2,1,0:T(8,128)(2,1)S(1)}, bf16[4,64,192]{2,1,0:T(8,128)(2,1)S(1)}, u32[]{:S(2)}, u32[]{:S(2)}) collective-permute-start(bf16[4,64,192]{2,1,0:T(8,128)(2,1)S(1)} %get-tuple-element.74), channel_id=1, source_target_pairs={{0,3},{1,2},{2,1},{3,0},{4,7},{5,6},{6,5},{7,4},{8,11},{9,10},{10,... | collective-permute-start | bytes 294920 | tf_op jit(solution)/shard_map/ppermute | solution.py:453
  195.5 11.4 %collective-permute-start.36 = (bf16[2,16,768]{2,1,0:T(8,128)(2,1)S(1)}, bf16[2,16,768]{2,1,0:T(8,128)(2,1)S(1)}, u32[]{:S(2)}, u32[]{:S(2)}) collective-permute-start(bf16[2,16,768]{2,1,0:T(8,128)(2,1)S(1)} %get-tuple-element.96), channel_id=1, source_target_pairs={{0,4},{1,5},{2,6},{3,7},{4,0},{5,1},{6,2},{7,3},{8,12},{9,13},{10,... | collective-permute-start | bytes 147464 | tf_op jit(solution)/shard_map/ppermute | solution.py:453
  201.4 16.9 %collective-permute-start.24 = (bf16[4,16,768]{2,1,0:T(8,128)(2,1)S(1)}, bf16[4,16,768]{2,1,0:T(8,128)(2,1)S(1)}, u32[]{:S(2)}, u32[]{:S(2)}) collective-permute-start(bf16[4,16,768]{2,1,0:T(8,128)(2,1)S(1)} %get-tuple-element.77), channel_id=1, source_target_pairs={{0,4},{1,5},{2,6},{3,7},{4,0},{5,1},{6,2},{7,3},{8,12},{9,13},{10,... | collective-permute-start | bytes 294920 | tf_op jit(solution)/shard_map/ppermute | solution.py:453
  201.5 16.8 %collective-permute-start.25 = (bf16[4,16,768]{2,1,0:T(8,128)(2,1)S(1)}, bf16[4,16,768]{2,1,0:T(8,128)(2,1)S(1)}, u32[]{:S(2)}, u32[]{:S(2)}) collective-permute-start(bf16[4,16,768]{2,1,0:T(8,128)(2,1)S(1)} %get-tuple-element.78), channel_id=1, source_target_pairs={{0,8},{1,9},{2,10},{3,11},{4,12},{5,13},{6,14},{7,15},{8,0},{9,1},... | collective-permute-start | bytes 294920 | tf_op jit(solution)/shard_map/ppermute | solution.py:453
  205.4 12.9 %collective-permute-start.26 = (bf16[4,16,768]{2,1,0:T(8,128)(2,1)S(1)}, bf16[4,16,768]{2,1,0:T(8,128)(2,1)S(1)}, u32[]{:S(2)}, u32[]{:S(2)}) collective-permute-start(bf16[4,16,768]{2,1,0:T(8,128)(2,1)S(1)} %get-tuple-element.79), channel_id=1, source_target_pairs={{0,12},{1,13},{2,14},{3,15},{4,8},{5,9},{6,10},{7,11},{8,4},{9,5},... | collective-permute-start | bytes 294920 | tf_op jit(solution)/shard_map/ppermute | solution.py:453
  205.8 12.4 %collective-permute-start.37 = (bf16[2,16,768]{2,1,0:T(8,128)(2,1)S(1)}, bf16[2,16,768]{2,1,0:T(8,128)(2,1)S(1)}, u32[]{:S(2)}, u32[]{:S(2)}) collective-permute-start(bf16[2,16,768]{2,1,0:T(8,128)(2,1)S(1)} %get-tuple-element.97), channel_id=1, source_target_pairs={{0,8},{1,9},{2,10},{3,11},{4,12},{5,13},{6,14},{7,15},{8,0},{9,1},... | collective-permute-start | bytes 147464 | tf_op jit(solution)/shard_map/ppermute | solution.py:453
  206.9 11.3 %collective-permute-start.38 = (bf16[2,16,768]{2,1,0:T(8,128)(2,1)S(1)}, bf16[2,16,768]{2,1,0:T(8,128)(2,1)S(1)}, u32[]{:S(2)}, u32[]{:S(2)}) collective-permute-start(bf16[2,16,768]{2,1,0:T(8,128)(2,1)S(1)} %get-tuple-element.98), channel_id=1, source_target_pairs={{0,12},{1,13},{2,14},{3,15},{4,8},{5,9},{6,10},{7,11},{8,4},{9,5},... | collective-permute-start | bytes 147464 | tf_op jit(solution)/shard_map/ppermute | solution.py:453
  (28 other events, 379.7 us)
